TPU v7x, 32 devices: a whole 2x2x4 slice. The times are simulated.
32 devices in a mesh: frame: 8 (over z, y), row: 4 (over x, core).
Axes of the slice: x: 2, y: 2, z: 4, core: 2. Of those that a mesh axis runs over, the one named last changes fastest.
Arguments:
- queries: bfloat16 [8, 640, 2560], P('frame', 'row'), may hold values from -6 to 6
- keys: bfloat16 [8, 640, 2560], P('frame', 'row'), may hold values from -6 to 6
- values: bfloat16 [8, 640, 2560], P('frame', 'row'), may hold values from -6 to 6
- band: int32 [8, 5], P('frame'), may hold values from -1 to 1, as said below
Outputs:
- attended: bfloat16 [8, 640, 2560], P('frame', 'row')
Inputs may be any that keep to these rules, and one draw needn't show every extreme that they name: band[f, 0] and band[f, 4] are -1 or 0; band[f, 1] and band[f, 3] are -1, 0 or 1; band[f, 2] is 0 or 1.
All inputs are finite; a program needn't handle non-finite values.
Results may differ from a plain program's by a relative error of at most 0.0033.
Values may be sent and summed in bfloat16 or wider, within the bound.
No kernel may reach another device: no remote copies, remote signals or barrier semaphores. Data moves between devices by JAX's collectives and lax.ppermute only.
A program may use at most 128 MiB of HBM per device.

v0:
```python
import math

import jax
import jax.numpy as jnp
from jax import lax
from jax.sharding import PartitionSpec as P

HEAD = 128


def passed_along(value, axis, by):
    count = lax.axis_size(axis)
    return lax.ppermute(value, axis, [(i, (i + by) % count) for i in range(count)])


def extended(block, sides, width):
    for axis, dim in sides:
        count = lax.axis_size(axis)
        forward = [(i, i + 1) for i in range(count - 1)]
        backward = [(target, source) for source, target in forward]
        low = lax.ppermute(
            lax.slice_in_dim(block, block.shape[dim] - width, None, axis=dim), axis, forward
        )
        high = lax.ppermute(lax.slice_in_dim(block, 0, width, axis=dim), axis, backward)
        block = jnp.concatenate([low, block, high], axis=dim)
    return block


def attend(query_tile, key_all, value_all, keep_mask):
    tile_rows = query_tile.shape[0]
    head_count = query_tile.shape[1] // HEAD
    group_size = math.gcd(head_count, 4)
    results = []
    for head_start in range(0, head_count, group_size):
        low_col = head_start * HEAD
        high_col = low_col + group_size * HEAD
        query_group = query_tile[:, low_col:high_col].reshape(tile_rows, group_size, HEAD)
        key_group = key_all[:, low_col:high_col].reshape(-1, group_size, HEAD)
        value_group = value_all[:, low_col:high_col].reshape(-1, group_size, HEAD)
        scores = jnp.einsum(
            "qgd,kgd->gqk", query_group, key_group, preferred_element_type=jnp.float32
        ) * HEAD ** (-0.5)
        scores = jnp.where(keep_mask[None, None, :], scores, -jnp.inf)
        largest = jnp.max(scores, axis=2, keepdims=True)
        expo = jnp.exp(scores - largest)
        total = jnp.sum(expo, axis=2, keepdims=True)
        weights = expo.astype(jnp.bfloat16)
        summed = jnp.einsum(
            "gqk,kgd->qgd", weights, value_group, preferred_element_type=jnp.float32
        )
        normed = summed / jnp.transpose(total, (1, 0, 2))
        results.append(normed.reshape(tile_rows, group_size * HEAD).astype(jnp.bfloat16))
    return jnp.concatenate(results, 1)


def per_device(queries, keys, values, band):
    tile_rows = queries.shape[1]
    kv_pair = jnp.stack((keys[0], values[0]))
    prior_pair = passed_along(kv_pair, "frame", 1)
    later_pair = passed_along(kv_pair, "frame", -1)
    near_frames = jnp.stack((prior_pair, kv_pair, later_pair))
    kv_block = extended(near_frames, (("row", 2),), tile_rows)
    distant_prior = passed_along(kv_pair, "frame", 2)
    distant_later = passed_along(kv_pair, "frame", -2)
    band_index = lax.axis_index("row")
    band_count = lax.axis_size("row")
    band_row = band[0]
    pieces = [distant_prior]
    keep_flags = [band_row[0] >= 0]
    for frame_step in (-1, 0, 1):
        pieces.append(kv_block[frame_step + 1])
        for band_step in (-1, 0, 1):
            inside = (band_index + band_step >= 0) & (band_index + band_step < band_count)
            keep_flags.append(inside & (abs(band_step) <= band_row[frame_step + 2]))
    pieces.append(distant_later)
    keep_flags.append(band_row[4] >= 0)
    keep_mask = jnp.repeat(jnp.stack(keep_flags), tile_rows)
    kv_all = jnp.concatenate(pieces, 1)
    attended = attend(queries[0], kv_all[0], kv_all[1], keep_mask)
    return attended[None]


def solution(mesh):
    return jax.shard_map(
        per_device,
        mesh=mesh,
        in_specs=(
            P("frame", "row", None),
            P("frame", "row", None),
            P("frame", "row", None),
            P("frame", None),
        ),
        out_specs=P("frame", "row", None),
        check_vma=False,
    )
```

profile of v0, /device:TPU:27, one launch (start us, length us, event | category | flops | bytes accessed | tf_op | source)
XLA Modules:
  0.0 248.5 jit_solution(16337086575201427072)
XLA Ops:
  0.0 1.2 constant_dynamic-update-slice_fusion.1
  1.2 1.2 constant_dynamic-update-slice_fusion
  2.4 1.3 collective-permute-start.1
  4.8 68.5 %collective-permute-done.1 = bf16[2,160,2560]{2,1,0:T(8,128)(2,1)S(1)} collective-permute-done((bf16[2,160,2560]{2,1,0:T(8,128)(2,1)S(1)}, bf16[2,160,2560]{2,1,0:T(8,128)(2,1)S(1)}, u32[]{:S(2)}, u32[]{:S(2)}) %collective-permute-start.1) | collective-permute-done | bytes 1638432 | tf_op jit(solution)/shard_map/ppermute | solution.py:13
  73.3 2.9 %collective-permute-done.2 = bf16[2,160,2560]{2,1,0:T(8,128)(2,1)S(1)} collective-permute-done((bf16[2,160,2560]{2,1,0:T(8,128)(2,1)S(1)}, bf16[2,160,2560]{2,1,0:T(8,128)(2,1)S(1)}, u32[]{:S(2)}, u32[]{:S(2)}) %collective-permute-start.2) | collective-permute-done | bytes 1638432 | tf_op jit(solution)/shard_map/ppermute | solution.py:13
  76.2 2.8 %pad_maximum_fusion.1 = bf16[3,2,160,2560]{3,2,1,0:T(8,128)(2,1)} fusion(bf16[1,2,160,2560]{3,2,1,0:T(8,128)(2,1)S(1)} %bitcast.270, bf16[1,2,160,2560]{3,2,1,0:T(8,128)(2,1)S(1)} %bitcast.262, bf16[1,2,160,2560]{3,2,1,0:T(8,128)(2,1)S(1)} %bitcast.268), kind=kLoop, calls=%fused_computation.9 | loop fusion | flops 4915200 | bytes 9830400 | tf_op jit(solution)/shard_map/stack | solution.py:61
  79.0 1.3 collective-permute-start.3
  80.3 5.3 %collective-permute-start.4 = (bf16[3,2,160,2560]{3,2,1,0:T(8,128)(2,1)}, bf16[3,2,160,2560]{3,2,1,0:T(8,128)(2,1)}, u32[]{:S(2)}, u32[]{:S(2)}) collective-permute-start(bf16[3,2,160,2560]{3,2,1,0:T(8,128)(2,1)} %pad_maximum_fusion.1), channel_id=1, source_target_pairs={{1,0},{2,1},{3,2},{5,4},{6,5},{7,6},{9,8},{10,9},{11,10},{13,12},{... | collective-permute-start | bytes 14745608 | tf_op jit(solution)/shard_map/ppermute | solution.py:24
  85.8 1.2 collective-permute-start.5
  92.9 2.2 slice_bitcast_fusion.6
  95.1 63.4 %collective-permute-done = bf16[2,160,2560]{2,1,0:T(8,128)(2,1)} collective-permute-done((bf16[2,160,2560]{2,1,0:T(8,128)(2,1)S(1)}, bf16[2,160,2560]{2,1,0:T(8,128)(2,1)}, u32[]{:S(2)}, u32[]{:S(2)}) %collective-permute-start) | collective-permute-done | bytes 1638432 | tf_op jit(solution)/shard_map/ppermute | solution.py:13
  158.6 2.7 %constant_dynamic-update-slice_fusion.3 = bf16[2,1760,2560]{2,1,0:T(8,128)(2,1)} fusion(bf16[2,160,2560]{2,1,0:T(8,128)(2,1)} %collective-permute-done), kind=kLoop, calls=%fused_computation.113 | loop fusion | bytes 3276800
  161.3 6.6 %pad_maximum_fusion = bf16[3,2,480,2560]{3,2,1,0:T(8,128)(2,1)S(1)} fusion(bf16[3,2,160,2560]{3,2,1,0:T(8,128)(2,1)} %collective-permute-done.4, bf16[1,2,160,2560]{3,2,1,0:T(8,128)(2,1)S(1)} %bitcast.271, bf16[1,2,160,2560]{3,2,1,0:T(8,128)(2,1)S(1)} %bitcast.263, bf16[1,2,160,2560]{3,2,1,0:T(8,128)(2,1)S(1)} %bitcast.269, ...), kind=kLoop, calls=%fused_computation | loop fusion | flops 73728000 | bytes 29491200 | tf_op jit(solution)/shard_map/concatenate | solution.py:25
  167.9 2.5 fusion.2
  170.4 2.6 %fusion.1 = bf16[2,1760,2560]{2,1,0:T(8,128)(2,1)} fusion(bf16[2,1760,2560]{2,1,0:T(8,128)(2,1)} %fusion.2, bf16[3,2,480,2560]{3,2,1,0:T(8,128)(2,1)S(1)} %pad_maximum_fusion), kind=kLoop, calls=%fused_computation.6 | loop fusion | bytes 9830400
  172.9 2.5 fusion
  175.4 2.7 %constant_dynamic-update-slice_fusion.2 = bf16[2,1760,2560]{2,1,0:T(8,128)(2,1)} fusion(bf16[2,1760,2560]{2,1,0:T(8,128)(2,1)} %fusion, bf16[2,160,2560]{2,1,0:T(8,128)(2,1)} %collective-permute-done.5), kind=kLoop, calls=%fused_computation.112 | loop fusion | bytes 3276800 | tf_op jit(solution)/shard_map/concatenate | solution.py:78
  178.1 6.8 %slice_bitcast_fusion = (bf16[1760,2560]{1,0:T(8,128)(2,1)S(1)}, bf16[1760,2560]{1,0:T(8,128)(2,1)S(1)}) fusion(bf16[2,1760,2560]{2,1,0:T(8,128)(2,1)} %constant_dynamic-update-slice_fusion.2), kind=kLoop, calls=%fused_computation.1 | loop fusion | bytes 36044800 | tf_op jit(solution)/shard_map/squeeze | solution.py:79
  184.9 6.3 %fusion.133 = (bf16[1760,512]{1,0:T(8,128)(2,1)}, bf16[1760,512]{1,0:T(8,128)(2,1)}, bf16[1760,512]{1,0:T(8,128)(2,1)}, bf16[1760,512]{1,0:T(8,128)(2,1)}, bf16[...) fusion(bf16[1760,2560]{1,0:T(8,128)(2,1)S(1)} %get-tuple-elemen, ...), kind=kLoop, calls=%fused_computation.124 | loop fusion | bytes 36044800 | tf_op jit(solution)/shard_map/slice | solution.py:39
  191.2 2.8 %copy.6 = bf16[1760,512]{0,1:T(8,128)(2,1)S(1)} copy(bf16[1760,512]{1,0:T(8,128)(2,1)} %get-tuple-element.39) | data formatting | bytes 3604480 | tf_op jit(solution)/shard_map/slice | solution.py:38
  194.0 3.9 %copy.30 = bf16[1760,512]{0,1:T(8,128)(2,1)} copy(bf16[1760,512]{1,0:T(8,128)(2,1)} %get-tuple-element.42) | data formatting | bytes 3604480 | tf_op jit(solution)/shard_map/slice | solution.py:38
  197.9 3.8 %copy.24 = bf16[1760,512]{0,1:T(8,128)(2,1)} copy(bf16[1760,512]{1,0:T(8,128)(2,1)} %get-tuple-element.43) | data formatting | bytes 3604480 | tf_op jit(solution)/shard_map/slice | solution.py:38
  201.7 3.8 %copy.18 = bf16[1760,512]{0,1:T(8,128)(2,1)} copy(bf16[1760,512]{1,0:T(8,128)(2,1)} %get-tuple-element.41) | data formatting | bytes 3604480 | tf_op jit(solution)/shard_map/slice | solution.py:38
  205.5 3.8 %copy.12 = bf16[1760,512]{0,1:T(8,128)(2,1)} copy(bf16[1760,512]{1,0:T(8,128)(2,1)} %get-tuple-element.40) | data formatting | bytes 3604480 | tf_op jit(solution)/shard_map/slice | solution.py:38
  209.3 3.8 %copy.29 = bf16[1760,512]{0,1:T(8,128)(2,1)} copy(bf16[1760,512]{1,0:T(8,128)(2,1)} %get-tuple-element.17) | data formatting | bytes 3604480 | tf_op jit(solution)/shard_map/slice | solution.py:39
  213.1 3.9 %copy.23 = bf16[1760,512]{0,1:T(8,128)(2,1)} copy(bf16[1760,512]{1,0:T(8,128)(2,1)} %get-tuple-element.18) | data formatting | bytes 3604480 | tf_op jit(solution)/shard_map/slice | solution.py:39
  217.0 3.8 %copy.17 = bf16[1760,512]{0,1:T(8,128)(2,1)} copy(bf16[1760,512]{1,0:T(8,128)(2,1)} %get-tuple-element.19) | data formatting | bytes 3604480 | tf_op jit(solution)/shard_map/slice | solution.py:39
  220.8 3.8 %copy.11 = bf16[1760,512]{0,1:T(8,128)(2,1)} copy(bf16[1760,512]{1,0:T(8,128)(2,1)} %get-tuple-element.20) | data formatting | bytes 3604480 | tf_op jit(solution)/shard_map/slice | solution.py:39
  224.6 3.8 %copy.5 = bf16[1760,512]{0,1:T(8,128)(2,1)} copy(bf16[1760,512]{1,0:T(8,128)(2,1)} %get-tuple-element.21) | data formatting | bytes 3604480 | tf_op jit(solution)/shard_map/slice | solution.py:39
  232.3 1.4 bitcast_reduce_fusion
  233.8 3.8 %fusion.16 = (f32[4,160]{1,0:T(4,128)S(1)}, f32[4,160]{1,0:T(4,128)S(1)}, f32[4,160]{1,0:T(4,128)S(1)}, f32[4,160]{1,0:T(4,128)S(1)}, f32[4,160]{1,0:T(4,128)S(1)}, /*index=5*/f32[4,1760,160]{1,2,0:T(8,128)S(1)}) fusion(f32[4,1760,160]{1,2,0:T(8,128)S(1)} %get-tuple-element.37, f32[4,160]{1,0:T(4,128)S(1)} %get-tuple-element.10, ...), kind=kOutput, calls=%fused_computation.38 | convolution fusion | flops 307504000 | bytes 24513760 | tf_op jit(solution)/shard_map/qgd,kgd->gqk/dot_general | solution.py:40
  240.2 3.2 %fusion.14 = (f32[4,160]{1,0:T(4,128)S(1)}, f32[4,160]{1,0:T(4,128)S(1)}, f32[4,160]{1,0:T(4,128)S(1)}) fusion(f32[4,1760,160]{1,2,0:T(8,128)S(1)} %fusion.111, f32[4,160]{1,0:T(4,128)S(1)} %get-tuple-element.8, pred[1760]{0:T(1024)(128)(4,1)S(1)} %broadcast_in_dim.57, f32[4,160]{1,0:T(4,128)S(1)} %get-tuple-element.6, ...), kind=kLoop, calls=%fused_computation.36 | loop fusion | flops 13514880 | bytes 13533920 | tf_op jit(solution)/shard_map/reduce_sum | solution.py:46
  (56 shorter events, 13.7 us)
Async XLA Ops:
  2.4 70.9 %collective-permute-start.1 = (bf16[2,160,2560]{2,1,0:T(8,128)(2,1)S(1)}, bf16[2,160,2560]{2,1,0:T(8,128)(2,1)S(1)}, u32[]{:S(2)}, u32[]{:S(2)}) collective-permute-start(bf16[2,160,2560]{2,1,0:T(8,128)(2,1)S(1)} %constant_dynamic-update-slice_fusion), channel_id=1, source_target_pairs={{0,4},{4,8},{8,12},{12,16},{16,20},{20,24},{24,28},{28,0},{1,5},{5... | collective-permute-start | bytes 4915208 | tf_op jit(solution)/shard_map/ppermute | solution.py:13
  3.7 72.5 %collective-permute-start.2 = (bf16[2,160,2560]{2,1,0:T(8,128)(2,1)S(1)}, bf16[2,160,2560]{2,1,0:T(8,128)(2,1)S(1)}, u32[]{:S(2)}, u32[]{:S(2)}) collective-permute-start(bf16[2,160,2560]{2,1,0:T(8,128)(2,1)S(1)} %constant_dynamic-update-slice_fusion), channel_id=1, source_target_pairs={{0,28},{4,0},{8,4},{12,8},{16,12},{20,16},{24,20},{28,24},{1,29},{... | collective-permute-start | bytes 4915208 | tf_op jit(solution)/shard_map/ppermute | solution.py:13
  76.2 2.8 %copy-start.3 = (bf16[2,160,2560]{2,1,0:T(8,128)(2,1)}, bf16[2,160,2560]{2,1,0:T(8,128)(2,1)S(1)}, u32[]{:S(2)}) copy-start(bf16[2,160,2560]{2,1,0:T(8,128)(2,1)S(1)} %collective-permute-done.2) | copy-start | bytes 4915204
  76.2 10.8 %copy-start.16 = (s32[1,5]{1,0:T(1,128)S(1)}, s32[1,5]{1,0:T(1,128)}, u32[]{:S(2)}) copy-start(s32[1,5]{1,0:T(1,128)} %param.7) | copy-start | bytes 64
  79.0 82.3 %collective-permute-start.3 = (bf16[3,2,160,2560]{3,2,1,0:T(8,128)(2,1)}, bf16[3,2,160,2560]{3,2,1,0:T(8,128)(2,1)}, u32[]{:S(2)}, u32[]{:S(2)}) collective-permute-start(bf16[3,2,160,2560]{3,2,1,0:T(8,128)(2,1)} %pad_maximum_fusion.1), channel_id=1, source_target_pairs={{0,1},{1,2},{2,3},{4,5},{5,6},{6,7},{8,9},{9,10},{10,11},{12,13},{... | collective-permute-start | bytes 14745608 | tf_op jit(solution)/shard_map/ppermute | solution.py:21
  80.3 81.0 %collective-permute-start.4 = (bf16[3,2,160,2560]{3,2,1,0:T(8,128)(2,1)}, bf16[3,2,160,2560]{3,2,1,0:T(8,128)(2,1)}, u32[]{:S(2)}, u32[]{:S(2)}) collective-permute-start(bf16[3,2,160,2560]{3,2,1,0:T(8,128)(2,1)} %pad_maximum_fusion.1), channel_id=1, source_target_pairs={{1,0},{2,1},{3,2},{5,4},{6,5},{7,6},{9,8},{10,9},{11,10},{13,12},{... | collective-permute-start | bytes 14745608 | tf_op jit(solution)/shard_map/ppermute | solution.py:24
  85.5 73.0 %collective-permute-start = (bf16[2,160,2560]{2,1,0:T(8,128)(2,1)S(1)}, bf16[2,160,2560]{2,1,0:T(8,128)(2,1)}, u32[]{:S(2)}, u32[]{:S(2)}) collective-permute-start(bf16[2,160,2560]{2,1,0:T(8,128)(2,1)S(1)} %constant_dynamic-update-slice_fusion), channel_id=1, source_target_pairs={{0,8},{4,12},{8,16},{12,20},{16,24},{20,28},{24,0},{28,4},{1,9},{5... | collective-permute-start | bytes 4915208 | tf_op jit(solution)/shard_map/ppermute | solution.py:13
  85.8 89.6 %collective-permute-start.5 = (bf16[2,160,2560]{2,1,0:T(8,128)(2,1)S(1)}, bf16[2,160,2560]{2,1,0:T(8,128)(2,1)}, u32[]{:S(2)}, u32[]{:S(2)}) collective-permute-start(bf16[2,160,2560]{2,1,0:T(8,128)(2,1)S(1)} %constant_dynamic-update-slice_fusion), channel_id=1, source_target_pairs={{0,24},{4,28},{8,0},{12,4},{16,8},{20,12},{24,16},{28,20},{1,25},{... | collective-permute-start | bytes 4915208 | tf_op jit(solution)/shard_map/ppermute | solution.py:13
  92.9 68.4 %copy-start.4 = (bf16[2,160,2560]{2,1,0:T(8,128)(2,1)S(1)}, bf16[2,160,2560]{2,1,0:T(8,128)(2,1)}, u32[]{:S(2)}) copy-start(bf16[2,160,2560]{2,1,0:T(8,128)(2,1)} %copy-done.3) | copy-start | bytes 4915204
  217.0 11.5 %copy-start.12 = (bf16[20,4,8,128]{3,2,1,0:T(8,128)(2,1)S(1)}, bf16[20,4,8,128]{3,2,1,0:T(8,128)(2,1)}, u32[]{:S(2)}) copy-start(bf16[20,4,8,128]{3,2,1,0:T(8,128)(2,1)} %get-tuple-element.31) | copy-start | bytes 491524
  224.6 4.6 %copy-start.11 = (bf16[20,4,8,128]{3,2,1,0:T(8,128)(2,1)S(1)}, bf16[20,4,8,128]{3,2,1,0:T(8,128)(2,1)}, u32[]{:S(2)}) copy-start(bf16[20,4,8,128]{3,2,1,0:T(8,128)(2,1)} %get-tuple-element.27) | copy-start | bytes 491524
  228.5 1.5 copy-start.1
  229.2 1.6 copy-start
  230.7 1.5 copy-start.2
  230.7 1.5 copy-start.13
  232.3 1.5 copy-start.9
  232.3 1.5 copy-start.14
  233.8 3.8 %copy-start.10 = (bf16[1760,512]{0,1:T(8,128)(2,1)S(1)}, bf16[1760,512]{0,1:T(8,128)(2,1)}, u32[]{:S(2)}) copy-start(bf16[1760,512]{0,1:T(8,128)(2,1)} %copy.5) | copy-start | bytes 5406724
  237.6 1.5 copy-start.8
  240.2 3.2 %copy-start.7 = (bf16[1760,512]{0,1:T(8,128)(2,1)S(1)}, bf16[1760,512]{0,1:T(8,128)(2,1)}, u32[]{:S(2)}) copy-start(bf16[1760,512]{0,1:T(8,128)(2,1)} %copy.23) | copy-start | bytes 5406724
  243.4 1.5 copy-start.6
  244.9 1.5 copy-start.5
  247.6 0.9 copy-start.15
where the time goes:
time: 250 us; the launch traced here: 248 us
  waiting for transfers between devices  135 us (54%)
  local copies, waits for them, and re-layouts  72.6 us (29%)
  matrix products  12.8 us (5%)
  other arithmetic  12.6 us (5%)
  starting transfers between devices  10.4 us (4%)
  between operations  5.21 us (2%)
    ppermute x4, waiting for transfers between devices, passed_along(): lax.ppermute(value, axis, [(i, (i + by) % count) for i in range(count)])  135 us
    slice x6, local copies, waits for them, and re-layouts, attend(): value_group = value_all[:, low_col:high_col].reshape(-1, group_size, HEAD)  25.4 us
    slice x5, local copies, waits for them, and re-layouts, attend(): key_group = key_all[:, low_col:high_col].reshape(-1, group_size, HEAD)  18.1 us
    unnamed x44, local copies, waits for them, and re-layouts  17.4 us
    dot_general x5, matrix products, attend(): jnp.einsum('qgd,kgd->gqk', query_group, key_group, preferred_element_type...  7.42 us
    squeeze x1, local copies, waits for them, and re-layouts, per_device(): attended = attend(queries[0], kv_all[0], kv_all[1], keep_mask)  6.78 us
    concatenate x1, other arithmetic, extended(): block = jnp.concatenate([low, block, high], axis=dim)  6.61 us
    dot_general x5, matrix products, attend(): jnp.einsum('gqk,kgd->qgd', weights, value_group, preferred_element_type=j...  5.35 us
  transfers between devices with their start and end apart: 6, of which 3 were waited for; matrix products, arithmetic and copies ran while one was open for 8% of the time, Pallas kernels for 0%

commit v1 on v0

v1 whole, which is shorter than its diff:
```python
import functools

import jax
import jax.numpy as jnp
from jax import lax
from jax.experimental import pallas as pl
from jax.experimental.pallas import tpu as pltpu
from jax.sharding import PartitionSpec as P


HEAD = 128
LANES = 128
GROUP = 5
NEG = -1e30


def scores_of(query, key):
    return lax.dot_general(
        query, key, (((1,), (1,)), ((), ())), preferred_element_type=jnp.float32
    ) * HEAD ** (-0.5)


def softmax_part(query, keys, values, keeps):
    scores = [
        jnp.where(keep, scores_of(query, key), NEG) for key, keep in zip(keys, keeps)
    ]
    largest = functools.reduce(
        jnp.maximum, [jnp.max(score, axis=1, keepdims=True) for score in scores]
    )
    total = 0.0
    summed = 0.0
    for score, value in zip(scores, values):
        expo = jnp.exp(score - largest)
        total = total + jnp.sum(expo, axis=1, keepdims=True)
        summed = summed + jnp.dot(
            expo.astype(jnp.bfloat16), value, preferred_element_type=jnp.float32
        )
    return summed / total, largest + jnp.log(total)


def column(index):
    return slice(index * HEAD, (index + 1) * HEAD)


def store_lane(ref, head, lane_value, first):
    lanes = lax.broadcasted_iota(jnp.int32, ref.shape, 1)
    before = jnp.where(first, jnp.full(ref.shape, NEG, jnp.float32), ref[...])
    for at, value in enumerate(lane_value):
        before = jnp.where(lanes == head + at, value, before)
    ref[...] = before


def parts_kernel(query_count, key_count, group, keep_ref, *refs):
    queries = refs[:query_count]
    keys = refs[query_count : query_count + key_count]
    values = refs[query_count + key_count : query_count + 2 * key_count]
    outs = refs[query_count + 2 * key_count :]
    step = pl.program_id(0)
    for at in range(query_count):
        keeps = [keep_ref[at * key_count + i] != 0 for i in range(key_count)]
        logs = []
        for head in range(group):
            cols = column(head)
            attended, log_total = softmax_part(
                queries[at][:, cols],
                [key[:, cols] for key in keys],
                [value[:, cols] for value in values],
                keeps,
            )
            outs[2 * at][:, cols] = attended.astype(outs[2 * at].dtype)
            logs.append(log_total)
        store_lane(outs[2 * at + 1], step * group, logs, step == 0)


def wide_spec(rows, group):
    return pl.BlockSpec((None, rows, group * HEAD), lambda step: (0, 0, step))


def lane_spec(rows):
    return pl.BlockSpec((rows, LANES), lambda step: (0, 0))


def parts(queries, keys, values, keeps, out_types):
    rows, width = queries[0].shape[1:]
    steps = width // HEAD // GROUP
    wide = wide_spec(rows, GROUP)
    blocks = len(queries) * len(keys)
    return pl.pallas_call(
        functools.partial(parts_kernel, len(queries), len(keys), GROUP),
        grid=(steps,),
        in_specs=[pl.BlockSpec(memory_space=pltpu.SMEM)]
        + [wide] * (len(queries) + 2 * len(keys)),
        out_specs=[wide, lane_spec(rows)] * len(queries),
        out_shape=[
            item
            for kind in out_types
            for item in (
                jax.ShapeDtypeStruct((1, rows, width), kind),
                jax.ShapeDtypeStruct((rows, LANES), jnp.float32),
            )
        ],
        cost_estimate=pl.CostEstimate(
            flops=4 * rows * rows * width * blocks,
            bytes_accessed=2 * rows * width * (2 * len(queries) + 2 * len(keys)),
            transcendentals=rows * rows * width // HEAD * blocks,
        ),
    )(keeps, *queries, *keys, *values)


def shares(logs):
    largest = functools.reduce(jnp.maximum, logs)
    expos = [jnp.exp(log - largest) for log in logs]
    total = sum(expos)
    return [expo / total for expo in expos], largest + jnp.log(total)


def merge_kernel(count, group, keep_ref, *refs):
    blocks, log_refs = refs[:count], refs[count : 2 * count]
    out_ref, out_log_ref = refs[2 * count :]
    step = pl.program_id(0)
    logs = [
        jnp.where(keep_ref[i] != 0, log_ref[...], NEG) for i, log_ref in enumerate(log_refs)
    ]
    weights, log_total = shares(logs)
    out_log_ref[...] = log_total
    shift = lax.rem(LANES - step * group, LANES)
    weights = [pltpu.roll(weight, shift, 1) for weight in weights]
    for head in range(group):
        cols = column(head)
        out_ref[:, cols] = sum(
            weight[:, head : head + 1] * block[:, cols].astype(jnp.float32)
            for weight, block in zip(weights, blocks)
        ).astype(out_ref.dtype)


def merged(blocks, logs, keeps, kind):
    rows, width = blocks[0].shape[1:]
    wide = wide_spec(rows, GROUP)
    lane = lane_spec(rows)
    return pl.pallas_call(
        functools.partial(merge_kernel, len(blocks), GROUP),
        grid=(width // HEAD // GROUP,),
        in_specs=[pl.BlockSpec(memory_space=pltpu.SMEM)]
        + [wide] * len(blocks)
        + [lane] * len(blocks),
        out_specs=[wide, lane],
        out_shape=[
            jax.ShapeDtypeStruct((1, rows, width), kind),
            jax.ShapeDtypeStruct((rows, LANES), jnp.float32),
        ],
        cost_estimate=pl.CostEstimate(
            flops=2 * rows * width * len(blocks),
            bytes_accessed=2 * rows * width * (len(blocks) + 1),
            transcendentals=0,
        ),
    )(keeps, *blocks, *logs)


def final_kernel(count, group, keep_ref, query_ref, key_ref, value_ref, *refs):
    blocks, log_refs, out_ref = refs[:count], refs[count : 2 * count], refs[2 * count]
    step = pl.program_id(0)
    shift = lax.rem(LANES - step * group, LANES)
    logs = [
        pltpu.roll(jnp.where(keep_ref[1 + i] != 0, log_ref[...], NEG), shift, 1)
        for i, log_ref in enumerate(log_refs)
    ]
    keep = keep_ref[0] != 0
    for head in range(group):
        cols = column(head)
        attended, log_own = softmax_part(
            query_ref[:, cols], [key_ref[:, cols]], [value_ref[:, cols]], [keep]
        )
        weights, _ = shares([log_own] + [log[:, head : head + 1] for log in logs])
        total = weights[0] * attended
        for weight, block in zip(weights[1:], blocks):
            total = total + weight * block[:, cols].astype(jnp.float32)
        out_ref[:, cols] = total.astype(out_ref.dtype)


def final(query, key, value, blocks, logs, keeps):
    rows, width = query.shape[1:]
    wide = wide_spec(rows, GROUP)
    lane = lane_spec(rows)
    return pl.pallas_call(
        functools.partial(final_kernel, len(blocks), GROUP),
        grid=(width // HEAD // GROUP,),
        in_specs=[pl.BlockSpec(memory_space=pltpu.SMEM)]
        + [wide] * (3 + len(blocks))
        + [lane] * len(blocks),
        out_specs=wide,
        out_shape=jax.ShapeDtypeStruct((1, rows, width), query.dtype),
        cost_estimate=pl.CostEstimate(
            flops=4 * rows * rows * width,
            bytes_accessed=2 * rows * width * (len(blocks) + 4),
            transcendentals=rows * rows * width // HEAD,
        ),
    )(keeps, query, key, value, *blocks, *logs)


def per_device(queries, keys, values, band):
    frames, bands = lax.axis_size("frame"), lax.axis_size("row")
    toward = [(f, (f + 2) % frames) if f % 2 else (f, (f - 2) % frames) for f in range(frames)]
    away = [(target, source) for source, target in toward]
    twin = [(f, f ^ 1) for f in range(frames)]
    even = [(r, r ^ 1) for r in range(bands)]
    odd = [(r, r + 1) for r in range(1, bands - 1, 2)]
    odd += [(target, source) for source, target in odd]

    key_one = lax.ppermute(keys, "frame", toward)
    value_one = lax.ppermute(values, "frame", toward)
    key_two = lax.ppermute(keys, "frame", away)
    value_two = lax.ppermute(values, "frame", away)
    query_twin = lax.ppermute(queries, "frame", twin)
    band_twin = lax.ppermute(band, "frame", twin)
    query_even = lax.ppermute(queries, "row", even)
    query_odd = lax.ppermute(queries, "row", odd)
    twin_even = lax.ppermute(query_twin, "row", even)
    twin_odd = lax.ppermute(query_twin, "row", odd)

    is_odd = lax.axis_index("frame") % 2 == 1
    row = lax.axis_index("row")
    own, other = band[0], band_twin[0]
    has_odd = ((row > 0) & (row < bands - 1)).astype(jnp.int32)
    one = jnp.int32(1)
    other_own = jnp.where(is_odd, other[3], other[1])
    other_one = jnp.where(is_odd, other[1], other[3])
    own_one = jnp.where(is_odd, own[0], own[4])
    own_two = jnp.where(is_odd, own[4], own[0])

    def flags(*items):
        return jnp.stack([jnp.asarray(item).astype(jnp.int32) for item in items])

    half = jnp.bfloat16
    beside = own[2] >= 1
    even_part, even_log, odd_part, odd_log = parts(
        [query_even, query_odd], [keys], [values], flags(beside, beside), [half, half]
    )
    from_even = lax.ppermute((even_part, even_log), "row", even)
    from_odd = lax.ppermute((odd_part, odd_log), "row", odd)

    keep_two = (other_own >= 1, other_one >= 1)
    tw_even, tw_even_log, tw_odd, tw_odd_log = parts(
        [twin_even, twin_odd],
        [keys, key_one],
        [values, value_one],
        flags(*keep_two, *keep_two),
        [half, half],
    )
    tw_from_even = lax.ppermute((tw_even, tw_even_log), "row", even)
    tw_from_odd = lax.ppermute((tw_odd, tw_odd_log), "row", odd)

    tw_part, tw_log, own_part, own_log = parts(
        [query_twin, queries],
        [keys, key_one],
        [values, value_one],
        flags(other_own >= 0, other_one >= 0, one, own_one >= 0),
        [jnp.float32, jnp.float32],
    )
    tw_all, tw_all_log = merged(
        [tw_part, tw_from_even[0], tw_from_odd[0]],
        [tw_log, tw_from_even[1], tw_from_odd[1]],
        flags(one, one, has_odd),
        half,
    )
    from_twin = lax.ppermute((tw_all, tw_all_log), "frame", twin)
    return final(
        queries,
        key_two,
        value_two,
        [own_part, from_even[0], from_odd[0], from_twin[0]],
        [own_log, from_even[1], from_odd[1], from_twin[1]],
        flags(own_two >= 0, one, one, has_odd, one),
    )


def solution(mesh):
    return jax.shard_map(
        per_device,
        mesh=mesh,
        in_specs=(
            P("frame", "row", None),
            P("frame", "row", None),
            P("frame", "row", None),
            P("frame", None),
        ),
        out_specs=P("frame", "row", None),
        check_vma=False,
    )
```

time: 250 us -> 122 us (0.49)
  the two profiles are of different devices: /device:TPU:27 before, /device:TPU:9 now
where the time goes in v1:
time: 122 us; the launch traced here: 121 us
  Pallas kernels  38.6 us (32%)
  waiting for transfers between devices  35.4 us (29%)
  starting transfers between devices  33.9 us (28%)
  between operations  5.79 us (5%)
  local copies, waits for them, and re-layouts  4.78 us (4%)
  other arithmetic  2.63 us (2%)
    pallas_call x3, Pallas kernels, parts(): pl.pallas_call(functools.partial(parts_kernel, len(queries), len(keys), G...  23.9 us
    ppermute x2, waiting for transfers between devices, per_device(): from_twin = lax.ppermute((tw_all, tw_all_log), 'frame', twin)  14.8 us
    ppermute x1, waiting for transfers between devices, per_device(): query_twin = lax.ppermute(queries, 'frame', twin)  14.7 us
    pallas_call x1, Pallas kernels, final(): pl.pallas_call(functools.partial(final_kernel, len(blocks), GROUP), grid=...  9.75 us
    ppermute x2, starting transfers between devices, per_device(): tw_from_odd = lax.ppermute((tw_odd, tw_odd_log), 'row', odd)  6.11 us
    ppermute x2, starting transfers between devices, per_device(): from_odd = lax.ppermute((odd_part, odd_log), 'row', odd)  5.56 us
    pallas_call x1, Pallas kernels, merged(): pl.pallas_call(functools.partial(merge_kernel, len(blocks), GROUP), grid=...  5 us
    ppermute x1, waiting for transfers between devices, per_device(): value_one = lax.ppermute(values, 'frame', toward)  3.67 us
  transfers between devices with their start and end apart: 20, of which 5 were waited for; matrix products, arithmetic and copies ran while one was open for 4% of the time, Pallas kernels for 24%

profile of v1, /device:TPU:9, one launch (start us, length us, event | category | flops | bytes accessed | tf_op | source)
XLA Modules:
  0.0 121.1 jit_solution(14785621479103656966)
XLA Ops:
  0.0 1.2 %collective-permute-start.3 = (bf16[1,160,2560]{2,1,0:T(8,128)(2,1)}, bf16[1,160,2560]{2,1,0:T(8,128)(2,1)}, u32[]{:S(2)}, u32[]{:S(2)}) collective-permute-start(bf16[1,160,2560]{2,1,0:T(8,128)(2,1)} %query_ref.1), channel_id=1, source_target_pairs={{0,4},{4,0},{8,12},{12,8},{16,20},{20,16},{24,28},{28,24},{1,5},{5... | collective-permute-start | bytes 2457608 | tf_op jit(solution)/shard_map/ppermute | solution.py:213
  1.4 3.3 %collective-permute-start.5 = (bf16[1,160,2560]{2,1,0:T(8,128)(2,1)}, bf16[1,160,2560]{2,1,0:T(8,128)(2,1)S(1)}, u32[]{:S(2)}, u32[]{:S(2)}) collective-permute-start(bf16[1,160,2560]{2,1,0:T(8,128)(2,1)} %refs_4_.3), channel_id=1, source_target_pairs={{0,24},{4,12},{8,0},{12,20},{16,8},{20,28},{24,16},{28,4},{1,25},{... | collective-permute-start | bytes 2457608 | tf_op jit(solution)/shard_map/ppermute | solution.py:210
  4.7 14.7 %collective-permute-done.3.refs_0_ = bf16[1,160,2560]{2,1,0:T(8,128)(2,1)} collective-permute-done((bf16[1,160,2560]{2,1,0:T(8,128)(2,1)}, bf16[1,160,2560]{2,1,0:T(8,128)(2,1)}, u32[]{:S(2)}, u32[]{:S(2)}) %collective-permute-start.3) | collective-permute-done | bytes 819232 | tf_op jit(solution)/shard_map/ppermute | solution.py:213
  19.4 1.5 %collective-permute-start.10 = (bf16[1,160,2560]{2,1,0:T(8,128)(2,1)}, bf16[1,160,2560]{2,1,0:T(8,128)(2,1)}, u32[]{:S(2)}, u32[]{:S(2)}) collective-permute-start(bf16[1,160,2560]{2,1,0:T(8,128)(2,1)} %collective-permute-done.3.refs_0_), channel_id=1, source_target_pairs={{0,1},{1,0},{2,3},{3,2},{4,5},{5,4},{6,7},{7,6},{8,9},{9,8},{10,11... | collective-permute-start | bytes 2457608 | tf_op jit(solution)/shard_map/ppermute | solution.py:217
  21.0 3.0 %collective-permute-start.11 = (bf16[1,160,2560]{2,1,0:T(8,128)(2,1)}, bf16[1,160,2560]{2,1,0:T(8,128)(2,1)}, u32[]{:S(2)}, u32[]{:S(2)}) collective-permute-start(bf16[1,160,2560]{2,1,0:T(8,128)(2,1)} %collective-permute-done.3.refs_0_), channel_id=1, source_target_pairs={{1,2},{2,1},{5,6},{6,5},{9,10},{10,9},{13,14},{14,13},{17,18},{18,... | collective-permute-start | bytes 2457608 | tf_op jit(solution)/shard_map/ppermute | solution.py:218
  24.0 1.3 %collective-permute-start.2 = (s32[1,5]{1,0:T(1,128)}, s32[1,5]{1,0:T(1,128)S(1)}, u32[]{:S(2)}, u32[]{:S(2)}) collective-permute-start(s32[1,5]{1,0:T(1,128)} %param.7), channel_id=1, source_target_pairs={{0,4},{4,0},{8,12},{12,8},{16,20},{20,16},{24,28},{28,24},{1,5},{5... | collective-permute-start | bytes 68 | tf_op jit(solution)/shard_map/ppermute | solution.py:214
  25.3 1.6 %collective-permute-done.2 = s32[1,5]{1,0:T(1,128)S(1)} collective-permute-done((s32[1,5]{1,0:T(1,128)}, s32[1,5]{1,0:T(1,128)S(1)}, u32[]{:S(2)}, u32[]{:S(2)}) %collective-permute-start.2) | collective-permute-done | bytes 52 | tf_op jit(solution)/shard_map/ppermute | solution.py:214
  26.9 0.6 fusion.1
  30.1 3.4 %collective-permute-start.7 = (bf16[1,160,2560]{2,1,0:T(8,128)(2,1)}, bf16[1,160,2560]{2,1,0:T(8,128)(2,1)}, u32[]{:S(2)}, u32[]{:S(2)}) collective-permute-start(bf16[1,160,2560]{2,1,0:T(8,128)(2,1)} %query_ref.1), channel_id=1, source_target_pairs={{1,2},{2,1},{5,6},{6,5},{9,10},{10,9},{13,14},{14,13},{17,18},{18,... | collective-permute-start | bytes 2457608 | tf_op jit(solution)/shard_map/ppermute | solution.py:216
  33.5 0.7 add_convert_fusion.2.keep_ref
  34.2 3.7 %collective-permute-done.5.refs_5_ = bf16[1,160,2560]{2,1,0:T(8,128)(2,1)S(1)} collective-permute-done((bf16[1,160,2560]{2,1,0:T(8,128)(2,1)}, bf16[1,160,2560]{2,1,0:T(8,128)(2,1)S(1)}, u32[]{:S(2)}, u32[]{:S(2)}) %collective-permute-start.5) | collective-permute-done | bytes 819232 | tf_op jit(solution)/shard_map/ppermute | solution.py:210
  37.9 1.0 copy-done.3
  38.9 8.6 %shard_map.48 = (bf16[1,160,2560]{2,1,0:T(8,128)(2,1)}, f32[160,128]{1,0:T(8,128)}, bf16[1,160,2560]{2,1,0:T(8,128)(2,1)}, f32[160,128]{1,0:T(8,128)}) custom-call(s32[4]{0:T(128)} %add_convert_fusion.2.keep_ref, bf16[1,160,2560]{2,1,0:T(8,128)(2,1)} %collective-permute-done.10.refs_0_, bf16[1,160,2560]{2,1,0:T(8,128)(2,1)} %collective-permute-done.11.refs_1_, ...), custom_call_target="tpu_custom_call" | custom-call | flops 1048576000 | bytes 6553600 | tf_op jit(solution)/shard_map/pallas_call | solution.py:88
  47.4 1.8 %collective-permute-start.12 = (bf16[1,160,2560]{2,1,0:T(8,128)(2,1)}, bf16[1,160,2560]{2,1,0:T(8,128)(2,1)S(1)}, u32[]{:S(2)}, u32[]{:S(2)}) collective-permute-start(bf16[1,160,2560]{2,1,0:T(8,128)(2,1)} %get-tuple-element.23), channel_id=1, source_target_pairs={{0,1},{1,0},{2,3},{3,2},{4,5},{5,4},{6,7},{7,6},{8,9},{9,8},{10,11... | collective-permute-start | bytes 2457608 | tf_op jit(solution)/shard_map/ppermute | solution.py:249
  49.3 3.0 %collective-permute-start.13 = (bf16[1,160,2560]{2,1,0:T(8,128)(2,1)}, bf16[1,160,2560]{2,1,0:T(8,128)(2,1)S(1)}, u32[]{:S(2)}, u32[]{:S(2)}) collective-permute-start(bf16[1,160,2560]{2,1,0:T(8,128)(2,1)} %get-tuple-element.24), channel_id=1, source_target_pairs={{1,2},{2,1},{5,6},{6,5},{9,10},{10,9},{13,14},{14,13},{17,18},{18,... | collective-permute-start | bytes 2457608 | tf_op jit(solution)/shard_map/ppermute | solution.py:250
  52.3 1.3 %collective-permute-start = (bf16[1,160,2560]{2,1,0:T(8,128)(2,1)S(1)}, bf16[1,160,2560]{2,1,0:T(8,128)(2,1)}, u32[]{:S(2)}, u32[]{:S(2)}) collective-permute-start(bf16[1,160,2560]{2,1,0:T(8,128)(2,1)S(1)} %copy-done), channel_id=1, source_target_pairs={{24,0},{12,4},{0,8},{20,12},{8,16},{28,20},{16,24},{4,28},{25,1},{... | collective-permute-start | bytes 2457608 | tf_op jit(solution)/shard_map/ppermute | solution.py:211
  53.7 0.6 fusion
  55.5 0.6 stack.74.keep_ref
  56.7 0.7 add_convert_fusion.1.keep_ref
  57.3 0.7 add_convert_fusion.keep_ref
  58.0 3.1 %collective-permute-start.1 = (bf16[1,160,2560]{2,1,0:T(8,128)(2,1)S(1)}, bf16[1,160,2560]{2,1,0:T(8,128)(2,1)}, u32[]{:S(2)}, u32[]{:S(2)}) collective-permute-start(bf16[1,160,2560]{2,1,0:T(8,128)(2,1)S(1)} %copy-done.1), channel_id=1, source_target_pairs={{24,0},{12,4},{0,8},{20,12},{8,16},{28,20},{16,24},{4,28},{25,1},{... | collective-permute-start | bytes 2457608 | tf_op jit(solution)/shard_map/ppermute | solution.py:212
  61.2 6.7 %shard_map.47 = (bf16[1,160,2560]{2,1,0:T(8,128)(2,1)}, f32[160,128]{1,0:T(8,128)}, bf16[1,160,2560]{2,1,0:T(8,128)(2,1)}, f32[160,128]{1,0:T(8,128)}) custom-call(s32[2]{0:T(128)} %add_convert_fusion.1.keep_ref, bf16[1,160,2560]{2,1,0:T(8,128)(2,1)} %collective-permute-done.6.refs_0_, bf16[1,160,2560]{2,1,0:T(8,128)(2,1)} %collective-permute-done.7.refs_1_, ...), custom_call_target="tpu_custom_call" | custom-call | flops 524288000 | bytes 4915200 | tf_op jit(solution)/shard_map/pallas_call | solution.py:88
  67.9 3.1 %collective-permute-start.15 = (f32[160,128]{1,0:T(8,128)S(1)}, f32[160,128]{1,0:T(8,128)S(1)}, u32[]{:S(2)}, u32[]{:S(2)}) collective-permute-start(f32[160,128]{1,0:T(8,128)S(1)} %copy-done.14), channel_id=1, source_target_pairs={{1,2},{2,1},{5,6},{6,5},{9,10},{10,9},{13,14},{14,13},{17,18},{18,... | collective-permute-start | bytes 245768 | tf_op jit(solution)/shard_map/ppermute | solution.py:250
  71.0 8.6 %shard_map.46 = (f32[1,160,2560]{2,1,0:T(8,128)}, f32[160,128]{1,0:T(8,128)}, f32[1,160,2560]{2,1,0:T(8,128)}, f32[160,128]{1,0:T(8,128)}) custom-call(s32[4]{0:T(128)} %add_convert_fusion.keep_ref, bf16[1,160,2560]{2,1,0:T(8,128)(2,1)} %collective-permute-done.3.refs_0_, bf16[1,160,2560]{2,1,0:T(8,128)(2,1)} %query_ref.1, bf16[1,160,2560]{2,1,0:T(8,128)(2,1)} %refs_2_.5, ...), custom_call_target="tpu_custom_call" | custom-call | flops 1048576000 | bytes 6553600 | tf_op jit(solution)/shard_map/pallas_call | solution.py:88
  79.7 2.5 %collective-permute-start.9 = (bf16[1,160,2560]{2,1,0:T(8,128)(2,1)}, bf16[1,160,2560]{2,1,0:T(8,128)(2,1)}, u32[]{:S(2)}, u32[]{:S(2)}) collective-permute-start(bf16[1,160,2560]{2,1,0:T(8,128)(2,1)} %get-tuple-element.21), channel_id=1, source_target_pairs={{1,2},{2,1},{5,6},{6,5},{9,10},{10,9},{13,14},{14,13},{17,18},{18,... | collective-permute-start | bytes 2457608 | tf_op jit(solution)/shard_map/ppermute | solution.py:239
  82.2 1.0 copy-done.5
  83.2 5.0 %shard_map.49 = (bf16[1,160,2560]{2,1,0:T(8,128)(2,1)}, f32[160,128]{1,0:T(8,128)}) custom-call(s32[3]{0:T(128)} %stack.74.keep_ref, f32[1,160,2560]{2,1,0:T(8,128)} %get-tuple-element.22.refs_0_, bf16[1,160,2560]{2,1,0:T(8,128)(2,1)} %copy-done.4, bf16[1,160,2560]{2,1,0:T(8,128)(2,1)} %copy-done.5, f32[160,128]{1,0:T(8,128)} %get-tuple-element.25.refs_3_, ...), custom_call_target="tpu_custom_call" | custom-call | flops 2457600 | bytes 3276800 | tf_op jit(solution)/shard_map/pallas_call | solution.py:140
  89.5 3.1 %collective-permute-start.18 = (f32[160,128]{1,0:T(8,128)S(1)}, f32[160,128]{1,0:T(8,128)S(1)}, u32[]{:S(2)}, u32[]{:S(2)}) collective-permute-start(f32[160,128]{1,0:T(8,128)S(1)} %copy-done.13), channel_id=1, source_target_pairs={{1,2},{2,1},{5,6},{6,5},{9,10},{10,9},{13,14},{14,13},{17,18},{18,... | collective-permute-start | bytes 245768 | tf_op jit(solution)/shard_map/ppermute | solution.py:239
  92.6 1.7 %collective-permute-start.19 = (f32[160,128]{1,0:T(8,128)}, f32[160,128]{1,0:T(8,128)S(1)}, u32[]{:S(2)}, u32[]{:S(2)}) collective-permute-start(f32[160,128]{1,0:T(8,128)} %get-tuple-element.32), channel_id=1, source_target_pairs={{0,4},{4,0},{8,12},{12,8},{16,20},{20,16},{24,28},{28,24},{1,5},{5... | collective-permute-start | bytes 245768 | tf_op jit(solution)/shard_map/ppermute | solution.py:265
  94.3 0.7 pad_add_fusion.keep_ref
  95.6 14.8 %collective-permute-done.19.refs_7_ = f32[160,128]{1,0:T(8,128)S(1)} collective-permute-done((f32[160,128]{1,0:T(8,128)}, f32[160,128]{1,0:T(8,128)S(1)}, u32[]{:S(2)}, u32[]{:S(2)}) %collective-permute-start.19) | collective-permute-done | bytes 81952 | tf_op jit(solution)/shard_map/ppermute | solution.py:265
  111.3 9.7 %shard_map.50 = bf16[1,160,2560]{2,1,0:T(8,128)(2,1)} custom-call(s32[5]{0:T(128)} %pad_add_fusion.keep_ref, bf16[1,160,2560]{2,1,0:T(8,128)(2,1)} %query_ref.1, bf16[1,160,2560]{2,1,0:T(8,128)(2,1)} %collective-permute-done.key_ref, bf16[1,160,2560]{2,1,0:T(8,128)(2,1)} %collective-permute-done.1.value_ref, f32[1,160,2560]{2,1,0:T(8,128)} %get-tuple-element.19.refs_0_, ...), custom_call_target="tpu_custom_call" | custom-call | flops 262144000 | bytes 6553600 | tf_op jit(solution)/shard_map/pallas_call | solution.py:184
  (53 shorter events, 1.9 us)
Async XLA Ops:
  0.0 19.4 %collective-permute-start.3 = (bf16[1,160,2560]{2,1,0:T(8,128)(2,1)}, bf16[1,160,2560]{2,1,0:T(8,128)(2,1)}, u32[]{:S(2)}, u32[]{:S(2)}) collective-permute-start(bf16[1,160,2560]{2,1,0:T(8,128)(2,1)} %query_ref.1), channel_id=1, source_target_pairs={{0,4},{4,0},{8,12},{12,8},{16,20},{20,16},{24,28},{28,24},{1,5},{5... | collective-permute-start | bytes 2457608 | tf_op jit(solution)/shard_map/ppermute | solution.py:213
  1.2 28.8 %collective-permute-start.4 = (bf16[1,160,2560]{2,1,0:T(8,128)(2,1)}, bf16[1,160,2560]{2,1,0:T(8,128)(2,1)S(1)}, u32[]{:S(2)}, u32[]{:S(2)}) collective-permute-start(bf16[1,160,2560]{2,1,0:T(8,128)(2,1)} %refs_2_.5), channel_id=1, source_target_pairs={{0,24},{4,12},{8,0},{12,20},{16,8},{20,28},{24,16},{28,4},{1,25},{... | collective-permute-start | bytes 2457608 | tf_op jit(solution)/shard_map/ppermute | solution.py:209
  1.4 36.4 %collective-permute-start.5 = (bf16[1,160,2560]{2,1,0:T(8,128)(2,1)}, bf16[1,160,2560]{2,1,0:T(8,128)(2,1)S(1)}, u32[]{:S(2)}, u32[]{:S(2)}) collective-permute-start(bf16[1,160,2560]{2,1,0:T(8,128)(2,1)} %refs_4_.3), channel_id=1, source_target_pairs={{0,24},{4,12},{8,0},{12,20},{16,8},{20,28},{24,16},{28,4},{1,25},{... | collective-permute-start | bytes 2457608 | tf_op jit(solution)/shard_map/ppermute | solution.py:210
  19.4 18.4 %collective-permute-start.10 = (bf16[1,160,2560]{2,1,0:T(8,128)(2,1)}, bf16[1,160,2560]{2,1,0:T(8,128)(2,1)}, u32[]{:S(2)}, u32[]{:S(2)}) collective-permute-start(bf16[1,160,2560]{2,1,0:T(8,128)(2,1)} %collective-permute-done.3.refs_0_), channel_id=1, source_target_pairs={{0,1},{1,0},{2,3},{3,2},{4,5},{5,4},{6,7},{7,6},{8,9},{9,8},{10,11... | collective-permute-start | bytes 2457608 | tf_op jit(solution)/shard_map/ppermute | solution.py:217
  21.0 16.9 %collective-permute-start.11 = (bf16[1,160,2560]{2,1,0:T(8,128)(2,1)}, bf16[1,160,2560]{2,1,0:T(8,128)(2,1)}, u32[]{:S(2)}, u32[]{:S(2)}) collective-permute-start(bf16[1,160,2560]{2,1,0:T(8,128)(2,1)} %collective-permute-done.3.refs_0_), channel_id=1, source_target_pairs={{1,2},{2,1},{5,6},{6,5},{9,10},{10,9},{13,14},{14,13},{17,18},{18,... | collective-permute-start | bytes 2457608 | tf_op jit(solution)/shard_map/ppermute | solution.py:218
  24.0 2.9 %collective-permute-start.2 = (s32[1,5]{1,0:T(1,128)}, s32[1,5]{1,0:T(1,128)S(1)}, u32[]{:S(2)}, u32[]{:S(2)}) collective-permute-start(s32[1,5]{1,0:T(1,128)} %param.7), channel_id=1, source_target_pairs={{0,4},{4,0},{8,12},{12,8},{16,20},{20,16},{24,28},{28,24},{1,5},{5... | collective-permute-start | bytes 68 | tf_op jit(solution)/shard_map/ppermute | solution.py:214
  26.9 30.4 %collective-permute-start.6 = (bf16[1,160,2560]{2,1,0:T(8,128)(2,1)}, bf16[1,160,2560]{2,1,0:T(8,128)(2,1)}, u32[]{:S(2)}, u32[]{:S(2)}) collective-permute-start(bf16[1,160,2560]{2,1,0:T(8,128)(2,1)} %query_ref.1), channel_id=1, source_target_pairs={{0,1},{1,0},{2,3},{3,2},{4,5},{5,4},{6,7},{7,6},{8,9},{9,8},{10,11... | collective-permute-start | bytes 2457608 | tf_op jit(solution)/shard_map/ppermute | solution.py:215
  30.1 7.8 %copy-start.2 = (bf16[1,160,2560]{2,1,0:T(8,128)(2,1)}, bf16[1,160,2560]{2,1,0:T(8,128)(2,1)S(1)}, u32[]{:S(2)}) copy-start(bf16[1,160,2560]{2,1,0:T(8,128)(2,1)S(1)} %collective-permute-done.4.refs_3_) | copy-start | bytes 2457604
  30.1 27.9 %collective-permute-start.7 = (bf16[1,160,2560]{2,1,0:T(8,128)(2,1)}, bf16[1,160,2560]{2,1,0:T(8,128)(2,1)}, u32[]{:S(2)}, u32[]{:S(2)}) collective-permute-start(bf16[1,160,2560]{2,1,0:T(8,128)(2,1)} %query_ref.1), channel_id=1, source_target_pairs={{1,2},{2,1},{5,6},{6,5},{9,10},{10,9},{13,14},{14,13},{17,18},{18,... | collective-permute-start | bytes 2457608 | tf_op jit(solution)/shard_map/ppermute | solution.py:216
  34.2 18.1 %copy-start = (bf16[1,160,2560]{2,1,0:T(8,128)(2,1)S(1)}, bf16[1,160,2560]{2,1,0:T(8,128)(2,1)}, u32[]{:S(2)}) copy-start(bf16[1,160,2560]{2,1,0:T(8,128)(2,1)} %refs_2_.5) | copy-start | bytes 2457604
  34.2 19.5 %copy-start.12 = (s32[1,5]{1,0:T(1,128)S(1)}, s32[1,5]{1,0:T(1,128)}, u32[]{:S(2)}) copy-start(s32[1,5]{1,0:T(1,128)} %param.7) | copy-start | bytes 64
  34.2 23.8 %copy-start.1 = (bf16[1,160,2560]{2,1,0:T(8,128)(2,1)S(1)}, bf16[1,160,2560]{2,1,0:T(8,128)(2,1)}, u32[]{:S(2)}) copy-start(bf16[1,160,2560]{2,1,0:T(8,128)(2,1)} %refs_4_.3) | copy-start | bytes 2457604
  47.4 32.2 %collective-permute-start.12 = (bf16[1,160,2560]{2,1,0:T(8,128)(2,1)}, bf16[1,160,2560]{2,1,0:T(8,128)(2,1)S(1)}, u32[]{:S(2)}, u32[]{:S(2)}) collective-permute-start(bf16[1,160,2560]{2,1,0:T(8,128)(2,1)} %get-tuple-element.23), channel_id=1, source_target_pairs={{0,1},{1,0},{2,3},{3,2},{4,5},{5,4},{6,7},{7,6},{8,9},{9,8},{10,11... | collective-permute-start | bytes 2457608 | tf_op jit(solution)/shard_map/ppermute | solution.py:249
  49.3 32.9 %collective-permute-start.13 = (bf16[1,160,2560]{2,1,0:T(8,128)(2,1)}, bf16[1,160,2560]{2,1,0:T(8,128)(2,1)S(1)}, u32[]{:S(2)}, u32[]{:S(2)}) collective-permute-start(bf16[1,160,2560]{2,1,0:T(8,128)(2,1)} %get-tuple-element.24), channel_id=1, source_target_pairs={{1,2},{2,1},{5,6},{6,5},{9,10},{10,9},{13,14},{14,13},{17,18},{18,... | collective-permute-start | bytes 2457608 | tf_op jit(solution)/shard_map/ppermute | solution.py:250
  52.3 35.9 %collective-permute-start = (bf16[1,160,2560]{2,1,0:T(8,128)(2,1)S(1)}, bf16[1,160,2560]{2,1,0:T(8,128)(2,1)}, u32[]{:S(2)}, u32[]{:S(2)}) collective-permute-start(bf16[1,160,2560]{2,1,0:T(8,128)(2,1)S(1)} %copy-done), channel_id=1, source_target_pairs={{24,0},{12,4},{0,8},{20,12},{8,16},{28,20},{16,24},{4,28},{25,1},{... | collective-permute-start | bytes 2457608 | tf_op jit(solution)/shard_map/ppermute | solution.py:211
  57.3 10.5 %collective-permute-start.14 = (f32[160,128]{1,0:T(8,128)}, f32[160,128]{1,0:T(8,128)S(1)}, u32[]{:S(2)}, u32[]{:S(2)}) collective-permute-start(f32[160,128]{1,0:T(8,128)} %get-tuple-element.26), channel_id=1, source_target_pairs={{0,1},{1,0},{2,3},{3,2},{4,5},{5,4},{6,7},{7,6},{8,9},{9,8},{10,11... | collective-permute-start | bytes 245768 | tf_op jit(solution)/shard_map/ppermute | solution.py:249
  58.0 9.9 %copy-start.14 = (f32[160,128]{1,0:T(8,128)S(1)}, f32[160,128]{1,0:T(8,128)}, u32[]{:S(2)}) copy-start(f32[160,128]{1,0:T(8,128)} %get-tuple-element.27) | copy-start | bytes 245764
  58.0 31.5 %collective-permute-start.1 = (bf16[1,160,2560]{2,1,0:T(8,128)(2,1)S(1)}, bf16[1,160,2560]{2,1,0:T(8,128)(2,1)}, u32[]{:S(2)}, u32[]{:S(2)}) collective-permute-start(bf16[1,160,2560]{2,1,0:T(8,128)(2,1)S(1)} %copy-done.1), channel_id=1, source_target_pairs={{24,0},{12,4},{0,8},{20,12},{8,16},{28,20},{16,24},{4,28},{25,1},{... | collective-permute-start | bytes 2457608 | tf_op jit(solution)/shard_map/ppermute | solution.py:212
  67.9 11.7 %copy-start.10 = (f32[160,128]{1,0:T(8,128)}, f32[160,128]{1,0:T(8,128)S(1)}, u32[]{:S(2)}) copy-start(f32[160,128]{1,0:T(8,128)S(1)} %collective-permute-done.14.refs_4_) | copy-start | bytes 245764
  67.9 11.7 %collective-permute-start.15 = (f32[160,128]{1,0:T(8,128)S(1)}, f32[160,128]{1,0:T(8,128)S(1)}, u32[]{:S(2)}, u32[]{:S(2)}) collective-permute-start(f32[160,128]{1,0:T(8,128)S(1)} %copy-done.14), channel_id=1, source_target_pairs={{1,2},{2,1},{5,6},{6,5},{9,10},{10,9},{13,14},{14,13},{17,18},{18,... | collective-permute-start | bytes 245768 | tf_op jit(solution)/shard_map/ppermute | solution.py:250
  79.6 2.6 %copy-start.11 = (f32[160,128]{1,0:T(8,128)}, f32[160,128]{1,0:T(8,128)S(1)}, u32[]{:S(2)}) copy-start(f32[160,128]{1,0:T(8,128)S(1)} %collective-permute-done.15.refs_5_) | copy-start | bytes 245764
  79.6 16.0 %collective-permute-start.8 = (bf16[1,160,2560]{2,1,0:T(8,128)(2,1)}, bf16[1,160,2560]{2,1,0:T(8,128)(2,1)}, u32[]{:S(2)}, u32[]{:S(2)}) collective-permute-start(bf16[1,160,2560]{2,1,0:T(8,128)(2,1)} %get-tuple-element.20), channel_id=1, source_target_pairs={{0,1},{1,0},{2,3},{3,2},{4,5},{5,4},{6,7},{7,6},{8,9},{9,8},{10,11... | collective-permute-start | bytes 2457608 | tf_op jit(solution)/shard_map/ppermute | solution.py:238
  79.7 2.5 %copy-start.4 = (bf16[1,160,2560]{2,1,0:T(8,128)(2,1)}, bf16[1,160,2560]{2,1,0:T(8,128)(2,1)S(1)}, u32[]{:S(2)}) copy-start(bf16[1,160,2560]{2,1,0:T(8,128)(2,1)S(1)} %collective-permute-done.12.refs_1_) | copy-start | bytes 2457604
  79.7 15.9 %collective-permute-start.9 = (bf16[1,160,2560]{2,1,0:T(8,128)(2,1)}, bf16[1,160,2560]{2,1,0:T(8,128)(2,1)}, u32[]{:S(2)}, u32[]{:S(2)}) collective-permute-start(bf16[1,160,2560]{2,1,0:T(8,128)(2,1)} %get-tuple-element.21), channel_id=1, source_target_pairs={{1,2},{2,1},{5,6},{6,5},{9,10},{10,9},{13,14},{14,13},{17,18},{18,... | collective-permute-start | bytes 2457608 | tf_op jit(solution)/shard_map/ppermute | solution.py:239
  83.2 5.0 %copy-start.15 = (f32[160,128]{1,0:T(8,128)S(1)}, f32[160,128]{1,0:T(8,128)}, u32[]{:S(2)}) copy-start(f32[160,128]{1,0:T(8,128)} %get-tuple-element.30) | copy-start | bytes 245764
  83.2 6.3 %copy-start.13 = (f32[160,128]{1,0:T(8,128)S(1)}, f32[160,128]{1,0:T(8,128)}, u32[]{:S(2)}) copy-start(f32[160,128]{1,0:T(8,128)} %get-tuple-element.31) | copy-start | bytes 245764
  88.2 22.2 %collective-permute-start.16 = (bf16[1,160,2560]{2,1,0:T(8,128)(2,1)}, bf16[1,160,2560]{2,1,0:T(8,128)(2,1)S(1)}, u32[]{:S(2)}, u32[]{:S(2)}) collective-permute-start(bf16[1,160,2560]{2,1,0:T(8,128)(2,1)} %get-tuple-element.28), channel_id=1, source_target_pairs={{0,4},{4,0},{8,12},{12,8},{16,20},{20,16},{24,28},{28,24},{1,5},{5... | collective-permute-start | bytes 2457608 | tf_op jit(solution)/shard_map/ppermute | solution.py:265
  88.2 4.4 %collective-permute-start.17 = (f32[160,128]{1,0:T(8,128)S(1)}, f32[160,128]{1,0:T(8,128)S(1)}, u32[]{:S(2)}, u32[]{:S(2)}) collective-permute-start(f32[160,128]{1,0:T(8,128)S(1)} %copy-done.15), channel_id=1, source_target_pairs={{0,1},{1,0},{2,3},{3,2},{4,5},{5,4},{6,7},{7,6},{8,9},{9,8},{10,11... | collective-permute-start | bytes 245768 | tf_op jit(solution)/shard_map/ppermute | solution.py:238
  89.5 6.1 %collective-permute-start.18 = (f32[160,128]{1,0:T(8,128)S(1)}, f32[160,128]{1,0:T(8,128)S(1)}, u32[]{:S(2)}, u32[]{:S(2)}) collective-permute-start(f32[160,128]{1,0:T(8,128)S(1)} %copy-done.13), channel_id=1, source_target_pairs={{1,2},{2,1},{5,6},{6,5},{9,10},{10,9},{13,14},{14,13},{17,18},{18,... | collective-permute-start | bytes 245768 | tf_op jit(solution)/shard_map/ppermute | solution.py:239
  92.6 17.8 %copy-start.7 = (f32[160,128]{1,0:T(8,128)}, f32[160,128]{1,0:T(8,128)S(1)}, u32[]{:S(2)}) copy-start(f32[160,128]{1,0:T(8,128)S(1)} %collective-permute-done.17.refs_5_) | copy-start | bytes 245764
  92.6 17.8 %collective-permute-start.19 = (f32[160,128]{1,0:T(8,128)}, f32[160,128]{1,0:T(8,128)S(1)}, u32[]{:S(2)}, u32[]{:S(2)}) collective-permute-start(f32[160,128]{1,0:T(8,128)} %get-tuple-element.32), channel_id=1, source_target_pairs={{0,4},{4,0},{8,12},{12,8},{16,20},{20,16},{24,28},{28,24},{1,5},{5... | collective-permute-start | bytes 245768 | tf_op jit(solution)/shard_map/ppermute | solution.py:265
  95.5 14.9 %copy-start.8 = (f32[160,128]{1,0:T(8,128)}, f32[160,128]{1,0:T(8,128)S(1)}, u32[]{:S(2)}) copy-start(f32[160,128]{1,0:T(8,128)S(1)} %collective-permute-done.18.refs_6_) | copy-start | bytes 245764
  (4 other events, 3.5 us)

commit v2 on v0

v2 whole, which is shorter than its diff:
```python
import functools

import jax
import jax.numpy as jnp
from jax import lax
from jax.experimental import pallas as pl
from jax.experimental.pallas import tpu as pltpu
from jax.sharding import PartitionSpec as P


HEAD = 128
NEG = -1e30
RATE = HEAD ** (-0.5) * 1.4426950408889634
THIRD = 32
VMEM = pl.BlockSpec(memory_space=pltpu.VMEM)
SMEM = pl.BlockSpec(memory_space=pltpu.SMEM)
GRANT = pltpu.CompilerParams(vmem_limit_bytes=16 << 20)


def column(index):
    return slice(index * HEAD, (index + 1) * HEAD)


def raw_scores(key, query):
    return lax.dot_general(
        key, query, (((1,), (1,)), ((), ())), preferred_element_type=jnp.float32
    )


def weighted(value, weights):
    return lax.dot_general(
        value, weights, (((0,), (0,)), ((), ())), preferred_element_type=jnp.float32
    )


def softmax_rows(raw):
    largest = functools.reduce(
        jnp.maximum, [jnp.max(part, axis=0, keepdims=True) for part in raw]
    )
    expos = [jnp.exp2((part - largest) * RATE) for part in raw]
    total = sum(jnp.sum(expo, axis=0, keepdims=True) for expo in expos)
    return [expo.astype(jnp.bfloat16) for expo in expos], total, largest


def store_log(scratch, at, log, packed):
    if not packed:
        scratch[at : at + 1, :] = log
        return
    high = log.astype(jnp.bfloat16).astype(jnp.float32)
    middle = (log - high).astype(jnp.bfloat16).astype(jnp.float32)
    for place, part in enumerate((high, middle, log - high - middle)):
        scratch[place * THIRD + at : place * THIRD + at + 1, :] = part


def read_log(block, heads, packed):
    log = block[0, :, column(heads)].astype(jnp.float32)
    if not packed:
        return log
    return log + pltpu.roll(log, HEAD - THIRD, 1) + pltpu.roll(log, HEAD - 2 * THIRD, 1)


def parts_kernel(query_count, key_count, first, heads, kinds, keep_ref, *refs):
    queries = refs[:query_count]
    keys = refs[query_count : query_count + key_count]
    values = refs[query_count + key_count : query_count + 2 * key_count]
    outs = refs[query_count + 2 * key_count : -2]
    log_scratch, packed_scratch = refs[-2:]
    rows = queries[0].shape[1]
    wide = query_count * rows
    lane = lax.broadcasted_iota(jnp.int32, (1, wide), 1)
    biases = []
    for i in range(key_count):
        bias = jnp.zeros((1, wide), jnp.float32)
        for at in range(query_count):
            kept = jnp.where(keep_ref[at * key_count + i] != 0, 0.0, NEG)
            bias = jnp.where(lane >= at * rows, kept, bias)
        biases.append(bias)
    log_scratch[...] = jnp.zeros(log_scratch.shape, jnp.float32)
    packed_scratch[...] = jnp.zeros(packed_scratch.shape, jnp.float32)

    def score(n):
        cols = column(first + n)
        query = jnp.concatenate([ref[0, :, cols] for ref in queries], 0)
        return [raw_scores(key[0, :, cols], query) + bias for key, bias in zip(keys, biases)]

    def attend(n, weights, total, largest):
        cols = column(first + n)
        summed = sum(weighted(value[0, :, cols], part) for value, part in zip(values, weights))
        log = largest * RATE + jnp.log2(total)
        store_log(log_scratch, n, log, False)
        store_log(packed_scratch, n, log, True)
        normed = (summed * (1.0 / total)).T
        for at, out in enumerate(outs):
            out[0, :, column(n)] = normed[at * rows : (at + 1) * rows].astype(out.dtype)

    raw = score(0)
    before = None
    for n in range(heads):
        later = score(n + 1) if n + 1 < heads else None
        now = softmax_rows(raw)
        if before is not None:
            attend(n - 1, *before)
        before, raw = now, later
    attend(heads - 1, *before)
    logs = {False: log_scratch[...].T, True: packed_scratch[...].T}
    for at, (out, kind) in enumerate(zip(outs, kinds)):
        log = logs[kind == jnp.bfloat16][at * rows : (at + 1) * rows]
        out[0, :, column(heads)] = log.astype(out.dtype)


def parts(queries, keys, values, keeps, kinds, first, heads):
    rows = queries[0].shape[1]
    wide = len(queries) * rows
    blocks = len(queries) * len(keys)
    width = heads * HEAD
    return pl.pallas_call(
        functools.partial(parts_kernel, len(queries), len(keys), first, heads, kinds),
        in_specs=[SMEM] + [VMEM] * (len(queries) + 2 * len(keys)),
        out_specs=[VMEM] * len(queries),
        out_shape=[
            jax.ShapeDtypeStruct((1, rows, width + HEAD), kind) for kind in kinds
        ],
        scratch_shapes=[pltpu.VMEM((HEAD, wide), jnp.float32)] * 2,
        compiler_params=GRANT,
        cost_estimate=pl.CostEstimate(
            flops=4 * rows * rows * width * blocks,
            bytes_accessed=2 * rows * width * (2 * len(queries) + 2 * len(keys)),
            transcendentals=rows * rows * heads * blocks,
        ),
    )(keeps, *queries, *keys, *values)


def shares(logs):
    largest = functools.reduce(jnp.maximum, logs)
    expos = [jnp.exp2(log - largest) for log in logs]
    total = sum(expos)
    inverse = 1.0 / total
    return [expo * inverse for expo in expos], largest + jnp.log2(total)


def merge_kernel(heads, packs, keep_ref, *refs):
    blocks, out_ref = refs[:-1], refs[-1]
    logs = [
        jnp.where(keep_ref[i] != 0, read_log(block, heads, pack), NEG)
        for i, (block, pack) in enumerate(zip(blocks, packs))
    ]
    weights, log = shares(logs)
    for n in range(heads):
        cols = column(n)
        out_ref[0, :, cols] = sum(
            weight[:, n : n + 1] * block[0, :, cols].astype(jnp.float32)
            for weight, block in zip(weights, blocks)
        ).astype(out_ref.dtype)
    lane = lax.broadcasted_iota(jnp.int32, log.shape, 1)
    high = log.astype(jnp.bfloat16).astype(jnp.float32)
    middle = (log - high).astype(jnp.bfloat16).astype(jnp.float32)
    low = log - high - middle
    packed = jnp.where(
        lane < THIRD,
        high,
        jnp.where(
            lane < 2 * THIRD, pltpu.roll(middle, THIRD, 1), pltpu.roll(low, 2 * THIRD, 1)
        ),
    )
    out_ref[0, :, column(heads)] = packed.astype(out_ref.dtype)


def merged(blocks, keeps):
    rows, width = blocks[0].shape[1:]
    heads = width // HEAD - 1
    packs = tuple(block.dtype == jnp.bfloat16 for block in blocks)
    return pl.pallas_call(
        functools.partial(merge_kernel, heads, packs),
        in_specs=[SMEM] + [VMEM] * len(blocks),
        out_specs=VMEM,
        out_shape=jax.ShapeDtypeStruct((1, rows, width), jnp.bfloat16),
        compiler_params=GRANT,
        cost_estimate=pl.CostEstimate(
            flops=2 * rows * width * len(blocks),
            bytes_accessed=2 * rows * width * (len(blocks) + 1),
            transcendentals=0,
        ),
    )(keeps, *blocks)


def absorb_kernel(heads, groups, last, keep_ref, query_ref, key_ref, value_ref, *refs):
    count = sum(len(group) for group in groups)
    pieces, out_ref = refs[:count], refs[count]
    weight_scratch, log_scratch, share_scratch, coef_scratch = refs[count + 1 :]
    rows = query_ref.shape[1]
    bias = jnp.where(keep_ref[0] != 0, 0.0, NEG)
    place = []
    at = 0
    for i, group in enumerate(groups):
        total_log = jnp.zeros((rows, HEAD), jnp.float32)
        lane = lax.broadcasted_iota(jnp.int32, (rows, HEAD), 1)
        where = {}
        for start, size, pack in group:
            log = read_log(pieces[at], size, pack)
            if start:
                log = pltpu.roll(log, start, 1)
            total_log = jnp.where(lane >= start, log, total_log)
            for n in range(size):
                where[start + n] = (at, n)
            at += 1
        log_scratch[i] = jnp.where(keep_ref[1 + i] != 0, total_log, NEG).T
        place.append(where)

    def score(n):
        return [raw_scores(key_ref[0, :, column(n)], query_ref[0, :, column(n)]) + bias]

    raw = score(0)
    for n in range(heads):
        later = score(n + 1) if n + 1 < heads else None
        (weights,), total, largest = softmax_rows(raw)
        weight_scratch[n] = weights
        logs = [log_scratch[i, n : n + 1, :] for i in range(len(groups))]
        portions, log = shares([largest * RATE + jnp.log2(total)] + logs)
        coef_scratch[n : n + 1, :] = portions[0] * (1.0 / total)
        for i, portion in enumerate(portions[1:]):
            share_scratch[i, n : n + 1, :] = portion
        if not last:
            log_scratch[0, n : n + 1, :] = log
        raw = later
    columns = [share_scratch[i].T for i in range(len(groups))]
    for n in range(heads):
        cols = column(n)
        summed = weighted(value_ref[0, :, cols], weight_scratch[n])
        out = (summed * coef_scratch[n : n + 1, :]).T
        for i in range(len(groups)):
            piece, index = place[i][n]
            block = pieces[piece][0, :, column(index)].astype(jnp.float32)
            out = out + columns[i][:, n : n + 1] * block
        out_ref[0, :, cols] = out.astype(out_ref.dtype)
    if not last:
        out_ref[0, :, column(heads)] = log_scratch[0].T


def absorbed(query, key, value, groups, keeps, last):
    rows, width = query.shape[1:]
    heads = width // HEAD
    kind = query.dtype if last else jnp.float32
    shapes, pieces = [], []
    for group in groups:
        shape, start = [], 0
        for piece in group:
            size = piece.shape[2] // HEAD - 1
            shape.append((start, size, piece.dtype == jnp.bfloat16))
            start += size
            pieces.append(piece)
        shapes.append(tuple(shape))
    table = pltpu.VMEM((len(groups), HEAD, rows), jnp.float32)
    return pl.pallas_call(
        functools.partial(absorb_kernel, heads, tuple(shapes), last),
        in_specs=[SMEM] + [VMEM] * (3 + len(pieces)),
        out_specs=VMEM,
        out_shape=jax.ShapeDtypeStruct((1, rows, width + (0 if last else HEAD)), kind),
        scratch_shapes=[
            pltpu.VMEM((heads, rows, rows), jnp.bfloat16),
            table,
            table,
            pltpu.VMEM((HEAD, rows), jnp.float32),
        ],
        compiler_params=GRANT,
        cost_estimate=pl.CostEstimate(
            flops=4 * rows * rows * width,
            bytes_accessed=2 * rows * width * (len(pieces) + 4),
            transcendentals=rows * rows * heads,
        ),
    )(keeps, query, key, value, *pieces)


def per_device(queries, keys, values, band):
    frames, bands = lax.axis_size("frame"), lax.axis_size("row")
    toward = [(f, (f + 2) % frames) if f % 2 else (f, (f - 2) % frames) for f in range(frames)]
    away = [(target, source) for source, target in toward]
    twin = [(f, f ^ 1) for f in range(frames)]
    even = [(r, r ^ 1) for r in range(bands)]
    odd = [(r, r + 1) for r in range(1, bands - 1, 2)]
    odd += [(target, source) for source, target in odd]

    key_one = lax.ppermute(keys, "frame", toward)
    value_one = lax.ppermute(values, "frame", toward)
    key_two = lax.ppermute(keys, "frame", away)
    value_two = lax.ppermute(values, "frame", away)
    query_twin = lax.ppermute(queries, "frame", twin)
    band_twin = lax.ppermute(band, "frame", twin)
    query_even = lax.ppermute(queries, "row", even)
    query_odd = lax.ppermute(queries, "row", odd)
    twin_even = lax.ppermute(query_twin, "row", even)
    twin_odd = lax.ppermute(query_twin, "row", odd)

    is_odd = lax.axis_index("frame") % 2 == 1
    row = lax.axis_index("row")
    own, other = band[0], band_twin[0]
    has_odd = (row > 0) & (row < bands - 1)
    other_own = jnp.where(is_odd, other[3], other[1])
    other_one = jnp.where(is_odd, other[1], other[3])
    own_one = jnp.where(is_odd, own[0], own[4])
    own_two = jnp.where(is_odd, own[4], own[0])

    def flags(*items):
        return jnp.stack([jnp.asarray(item).astype(jnp.int32) for item in items])

    narrow, full = jnp.bfloat16, jnp.float32
    heads = queries.shape[2] // HEAD
    spans = [(0, heads // 2), (heads // 2, heads - heads // 2)]

    beside = own[2] >= 1
    even_part, odd_part, own_part = parts(
        [query_even, query_odd, queries],
        [keys],
        [values],
        flags(beside, beside, True),
        (narrow, narrow, full),
        0,
        heads,
    )
    from_even = lax.ppermute(even_part, "row", even)
    from_odd = lax.ppermute(odd_part, "row", odd)

    keep_beside = (other_own >= 1, other_one >= 1)
    keep_other = flags(*keep_beside, *keep_beside, other_own >= 0, other_one >= 0)
    from_twin = []
    for first, size in spans:
        even_twin, odd_twin, own_twin = parts(
            [twin_even, twin_odd, query_twin],
            [keys, key_one],
            [values, value_one],
            keep_other,
            (narrow, narrow, full),
            first,
            size,
        )
        back_even = lax.ppermute(even_twin, "row", even)
        back_odd = lax.ppermute(odd_twin, "row", odd)
        whole = merged([own_twin, back_even, back_odd], flags(True, True, has_odd))
        from_twin.append(lax.ppermute(whole, "frame", twin))

    near = absorbed(
        queries,
        key_one,
        value_one,
        [[own_part], [from_even], [from_odd]],
        flags(own_one >= 0, True, True, has_odd),
        False,
    )
    return absorbed(
        queries,
        key_two,
        value_two,
        [[near], from_twin],
        flags(own_two >= 0, True, True),
        True,
    )


def solution(mesh):
    return jax.shard_map(
        per_device,
        mesh=mesh,
        in_specs=(
            P("frame", "row", None),
            P("frame", "row", None),
            P("frame", "row", None),
            P("frame", None),
        ),
        out_specs=P("frame", "row", None),
        check_vma=False,
    )
```

time: 250 us -> 116 us (0.46)
  the two profiles are of different devices: /device:TPU:27 before, /device:TPU:1 now
where the time goes in v2:
time: 116 us; the launch traced here: 115 us
  Pallas kernels  35.6 us (31%)
  starting transfers between devices  29 us (25%)
  waiting for transfers between devices  24.2 us (21%)
  local copies, waits for them, and re-layouts  21 us (18%)
  between operations  5.52 us (5%)
    unnamed x48, local copies, waits for them, and re-layouts  18.8 us
    pallas_call x2, Pallas kernels, absorbed(): pl.pallas_call(functools.partial(absorb_kernel, heads, tuple(shapes), las...  15.6 us
    pallas_call x3, Pallas kernels, parts(): pl.pallas_call(functools.partial(parts_kernel, len(queries), len(keys), f...  15.1 us
    ppermute x1, waiting for transfers between devices, per_device(): value_two = lax.ppermute(values, 'frame', away)  13.4 us
    ppermute x1, waiting for transfers between devices, per_device(): band_twin = lax.ppermute(band, 'frame', twin)  10.7 us
    ppermute x2, starting transfers between devices, per_device(): back_odd = lax.ppermute(odd_twin, 'row', odd)  5.54 us
    pallas_call x2, Pallas kernels, merged(): pl.pallas_call(functools.partial(merge_kernel, heads, packs), in_specs=[S...  4.94 us
    ppermute x1, starting transfers between devices, per_device(): key_one = lax.ppermute(keys, 'frame', toward)  3.32 us
  transfers between devices with their start and end apart: 18, of which 2 were waited for; matrix products, arithmetic and copies ran while one was open for 2% of the time, Pallas kernels for 24%

profile of v2, /device:TPU:1, one launch (start us, length us, event | category | flops | bytes accessed | tf_op | source)
XLA Modules:
  0.0 115.5 jit_solution(2713005824505898659)
XLA Ops:
  0.0 2.1 %collective-permute-start.9 = (bf16[1,160,2560]{2,1,0:T(8,128)(2,1)}, bf16[1,160,2560]{2,1,0:T(8,128)(2,1)}, u32[]{:S(2)}, u32[]{:S(2)}) collective-permute-start(bf16[1,160,2560]{2,1,0:T(8,128)(2,1)} %query_ref.3), channel_id=1, source_target_pairs={{0,4},{4,0},{8,12},{12,8},{16,20},{20,16},{24,28},{28,24},{1,5},{5... | collective-permute-start | bytes 2457608 | tf_op jit(solution)/shard_map/ppermute | solution.py:286
  2.1 1.0 collective-permute-start.4
  3.0 3.0 %collective-permute-start.5 = (bf16[1,160,2560]{2,1,0:T(8,128)(2,1)}, bf16[1,160,2560]{2,1,0:T(8,128)(2,1)S(1)}, u32[]{:S(2)}, u32[]{:S(2)}) collective-permute-start(bf16[1,160,2560]{2,1,0:T(8,128)(2,1)} %query_ref.3), channel_id=1, source_target_pairs={{1,2},{2,1},{5,6},{6,5},{9,10},{10,9},{13,14},{14,13},{17,18},{18,... | collective-permute-start | bytes 2457608 | tf_op jit(solution)/shard_map/ppermute | solution.py:289
  6.3 3.3 %collective-permute-start.2 = (bf16[1,160,2560]{2,1,0:T(8,128)(2,1)}, bf16[1,160,2560]{2,1,0:T(8,128)(2,1)S(1)}, u32[]{:S(2)}, u32[]{:S(2)}) collective-permute-start(bf16[1,160,2560]{2,1,0:T(8,128)(2,1)} %refs_3_.5), channel_id=1, source_target_pairs={{0,24},{4,12},{8,0},{12,20},{16,8},{20,28},{24,16},{28,4},{1,25},{... | collective-permute-start | bytes 2457608 | tf_op jit(solution)/shard_map/ppermute | solution.py:282
  9.6 10.7 %collective-permute-done.8 = s32[1,5]{1,0:T(1,128)S(1)} collective-permute-done((s32[1,5]{1,0:T(1,128)}, s32[1,5]{1,0:T(1,128)S(1)}, u32[]{:S(2)}, u32[]{:S(2)}) %collective-permute-start.8) | collective-permute-done | bytes 52 | tf_op jit(solution)/shard_map/ppermute | solution.py:287
  20.3 3.3 %collective-permute-start.3 = (bf16[1,160,2560]{2,1,0:T(8,128)(2,1)}, bf16[1,160,2560]{2,1,0:T(8,128)(2,1)S(1)}, u32[]{:S(2)}, u32[]{:S(2)}) collective-permute-start(bf16[1,160,2560]{2,1,0:T(8,128)(2,1)} %refs_5_.3), channel_id=1, source_target_pairs={{0,24},{4,12},{8,0},{12,20},{16,8},{20,28},{24,16},{28,4},{1,25},{... | collective-permute-start | bytes 2457608 | tf_op jit(solution)/shard_map/ppermute | solution.py:283
  23.6 1.8 %collective-permute-start.10 = (bf16[1,160,2560]{2,1,0:T(8,128)(2,1)}, bf16[1,160,2560]{2,1,0:T(8,128)(2,1)}, u32[]{:S(2)}, u32[]{:S(2)}) collective-permute-start(bf16[1,160,2560]{2,1,0:T(8,128)(2,1)} %collective-permute-done.9.refs_2_), channel_id=1, source_target_pairs={{0,1},{1,0},{2,3},{3,2},{4,5},{5,4},{6,7},{7,6},{8,9},{9,8},{10,11... | collective-permute-start | bytes 2457608 | tf_op jit(solution)/shard_map/ppermute | solution.py:290
  26.3 3.0 %collective-permute-start.11 = (bf16[1,160,2560]{2,1,0:T(8,128)(2,1)}, bf16[1,160,2560]{2,1,0:T(8,128)(2,1)}, u32[]{:S(2)}, u32[]{:S(2)}) collective-permute-start(bf16[1,160,2560]{2,1,0:T(8,128)(2,1)} %collective-permute-done.9.refs_2_), channel_id=1, source_target_pairs={{1,2},{2,1},{5,6},{6,5},{9,10},{10,9},{13,14},{14,13},{17,18},{18,... | collective-permute-start | bytes 2457608 | tf_op jit(solution)/shard_map/ppermute | solution.py:291
  29.3 1.4 %fusion.1 = (s32[1,1]{1,0:T(1,128)}, s32[1,1]{1,0:T(1,128)}, s32[1,1]{1,0:T(1,128)}) fusion(s32[1,5]{1,0:T(1,128)} %param.7), kind=kLoop, calls=%fused_computation.4 | loop fusion | bytes 24 | tf_op jit(solution)/shard_map/slice | solution.py:309
  35.4 1.1 copy-done
  36.6 1.1 copy-done.2
  37.7 1.1 copy-done.4
  38.8 1.1 copy-done.15
  40.0 1.1 copy-done.17
  41.1 4.8 %shard_map.46 = (bf16[1,160,2688]{2,1,0:T(8,128)(2,1)}, bf16[1,160,2688]{2,1,0:T(8,128)(2,1)}, f32[1,160,2688]{2,1,0:T(8,128)S(1)}) custom-call(s32[3]{0:T(128)S(1)} %add_convert_fusion.keep_ref, bf16[1,160,2560]{2,1,0:T(8,128)(2,1)S(1)} %copy-done.15, bf16[1,160,2560]{2,1,0:T(8,128)(2,1)S(1)} %copy-done.17, bf16[1,160,2560]{2,1,0:T(8,128)(2,1)S(1)} %copy-done.4, ...), custom_call_target="tpu_custom_call" | custom-call | flops 786432000 | bytes 6553600 | tf_op jit(solution)/shard_map/pallas_call | solution.py:116
  45.9 1.2 %copy-done.8 = f32[1,160,2688]{2,1,0:T(8,128)} copy-done((f32[1,160,2688]{2,1,0:T(8,128)}, f32[1,160,2688]{2,1,0:T(8,128)S(1)}, u32[]{:S(2)}) %copy-start.8) | copy-done | bytes 1720344
  47.2 4.9 %shard_map.50 = (bf16[1,160,1408]{2,1,0:T(8,128)(2,1)S(1)}, bf16[1,160,1408]{2,1,0:T(8,128)(2,1)S(1)}, f32[1,160,1408]{2,1,0:T(8,128)S(1)}) custom-call(s32[6]{0:T(128)S(1)} %stack.80.keep_ref, bf16[1,160,2560]{2,1,0:T(8,128)(2,1)} %collective-permute-done.10.refs_0_, bf16[1,160,2560]{2,1,0:T(8,128)(2,1)} %collective-permute-done.11.refs_1_, ...), custom_call_target="tpu_custom_call" | custom-call | flops 786432000 | bytes 4096000 | tf_op jit(solution)/shard_map/pallas_call | solution.py:116
  53.5 2.5 %collective-permute-start.16 = (bf16[1,160,1408]{2,1,0:T(8,128)(2,1)S(1)}, bf16[1,160,1408]{2,1,0:T(8,128)(2,1)S(1)}, u32[]{:S(2)}, u32[]{:S(2)}) collective-permute-start(bf16[1,160,1408]{2,1,0:T(8,128)(2,1)S(1)} %get-tuple-element.22), channel_id=1, source_target_pairs={{1,2},{2,1},{5,6},{6,5},{9,10},{10,9},{13,14},{14,13},{17,18},{18,... | collective-permute-start | bytes 1351688 | tf_op jit(solution)/shard_map/ppermute | solution.py:336
  56.1 5.4 %shard_map.48 = (bf16[1,160,1408]{2,1,0:T(8,128)(2,1)S(1)}, bf16[1,160,1408]{2,1,0:T(8,128)(2,1)}, f32[1,160,1408]{2,1,0:T(8,128)S(1)}) custom-call(s32[6]{0:T(128)S(1)} %stack.80.keep_ref, bf16[1,160,2560]{2,1,0:T(8,128)(2,1)} %collective-permute-done.10.refs_0_, bf16[1,160,2560]{2,1,0:T(8,128)(2,1)} %collective-permute-done.11.refs_1_, ...), custom_call_target="tpu_custom_call" | custom-call | flops 786432000 | bytes 4096000 | tf_op jit(solution)/shard_map/pallas_call | solution.py:116
  62.4 3.0 %collective-permute-start.13 = (bf16[1,160,1408]{2,1,0:T(8,128)(2,1)}, bf16[1,160,1408]{2,1,0:T(8,128)(2,1)}, u32[]{:S(2)}, u32[]{:S(2)}) collective-permute-start(bf16[1,160,1408]{2,1,0:T(8,128)(2,1)} %get-tuple-element.19), channel_id=1, source_target_pairs={{1,2},{2,1},{5,6},{6,5},{9,10},{10,9},{13,14},{14,13},{17,18},{18,... | collective-permute-start | bytes 1351688 | tf_op jit(solution)/shard_map/ppermute | solution.py:336
  66.2 2.5 %collective-permute-start.7 = (bf16[1,160,2688]{2,1,0:T(8,128)(2,1)}, bf16[1,160,2688]{2,1,0:T(8,128)(2,1)}, u32[]{:S(2)}, u32[]{:S(2)}) collective-permute-start(bf16[1,160,2688]{2,1,0:T(8,128)(2,1)} %get-tuple-element.16), channel_id=1, source_target_pairs={{1,2},{2,1},{5,6},{6,5},{9,10},{10,9},{13,14},{14,13},{17,18},{18,... | collective-permute-start | bytes 2580488 | tf_op jit(solution)/shard_map/ppermute | solution.py:320
  70.4 1.2 %copy-done.13 = f32[1,160,1408]{2,1,0:T(8,128)S(1)} copy-done((f32[1,160,1408]{2,1,0:T(8,128)S(1)}, f32[1,160,1408]{2,1,0:T(8,128)}, u32[]{:S(2)}) %copy-start.13) | copy-done | bytes 901144
  71.7 1.0 copy-done.19
  72.7 1.0 copy-done.21
  73.7 2.2 %shard_map.51 = bf16[1,160,1408]{2,1,0:T(8,128)(2,1)} custom-call(s32[3]{0:T(128)S(1)} %stack.74.keep_ref, f32[1,160,1408]{2,1,0:T(8,128)S(1)} %copy-done.13, bf16[1,160,1408]{2,1,0:T(8,128)(2,1)S(1)} %copy-done.19, bf16[1,160,1408]{2,1,0:T(8,128)(2,1)S(1)} %copy-done.21), custom_call_target="tpu_custom_call" | custom-call | flops 1351680 | bytes 1802240 | tf_op jit(solution)/shard_map/pallas_call | solution.py:172
  75.9 2.7 %collective-permute-start.17 = (bf16[1,160,1408]{2,1,0:T(8,128)(2,1)}, bf16[1,160,1408]{2,1,0:T(8,128)(2,1)}, u32[]{:S(2)}, u32[]{:S(2)}) collective-permute-start(bf16[1,160,1408]{2,1,0:T(8,128)(2,1)} %shard_map.51), channel_id=1, source_target_pairs={{0,4},{4,0},{8,12},{12,8},{16,20},{20,16},{24,28},{28,24},{1,5},{5... | collective-permute-start | bytes 1351688 | tf_op jit(solution)/shard_map/ppermute | solution.py:338
  78.6 2.7 %shard_map.49 = bf16[1,160,1408]{2,1,0:T(8,128)(2,1)} custom-call(s32[3]{0:T(128)S(1)} %stack.74.keep_ref, f32[1,160,1408]{2,1,0:T(8,128)S(1)} %copy-done.11, bf16[1,160,1408]{2,1,0:T(8,128)(2,1)S(1)} %copy-done.23, bf16[1,160,1408]{2,1,0:T(8,128)(2,1)} %collective-permute-done.13.refs_2_), custom_call_target="tpu_custom_call" | custom-call | flops 1351680 | bytes 1802240 | tf_op jit(solution)/shard_map/pallas_call | solution.py:172
  83.8 1.1 copy-done.7
  85.0 1.5 %copy-done.9 = f32[1,160,2688]{2,1,0:T(8,128)S(1)} copy-done((f32[1,160,2688]{2,1,0:T(8,128)S(1)}, f32[1,160,2688]{2,1,0:T(8,128)}, u32[]{:S(2)}) %copy-start.9) | copy-done | bytes 1720344
  86.4 7.5 %shard_map.47.refs_0_ = f32[1,160,2688]{2,1,0:T(8,128)S(1)} custom-call(s32[4]{0:T(128)S(1)} %pad_add_fusion.keep_ref, bf16[1,160,2560]{2,1,0:T(8,128)(2,1)S(1)} %copy-done.5, bf16[1,160,2560]{2,1,0:T(8,128)(2,1)S(1)} %collective-permute-done.2.key_ref.refs_4_, bf16[1,160,2560]{2,1,0:T(8,128)(2,1)S(1)} %copy-done.7, f32[1,160,2688]{2,1,0:T(8,128)S(1)} %copy-done.9, ...), custom_call_target="tpu_custom_call" | custom-call | flops 262144000 | bytes 5734400 | tf_op jit(solution)/shard_map/pallas_call | solution.py:253
  93.9 13.4 %collective-permute-done.1.value_ref = bf16[1,160,2560]{2,1,0:T(8,128)(2,1)} collective-permute-done((bf16[1,160,2560]{2,1,0:T(8,128)(2,1)S(1)}, bf16[1,160,2560]{2,1,0:T(8,128)(2,1)}, u32[]{:S(2)}, u32[]{:S(2)}) %collective-permute-start.1) | collective-permute-done | bytes 819232 | tf_op jit(solution)/shard_map/ppermute | solution.py:285
  107.4 8.1 %shard_map.52 = bf16[1,160,2560]{2,1,0:T(8,128)(2,1)} custom-call(s32[3]{0:T(128)S(1)} %pad_convert_fusion.keep_ref, bf16[1,160,2560]{2,1,0:T(8,128)(2,1)S(1)} %copy-done.5, bf16[1,160,2560]{2,1,0:T(8,128)(2,1)} %collective-permute-done.key_ref, bf16[1,160,2560]{2,1,0:T(8,128)(2,1)} %collective-permute-done.1.value_ref, ...), custom_call_target="tpu_custom_call" | custom-call | flops 262144000 | bytes 5734400 | tf_op jit(solution)/shard_map/pallas_call | solution.py:253
  (68 shorter events, 7.8 us)
Async XLA Ops:
  0.0 23.6 %collective-permute-start.9 = (bf16[1,160,2560]{2,1,0:T(8,128)(2,1)}, bf16[1,160,2560]{2,1,0:T(8,128)(2,1)}, u32[]{:S(2)}, u32[]{:S(2)}) collective-permute-start(bf16[1,160,2560]{2,1,0:T(8,128)(2,1)} %query_ref.3), channel_id=1, source_target_pairs={{0,4},{4,0},{8,12},{12,8},{16,20},{20,16},{24,28},{28,24},{1,5},{5... | collective-permute-start | bytes 2457608 | tf_op jit(solution)/shard_map/ppermute | solution.py:286
  2.1 23.3 %collective-permute-start.4 = (bf16[1,160,2560]{2,1,0:T(8,128)(2,1)}, bf16[1,160,2560]{2,1,0:T(8,128)(2,1)S(1)}, u32[]{:S(2)}, u32[]{:S(2)}) collective-permute-start(bf16[1,160,2560]{2,1,0:T(8,128)(2,1)} %query_ref.3), channel_id=1, source_target_pairs={{0,1},{1,0},{2,3},{3,2},{4,5},{5,4},{6,7},{7,6},{8,9},{9,8},{10,11... | collective-permute-start | bytes 2457608 | tf_op jit(solution)/shard_map/ppermute | solution.py:288
  3.0 31.5 %collective-permute-start.5 = (bf16[1,160,2560]{2,1,0:T(8,128)(2,1)}, bf16[1,160,2560]{2,1,0:T(8,128)(2,1)S(1)}, u32[]{:S(2)}, u32[]{:S(2)}) collective-permute-start(bf16[1,160,2560]{2,1,0:T(8,128)(2,1)} %query_ref.3), channel_id=1, source_target_pairs={{1,2},{2,1},{5,6},{6,5},{9,10},{10,9},{13,14},{14,13},{17,18},{18,... | collective-permute-start | bytes 2457608 | tf_op jit(solution)/shard_map/ppermute | solution.py:289
  6.0 14.3 %collective-permute-start.8 = (s32[1,5]{1,0:T(1,128)}, s32[1,5]{1,0:T(1,128)S(1)}, u32[]{:S(2)}, u32[]{:S(2)}) collective-permute-start(s32[1,5]{1,0:T(1,128)} %param.7), channel_id=1, source_target_pairs={{0,4},{4,0},{8,12},{12,8},{16,20},{20,16},{24,28},{28,24},{1,5},{5... | collective-permute-start | bytes 68 | tf_op jit(solution)/shard_map/ppermute | solution.py:287
  6.3 40.8 %collective-permute-start.2 = (bf16[1,160,2560]{2,1,0:T(8,128)(2,1)}, bf16[1,160,2560]{2,1,0:T(8,128)(2,1)S(1)}, u32[]{:S(2)}, u32[]{:S(2)}) collective-permute-start(bf16[1,160,2560]{2,1,0:T(8,128)(2,1)} %refs_3_.5), channel_id=1, source_target_pairs={{0,24},{4,12},{8,0},{12,20},{16,8},{20,28},{24,16},{28,4},{1,25},{... | collective-permute-start | bytes 2457608 | tf_op jit(solution)/shard_map/ppermute | solution.py:282
  20.3 26.8 %collective-permute-start.3 = (bf16[1,160,2560]{2,1,0:T(8,128)(2,1)}, bf16[1,160,2560]{2,1,0:T(8,128)(2,1)S(1)}, u32[]{:S(2)}, u32[]{:S(2)}) collective-permute-start(bf16[1,160,2560]{2,1,0:T(8,128)(2,1)} %refs_5_.3), channel_id=1, source_target_pairs={{0,24},{4,12},{8,0},{12,20},{16,8},{20,28},{24,16},{28,4},{1,25},{... | collective-permute-start | bytes 2457608 | tf_op jit(solution)/shard_map/ppermute | solution.py:283
  23.6 23.6 %collective-permute-start.10 = (bf16[1,160,2560]{2,1,0:T(8,128)(2,1)}, bf16[1,160,2560]{2,1,0:T(8,128)(2,1)}, u32[]{:S(2)}, u32[]{:S(2)}) collective-permute-start(bf16[1,160,2560]{2,1,0:T(8,128)(2,1)} %collective-permute-done.9.refs_2_), channel_id=1, source_target_pairs={{0,1},{1,0},{2,3},{3,2},{4,5},{5,4},{6,7},{7,6},{8,9},{9,8},{10,11... | collective-permute-start | bytes 2457608 | tf_op jit(solution)/shard_map/ppermute | solution.py:290
  26.3 20.9 %collective-permute-start.11 = (bf16[1,160,2560]{2,1,0:T(8,128)(2,1)}, bf16[1,160,2560]{2,1,0:T(8,128)(2,1)}, u32[]{:S(2)}, u32[]{:S(2)}) collective-permute-start(bf16[1,160,2560]{2,1,0:T(8,128)(2,1)} %collective-permute-done.9.refs_2_), channel_id=1, source_target_pairs={{1,2},{2,1},{5,6},{6,5},{9,10},{10,9},{13,14},{14,13},{17,18},{18,... | collective-permute-start | bytes 2457608 | tf_op jit(solution)/shard_map/ppermute | solution.py:291
  35.4 1.1 copy-start
  36.6 1.1 copy-start.2
  38.8 1.1 copy-start.15
  40.0 1.1 copy-start.17
  41.1 6.1 %copy-start.1 = (bf16[1,160,2560]{2,1,0:T(8,128)(2,1)S(1)}, bf16[1,160,2560]{2,1,0:T(8,128)(2,1)}, u32[]{:S(2)}) copy-start(bf16[1,160,2560]{2,1,0:T(8,128)(2,1)} %refs_3_.5) | copy-start | bytes 2457604
  41.1 6.1 %copy-start.3 = (bf16[1,160,2560]{2,1,0:T(8,128)(2,1)S(1)}, bf16[1,160,2560]{2,1,0:T(8,128)(2,1)}, u32[]{:S(2)}) copy-start(bf16[1,160,2560]{2,1,0:T(8,128)(2,1)} %refs_5_.3) | copy-start | bytes 2457604
  45.9 1.2 %copy-start.8 = (f32[1,160,2688]{2,1,0:T(8,128)}, f32[1,160,2688]{2,1,0:T(8,128)S(1)}, u32[]{:S(2)}) copy-start(f32[1,160,2688]{2,1,0:T(8,128)S(1)} %get-tuple-element.14.refs_0_) | copy-start | bytes 5160964
  47.1 34.2 %collective-permute-start.6 = (bf16[1,160,2688]{2,1,0:T(8,128)(2,1)}, bf16[1,160,2688]{2,1,0:T(8,128)(2,1)}, u32[]{:S(2)}, u32[]{:S(2)}) collective-permute-start(bf16[1,160,2688]{2,1,0:T(8,128)(2,1)} %get-tuple-element.15), channel_id=1, source_target_pairs={{0,1},{1,0},{2,3},{3,2},{4,5},{5,4},{6,7},{7,6},{8,9},{9,8},{10,11... | collective-permute-start | bytes 2580488 | tf_op jit(solution)/shard_map/ppermute | solution.py:319
  47.1 8.9 %copy-start.6 = (bf16[1,160,2560]{2,1,0:T(8,128)(2,1)}, bf16[1,160,2560]{2,1,0:T(8,128)(2,1)S(1)}, u32[]{:S(2)}) copy-start(bf16[1,160,2560]{2,1,0:T(8,128)(2,1)S(1)} %collective-permute-done.3.value_ref.refs_6_) | copy-start | bytes 2457604
  53.0 12.4 %collective-permute-start.15 = (bf16[1,160,1408]{2,1,0:T(8,128)(2,1)S(1)}, bf16[1,160,1408]{2,1,0:T(8,128)(2,1)S(1)}, u32[]{:S(2)}, u32[]{:S(2)}) collective-permute-start(bf16[1,160,1408]{2,1,0:T(8,128)(2,1)S(1)} %get-tuple-element.21), channel_id=1, source_target_pairs={{0,1},{1,0},{2,3},{3,2},{4,5},{5,4},{6,7},{7,6},{8,9},{9,8},{10,11... | collective-permute-start | bytes 1351688 | tf_op jit(solution)/shard_map/ppermute | solution.py:335
  53.5 15.2 %collective-permute-start.16 = (bf16[1,160,1408]{2,1,0:T(8,128)(2,1)S(1)}, bf16[1,160,1408]{2,1,0:T(8,128)(2,1)S(1)}, u32[]{:S(2)}, u32[]{:S(2)}) collective-permute-start(bf16[1,160,1408]{2,1,0:T(8,128)(2,1)S(1)} %get-tuple-element.22), channel_id=1, source_target_pairs={{1,2},{2,1},{5,6},{6,5},{9,10},{10,9},{13,14},{14,13},{17,18},{18,... | collective-permute-start | bytes 1351688 | tf_op jit(solution)/shard_map/ppermute | solution.py:336
  62.4 7.1 %collective-permute-start.12 = (bf16[1,160,1408]{2,1,0:T(8,128)(2,1)S(1)}, bf16[1,160,1408]{2,1,0:T(8,128)(2,1)S(1)}, u32[]{:S(2)}, u32[]{:S(2)}) collective-permute-start(bf16[1,160,1408]{2,1,0:T(8,128)(2,1)S(1)} %get-tuple-element.18), channel_id=1, source_target_pairs={{0,1},{1,0},{2,3},{3,2},{4,5},{5,4},{6,7},{7,6},{8,9},{9,8},{10,11... | collective-permute-start | bytes 1351688 | tf_op jit(solution)/shard_map/ppermute | solution.py:335
  62.4 13.5 %collective-permute-start.13 = (bf16[1,160,1408]{2,1,0:T(8,128)(2,1)}, bf16[1,160,1408]{2,1,0:T(8,128)(2,1)}, u32[]{:S(2)}, u32[]{:S(2)}) collective-permute-start(bf16[1,160,1408]{2,1,0:T(8,128)(2,1)} %get-tuple-element.19), channel_id=1, source_target_pairs={{1,2},{2,1},{5,6},{6,5},{9,10},{10,9},{13,14},{14,13},{17,18},{18,... | collective-permute-start | bytes 1351688 | tf_op jit(solution)/shard_map/ppermute | solution.py:336
  66.2 17.6 %collective-permute-start.7 = (bf16[1,160,2688]{2,1,0:T(8,128)(2,1)}, bf16[1,160,2688]{2,1,0:T(8,128)(2,1)}, u32[]{:S(2)}, u32[]{:S(2)}) collective-permute-start(bf16[1,160,2688]{2,1,0:T(8,128)(2,1)} %get-tuple-element.16), channel_id=1, source_target_pairs={{1,2},{2,1},{5,6},{6,5},{9,10},{10,9},{13,14},{14,13},{17,18},{18,... | collective-permute-start | bytes 2580488 | tf_op jit(solution)/shard_map/ppermute | solution.py:320
  69.6 24.4 %collective-permute-start = (bf16[1,160,2560]{2,1,0:T(8,128)(2,1)S(1)}, bf16[1,160,2560]{2,1,0:T(8,128)(2,1)}, u32[]{:S(2)}, u32[]{:S(2)}) collective-permute-start(bf16[1,160,2560]{2,1,0:T(8,128)(2,1)S(1)} %copy-done.1), channel_id=1, source_target_pairs={{24,0},{12,4},{0,8},{20,12},{8,16},{28,20},{16,24},{4,28},{25,1},{... | collective-permute-start | bytes 2457608 | tf_op jit(solution)/shard_map/ppermute | solution.py:284
  70.3 37.1 %collective-permute-start.1 = (bf16[1,160,2560]{2,1,0:T(8,128)(2,1)S(1)}, bf16[1,160,2560]{2,1,0:T(8,128)(2,1)}, u32[]{:S(2)}, u32[]{:S(2)}) collective-permute-start(bf16[1,160,2560]{2,1,0:T(8,128)(2,1)S(1)} %copy-done.3), channel_id=1, source_target_pairs={{24,0},{12,4},{0,8},{20,12},{8,16},{28,20},{16,24},{4,28},{25,1},{... | collective-permute-start | bytes 2457608 | tf_op jit(solution)/shard_map/ppermute | solution.py:285
  70.3 8.3 %copy-start.11 = (f32[1,160,1408]{2,1,0:T(8,128)S(1)}, f32[1,160,1408]{2,1,0:T(8,128)}, u32[]{:S(2)}) copy-start(f32[1,160,1408]{2,1,0:T(8,128)} %copy-done.10) | copy-start | bytes 2703364
  70.4 1.2 %copy-start.13 = (f32[1,160,1408]{2,1,0:T(8,128)S(1)}, f32[1,160,1408]{2,1,0:T(8,128)}, u32[]{:S(2)}) copy-start(f32[1,160,1408]{2,1,0:T(8,128)} %copy-done.12) | copy-start | bytes 2703364
  73.7 4.9 %copy-start.23 = (bf16[1,160,1408]{2,1,0:T(8,128)(2,1)S(1)}, bf16[1,160,1408]{2,1,0:T(8,128)(2,1)}, u32[]{:S(2)}) copy-start(bf16[1,160,1408]{2,1,0:T(8,128)(2,1)} %copy-done.22) | copy-start | bytes 1351684
  73.7 10.2 %copy-start.5 = (bf16[1,160,2560]{2,1,0:T(8,128)(2,1)S(1)}, bf16[1,160,2560]{2,1,0:T(8,128)(2,1)}, u32[]{:S(2)}) copy-start(bf16[1,160,2560]{2,1,0:T(8,128)(2,1)} %query_ref.3) | copy-start | bytes 2457604
  75.9 31.5 %collective-permute-start.17 = (bf16[1,160,1408]{2,1,0:T(8,128)(2,1)}, bf16[1,160,1408]{2,1,0:T(8,128)(2,1)}, u32[]{:S(2)}, u32[]{:S(2)}) collective-permute-start(bf16[1,160,1408]{2,1,0:T(8,128)(2,1)} %shard_map.51), channel_id=1, source_target_pairs={{0,4},{4,0},{8,12},{12,8},{16,20},{20,16},{24,28},{28,24},{1,5},{5... | collective-permute-start | bytes 1351688 | tf_op jit(solution)/shard_map/ppermute | solution.py:338
  81.3 26.1 %collective-permute-start.14 = (bf16[1,160,1408]{2,1,0:T(8,128)(2,1)}, bf16[1,160,1408]{2,1,0:T(8,128)(2,1)}, u32[]{:S(2)}, u32[]{:S(2)}) collective-permute-start(bf16[1,160,1408]{2,1,0:T(8,128)(2,1)} %shard_map.49), channel_id=1, source_target_pairs={{0,4},{4,0},{8,12},{12,8},{16,20},{20,16},{24,28},{28,24},{1,5},{5... | collective-permute-start | bytes 1351688 | tf_op jit(solution)/shard_map/ppermute | solution.py:338
  83.8 1.1 copy-start.7
  85.0 1.5 %copy-start.9 = (f32[1,160,2688]{2,1,0:T(8,128)S(1)}, f32[1,160,2688]{2,1,0:T(8,128)}, u32[]{:S(2)}) copy-start(f32[1,160,2688]{2,1,0:T(8,128)} %copy-done.8) | copy-start | bytes 5160964
  (10 other events, 9.1 us)

commit v3 on v2

v3 whole, which is shorter than its diff:
```python
import functools

import jax
import jax.numpy as jnp
from jax import lax
from jax.experimental import pallas as pl
from jax.experimental.pallas import tpu as pltpu
from jax.sharding import PartitionSpec as P


HEAD = 128
NEG = -1e30
RATE = HEAD ** (-0.5) * 1.4426950408889634
THIRD = 32
VMEM = pl.BlockSpec(memory_space=pltpu.VMEM)
SMEM = pl.BlockSpec(memory_space=pltpu.SMEM)
GRANT = pltpu.CompilerParams(vmem_limit_bytes=16 << 20)


def column(index):
    return slice(index * HEAD, (index + 1) * HEAD)


def raw_scores(key, query):
    return lax.dot_general(
        key, query, (((1,), (1,)), ((), ())), preferred_element_type=jnp.float32
    )


def weighted(value, weights):
    return lax.dot_general(
        value, weights, (((0,), (0,)), ((), ())), preferred_element_type=jnp.float32
    )


def softmax_rows(raw):
    largest = functools.reduce(
        jnp.maximum, [jnp.max(part, axis=0, keepdims=True) for part in raw]
    )
    expos = [jnp.exp2((part - largest) * RATE) for part in raw]
    total = sum(jnp.sum(expo, axis=0, keepdims=True) for expo in expos)
    return [expo.astype(jnp.bfloat16) for expo in expos], total, largest


def thirds(value):
    high = value.astype(jnp.bfloat16).astype(jnp.float32)
    middle = (value - high).astype(jnp.bfloat16).astype(jnp.float32)
    return high, middle, value - high - middle


def packed(value):
    lane = lax.broadcasted_iota(jnp.int32, value.shape, 1)
    high, middle, low = thirds(value)
    rest = jnp.where(
        lane < 2 * THIRD, pltpu.roll(middle, THIRD, 1), pltpu.roll(low, 2 * THIRD, 1)
    )
    return jnp.where(lane < THIRD, high, rest).astype(jnp.bfloat16)


def read_log(block, heads):
    log = block[0, :, column(heads)].astype(jnp.float32)
    if block.dtype == jnp.float32:
        return log
    return log + pltpu.roll(log, HEAD - THIRD, 1) + pltpu.roll(log, HEAD - 2 * THIRD, 1)


def spread(table, n):
    row = lax.broadcasted_iota(jnp.int32, (HEAD, HEAD), 0)
    chosen = (row == n) | (row == THIRD + n) | (row == 2 * THIRD + n)
    return jnp.dot(
        table,
        jnp.where(chosen, 1.0, 0.0).astype(jnp.bfloat16),
        preferred_element_type=jnp.float32,
    )


def shares(logs):
    largest = functools.reduce(jnp.maximum, logs)
    expos = [jnp.exp2(log - largest) for log in logs]
    total = sum(expos)
    inverse = 1.0 / total
    return [expo * inverse for expo in expos], largest + jnp.log2(total)


def kept(rule, band_ref, twin_ref):
    odd_frame = lax.axis_index("frame") % 2 == 1
    row = lax.axis_index("row")
    return rule(
        [band_ref[0, i] for i in range(5)],
        [twin_ref[0, i] for i in range(5)] if twin_ref is not None else None,
        odd_frame,
        (row > 0) & (row < lax.axis_size("row") - 1),
    )


def parts_kernel(query_count, key_count, first, heads, rule, *refs):
    band_ref, twin_ref, refs = refs[0], refs[1], refs[2:]
    queries = refs[:query_count]
    keys = refs[query_count : query_count + key_count]
    values = refs[query_count + key_count : query_count + 2 * key_count]
    outs = refs[query_count + 2 * key_count : -1]
    log_scratch = refs[-1]
    rows = queries[0].shape[1]
    wide = query_count * rows
    lane = lax.broadcasted_iota(jnp.int32, (1, wide), 1)
    keeps = kept(rule, band_ref, twin_ref)
    biases = []
    for i in range(key_count):
        bias = jnp.zeros((1, wide), jnp.float32)
        for at in range(query_count):
            if keeps[at][i] is not True:
                bias = jnp.where(
                    (lane >= at * rows) & (lane < (at + 1) * rows),
                    jnp.where(keeps[at][i], 0.0, NEG),
                    bias,
                )
        biases.append(bias)
    log_scratch[...] = jnp.zeros(log_scratch.shape, jnp.float32)

    def of(ref, n):
        start = 0 if ref.shape[2] == heads * HEAD else first
        return ref[0, :, column(start + n)]

    def score(n):
        query = jnp.concatenate([of(ref, n) for ref in queries], 0)
        return [raw_scores(of(key, n), query) + bias for key, bias in zip(keys, biases)]

    def attend(n, weights, total, largest):
        summed = sum(weighted(of(value, n), part) for value, part in zip(values, weights))
        log_scratch[n : n + 1, :] = largest * RATE + jnp.log2(total)
        normed = (summed * (1.0 / total)).T
        for at, out in enumerate(outs):
            out[0, :, column(n)] = normed[at * rows : (at + 1) * rows].astype(out.dtype)

    raw = score(0)
    before = None
    for n in range(heads):
        later = score(n + 1) if n + 1 < heads else None
        now = softmax_rows(raw)
        if before is not None:
            attend(n - 1, *before)
        before, raw = now, later
    attend(heads - 1, *before)
    logs = log_scratch[...].T
    for at, out in enumerate(outs):
        log = logs[at * rows : (at + 1) * rows]
        out[0, :, column(heads)] = log if out.dtype == jnp.float32 else packed(log)


def parts(bands, queries, keys, values, rule, kinds, first, heads):
    rows = queries[0].shape[1]
    wide = len(queries) * rows
    blocks = len(queries) * len(keys)
    width = heads * HEAD
    return pl.pallas_call(
        functools.partial(parts_kernel, len(queries), len(keys), first, heads, rule),
        in_specs=[SMEM] * 2 + [VMEM] * (len(queries) + 2 * len(keys)),
        out_specs=[VMEM] * len(queries),
        out_shape=[
            jax.ShapeDtypeStruct((1, rows, width + HEAD), kind) for kind in kinds
        ],
        scratch_shapes=[pltpu.VMEM((HEAD, wide), jnp.float32)],
        compiler_params=GRANT,
        cost_estimate=pl.CostEstimate(
            flops=4 * rows * rows * width * blocks,
            bytes_accessed=2 * rows * width * (2 * len(queries) + 2 * len(keys)),
            transcendentals=rows * rows * heads * blocks,
        ),
    )(*bands, *queries, *keys, *values)


def merge_kernel(heads, rule, band_ref, *refs):
    blocks, out_ref = refs[:-1], refs[-1]
    keeps = kept(rule, band_ref, None)
    logs = []
    for keep, block in zip(keeps, blocks):
        log = read_log(block, heads)
        logs.append(log if keep is True else jnp.where(keep, log, NEG))
    weights, log = shares(logs)
    tables = [packed(weight) for weight in weights]
    for n in range(heads):
        cols = column(n)
        out_ref[0, :, cols] = sum(
            spread(table, n) * block[0, :, cols].astype(jnp.float32)
            for table, block in zip(tables, blocks)
        ).astype(out_ref.dtype)
    out_ref[0, :, column(heads)] = packed(log)


def merged(band, blocks, rule):
    rows, width = blocks[0].shape[1:]
    heads = width // HEAD - 1
    return pl.pallas_call(
        functools.partial(merge_kernel, heads, rule),
        in_specs=[SMEM] + [VMEM] * len(blocks),
        out_specs=VMEM,
        out_shape=jax.ShapeDtypeStruct((1, rows, width), jnp.bfloat16),
        compiler_params=GRANT,
        cost_estimate=pl.CostEstimate(
            flops=2 * rows * width * len(blocks),
            bytes_accessed=2 * rows * width * (len(blocks) + 1),
            transcendentals=0,
        ),
    )(band, *blocks)


def score_kernel(rule, band_ref, query_ref, *refs):
    keys, (weight_ref, table_ref, scratch) = refs[:-3], refs[-3:]
    bias = jnp.where(kept(rule, band_ref, None)[0], 0.0, NEG)
    places = [(key, n) for key in keys for n in range(key.shape[2] // HEAD)]
    scratch[...] = jnp.zeros(scratch.shape, jnp.float32)

    def score(at):
        key, n = places[at]
        return [raw_scores(key[0, :, column(n)], query_ref[0, :, column(at)]) + bias]

    raw = score(0)
    for n in range(len(places)):
        later = score(n + 1) if n + 1 < len(places) else None
        (weights,), total, largest = softmax_rows(raw)
        weight_ref[n] = weights
        scratch[0, n : n + 1, :] = largest * RATE + jnp.log2(total)
        scratch[1, n : n + 1, :] = 1.0 / total
        raw = later
    table_ref[0] = scratch[0].T
    table_ref[1] = scratch[1].T


def scored(band, query, keys, rule):
    rows, width = query.shape[1:]
    heads = width // HEAD
    return pl.pallas_call(
        functools.partial(score_kernel, rule),
        in_specs=[SMEM] + [VMEM] * (1 + len(keys)),
        out_specs=[VMEM] * 2,
        out_shape=[
            jax.ShapeDtypeStruct((heads, rows, rows), jnp.bfloat16),
            jax.ShapeDtypeStruct((2, rows, HEAD), jnp.float32),
        ],
        scratch_shapes=[pltpu.VMEM((2, HEAD, rows), jnp.float32)],
        compiler_params=GRANT,
        cost_estimate=pl.CostEstimate(
            flops=2 * rows * rows * width,
            bytes_accessed=6 * rows * width,
            transcendentals=rows * rows * heads,
        ),
    )(band, query, *keys)


def combine_kernel(value_count, groups, heads, rule, last, band_ref, weight_ref, table_ref, *refs):
    values, refs = refs[:value_count], refs[value_count:]
    pieces, out_ref = refs[:-1], refs[-1]
    keeps = kept(rule, band_ref, None)
    rows = out_ref.shape[1]
    lane = lax.broadcasted_iota(jnp.int32, (rows, HEAD), 1)
    value_at = [(value, n) for value in values for n in range(value.shape[2] // HEAD)]
    logs = [table_ref[0]]
    places = []
    at = 0
    for keep, group in zip(keeps, groups):
        log = None
        place = []
        for size in group:
            part = read_log(pieces[at], size)
            if log is None:
                log = part
            else:
                log = jnp.where(lane >= len(place), pltpu.roll(part, len(place), 1), log)
            place += [(at, n) for n in range(size)]
            at += 1
        logs.append(log if keep is True else jnp.where(keep, log, NEG))
        places.append(place)
    weights, log = shares(logs)
    weights[0] = weights[0] * table_ref[1]
    tables = [packed(weight) for weight in weights]
    for n in range(heads):
        value, index = value_at[n]
        out = weighted(value[0, :, column(index)], weight_ref[n]).T * spread(tables[0], n)
        for table, place in zip(tables[1:], places):
            piece, index = place[n]
            block = pieces[piece][0, :, column(index)].astype(jnp.float32)
            out = out + spread(table, n) * block
        out_ref[0, :, column(n)] = out.astype(out_ref.dtype)
    if not last:
        out_ref[0, :, column(heads)] = log


def combined(band, score, values, groups, rule, last):
    weights, table = score
    heads, rows = weights.shape[:2]
    width = heads * HEAD
    kind = values[0].dtype if last else jnp.float32
    sizes = tuple(tuple(piece.shape[2] // HEAD - 1 for piece in group) for group in groups)
    pieces = [piece for group in groups for piece in group]
    return pl.pallas_call(
        functools.partial(combine_kernel, len(values), sizes, heads, rule, last),
        in_specs=[SMEM] + [VMEM] * (2 + len(values) + len(pieces)),
        out_specs=VMEM,
        out_shape=jax.ShapeDtypeStruct((1, rows, width + (0 if last else HEAD)), kind),
        compiler_params=GRANT,
        cost_estimate=pl.CostEstimate(
            flops=2 * rows * rows * width,
            bytes_accessed=2 * rows * width * (len(pieces) + 4),
            transcendentals=0,
        ),
    )(band, weights, table, *values, *pieces)


def per_device(queries, keys, values, band):
    frames, bands = lax.axis_size("frame"), lax.axis_size("row")
    toward = [(f, (f + 2) % frames) if f % 2 else (f, (f - 2) % frames) for f in range(frames)]
    away = [(target, source) for source, target in toward]
    twin = [(f, f ^ 1) for f in range(frames)]
    even = [(r, r ^ 1) for r in range(bands)]
    odd = [(r, r + 1) for r in range(1, bands - 1, 2)]
    odd += [(target, source) for source, target in odd]

    narrow, full = jnp.bfloat16, jnp.float32
    heads = queries.shape[2] // HEAD
    half = heads // 2
    spans = [(0, half), (half, heads - half)]

    near = []
    for first, size in spans:
        cut = slice(first * HEAD, (first + size) * HEAD)
        near.append(
            (
                lax.ppermute(keys[:, :, cut], "frame", toward),
                lax.ppermute(values[:, :, cut], "frame", toward),
            )
        )
    key_two = lax.ppermute(keys, "frame", away)
    value_two = lax.ppermute(values, "frame", away)
    query_twin = []
    for first, size in spans:
        cut = slice(first * HEAD, (first + size) * HEAD)
        query_twin.append(lax.ppermute(queries[:, :, cut], "frame", twin))
    band_twin = lax.ppermute(band, "frame", twin)
    query_even = lax.ppermute(queries, "row", even)
    query_odd = lax.ppermute(queries, "row", odd)
    twin_even = [lax.ppermute(query_twin[span], "row", even) for span in (0, 1)]
    twin_odd = [lax.ppermute(query_twin[span], "row", odd) for span in (0, 1)]

    def beside_rule(own, other, odd_frame, has_odd):
        return [[own[2] >= 1], [own[2] >= 1], [True]]

    even_part, odd_part, own_part = parts(
        (band, band),
        [query_even, query_odd, queries],
        [keys],
        [values],
        beside_rule,
        (narrow, narrow, full),
        0,
        heads,
    )
    from_even = lax.ppermute(even_part, "row", even)
    from_odd = lax.ppermute(odd_part, "row", odd)

    def twin_rule(own, other, odd_frame, has_odd):
        here = jnp.where(odd_frame, other[3], other[1])
        there = jnp.where(odd_frame, other[1], other[3])
        beside = [here >= 1, there >= 1]
        return [beside, beside, [here >= 0, there >= 0]]

    from_twin = []
    for span, (first, size) in enumerate(spans):
        even_twin, odd_twin, own_twin = parts(
            (band, band_twin),
            [twin_even[span], twin_odd[span], query_twin[span]],
            [keys, near[span][0]],
            [values, near[span][1]],
            twin_rule,
            (narrow, narrow, full),
            first,
            size,
        )
        back_even = lax.ppermute(even_twin, "row", even)
        back_odd = lax.ppermute(odd_twin, "row", odd)
        whole = merged(
            band,
            [own_twin, back_even, back_odd],
            lambda own, other, odd_frame, has_odd: [True, True, has_odd],
        )
        from_twin.append(lax.ppermute(whole, "frame", twin))

    near_score = scored(
        band,
        queries,
        [pair[0] for pair in near],
        lambda own, other, odd_frame, has_odd: [jnp.where(odd_frame, own[0], own[4]) >= 0],
    )
    near_all = combined(
        band,
        near_score,
        [pair[1] for pair in near],
        [[own_part], [from_even], [from_odd]],
        lambda own, other, odd_frame, has_odd: [True, True, has_odd],
        False,
    )
    far_score = scored(
        band,
        queries,
        [key_two],
        lambda own, other, odd_frame, has_odd: [jnp.where(odd_frame, own[4], own[0]) >= 0],
    )
    return combined(
        band,
        far_score,
        [value_two],
        [[near_all], from_twin],
        lambda own, other, odd_frame, has_odd: [True, True],
        True,
    )


def solution(mesh):
    return jax.shard_map(
        per_device,
        mesh=mesh,
        in_specs=(
            P("frame", "row", None),
            P("frame", "row", None),
            P("frame", "row", None),
            P("frame", None),
        ),
        out_specs=P("frame", "row", None),
        check_vma=False,
    )
```

time: 116 us -> 97.6 us (0.84)
  the two profiles are of different devices: /device:TPU:1 before, /device:TPU:0 now
where the time goes in v3:
time: 97.6 us; the launch traced here: 97.3 us
  waiting for transfers between devices  37.6 us (39%)
  starting transfers between devices  34 us (35%)
  Pallas kernels  24.1 us (25%)
  local copies, waits for them, and re-layouts  1.43 us (1%)
    ppermute x1, waiting for transfers between devices, per_device(): band_twin = lax.ppermute(band, 'frame', twin)  12 us
    pallas_call x3, Pallas kernels, parts(): pl.pallas_call(functools.partial(parts_kernel, len(queries), len(keys), f...  11.2 us
    ppermute x1, waiting for transfers between devices, per_device(): value_two = lax.ppermute(values, 'frame', away)  10.4 us
    ppermute x1, waiting for transfers between devices, per_device(): key_two = lax.ppermute(keys, 'frame', away)  9.15 us
    ppermute x2, starting transfers between devices, per_device(): lax.ppermute(keys[:, :, cut], 'frame', toward)  7.48 us
    pallas_call x2, Pallas kernels, combined(): pl.pallas_call(functools.partial(combine_kernel, len(values), sizes, head...  6.44 us
    ppermute x2, starting transfers between devices, per_device(): lax.ppermute(values[:, :, cut], 'frame', toward)  4.78 us
    pallas_call x2, Pallas kernels, scored(): pl.pallas_call(functools.partial(score_kernel, rule), in_specs=[SMEM] + [...  4.04 us
  transfers between devices with their start and end apart: 23, of which 5 were waited for; matrix products, arithmetic and copies ran while one was open for 0% of the time, Pallas kernels for 21%

profile of v3, /device:TPU:0, one launch (start us, length us, event | category | flops | bytes accessed | tf_op | source)
XLA Modules:
  0.0 97.3 jit_solution(16842649610829104720)
XLA Ops:
  0.0 1.3 %fusion = (bf16[1,160,1280]{2,1,0:T(8,128)(2,1)S(1)}, bf16[1,160,1280]{2,1,0:T(8,128)(2,1)S(1)}) fusion(bf16[1,160,2560]{2,1,0:T(8,128)(2,1)} %refs_4_.1), kind=kLoop, calls=%fused_computation | loop fusion | bytes 1638400 | tf_op jit(solution)/shard_map/slice | solution.py:337
  1.3 3.1 %collective-permute-start.17 = (bf16[1,160,1280]{2,1,0:T(8,128)(2,1)S(1)}, bf16[1,160,1280]{2,1,0:T(8,128)(2,1)S(1)}, u32[]{:S(2)}, u32[]{:S(2)}) collective-permute-start(bf16[1,160,1280]{2,1,0:T(8,128)(2,1)S(1)} %get-tuple-element.31), channel_id=1, source_target_pairs={{0,4},{4,0},{8,12},{12,8},{16,20},{20,16},{24,28},{28,24},{1,5},{5... | collective-permute-start | bytes 1228808 | tf_op jit(solution)/shard_map/ppermute | solution.py:337
  4.5 3.7 %collective-permute-start.3 = (bf16[1,160,1280]{2,1,0:T(8,128)(2,1)S(1)}, bf16[1,160,1280]{2,1,0:T(8,128)(2,1)S(1)}, u32[]{:S(2)}, u32[]{:S(2)}) collective-permute-start(bf16[1,160,1280]{2,1,0:T(8,128)(2,1)S(1)} %get-tuple-element.35), channel_id=1, source_target_pairs={{0,24},{4,12},{8,0},{12,20},{16,8},{20,28},{24,16},{28,4},{1,25},{... | collective-permute-start | bytes 1228808 | tf_op jit(solution)/shard_map/ppermute | solution.py:328
  8.2 0.5 collective-permute-start.5
  8.7 2.0 %collective-permute-start.10 = (s32[1,5]{1,0:T(1,128)S(1)}, s32[1,5]{1,0:T(1,128)S(1)}, u32[]{:S(2)}, u32[]{:S(2)}) collective-permute-start(s32[1,5]{1,0:T(1,128)S(1)} %copy-done.3), channel_id=1, source_target_pairs={{0,4},{4,0},{8,12},{12,8},{16,20},{20,16},{24,28},{28,24},{1,5},{5... | collective-permute-start | bytes 68 | tf_op jit(solution)/shard_map/ppermute | solution.py:338
  10.7 12.0 %collective-permute-done.10.refs_1_ = s32[1,5]{1,0:T(1,128)S(1)} collective-permute-done((s32[1,5]{1,0:T(1,128)S(1)}, s32[1,5]{1,0:T(1,128)S(1)}, u32[]{:S(2)}, u32[]{:S(2)}) %collective-permute-start.10) | collective-permute-done | bytes 52 | tf_op jit(solution)/shard_map/ppermute | solution.py:338
  22.7 3.8 %collective-permute-start.2 = (bf16[1,160,1280]{2,1,0:T(8,128)(2,1)S(1)}, bf16[1,160,1280]{2,1,0:T(8,128)(2,1)S(1)}, u32[]{:S(2)}, u32[]{:S(2)}) collective-permute-start(bf16[1,160,1280]{2,1,0:T(8,128)(2,1)S(1)} %get-tuple-element.36), channel_id=1, source_target_pairs={{0,24},{4,12},{8,0},{12,20},{16,8},{20,28},{24,16},{28,4},{1,25},{... | collective-permute-start | bytes 1228808 | tf_op jit(solution)/shard_map/ppermute | solution.py:328
  26.6 0.7 collective-permute-start.19
  27.3 2.9 %collective-permute-start.6 = (bf16[1,160,2560]{2,1,0:T(8,128)(2,1)S(1)}, bf16[1,160,2560]{2,1,0:T(8,128)(2,1)S(1)}, u32[]{:S(2)}, u32[]{:S(2)}) collective-permute-start(bf16[1,160,2560]{2,1,0:T(8,128)(2,1)S(1)} %copy-done.1), channel_id=1, source_target_pairs={{0,1},{1,0},{2,3},{3,2},{4,5},{5,4},{6,7},{7,6},{8,9},{9,8},{10,11... | collective-permute-start | bytes 2457608 | tf_op jit(solution)/shard_map/ppermute | solution.py:339
  30.2 0.7 collective-permute-start.7
  30.9 3.5 %collective-permute-done.2.refs_0_.refs_6_ = bf16[1,160,1280]{2,1,0:T(8,128)(2,1)S(1)} collective-permute-done((bf16[1,160,1280]{2,1,0:T(8,128)(2,1)S(1)}, bf16[1,160,1280]{2,1,0:T(8,128)(2,1)S(1)}, u32[]{:S(2)}, u32[]{:S(2)}) %collective-permute-start.2) | collective-permute-done | bytes 409632 | tf_op jit(solution)/shard_map/ppermute | solution.py:328
  34.3 4.3 %collective-permute-start.4 = (bf16[1,160,1280]{2,1,0:T(8,128)(2,1)S(1)}, bf16[1,160,1280]{2,1,0:T(8,128)(2,1)S(1)}, u32[]{:S(2)}, u32[]{:S(2)}) collective-permute-start(bf16[1,160,1280]{2,1,0:T(8,128)(2,1)S(1)} %get-tuple-element.34), channel_id=1, source_target_pairs={{0,24},{4,12},{8,0},{12,20},{16,8},{20,28},{24,16},{28,4},{1,25},{... | collective-permute-start | bytes 1228808 | tf_op jit(solution)/shard_map/ppermute | solution.py:329
  38.6 0.7 collective-permute-start.13
  39.3 3.8 %shard_map.52 = (bf16[1,160,1408]{2,1,0:T(8,128)(2,1)S(1)}, bf16[1,160,1408]{2,1,0:T(8,128)(2,1)S(1)}, f32[1,160,1408]{2,1,0:T(8,128)S(1)}) custom-call(s32[1,5]{1,0:T(1,128)S(1)} %copy-done.3, s32[1,5]{1,0:T(1,128)S(1)} %collective-permute-done.10.refs_1_, bf16[1,160,1280]{2,1,0:T(8,128)(2,1)S(1)} %collective-permute-done.18.refs_2_, ...), custom_call_target="tpu_custom_call" | custom-call | flops 786432000 | bytes 4096000 | tf_op jit(solution)/shard_map/pallas_call | solution.py:155
  43.1 2.4 %collective-permute-done.4.refs_0_.refs_8_ = bf16[1,160,1280]{2,1,0:T(8,128)(2,1)S(1)} collective-permute-done((bf16[1,160,1280]{2,1,0:T(8,128)(2,1)S(1)}, bf16[1,160,1280]{2,1,0:T(8,128)(2,1)S(1)}, u32[]{:S(2)}, u32[]{:S(2)}) %collective-permute-start.4) | collective-permute-done | bytes 409632 | tf_op jit(solution)/shard_map/ppermute | solution.py:329
  46.0 0.7 collective-permute-start.21
  46.7 3.8 %shard_map.50 = (bf16[1,160,1408]{2,1,0:T(8,128)(2,1)S(1)}, bf16[1,160,1408]{2,1,0:T(8,128)(2,1)S(1)}, f32[1,160,1408]{2,1,0:T(8,128)S(1)}) custom-call(s32[1,5]{1,0:T(1,128)S(1)} %copy-done.3, s32[1,5]{1,0:T(1,128)S(1)} %collective-permute-done.10.refs_1_, bf16[1,160,1280]{2,1,0:T(8,128)(2,1)S(1)} %collective-permute-done.12.refs_2_, ...), custom_call_target="tpu_custom_call" | custom-call | flops 786432000 | bytes 4096000 | tf_op jit(solution)/shard_map/pallas_call | solution.py:155
  50.5 2.8 %collective-permute-start.14 = (bf16[1,160,1408]{2,1,0:T(8,128)(2,1)S(1)}, bf16[1,160,1408]{2,1,0:T(8,128)(2,1)S(1)}, u32[]{:S(2)}, u32[]{:S(2)}) collective-permute-start(bf16[1,160,1408]{2,1,0:T(8,128)(2,1)S(1)} %get-tuple-element.26), channel_id=1, source_target_pairs={{0,1},{1,0},{2,3},{3,2},{4,5},{5,4},{6,7},{7,6},{8,9},{9,8},{10,11... | collective-permute-start | bytes 1351688 | tf_op jit(solution)/shard_map/ppermute | solution.py:378
  53.3 0.7 collective-permute-start.15
  54.0 3.6 %shard_map.48 = (bf16[1,160,2688]{2,1,0:T(8,128)(2,1)S(1)}, bf16[1,160,2688]{2,1,0:T(8,128)(2,1)S(1)}, f32[1,160,2688]{2,1,0:T(8,128)S(1)}) custom-call(s32[1,5]{1,0:T(1,128)S(1)} %copy-done.3, s32[1,5]{1,0:T(1,128)S(1)} %copy-done.3, bf16[1,160,2560]{2,1,0:T(8,128)(2,1)S(1)} %collective-permute-done.6.refs_2_, ...), custom_call_target="tpu_custom_call" | custom-call | flops 786432000 | bytes 6553600 | tf_op jit(solution)/shard_map/pallas_call | solution.py:155
  57.7 2.5 %collective-permute-start.8 = (bf16[1,160,2688]{2,1,0:T(8,128)(2,1)S(1)}, bf16[1,160,2688]{2,1,0:T(8,128)(2,1)S(1)}, u32[]{:S(2)}, u32[]{:S(2)}) collective-permute-start(bf16[1,160,2688]{2,1,0:T(8,128)(2,1)S(1)} %get-tuple-element.23), channel_id=1, source_target_pairs={{0,1},{1,0},{2,3},{3,2},{4,5},{5,4},{6,7},{7,6},{8,9},{9,8},{10,11... | collective-permute-start | bytes 2580488 | tf_op jit(solution)/shard_map/ppermute | solution.py:357
  60.1 0.7 collective-permute-start.9
  60.9 1.2 %collective-permute-start.1 = (bf16[1,160,2560]{2,1,0:T(8,128)(2,1)S(1)}, bf16[1,160,2560]{2,1,0:T(8,128)(2,1)S(1)}, u32[]{:S(2)}, u32[]{:S(2)}) collective-permute-start(bf16[1,160,2560]{2,1,0:T(8,128)(2,1)S(1)} %copy-done.2), channel_id=1, source_target_pairs={{24,0},{12,4},{0,8},{20,12},{8,16},{28,20},{16,24},{4,28},{25,1},{... | collective-permute-start | bytes 2457608 | tf_op jit(solution)/shard_map/ppermute | solution.py:333
  62.0 1.2 %shard_map.53 = bf16[1,160,1408]{2,1,0:T(8,128)(2,1)S(1)} custom-call(s32[1,5]{1,0:T(1,128)S(1)} %copy-done.3, f32[1,160,1408]{2,1,0:T(8,128)S(1)} %get-tuple-element.28.refs_0_, bf16[1,160,1408]{2,1,0:T(8,128)(2,1)S(1)} %collective-permute-done.20.refs_1_, bf16[1,160,1408]{2,1,0:T(8,128)(2,1)S(1)} %collective-permute-done.21.refs_2_), custom_call_target="tpu_custom_call" | custom-call | flops 1351680 | bytes 1802240 | tf_op jit(solution)/shard_map/pallas_call | solution.py:193
  63.3 2.6 %collective-permute-start.22 = (bf16[1,160,1408]{2,1,0:T(8,128)(2,1)S(1)}, bf16[1,160,1408]{2,1,0:T(8,128)(2,1)S(1)}, u32[]{:S(2)}, u32[]{:S(2)}) collective-permute-start(bf16[1,160,1408]{2,1,0:T(8,128)(2,1)S(1)} %shard_map.53), channel_id=1, source_target_pairs={{0,4},{4,0},{8,12},{12,8},{16,20},{20,16},{24,28},{28,24},{1,5},{5... | collective-permute-start | bytes 1351688 | tf_op jit(solution)/shard_map/ppermute | solution.py:385
  65.9 1.2 %shard_map.51 = bf16[1,160,1408]{2,1,0:T(8,128)(2,1)S(1)} custom-call(s32[1,5]{1,0:T(1,128)S(1)} %copy-done.3, f32[1,160,1408]{2,1,0:T(8,128)S(1)} %get-tuple-element.25.refs_0_, bf16[1,160,1408]{2,1,0:T(8,128)(2,1)S(1)} %collective-permute-done.14.refs_1_, bf16[1,160,1408]{2,1,0:T(8,128)(2,1)S(1)} %collective-permute-done.15.refs_2_), custom_call_target="tpu_custom_call" | custom-call | flops 1351680 | bytes 1802240 | tf_op jit(solution)/shard_map/pallas_call | solution.py:193
  67.1 9.2 %collective-permute-done.refs_0_ = bf16[1,160,2560]{2,1,0:T(8,128)(2,1)S(1)} collective-permute-done((bf16[1,160,2560]{2,1,0:T(8,128)(2,1)S(1)}, bf16[1,160,2560]{2,1,0:T(8,128)(2,1)S(1)}, u32[]{:S(2)}, u32[]{:S(2)}) %collective-permute-start) | collective-permute-done | bytes 819232 | tf_op jit(solution)/shard_map/ppermute | solution.py:332
  76.4 2.0 %shard_map.47 = (bf16[20,160,160]{2,1,0:T(8,128)(2,1)S(1)}, f32[2,160,128]{2,1,0:T(8,128)S(1)}) custom-call(s32[1,5]{1,0:T(1,128)S(1)} %copy-done.3, bf16[1,160,2560]{2,1,0:T(8,128)(2,1)S(1)} %copy-done.1, bf16[1,160,1280]{2,1,0:T(8,128)(2,1)S(1)} %collective-permute-done.2.refs_0_.refs_6_, bf16[1,160,1280]{2,1,0:T(8,128)(2,1)S(1)} %collective-permute-done.3.refs_1_.refs_6_), custom_call_target="tpu_custom_call" | custom-call | flops 131072000 | bytes 2457600 | tf_op jit(solution)/shard_map/pallas_call | solution.py:232
  78.4 2.0 %shard_map.46 = (bf16[20,160,160]{2,1,0:T(8,128)(2,1)S(1)}, f32[2,160,128]{2,1,0:T(8,128)S(1)}) custom-call(s32[1,5]{1,0:T(1,128)S(1)} %copy-done.3, bf16[1,160,2560]{2,1,0:T(8,128)(2,1)S(1)} %copy-done.1, bf16[1,160,2560]{2,1,0:T(8,128)(2,1)S(1)} %collective-permute-done.refs_0_), custom_call_target="tpu_custom_call" | custom-call | flops 131072000 | bytes 2457600 | tf_op jit(solution)/shard_map/pallas_call | solution.py:232
  80.4 2.4 %shard_map.49.refs_1_ = f32[1,160,2688]{2,1,0:T(8,128)S(1)} custom-call(s32[1,5]{1,0:T(1,128)S(1)} %copy-done.3, bf16[20,160,160]{2,1,0:T(8,128)(2,1)S(1)} %get-tuple-element.20.weight_ref, f32[2,160,128]{2,1,0:T(8,128)S(1)} %get-tuple-element.21.table_ref, bf16[1,160,1280]{2,1,0:T(8,128)(2,1)S(1)} %collective-permute-done.4.refs_0_.refs_8_, ...), custom_call_target="tpu_custom_call" | custom-call | flops 131072000 | bytes 5734400 | tf_op jit(solution)/shard_map/pallas_call | solution.py:295
  82.8 10.4 %collective-permute-done.1.refs_0_ = bf16[1,160,2560]{2,1,0:T(8,128)(2,1)S(1)} collective-permute-done((bf16[1,160,2560]{2,1,0:T(8,128)(2,1)S(1)}, bf16[1,160,2560]{2,1,0:T(8,128)(2,1)S(1)}, u32[]{:S(2)}, u32[]{:S(2)}) %collective-permute-start.1) | collective-permute-done | bytes 819232 | tf_op jit(solution)/shard_map/ppermute | solution.py:333
  93.2 4.1 %shard_map.54 = bf16[1,160,2560]{2,1,0:T(8,128)(2,1)} custom-call(s32[1,5]{1,0:T(1,128)S(1)} %copy-done.3, bf16[20,160,160]{2,1,0:T(8,128)(2,1)S(1)} %get-tuple-element.18.weight_ref, f32[2,160,128]{2,1,0:T(8,128)S(1)} %get-tuple-element.19.table_ref, bf16[1,160,2560]{2,1,0:T(8,128)(2,1)S(1)} %collective-permute-done.1.refs_0_, ...), custom_call_target="tpu_custom_call" | custom-call | flops 131072000 | bytes 5734400 | tf_op jit(solution)/shard_map/pallas_call | solution.py:295
  (34 shorter events, 0.7 us)
Async XLA Ops:
  0.0 4.4 %copy-start = (bf16[1,160,2560]{2,1,0:T(8,128)(2,1)S(1)}, bf16[1,160,2560]{2,1,0:T(8,128)(2,1)}, u32[]{:S(2)}) copy-start(bf16[1,160,2560]{2,1,0:T(8,128)(2,1)} %refs_5_.5) | copy-start | bytes 2457604
  0.0 8.1 %copy-start.2 = (bf16[1,160,2560]{2,1,0:T(8,128)(2,1)S(1)}, bf16[1,160,2560]{2,1,0:T(8,128)(2,1)}, u32[]{:S(2)}) copy-start(bf16[1,160,2560]{2,1,0:T(8,128)(2,1)} %refs_7_.3) | copy-start | bytes 2457604
  1.3 7.4 %copy-start.3 = (s32[1,5]{1,0:T(1,128)S(1)}, s32[1,5]{1,0:T(1,128)}, u32[]{:S(2)}) copy-start(s32[1,5]{1,0:T(1,128)} %band_ref.11) | copy-start | bytes 64
  1.3 26.0 %copy-start.1 = (bf16[1,160,2560]{2,1,0:T(8,128)(2,1)S(1)}, bf16[1,160,2560]{2,1,0:T(8,128)(2,1)}, u32[]{:S(2)}) copy-start(bf16[1,160,2560]{2,1,0:T(8,128)(2,1)} %refs_4_.1) | copy-start | bytes 2457604
  1.3 25.2 %collective-permute-start.17 = (bf16[1,160,1280]{2,1,0:T(8,128)(2,1)S(1)}, bf16[1,160,1280]{2,1,0:T(8,128)(2,1)S(1)}, u32[]{:S(2)}, u32[]{:S(2)}) collective-permute-start(bf16[1,160,1280]{2,1,0:T(8,128)(2,1)S(1)} %get-tuple-element.31), channel_id=1, source_target_pairs={{0,4},{4,0},{8,12},{12,8},{16,20},{20,16},{24,28},{28,24},{1,5},{5... | collective-permute-start | bytes 1228808 | tf_op jit(solution)/shard_map/ppermute | solution.py:337
  4.5 22.1 %collective-permute-start.3 = (bf16[1,160,1280]{2,1,0:T(8,128)(2,1)S(1)}, bf16[1,160,1280]{2,1,0:T(8,128)(2,1)S(1)}, u32[]{:S(2)}, u32[]{:S(2)}) collective-permute-start(bf16[1,160,1280]{2,1,0:T(8,128)(2,1)S(1)} %get-tuple-element.35), channel_id=1, source_target_pairs={{0,24},{4,12},{8,0},{12,20},{16,8},{20,28},{24,16},{28,4},{1,25},{... | collective-permute-start | bytes 1228808 | tf_op jit(solution)/shard_map/ppermute | solution.py:328
  8.2 19.1 %collective-permute-start.5 = (bf16[1,160,1280]{2,1,0:T(8,128)(2,1)S(1)}, bf16[1,160,1280]{2,1,0:T(8,128)(2,1)S(1)}, u32[]{:S(2)}, u32[]{:S(2)}) collective-permute-start(bf16[1,160,1280]{2,1,0:T(8,128)(2,1)S(1)} %get-tuple-element.33), channel_id=1, source_target_pairs={{0,24},{4,12},{8,0},{12,20},{16,8},{20,28},{24,16},{28,4},{1,25},{... | collective-permute-start | bytes 1228808 | tf_op jit(solution)/shard_map/ppermute | solution.py:329
  8.7 21.5 %collective-permute-start.11 = (bf16[1,160,1280]{2,1,0:T(8,128)(2,1)S(1)}, bf16[1,160,1280]{2,1,0:T(8,128)(2,1)S(1)}, u32[]{:S(2)}, u32[]{:S(2)}) collective-permute-start(bf16[1,160,1280]{2,1,0:T(8,128)(2,1)S(1)} %get-tuple-element.32), channel_id=1, source_target_pairs={{0,4},{4,0},{8,12},{12,8},{16,20},{20,16},{24,28},{28,24},{1,5},{5... | collective-permute-start | bytes 1228808 | tf_op jit(solution)/shard_map/ppermute | solution.py:337
  8.7 14.1 %collective-permute-start.10 = (s32[1,5]{1,0:T(1,128)S(1)}, s32[1,5]{1,0:T(1,128)S(1)}, u32[]{:S(2)}, u32[]{:S(2)}) collective-permute-start(s32[1,5]{1,0:T(1,128)S(1)} %copy-done.3), channel_id=1, source_target_pairs={{0,4},{4,0},{8,12},{12,8},{16,20},{20,16},{24,28},{28,24},{1,5},{5... | collective-permute-start | bytes 68 | tf_op jit(solution)/shard_map/ppermute | solution.py:338
  22.7 11.6 %collective-permute-start.2 = (bf16[1,160,1280]{2,1,0:T(8,128)(2,1)S(1)}, bf16[1,160,1280]{2,1,0:T(8,128)(2,1)S(1)}, u32[]{:S(2)}, u32[]{:S(2)}) collective-permute-start(bf16[1,160,1280]{2,1,0:T(8,128)(2,1)S(1)} %get-tuple-element.36), channel_id=1, source_target_pairs={{0,24},{4,12},{8,0},{12,20},{16,8},{20,28},{24,16},{28,4},{1,25},{... | collective-permute-start | bytes 1228808 | tf_op jit(solution)/shard_map/ppermute | solution.py:328
  26.6 12.1 %collective-permute-start.18 = (bf16[1,160,1280]{2,1,0:T(8,128)(2,1)S(1)}, bf16[1,160,1280]{2,1,0:T(8,128)(2,1)S(1)}, u32[]{:S(2)}, u32[]{:S(2)}) collective-permute-start(bf16[1,160,1280]{2,1,0:T(8,128)(2,1)S(1)} %collective-permute-done.17.refs_4_), channel_id=1, source_target_pairs={{0,1},{1,0},{2,3},{3,2},{4,5},{5,4},{6,7},{7,6},{8,9},{9,8},{10,11... | collective-permute-start | bytes 1228808 | tf_op jit(solution)/shard_map/ppermute | solution.py:341
  26.6 12.1 %collective-permute-start.19 = (bf16[1,160,1280]{2,1,0:T(8,128)(2,1)S(1)}, bf16[1,160,1280]{2,1,0:T(8,128)(2,1)S(1)}, u32[]{:S(2)}, u32[]{:S(2)}) collective-permute-start(bf16[1,160,1280]{2,1,0:T(8,128)(2,1)S(1)} %collective-permute-done.17.refs_4_), channel_id=1, source_target_pairs={{1,2},{2,1},{5,6},{6,5},{9,10},{10,9},{13,14},{14,13},{17,18},{18,... | collective-permute-start | bytes 1228808 | tf_op jit(solution)/shard_map/ppermute | solution.py:342
  27.3 26.0 %collective-permute-start.6 = (bf16[1,160,2560]{2,1,0:T(8,128)(2,1)S(1)}, bf16[1,160,2560]{2,1,0:T(8,128)(2,1)S(1)}, u32[]{:S(2)}, u32[]{:S(2)}) collective-permute-start(bf16[1,160,2560]{2,1,0:T(8,128)(2,1)S(1)} %copy-done.1), channel_id=1, source_target_pairs={{0,1},{1,0},{2,3},{3,2},{4,5},{5,4},{6,7},{7,6},{8,9},{9,8},{10,11... | collective-permute-start | bytes 2457608 | tf_op jit(solution)/shard_map/ppermute | solution.py:339
  30.2 23.1 %collective-permute-start.7 = (bf16[1,160,2560]{2,1,0:T(8,128)(2,1)S(1)}, bf16[1,160,2560]{2,1,0:T(8,128)(2,1)S(1)}, u32[]{:S(2)}, u32[]{:S(2)}) collective-permute-start(bf16[1,160,2560]{2,1,0:T(8,128)(2,1)S(1)} %copy-done.1), channel_id=1, source_target_pairs={{1,2},{2,1},{5,6},{6,5},{9,10},{10,9},{13,14},{14,13},{17,18},{18,... | collective-permute-start | bytes 2457608 | tf_op jit(solution)/shard_map/ppermute | solution.py:340
  34.3 11.2 %collective-permute-start.4 = (bf16[1,160,1280]{2,1,0:T(8,128)(2,1)S(1)}, bf16[1,160,1280]{2,1,0:T(8,128)(2,1)S(1)}, u32[]{:S(2)}, u32[]{:S(2)}) collective-permute-start(bf16[1,160,1280]{2,1,0:T(8,128)(2,1)S(1)} %get-tuple-element.34), channel_id=1, source_target_pairs={{0,24},{4,12},{8,0},{12,20},{16,8},{20,28},{24,16},{28,4},{1,25},{... | collective-permute-start | bytes 1228808 | tf_op jit(solution)/shard_map/ppermute | solution.py:329
  38.6 7.4 %collective-permute-start.12 = (bf16[1,160,1280]{2,1,0:T(8,128)(2,1)S(1)}, bf16[1,160,1280]{2,1,0:T(8,128)(2,1)S(1)}, u32[]{:S(2)}, u32[]{:S(2)}) collective-permute-start(bf16[1,160,1280]{2,1,0:T(8,128)(2,1)S(1)} %collective-permute-done.11.refs_4_), channel_id=1, source_target_pairs={{0,1},{1,0},{2,3},{3,2},{4,5},{5,4},{6,7},{7,6},{8,9},{9,8},{10,11... | collective-permute-start | bytes 1228808 | tf_op jit(solution)/shard_map/ppermute | solution.py:341
  38.6 8.1 %collective-permute-start.13 = (bf16[1,160,1280]{2,1,0:T(8,128)(2,1)S(1)}, bf16[1,160,1280]{2,1,0:T(8,128)(2,1)S(1)}, u32[]{:S(2)}, u32[]{:S(2)}) collective-permute-start(bf16[1,160,1280]{2,1,0:T(8,128)(2,1)S(1)} %collective-permute-done.11.refs_4_), channel_id=1, source_target_pairs={{1,2},{2,1},{5,6},{6,5},{9,10},{10,9},{13,14},{14,13},{17,18},{18,... | collective-permute-start | bytes 1228808 | tf_op jit(solution)/shard_map/ppermute | solution.py:342
  45.5 12.1 %collective-permute-start.20 = (bf16[1,160,1408]{2,1,0:T(8,128)(2,1)S(1)}, bf16[1,160,1408]{2,1,0:T(8,128)(2,1)S(1)}, u32[]{:S(2)}, u32[]{:S(2)}) collective-permute-start(bf16[1,160,1408]{2,1,0:T(8,128)(2,1)S(1)} %get-tuple-element.29), channel_id=1, source_target_pairs={{0,1},{1,0},{2,3},{3,2},{4,5},{5,4},{6,7},{7,6},{8,9},{9,8},{10,11... | collective-permute-start | bytes 1351688 | tf_op jit(solution)/shard_map/ppermute | solution.py:378
  46.0 14.1 %collective-permute-start.21 = (bf16[1,160,1408]{2,1,0:T(8,128)(2,1)S(1)}, bf16[1,160,1408]{2,1,0:T(8,128)(2,1)S(1)}, u32[]{:S(2)}, u32[]{:S(2)}) collective-permute-start(bf16[1,160,1408]{2,1,0:T(8,128)(2,1)S(1)} %get-tuple-element.30), channel_id=1, source_target_pairs={{1,2},{2,1},{5,6},{6,5},{9,10},{10,9},{13,14},{14,13},{17,18},{18,... | collective-permute-start | bytes 1351688 | tf_op jit(solution)/shard_map/ppermute | solution.py:379
  50.5 10.4 %collective-permute-start.14 = (bf16[1,160,1408]{2,1,0:T(8,128)(2,1)S(1)}, bf16[1,160,1408]{2,1,0:T(8,128)(2,1)S(1)}, u32[]{:S(2)}, u32[]{:S(2)}) collective-permute-start(bf16[1,160,1408]{2,1,0:T(8,128)(2,1)S(1)} %get-tuple-element.26), channel_id=1, source_target_pairs={{0,1},{1,0},{2,3},{3,2},{4,5},{5,4},{6,7},{7,6},{8,9},{9,8},{10,11... | collective-permute-start | bytes 1351688 | tf_op jit(solution)/shard_map/ppermute | solution.py:378
  53.3 23.0 %collective-permute-start = (bf16[1,160,2560]{2,1,0:T(8,128)(2,1)S(1)}, bf16[1,160,2560]{2,1,0:T(8,128)(2,1)S(1)}, u32[]{:S(2)}, u32[]{:S(2)}) collective-permute-start(bf16[1,160,2560]{2,1,0:T(8,128)(2,1)S(1)} %copy-done), channel_id=1, source_target_pairs={{24,0},{12,4},{0,8},{20,12},{8,16},{28,20},{16,24},{4,28},{25,1},{... | collective-permute-start | bytes 2457608 | tf_op jit(solution)/shard_map/ppermute | solution.py:332
  53.3 9.9 %collective-permute-start.15 = (bf16[1,160,1408]{2,1,0:T(8,128)(2,1)S(1)}, bf16[1,160,1408]{2,1,0:T(8,128)(2,1)S(1)}, u32[]{:S(2)}, u32[]{:S(2)}) collective-permute-start(bf16[1,160,1408]{2,1,0:T(8,128)(2,1)S(1)} %get-tuple-element.27), channel_id=1, source_target_pairs={{1,2},{2,1},{5,6},{6,5},{9,10},{10,9},{13,14},{14,13},{17,18},{18,... | collective-permute-start | bytes 1351688 | tf_op jit(solution)/shard_map/ppermute | solution.py:379
  57.7 22.8 %collective-permute-start.8 = (bf16[1,160,2688]{2,1,0:T(8,128)(2,1)S(1)}, bf16[1,160,2688]{2,1,0:T(8,128)(2,1)S(1)}, u32[]{:S(2)}, u32[]{:S(2)}) collective-permute-start(bf16[1,160,2688]{2,1,0:T(8,128)(2,1)S(1)} %get-tuple-element.23), channel_id=1, source_target_pairs={{0,1},{1,0},{2,3},{3,2},{4,5},{5,4},{6,7},{7,6},{8,9},{9,8},{10,11... | collective-permute-start | bytes 2580488 | tf_op jit(solution)/shard_map/ppermute | solution.py:357
  60.1 20.3 %collective-permute-start.9 = (bf16[1,160,2688]{2,1,0:T(8,128)(2,1)S(1)}, bf16[1,160,2688]{2,1,0:T(8,128)(2,1)S(1)}, u32[]{:S(2)}, u32[]{:S(2)}) collective-permute-start(bf16[1,160,2688]{2,1,0:T(8,128)(2,1)S(1)} %get-tuple-element.24), channel_id=1, source_target_pairs={{1,2},{2,1},{5,6},{6,5},{9,10},{10,9},{13,14},{14,13},{17,18},{18,... | collective-permute-start | bytes 2580488 | tf_op jit(solution)/shard_map/ppermute | solution.py:358
  60.9 32.4 %collective-permute-start.1 = (bf16[1,160,2560]{2,1,0:T(8,128)(2,1)S(1)}, bf16[1,160,2560]{2,1,0:T(8,128)(2,1)S(1)}, u32[]{:S(2)}, u32[]{:S(2)}) collective-permute-start(bf16[1,160,2560]{2,1,0:T(8,128)(2,1)S(1)} %copy-done.2), channel_id=1, source_target_pairs={{24,0},{12,4},{0,8},{20,12},{8,16},{28,20},{16,24},{4,28},{25,1},{... | collective-permute-start | bytes 2457608 | tf_op jit(solution)/shard_map/ppermute | solution.py:333
  63.3 30.0 %collective-permute-start.22 = (bf16[1,160,1408]{2,1,0:T(8,128)(2,1)S(1)}, bf16[1,160,1408]{2,1,0:T(8,128)(2,1)S(1)}, u32[]{:S(2)}, u32[]{:S(2)}) collective-permute-start(bf16[1,160,1408]{2,1,0:T(8,128)(2,1)S(1)} %shard_map.53), channel_id=1, source_target_pairs={{0,4},{4,0},{8,12},{12,8},{16,20},{20,16},{24,28},{28,24},{1,5},{5... | collective-permute-start | bytes 1351688 | tf_op jit(solution)/shard_map/ppermute | solution.py:385
  76.3 16.9 %collective-permute-start.16 = (bf16[1,160,1408]{2,1,0:T(8,128)(2,1)S(1)}, bf16[1,160,1408]{2,1,0:T(8,128)(2,1)S(1)}, u32[]{:S(2)}, u32[]{:S(2)}) collective-permute-start(bf16[1,160,1408]{2,1,0:T(8,128)(2,1)S(1)} %shard_map.51), channel_id=1, source_target_pairs={{0,4},{4,0},{8,12},{12,8},{16,20},{20,16},{24,28},{28,24},{1,5},{5... | collective-permute-start | bytes 1351688 | tf_op jit(solution)/shard_map/ppermute | solution.py:385

commit v4 on v3

--- a/solution.py
+++ b/solution.py
@@ -12,8 +12,10 @@
 NEG = -1e30
 RATE = HEAD ** (-0.5) * 1.4426950408889634
 THIRD = 32
+BATCH = 5
 VMEM = pl.BlockSpec(memory_space=pltpu.VMEM)
 SMEM = pl.BlockSpec(memory_space=pltpu.SMEM)
+HBM = pl.BlockSpec(memory_space=pltpu.HBM)
 GRANT = pltpu.CompilerParams(vmem_limit_bytes=16 << 20)
 
 
@@ -247,9 +249,9 @@
     )(band, query, *keys)
 
 
-def combine_kernel(value_count, groups, heads, rule, last, band_ref, weight_ref, table_ref, *refs):
+def blend_kernel(value_count, groups, heads, rule, band_ref, weight_ref, table_ref, *refs):
     values, refs = refs[:value_count], refs[value_count:]
-    pieces, out_ref = refs[:-1], refs[-1]
+    pieces, out_ref = refs[: sum(len(group) for group in groups)], refs[-2]
     keeps = kept(rule, band_ref, None)
     rows = out_ref.shape[1]
     lane = lax.broadcasted_iota(jnp.int32, (rows, HEAD), 1)
@@ -271,32 +273,40 @@
         logs.append(log if keep is True else jnp.where(keep, log, NEG))
         places.append(place)
     weights, log = shares(logs)
-    weights[0] = weights[0] * table_ref[1]
-    tables = [packed(weight) for weight in weights]
+    coef = (weights[0] * table_ref[1]).T
+    refs[-1][...] = coef
+    if values:
+        out_ref[0, :, column(heads)] = log
+    tables = [packed(weight) for weight in weights[1:]]
     for n in range(heads):
-        value, index = value_at[n]
-        out = weighted(value[0, :, column(index)], weight_ref[n]).T * spread(tables[0], n)
-        for table, place in zip(tables[1:], places):
+        out = 0.0
+        if values:
+            value, index = value_at[n]
+            summed = weighted(value[0, :, column(index)], weight_ref[n])
+            out = (summed * refs[-1][n : n + 1, :]).T
+        for table, place in zip(tables, places):
             piece, index = place[n]
             block = pieces[piece][0, :, column(index)].astype(jnp.float32)
             out = out + spread(table, n) * block
-        out_ref[0, :, column(n)] = out.astype(out_ref.dtype)
-    if not last:
-        out_ref[0, :, column(heads)] = log
-
-
-def combined(band, score, values, groups, rule, last):
+        out_ref[0, :, column(n)] = out
+
+
+def blended(band, score, values, groups, rule):
     weights, table = score
     heads, rows = weights.shape[:2]
     width = heads * HEAD
-    kind = values[0].dtype if last else jnp.float32
     sizes = tuple(tuple(piece.shape[2] // HEAD - 1 for piece in group) for group in groups)
     pieces = [piece for group in groups for piece in group]
-    return pl.pallas_call(
-        functools.partial(combine_kernel, len(values), sizes, heads, rule, last),
+    out_shape = jax.ShapeDtypeStruct((1, rows, width + (HEAD if values else 0)), jnp.float32)
+    coef = jax.ShapeDtypeStruct((HEAD, rows), jnp.float32)
+    if not values:
+        weights = table
+    out = pl.pallas_call(
+        functools.partial(blend_kernel, len(values), sizes, heads, rule),
         in_specs=[SMEM] + [VMEM] * (2 + len(values) + len(pieces)),
-        out_specs=VMEM,
-        out_shape=jax.ShapeDtypeStruct((1, rows, width + (0 if last else HEAD)), kind),
+        out_specs=[VMEM] if values else [VMEM, VMEM],
+        out_shape=[out_shape] if values else [out_shape, coef],
+        scratch_shapes=[pltpu.VMEM(coef.shape, coef.dtype)] if values else [],
         compiler_params=GRANT,
         cost_estimate=pl.CostEstimate(
             flops=2 * rows * rows * width,
@@ -304,6 +314,50 @@
             transcendentals=0,
         ),
     )(band, weights, table, *values, *pieces)
+    return out[0] if values else out
+
+
+def final_kernel(first, heads, weight_ref, coef_ref, value_ref, base_ref, *refs):
+    out_ref, scratch, sems = refs[-3:]
+    copies = []
+    for n in range(heads):
+        cols = column(first + n)
+        summed = weighted(value_ref[0, :, column(n)], weight_ref[first + n])
+        out = (summed * coef_ref[first + n : first + n + 1, :]).T + base_ref[0, :, cols]
+        scratch[:, column(n)] = out.astype(scratch.dtype)
+        if (n + 1) % BATCH == 0 or n + 1 == heads:
+            start = n // BATCH * BATCH
+            done = slice(start * HEAD, (n + 1) * HEAD)
+            target = slice((first + start) * HEAD, (first + n + 1) * HEAD)
+            copy = pltpu.make_async_copy(
+                scratch.at[:, done], out_ref.at[0, :, target], sems.at[n // BATCH]
+            )
+            copy.start()
+            copies.append(copy)
+    for copy in copies:
+        copy.wait()
+
+
+def finished(weights, coef, value, base, whole, first):
+    rows, width = base.shape[1:]
+    heads = value.shape[2] // HEAD
+    return pl.pallas_call(
+        functools.partial(final_kernel, first, heads),
+        in_specs=[VMEM] * 4 + [HBM] * (whole is not None),
+        out_specs=HBM,
+        out_shape=jax.ShapeDtypeStruct((1, rows, width), value.dtype),
+        scratch_shapes=[
+            pltpu.VMEM((rows, heads * HEAD), value.dtype),
+            pltpu.SemaphoreType.DMA((-(-heads // BATCH),)),
+        ],
+        input_output_aliases={4: 0} if whole is not None else {},
+        compiler_params=GRANT,
+        cost_estimate=pl.CostEstimate(
+            flops=2 * rows * rows * heads * HEAD,
+            bytes_accessed=8 * rows * heads * HEAD,
+            transcendentals=0,
+        ),
+    )(weights, coef, value, base, *([] if whole is None else [whole]))
 
 
 def per_device(queries, keys, values, band):
@@ -320,20 +374,15 @@
     half = heads // 2
     spans = [(0, half), (half, heads - half)]
 
-    near = []
-    for first, size in spans:
-        cut = slice(first * HEAD, (first + size) * HEAD)
-        near.append(
-            (
-                lax.ppermute(keys[:, :, cut], "frame", toward),
-                lax.ppermute(values[:, :, cut], "frame", toward),
-            )
-        )
+    cuts = [slice(first * HEAD, (first + size) * HEAD) for first, size in spans]
+    value_halves = [values[:, :, cut] for cut in cuts]
+
+    key_one = lax.ppermute(keys, "frame", toward)
+    value_one = [lax.ppermute(value_halves[span], "frame", toward) for span in (0, 1)]
     key_two = lax.ppermute(keys, "frame", away)
-    value_two = lax.ppermute(values, "frame", away)
+    value_two = [lax.ppermute(value_halves[span], "frame", away) for span in (0, 1)]
     query_twin = []
-    for first, size in spans:
-        cut = slice(first * HEAD, (first + size) * HEAD)
+    for cut in cuts:
         query_twin.append(lax.ppermute(queries[:, :, cut], "frame", twin))
     band_twin = lax.ppermute(band, "frame", twin)
     query_even = lax.ppermute(queries, "row", even)
@@ -368,8 +417,8 @@
         even_twin, odd_twin, own_twin = parts(
             (band, band_twin),
             [twin_even[span], twin_odd[span], query_twin[span]],
-            [keys, near[span][0]],
-            [values, near[span][1]],
+            [keys, key_one],
+            [values, value_one[span]],
             twin_rule,
             (narrow, narrow, full),
             first,
@@ -387,16 +436,15 @@
     near_score = scored(
         band,
         queries,
-        [pair[0] for pair in near],
+        [key_one],
         lambda own, other, odd_frame, has_odd: [jnp.where(odd_frame, own[0], own[4]) >= 0],
     )
-    near_all = combined(
+    near = blended(
         band,
         near_score,
-        [pair[1] for pair in near],
+        value_one,
         [[own_part], [from_even], [from_odd]],
         lambda own, other, odd_frame, has_odd: [True, True, has_odd],
-        False,
     )
     far_score = scored(
         band,
@@ -404,14 +452,17 @@
         [key_two],
         lambda own, other, odd_frame, has_odd: [jnp.where(odd_frame, own[4], own[0]) >= 0],
     )
-    return combined(
+    base, coef = blended(
         band,
         far_score,
-        [value_two],
-        [[near_all], from_twin],
+        [],
+        [[near], from_twin],
         lambda own, other, odd_frame, has_odd: [True, True],
-        True,
-    )
+    )
+    out = None
+    for span, (first, size) in enumerate(spans):
+        out = finished(far_score[0], coef, value_two[span], base, out, first)
+    return out
 
 
 def solution(mesh):

time: 97.6 us -> 101 us (1.035)
  starting transfers between devices: 34 us -> 40.8 us
  waiting for transfers between devices: 37.6 us -> 31.1 us
  Pallas kernels: 24.1 us -> 26.9 us
    ppermute x2, starting transfers between devices: 0.01 us -> 13.1 us  [per_device(): twin_even = [lax.ppermute(query_twin[span], 'row', even) for span in (0, 1)]]
    ppermute x5, waiting for transfers between devices: 16.3 us -> 8.65 us  [the longest x2 8.64 us: per_device(): lax.ppermute(value_halves[span], 'frame', away)]
    ppermute x5, starting transfers between devices: 13.4 us -> 9.15 us  [the longest x2 7.26 us: per_device(): lax.ppermute(value_halves[span], 'frame', toward)]
    ppermute x1, starting transfers between devices: 2.89 us -> 0.01 us  [per_device(): query_even = lax.ppermute(queries, 'row', even)]
    pallas_call x2 -> x4, Pallas kernels: 6.44 us -> 9.23 us  [the longest x2 5.48 us: blended(): pl.pallas_call(functools.partial(blend_kernel, len(values), sizes, heads,...]
    ppermute x1, starting transfers between devices: 0.01 us -> 1.8 us  [per_device(): key_two = lax.ppermute(keys, 'frame', away)]
  transfers between devices with their start and end apart: 23 -> 23, of which waited for: 5 -> 5; matrix products, arithmetic and copies ran while one was open for 0% -> 0% of each run, Pallas kernels for 21% -> 25%
where the time goes in v4:
time: 101 us
  starting transfers between devices  40.8 us (40%)
  waiting for transfers between devices  31.1 us (31%)
  Pallas kernels  26.9 us (27%)
  local copies, waits for them, and re-layouts  1.4 us (1%)
    ppermute x2, starting transfers between devices, per_device(): twin_even = [lax.ppermute(query_twin[span], 'row', even) for span in (0, 1)]  13.1 us
    ppermute x1, waiting for transfers between devices, per_device(): band_twin = lax.ppermute(band, 'frame', twin)  12.5 us
    pallas_call x3, Pallas kernels, parts(): pl.pallas_call(functools.partial(parts_kernel, len(queries), len(keys), f...  11.2 us
    ppermute x1, waiting for transfers between devices, per_device(): key_two = lax.ppermute(keys, 'frame', away)  9.19 us
    ppermute x2, waiting for transfers between devices, per_device(): lax.ppermute(value_halves[span], 'frame', away)  8.64 us
    ppermute x2, starting transfers between devices, per_device(): lax.ppermute(value_halves[span], 'frame', toward)  7.26 us
    pallas_call x2, Pallas kernels, blended(): pl.pallas_call(functools.partial(blend_kernel, len(values), sizes, heads,...  5.48 us
    pallas_call x2, Pallas kernels, scored(): pl.pallas_call(functools.partial(score_kernel, rule), in_specs=[SMEM] + [...  4.05 us
  transfers between devices with their start and end apart: 23, of which 5 were waited for; matrix products, arithmetic and copies ran while one was open for 0% of the time, Pallas kernels for 25%

profile of v4, /device:TPU:0, one launch (start us, length us, event | category | flops | bytes accessed | tf_op | source)
XLA Modules:
  0.0 100.5 jit_solution(7854262241350317912)
XLA Ops:
  0.0 1.3 %fusion = (bf16[1,160,1280]{2,1,0:T(8,128)(2,1)S(1)}, bf16[1,160,1280]{2,1,0:T(8,128)(2,1)S(1)}) fusion(bf16[1,160,2560]{2,1,0:T(8,128)(2,1)} %refs_4_.1), kind=kLoop, calls=%fused_computation | loop fusion | bytes 1638400 | tf_op jit(solution)/shard_map/slice | solution.py:386
  1.3 3.1 %collective-permute-start.15 = (bf16[1,160,1280]{2,1,0:T(8,128)(2,1)S(1)}, bf16[1,160,1280]{2,1,0:T(8,128)(2,1)S(1)}, u32[]{:S(2)}, u32[]{:S(2)}) collective-permute-start(bf16[1,160,1280]{2,1,0:T(8,128)(2,1)S(1)} %get-tuple-element.35), channel_id=1, source_target_pairs={{0,4},{4,0},{8,12},{12,8},{16,20},{20,16},{24,28},{28,24},{1,5},{5... | collective-permute-start | bytes 1228808 | tf_op jit(solution)/shard_map/ppermute | solution.py:386
  4.5 3.7 %collective-permute-start.3 = (bf16[1,160,1280]{2,1,0:T(8,128)(2,1)S(1)}, bf16[1,160,1280]{2,1,0:T(8,128)(2,1)S(1)}, u32[]{:S(2)}, u32[]{:S(2)}) collective-permute-start(bf16[1,160,1280]{2,1,0:T(8,128)(2,1)S(1)} %get-tuple-element.37), channel_id=1, source_target_pairs={{0,24},{4,12},{8,0},{12,20},{16,8},{20,28},{24,16},{28,4},{1,25},{... | collective-permute-start | bytes 1228808 | tf_op jit(solution)/shard_map/ppermute | solution.py:381
  8.7 1.5 %collective-permute-start.8 = (s32[1,5]{1,0:T(1,128)S(1)}, s32[1,5]{1,0:T(1,128)S(1)}, u32[]{:S(2)}, u32[]{:S(2)}) collective-permute-start(s32[1,5]{1,0:T(1,128)S(1)} %copy-done.3), channel_id=1, source_target_pairs={{0,4},{4,0},{8,12},{12,8},{16,20},{20,16},{24,28},{28,24},{1,5},{5... | collective-permute-start | bytes 68 | tf_op jit(solution)/shard_map/ppermute | solution.py:387
  10.2 12.5 %collective-permute-done.8.refs_1_ = s32[1,5]{1,0:T(1,128)S(1)} collective-permute-done((s32[1,5]{1,0:T(1,128)S(1)}, s32[1,5]{1,0:T(1,128)S(1)}, u32[]{:S(2)}, u32[]{:S(2)}) %collective-permute-start.8) | collective-permute-done | bytes 52 | tf_op jit(solution)/shard_map/ppermute | solution.py:387
  22.8 0.7 collective-permute-start.5
  23.5 3.1 %collective-permute-start.16 = (bf16[1,160,1280]{2,1,0:T(8,128)(2,1)S(1)}, bf16[1,160,1280]{2,1,0:T(8,128)(2,1)S(1)}, u32[]{:S(2)}, u32[]{:S(2)}) collective-permute-start(bf16[1,160,1280]{2,1,0:T(8,128)(2,1)S(1)} %collective-permute-done.15.refs_4_), channel_id=1, source_target_pairs={{0,1},{1,0},{2,3},{3,2},{4,5},{5,4},{6,7},{7,6},{8,9},{9,8},{10,11... | collective-permute-start | bytes 1228808 | tf_op jit(solution)/shard_map/ppermute | solution.py:390
  27.3 0.7 collective-permute-done.16.refs_2_
  28.0 3.6 %collective-permute-start.2 = (bf16[1,160,1280]{2,1,0:T(8,128)(2,1)S(1)}, bf16[1,160,1280]{2,1,0:T(8,128)(2,1)S(1)}, u32[]{:S(2)}, u32[]{:S(2)}) collective-permute-start(bf16[1,160,1280]{2,1,0:T(8,128)(2,1)S(1)} %get-tuple-element.38), channel_id=1, source_target_pairs={{0,24},{4,12},{8,0},{12,20},{16,8},{20,28},{24,16},{28,4},{1,25},{... | collective-permute-start | bytes 1228808 | tf_op jit(solution)/shard_map/ppermute | solution.py:381
  31.6 10.0 %collective-permute-start.10 = (bf16[1,160,1280]{2,1,0:T(8,128)(2,1)S(1)}, bf16[1,160,1280]{2,1,0:T(8,128)(2,1)S(1)}, u32[]{:S(2)}, u32[]{:S(2)}) collective-permute-start(bf16[1,160,1280]{2,1,0:T(8,128)(2,1)S(1)} %collective-permute-done.9.refs_4_), channel_id=1, source_target_pairs={{0,1},{1,0},{2,3},{3,2},{4,5},{5,4},{6,7},{7,6},{8,9},{9,8},{10,11... | collective-permute-start | bytes 1228808 | tf_op jit(solution)/shard_map/ppermute | solution.py:390
  42.3 3.8 %shard_map.52 = (bf16[1,160,1408]{2,1,0:T(8,128)(2,1)S(1)}, bf16[1,160,1408]{2,1,0:T(8,128)(2,1)S(1)}, f32[1,160,1408]{2,1,0:T(8,128)S(1)}) custom-call(s32[1,5]{1,0:T(1,128)S(1)} %copy-done.3, s32[1,5]{1,0:T(1,128)S(1)} %collective-permute-done.8.refs_1_, bf16[1,160,1280]{2,1,0:T(8,128)(2,1)S(1)} %collective-permute-done.16.refs_2_, ...), custom_call_target="tpu_custom_call" | custom-call | flops 786432000 | bytes 4096000 | tf_op jit(solution)/shard_map/pallas_call | solution.py:157
  46.1 2.3 %collective-permute-start.18 = (bf16[1,160,1408]{2,1,0:T(8,128)(2,1)S(1)}, bf16[1,160,1408]{2,1,0:T(8,128)(2,1)S(1)}, u32[]{:S(2)}, u32[]{:S(2)}) collective-permute-start(bf16[1,160,1408]{2,1,0:T(8,128)(2,1)S(1)} %get-tuple-element.31), channel_id=1, source_target_pairs={{0,1},{1,0},{2,3},{3,2},{4,5},{5,4},{6,7},{7,6},{8,9},{9,8},{10,11... | collective-permute-start | bytes 1351688 | tf_op jit(solution)/shard_map/ppermute | solution.py:427
  48.4 0.7 collective-permute-start.19
  49.1 3.6 %shard_map.48 = (bf16[1,160,2688]{2,1,0:T(8,128)(2,1)S(1)}, bf16[1,160,2688]{2,1,0:T(8,128)(2,1)S(1)}, f32[1,160,2688]{2,1,0:T(8,128)S(1)}) custom-call(s32[1,5]{1,0:T(1,128)S(1)} %copy-done.3, s32[1,5]{1,0:T(1,128)S(1)} %copy-done.3, bf16[1,160,2560]{2,1,0:T(8,128)(2,1)S(1)} %collective-permute-done.4.refs_2_, ...), custom_call_target="tpu_custom_call" | custom-call | flops 786432000 | bytes 6553600 | tf_op jit(solution)/shard_map/pallas_call | solution.py:157
  52.7 2.0 %collective-permute-start.6 = (bf16[1,160,2688]{2,1,0:T(8,128)(2,1)S(1)}, bf16[1,160,2688]{2,1,0:T(8,128)(2,1)S(1)}, u32[]{:S(2)}, u32[]{:S(2)}) collective-permute-start(bf16[1,160,2688]{2,1,0:T(8,128)(2,1)S(1)} %get-tuple-element.25), channel_id=1, source_target_pairs={{0,1},{1,0},{2,3},{3,2},{4,5},{5,4},{6,7},{7,6},{8,9},{9,8},{10,11... | collective-permute-start | bytes 2580488 | tf_op jit(solution)/shard_map/ppermute | solution.py:406
  54.8 1.8 %collective-permute-start = (bf16[1,160,2560]{2,1,0:T(8,128)(2,1)S(1)}, bf16[1,160,2560]{2,1,0:T(8,128)(2,1)S(1)}, u32[]{:S(2)}, u32[]{:S(2)}) collective-permute-start(bf16[1,160,2560]{2,1,0:T(8,128)(2,1)S(1)} %copy-done.2), channel_id=1, source_target_pairs={{24,0},{12,4},{0,8},{20,12},{8,16},{28,20},{16,24},{4,28},{25,1},{... | collective-permute-start | bytes 2457608 | tf_op jit(solution)/shard_map/ppermute | solution.py:382
  56.6 3.7 %shard_map.50 = (bf16[1,160,1408]{2,1,0:T(8,128)(2,1)S(1)}, bf16[1,160,1408]{2,1,0:T(8,128)(2,1)S(1)}, f32[1,160,1408]{2,1,0:T(8,128)S(1)}) custom-call(s32[1,5]{1,0:T(1,128)S(1)} %copy-done.3, s32[1,5]{1,0:T(1,128)S(1)} %collective-permute-done.8.refs_1_, bf16[1,160,1280]{2,1,0:T(8,128)(2,1)S(1)} %collective-permute-done.10.refs_2_, ...), custom_call_target="tpu_custom_call" | custom-call | flops 786432000 | bytes 4096000 | tf_op jit(solution)/shard_map/pallas_call | solution.py:157
  60.4 0.7 collective-permute-start.13
  61.1 0.9 collective-permute-start.7
  62.0 1.2 %shard_map.53 = bf16[1,160,1408]{2,1,0:T(8,128)(2,1)S(1)} custom-call(s32[1,5]{1,0:T(1,128)S(1)} %copy-done.3, f32[1,160,1408]{2,1,0:T(8,128)S(1)} %get-tuple-element.30.refs_0_, bf16[1,160,1408]{2,1,0:T(8,128)(2,1)S(1)} %collective-permute-done.18.refs_1_, bf16[1,160,1408]{2,1,0:T(8,128)(2,1)S(1)} %collective-permute-done.19.refs_2_), custom_call_target="tpu_custom_call" | custom-call | flops 1351680 | bytes 1802240 | tf_op jit(solution)/shard_map/pallas_call | solution.py:195
  63.2 3.3 %collective-permute-start.20 = (bf16[1,160,1408]{2,1,0:T(8,128)(2,1)S(1)}, bf16[1,160,1408]{2,1,0:T(8,128)(2,1)S(1)}, u32[]{:S(2)}, u32[]{:S(2)}) collective-permute-start(bf16[1,160,1408]{2,1,0:T(8,128)(2,1)S(1)} %shard_map.53), channel_id=1, source_target_pairs={{0,4},{4,0},{8,12},{12,8},{16,20},{20,16},{24,28},{28,24},{1,5},{5... | collective-permute-start | bytes 1351688 | tf_op jit(solution)/shard_map/ppermute | solution.py:434
  66.5 1.2 %shard_map.51 = bf16[1,160,1408]{2,1,0:T(8,128)(2,1)S(1)} custom-call(s32[1,5]{1,0:T(1,128)S(1)} %copy-done.3, f32[1,160,1408]{2,1,0:T(8,128)S(1)} %get-tuple-element.27.refs_0_, bf16[1,160,1408]{2,1,0:T(8,128)(2,1)S(1)} %collective-permute-done.12.refs_1_, bf16[1,160,1408]{2,1,0:T(8,128)(2,1)S(1)} %collective-permute-done.13.refs_2_), custom_call_target="tpu_custom_call" | custom-call | flops 1351680 | bytes 1802240 | tf_op jit(solution)/shard_map/pallas_call | solution.py:195
  67.8 9.2 %collective-permute-done.refs_0_ = bf16[1,160,2560]{2,1,0:T(8,128)(2,1)S(1)} collective-permute-done((bf16[1,160,2560]{2,1,0:T(8,128)(2,1)S(1)}, bf16[1,160,2560]{2,1,0:T(8,128)(2,1)S(1)}, u32[]{:S(2)}, u32[]{:S(2)}) %collective-permute-start) | collective-permute-done | bytes 819232 | tf_op jit(solution)/shard_map/ppermute | solution.py:382
  77.0 1.3 %collective-permute-start.21 = (bf16[1,160,1280]{2,1,0:T(8,128)(2,1)S(1)}, bf16[1,160,1280]{2,1,0:T(8,128)(2,1)S(1)}, u32[]{:S(2)}, u32[]{:S(2)}) collective-permute-start(bf16[1,160,1280]{2,1,0:T(8,128)(2,1)S(1)} %get-tuple-element.37), channel_id=1, source_target_pairs={{24,0},{12,4},{0,8},{20,12},{8,16},{28,20},{16,24},{4,28},{25,1},{... | collective-permute-start | bytes 1228808 | tf_op jit(solution)/shard_map/ppermute | solution.py:383
  78.4 2.0 %shard_map.47 = (bf16[20,160,160]{2,1,0:T(8,128)(2,1)S(1)}, f32[2,160,128]{2,1,0:T(8,128)S(1)}) custom-call(s32[1,5]{1,0:T(1,128)S(1)} %copy-done.3, bf16[1,160,2560]{2,1,0:T(8,128)(2,1)S(1)} %copy-done, bf16[1,160,2560]{2,1,0:T(8,128)(2,1)S(1)} %collective-permute-done.1.refs_0_.refs_6_), custom_call_target="tpu_custom_call" | custom-call | flops 131072000 | bytes 2457600 | tf_op jit(solution)/shard_map/pallas_call | solution.py:234
  80.4 2.0 %shard_map.46 = (bf16[20,160,160]{2,1,0:T(8,128)(2,1)S(1)}, f32[2,160,128]{2,1,0:T(8,128)S(1)}) custom-call(s32[1,5]{1,0:T(1,128)S(1)} %copy-done.3, bf16[1,160,2560]{2,1,0:T(8,128)(2,1)S(1)} %copy-done, bf16[1,160,2560]{2,1,0:T(8,128)(2,1)S(1)} %collective-permute-done.refs_0_), custom_call_target="tpu_custom_call" | custom-call | flops 131072000 | bytes 2457600 | tf_op jit(solution)/shard_map/pallas_call | solution.py:234
  82.4 4.1 %shard_map.49.refs_0_ = f32[1,160,2688]{2,1,0:T(8,128)S(1)} custom-call(s32[1,5]{1,0:T(1,128)S(1)} %copy-done.3, bf16[20,160,160]{2,1,0:T(8,128)(2,1)S(1)} %get-tuple-element.22.weight_ref, f32[2,160,128]{2,1,0:T(8,128)S(1)} %get-tuple-element.23.table_ref, bf16[1,160,1280]{2,1,0:T(8,128)(2,1)S(1)} %collective-permute-done.2.refs_0_.refs_8_, ...), custom_call_target="tpu_custom_call" | custom-call | flops 131072000 | bytes 5734400 | tf_op jit(solution)/shard_map/pallas_call | solution.py:304
  86.6 1.4 %shard_map.54 = (f32[1,160,2560]{2,1,0:T(8,128)S(1)}, f32[128,160]{1,0:T(8,128)S(1)}) custom-call(s32[1,5]{1,0:T(1,128)S(1)} %copy-done.3, f32[2,160,128]{2,1,0:T(8,128)S(1)} %get-tuple-element.21.weight_ref.table_ref, f32[2,160,128]{2,1,0:T(8,128)S(1)} %get-tuple-element.21.weight_ref.table_ref, f32[1,160,2688]{2,1,0:T(8,128)S(1)} %shard_map.49.refs_0_, ...), custom_call_target="tpu_custom_call" | custom-call | flops 131072000 | bytes 5734400 | tf_op jit(solution)/shard_map/pallas_call | solution.py:304
  87.9 3.2 %collective-permute-done.22.value_ref = bf16[1,160,1280]{2,1,0:T(8,128)(2,1)S(1)} collective-permute-done((bf16[1,160,1280]{2,1,0:T(8,128)(2,1)S(1)}, bf16[1,160,1280]{2,1,0:T(8,128)(2,1)S(1)}, u32[]{:S(2)}, u32[]{:S(2)}) %collective-permute-start.22) | collective-permute-done | bytes 409632 | tf_op jit(solution)/shard_map/ppermute | solution.py:383
  91.2 1.9 %shard_map.55.refs_0_ = bf16[1,160,2560]{2,1,0:T(8,128)(2,1)} custom-call(bf16[20,160,160]{2,1,0:T(8,128)(2,1)S(1)} %get-tuple-element.20.weight_ref, f32[128,160]{1,0:T(8,128)S(1)} %get-tuple-element.33.coef_ref, bf16[1,160,1280]{2,1,0:T(8,128)(2,1)S(1)} %collective-permute-done.22.value_ref, f32[1,160,2560]{2,1,0:T(8,128)S(1)} %get-tuple-element.34.base_ref), custom_call_target="tpu_custom_call" | custom-call | flops 65536000 | bytes 1638400 | tf_op jit(solution)/shard_map/pallas_call | solution.py:344
  93.1 5.4 %collective-permute-done.21.value_ref = bf16[1,160,1280]{2,1,0:T(8,128)(2,1)S(1)} collective-permute-done((bf16[1,160,1280]{2,1,0:T(8,128)(2,1)S(1)}, bf16[1,160,1280]{2,1,0:T(8,128)(2,1)S(1)}, u32[]{:S(2)}, u32[]{:S(2)}) %collective-permute-start.21) | collective-permute-done | bytes 409632 | tf_op jit(solution)/shard_map/ppermute | solution.py:383
  98.5 1.9 %shard_map.56 = bf16[1,160,2560]{2,1,0:T(8,128)(2,1)} custom-call(bf16[20,160,160]{2,1,0:T(8,128)(2,1)S(1)} %get-tuple-element.20.weight_ref, f32[128,160]{1,0:T(8,128)S(1)} %get-tuple-element.33.coef_ref, bf16[1,160,1280]{2,1,0:T(8,128)(2,1)S(1)} %collective-permute-done.21.value_ref, ...), custom_call_target="tpu_custom_call", output_to_operand_aliasing={{}: (4, {})} | custom-call | flops 65536000 | bytes 1638400 | tf_op jit(solution)/shard_map/pallas_call | solution.py:344
  (35 shorter events, 2.2 us)
Async XLA Ops:
  0.0 22.8 %copy-start = (bf16[1,160,2560]{2,1,0:T(8,128)(2,1)S(1)}, bf16[1,160,2560]{2,1,0:T(8,128)(2,1)}, u32[]{:S(2)}) copy-start(bf16[1,160,2560]{2,1,0:T(8,128)(2,1)} %refs_4_.1) | copy-start | bytes 2457604
  0.0 4.4 %copy-start.1 = (bf16[1,160,2560]{2,1,0:T(8,128)(2,1)S(1)}, bf16[1,160,2560]{2,1,0:T(8,128)(2,1)}, u32[]{:S(2)}) copy-start(bf16[1,160,2560]{2,1,0:T(8,128)(2,1)} %refs_7_.3) | copy-start | bytes 2457604
  0.0 8.1 %copy-start.2 = (bf16[1,160,2560]{2,1,0:T(8,128)(2,1)S(1)}, bf16[1,160,2560]{2,1,0:T(8,128)(2,1)}, u32[]{:S(2)}) copy-start(bf16[1,160,2560]{2,1,0:T(8,128)(2,1)} %refs_5_.5) | copy-start | bytes 2457604
  0.0 8.7 %copy-start.3 = (s32[1,5]{1,0:T(1,128)S(1)}, s32[1,5]{1,0:T(1,128)}, u32[]{:S(2)}) copy-start(s32[1,5]{1,0:T(1,128)} %band_ref.11) | copy-start | bytes 64
  1.3 21.4 %collective-permute-start.15 = (bf16[1,160,1280]{2,1,0:T(8,128)(2,1)S(1)}, bf16[1,160,1280]{2,1,0:T(8,128)(2,1)S(1)}, u32[]{:S(2)}, u32[]{:S(2)}) collective-permute-start(bf16[1,160,1280]{2,1,0:T(8,128)(2,1)S(1)} %get-tuple-element.35), channel_id=1, source_target_pairs={{0,4},{4,0},{8,12},{12,8},{16,20},{20,16},{24,28},{28,24},{1,5},{5... | collective-permute-start | bytes 1228808 | tf_op jit(solution)/shard_map/ppermute | solution.py:386
  4.5 19.0 %collective-permute-start.3 = (bf16[1,160,1280]{2,1,0:T(8,128)(2,1)S(1)}, bf16[1,160,1280]{2,1,0:T(8,128)(2,1)S(1)}, u32[]{:S(2)}, u32[]{:S(2)}) collective-permute-start(bf16[1,160,1280]{2,1,0:T(8,128)(2,1)S(1)} %get-tuple-element.37), channel_id=1, source_target_pairs={{0,24},{4,12},{8,0},{12,20},{16,8},{20,28},{24,16},{28,4},{1,25},{... | collective-permute-start | bytes 1228808 | tf_op jit(solution)/shard_map/ppermute | solution.py:381
  8.1 18.5 %collective-permute-start.9 = (bf16[1,160,1280]{2,1,0:T(8,128)(2,1)S(1)}, bf16[1,160,1280]{2,1,0:T(8,128)(2,1)S(1)}, u32[]{:S(2)}, u32[]{:S(2)}) collective-permute-start(bf16[1,160,1280]{2,1,0:T(8,128)(2,1)S(1)} %get-tuple-element.36), channel_id=1, source_target_pairs={{0,4},{4,0},{8,12},{12,8},{16,20},{20,16},{24,28},{28,24},{1,5},{5... | collective-permute-start | bytes 1228808 | tf_op jit(solution)/shard_map/ppermute | solution.py:386
  8.1 33.5 %collective-permute-start.1 = (bf16[1,160,2560]{2,1,0:T(8,128)(2,1)S(1)}, bf16[1,160,2560]{2,1,0:T(8,128)(2,1)S(1)}, u32[]{:S(2)}, u32[]{:S(2)}) collective-permute-start(bf16[1,160,2560]{2,1,0:T(8,128)(2,1)S(1)} %copy-done.2), channel_id=1, source_target_pairs={{0,24},{4,12},{8,0},{12,20},{16,8},{20,28},{24,16},{28,4},{1,25},{... | collective-permute-start | bytes 2457608 | tf_op jit(solution)/shard_map/ppermute | solution.py:380
  8.7 14.0 %collective-permute-start.8 = (s32[1,5]{1,0:T(1,128)S(1)}, s32[1,5]{1,0:T(1,128)S(1)}, u32[]{:S(2)}, u32[]{:S(2)}) collective-permute-start(s32[1,5]{1,0:T(1,128)S(1)} %copy-done.3), channel_id=1, source_target_pairs={{0,4},{4,0},{8,12},{12,8},{16,20},{20,16},{24,28},{28,24},{1,5},{5... | collective-permute-start | bytes 68 | tf_op jit(solution)/shard_map/ppermute | solution.py:387
  22.8 23.3 %collective-permute-start.4 = (bf16[1,160,2560]{2,1,0:T(8,128)(2,1)S(1)}, bf16[1,160,2560]{2,1,0:T(8,128)(2,1)S(1)}, u32[]{:S(2)}, u32[]{:S(2)}) collective-permute-start(bf16[1,160,2560]{2,1,0:T(8,128)(2,1)S(1)} %copy-done), channel_id=1, source_target_pairs={{0,1},{1,0},{2,3},{3,2},{4,5},{5,4},{6,7},{7,6},{8,9},{9,8},{10,11... | collective-permute-start | bytes 2457608 | tf_op jit(solution)/shard_map/ppermute | solution.py:388
  22.8 25.6 %collective-permute-start.5 = (bf16[1,160,2560]{2,1,0:T(8,128)(2,1)S(1)}, bf16[1,160,2560]{2,1,0:T(8,128)(2,1)S(1)}, u32[]{:S(2)}, u32[]{:S(2)}) collective-permute-start(bf16[1,160,2560]{2,1,0:T(8,128)(2,1)S(1)} %copy-done), channel_id=1, source_target_pairs={{1,2},{2,1},{5,6},{6,5},{9,10},{10,9},{13,14},{14,13},{17,18},{18,... | collective-permute-start | bytes 2457608 | tf_op jit(solution)/shard_map/ppermute | solution.py:389
  23.5 4.5 %collective-permute-start.16 = (bf16[1,160,1280]{2,1,0:T(8,128)(2,1)S(1)}, bf16[1,160,1280]{2,1,0:T(8,128)(2,1)S(1)}, u32[]{:S(2)}, u32[]{:S(2)}) collective-permute-start(bf16[1,160,1280]{2,1,0:T(8,128)(2,1)S(1)} %collective-permute-done.15.refs_4_), channel_id=1, source_target_pairs={{0,1},{1,0},{2,3},{3,2},{4,5},{5,4},{6,7},{7,6},{8,9},{9,8},{10,11... | collective-permute-start | bytes 1228808 | tf_op jit(solution)/shard_map/ppermute | solution.py:390
  26.6 5.0 %collective-permute-start.17 = (bf16[1,160,1280]{2,1,0:T(8,128)(2,1)S(1)}, bf16[1,160,1280]{2,1,0:T(8,128)(2,1)S(1)}, u32[]{:S(2)}, u32[]{:S(2)}) collective-permute-start(bf16[1,160,1280]{2,1,0:T(8,128)(2,1)S(1)} %collective-permute-done.15.refs_4_), channel_id=1, source_target_pairs={{1,2},{2,1},{5,6},{6,5},{9,10},{10,9},{13,14},{14,13},{17,18},{18,... | collective-permute-start | bytes 1228808 | tf_op jit(solution)/shard_map/ppermute | solution.py:391
  28.0 24.8 %collective-permute-start.2 = (bf16[1,160,1280]{2,1,0:T(8,128)(2,1)S(1)}, bf16[1,160,1280]{2,1,0:T(8,128)(2,1)S(1)}, u32[]{:S(2)}, u32[]{:S(2)}) collective-permute-start(bf16[1,160,1280]{2,1,0:T(8,128)(2,1)S(1)} %get-tuple-element.38), channel_id=1, source_target_pairs={{0,24},{4,12},{8,0},{12,20},{16,8},{20,28},{24,16},{28,4},{1,25},{... | collective-permute-start | bytes 1228808 | tf_op jit(solution)/shard_map/ppermute | solution.py:381
  31.6 23.2 %collective-permute-start.10 = (bf16[1,160,1280]{2,1,0:T(8,128)(2,1)S(1)}, bf16[1,160,1280]{2,1,0:T(8,128)(2,1)S(1)}, u32[]{:S(2)}, u32[]{:S(2)}) collective-permute-start(bf16[1,160,1280]{2,1,0:T(8,128)(2,1)S(1)} %collective-permute-done.9.refs_4_), channel_id=1, source_target_pairs={{0,1},{1,0},{2,3},{3,2},{4,5},{5,4},{6,7},{7,6},{8,9},{9,8},{10,11... | collective-permute-start | bytes 1228808 | tf_op jit(solution)/shard_map/ppermute | solution.py:390
  41.6 14.9 %collective-permute-start.11 = (bf16[1,160,1280]{2,1,0:T(8,128)(2,1)S(1)}, bf16[1,160,1280]{2,1,0:T(8,128)(2,1)S(1)}, u32[]{:S(2)}, u32[]{:S(2)}) collective-permute-start(bf16[1,160,1280]{2,1,0:T(8,128)(2,1)S(1)} %collective-permute-done.9.refs_4_), channel_id=1, source_target_pairs={{1,2},{2,1},{5,6},{6,5},{9,10},{10,9},{13,14},{14,13},{17,18},{18,... | collective-permute-start | bytes 1228808 | tf_op jit(solution)/shard_map/ppermute | solution.py:391
  46.1 14.3 %collective-permute-start.18 = (bf16[1,160,1408]{2,1,0:T(8,128)(2,1)S(1)}, bf16[1,160,1408]{2,1,0:T(8,128)(2,1)S(1)}, u32[]{:S(2)}, u32[]{:S(2)}) collective-permute-start(bf16[1,160,1408]{2,1,0:T(8,128)(2,1)S(1)} %get-tuple-element.31), channel_id=1, source_target_pairs={{0,1},{1,0},{2,3},{3,2},{4,5},{5,4},{6,7},{7,6},{8,9},{9,8},{10,11... | collective-permute-start | bytes 1351688 | tf_op jit(solution)/shard_map/ppermute | solution.py:427
  48.4 12.7 %collective-permute-start.19 = (bf16[1,160,1408]{2,1,0:T(8,128)(2,1)S(1)}, bf16[1,160,1408]{2,1,0:T(8,128)(2,1)S(1)}, u32[]{:S(2)}, u32[]{:S(2)}) collective-permute-start(bf16[1,160,1408]{2,1,0:T(8,128)(2,1)S(1)} %get-tuple-element.32), channel_id=1, source_target_pairs={{1,2},{2,1},{5,6},{6,5},{9,10},{10,9},{13,14},{14,13},{17,18},{18,... | collective-permute-start | bytes 1351688 | tf_op jit(solution)/shard_map/ppermute | solution.py:428
  52.7 24.3 %collective-permute-start.6 = (bf16[1,160,2688]{2,1,0:T(8,128)(2,1)S(1)}, bf16[1,160,2688]{2,1,0:T(8,128)(2,1)S(1)}, u32[]{:S(2)}, u32[]{:S(2)}) collective-permute-start(bf16[1,160,2688]{2,1,0:T(8,128)(2,1)S(1)} %get-tuple-element.25), channel_id=1, source_target_pairs={{0,1},{1,0},{2,3},{3,2},{4,5},{5,4},{6,7},{7,6},{8,9},{9,8},{10,11... | collective-permute-start | bytes 2580488 | tf_op jit(solution)/shard_map/ppermute | solution.py:406
  54.8 22.3 %collective-permute-start = (bf16[1,160,2560]{2,1,0:T(8,128)(2,1)S(1)}, bf16[1,160,2560]{2,1,0:T(8,128)(2,1)S(1)}, u32[]{:S(2)}, u32[]{:S(2)}) collective-permute-start(bf16[1,160,2560]{2,1,0:T(8,128)(2,1)S(1)} %copy-done.2), channel_id=1, source_target_pairs={{24,0},{12,4},{0,8},{20,12},{8,16},{28,20},{16,24},{4,28},{25,1},{... | collective-permute-start | bytes 2457608 | tf_op jit(solution)/shard_map/ppermute | solution.py:382
  60.3 2.9 %collective-permute-start.12 = (bf16[1,160,1408]{2,1,0:T(8,128)(2,1)S(1)}, bf16[1,160,1408]{2,1,0:T(8,128)(2,1)S(1)}, u32[]{:S(2)}, u32[]{:S(2)}) collective-permute-start(bf16[1,160,1408]{2,1,0:T(8,128)(2,1)S(1)} %get-tuple-element.28), channel_id=1, source_target_pairs={{0,1},{1,0},{2,3},{3,2},{4,5},{5,4},{6,7},{7,6},{8,9},{9,8},{10,11... | collective-permute-start | bytes 1351688 | tf_op jit(solution)/shard_map/ppermute | solution.py:427
  60.4 6.2 %collective-permute-start.13 = (bf16[1,160,1408]{2,1,0:T(8,128)(2,1)S(1)}, bf16[1,160,1408]{2,1,0:T(8,128)(2,1)S(1)}, u32[]{:S(2)}, u32[]{:S(2)}) collective-permute-start(bf16[1,160,1408]{2,1,0:T(8,128)(2,1)S(1)} %get-tuple-element.29), channel_id=1, source_target_pairs={{1,2},{2,1},{5,6},{6,5},{9,10},{10,9},{13,14},{14,13},{17,18},{18,... | collective-permute-start | bytes 1351688 | tf_op jit(solution)/shard_map/ppermute | solution.py:428
  61.1 21.3 %collective-permute-start.7 = (bf16[1,160,2688]{2,1,0:T(8,128)(2,1)S(1)}, bf16[1,160,2688]{2,1,0:T(8,128)(2,1)S(1)}, u32[]{:S(2)}, u32[]{:S(2)}) collective-permute-start(bf16[1,160,2688]{2,1,0:T(8,128)(2,1)S(1)} %get-tuple-element.26), channel_id=1, source_target_pairs={{1,2},{2,1},{5,6},{6,5},{9,10},{10,9},{13,14},{14,13},{17,18},{18,... | collective-permute-start | bytes 2580488 | tf_op jit(solution)/shard_map/ppermute | solution.py:407
  63.2 23.3 %collective-permute-start.20 = (bf16[1,160,1408]{2,1,0:T(8,128)(2,1)S(1)}, bf16[1,160,1408]{2,1,0:T(8,128)(2,1)S(1)}, u32[]{:S(2)}, u32[]{:S(2)}) collective-permute-start(bf16[1,160,1408]{2,1,0:T(8,128)(2,1)S(1)} %shard_map.53), channel_id=1, source_target_pairs={{0,4},{4,0},{8,12},{12,8},{16,20},{20,16},{24,28},{28,24},{1,5},{5... | collective-permute-start | bytes 1351688 | tf_op jit(solution)/shard_map/ppermute | solution.py:434
  67.8 18.8 %collective-permute-start.14 = (bf16[1,160,1408]{2,1,0:T(8,128)(2,1)S(1)}, bf16[1,160,1408]{2,1,0:T(8,128)(2,1)S(1)}, u32[]{:S(2)}, u32[]{:S(2)}) collective-permute-start(bf16[1,160,1408]{2,1,0:T(8,128)(2,1)S(1)} %shard_map.51), channel_id=1, source_target_pairs={{0,4},{4,0},{8,12},{12,8},{16,20},{20,16},{24,28},{28,24},{1,5},{5... | collective-permute-start | bytes 1351688 | tf_op jit(solution)/shard_map/ppermute | solution.py:434
  77.0 14.1 %collective-permute-start.22 = (bf16[1,160,1280]{2,1,0:T(8,128)(2,1)S(1)}, bf16[1,160,1280]{2,1,0:T(8,128)(2,1)S(1)}, u32[]{:S(2)}, u32[]{:S(2)}) collective-permute-start(bf16[1,160,1280]{2,1,0:T(8,128)(2,1)S(1)} %get-tuple-element.38), channel_id=1, source_target_pairs={{24,0},{12,4},{0,8},{20,12},{8,16},{28,20},{16,24},{4,28},{25,1},{... | collective-permute-start | bytes 1228808 | tf_op jit(solution)/shard_map/ppermute | solution.py:383
  77.0 21.4 %collective-permute-start.21 = (bf16[1,160,1280]{2,1,0:T(8,128)(2,1)S(1)}, bf16[1,160,1280]{2,1,0:T(8,128)(2,1)S(1)}, u32[]{:S(2)}, u32[]{:S(2)}) collective-permute-start(bf16[1,160,1280]{2,1,0:T(8,128)(2,1)S(1)} %get-tuple-element.37), channel_id=1, source_target_pairs={{24,0},{12,4},{0,8},{20,12},{8,16},{28,20},{16,24},{4,28},{25,1},{... | collective-permute-start | bytes 1228808 | tf_op jit(solution)/shard_map/ppermute | solution.py:383

commit v5 on v4

--- a/solution.py
+++ b/solution.py
@@ -95,12 +95,20 @@
     )
 
 
-def parts_kernel(query_count, key_count, first, heads, rule, *refs):
+def grouped(refs, sizes):
+    groups, at = [], 0
+    for size in sizes:
+        groups.append(refs[at : at + size])
+        at += size
+    return groups
+
+
+def parts_kernel(query_count, key_count, shares_of, first, heads, rule, *refs):
     band_ref, twin_ref, refs = refs[0], refs[1], refs[2:]
     queries = refs[:query_count]
     keys = refs[query_count : query_count + key_count]
-    values = refs[query_count + key_count : query_count + 2 * key_count]
-    outs = refs[query_count + 2 * key_count : -1]
+    values = grouped(refs[query_count + key_count : query_count + key_count + sum(shares_of)], shares_of)
+    outs = refs[query_count + key_count + sum(shares_of) : -1]
     log_scratch = refs[-1]
     rows = queries[0].shape[1]
     wide = query_count * rows
@@ -128,7 +136,10 @@
         return [raw_scores(of(key, n), query) + bias for key, bias in zip(keys, biases)]
 
     def attend(n, weights, total, largest):
-        summed = sum(weighted(of(value, n), part) for value, part in zip(values, weights))
+        summed = sum(
+            weighted(sum(of(ref, n) for ref in value), part)
+            for value, part in zip(values, weights)
+        )
         log_scratch[n : n + 1, :] = largest * RATE + jnp.log2(total)
         normed = (summed * (1.0 / total)).T
         for at, out in enumerate(outs):
@@ -154,9 +165,13 @@
     wide = len(queries) * rows
     blocks = len(queries) * len(keys)
     width = heads * HEAD
+    shares_of = tuple(len(value) for value in values)
+    flat = [piece for value in values for piece in value]
     return pl.pallas_call(
-        functools.partial(parts_kernel, len(queries), len(keys), first, heads, rule),
-        in_specs=[SMEM] * 2 + [VMEM] * (len(queries) + 2 * len(keys)),
+        functools.partial(
+            parts_kernel, len(queries), len(keys), shares_of, first, heads, rule
+        ),
+        in_specs=[SMEM] * 2 + [VMEM] * (len(queries) + len(keys) + len(flat)),
         out_specs=[VMEM] * len(queries),
         out_shape=[
             jax.ShapeDtypeStruct((1, rows, width + HEAD), kind) for kind in kinds
@@ -168,7 +183,7 @@
             bytes_accessed=2 * rows * width * (2 * len(queries) + 2 * len(keys)),
             transcendentals=rows * rows * heads * blocks,
         ),
-    )(*bands, *queries, *keys, *values)
+    )(*bands, *queries, *keys, *flat)
 
 
 def merge_kernel(heads, rule, band_ref, *refs):
@@ -206,7 +221,7 @@
     )(band, *blocks)
 
 
-def score_kernel(rule, band_ref, query_ref, *refs):
+def score_kernel(rule, upright, band_ref, query_ref, *refs):
     keys, (weight_ref, table_ref, scratch) = refs[:-3], refs[-3:]
     bias = jnp.where(kept(rule, band_ref, None)[0], 0.0, NEG)
     places = [(key, n) for key in keys for n in range(key.shape[2] // HEAD)]
@@ -220,7 +235,7 @@
     for n in range(len(places)):
         later = score(n + 1) if n + 1 < len(places) else None
         (weights,), total, largest = softmax_rows(raw)
-        weight_ref[n] = weights
+        weight_ref[n] = weights.T if upright else weights
         scratch[0, n : n + 1, :] = largest * RATE + jnp.log2(total)
         scratch[1, n : n + 1, :] = 1.0 / total
         raw = later
@@ -228,11 +243,11 @@
     table_ref[1] = scratch[1].T
 
 
-def scored(band, query, keys, rule):
+def scored(band, query, keys, rule, upright):
     rows, width = query.shape[1:]
     heads = width // HEAD
     return pl.pallas_call(
-        functools.partial(score_kernel, rule),
+        functools.partial(score_kernel, rule, upright),
         in_specs=[SMEM] + [VMEM] * (1 + len(keys)),
         out_specs=[VMEM] * 2,
         out_shape=[
@@ -249,13 +264,13 @@
     )(band, query, *keys)
 
 
-def blend_kernel(value_count, groups, heads, rule, band_ref, weight_ref, table_ref, *refs):
-    values, refs = refs[:value_count], refs[value_count:]
+def blend_kernel(shares_of, groups, heads, rule, band_ref, weight_ref, table_ref, *refs):
+    values, refs = grouped(refs[: sum(shares_of)], shares_of), refs[sum(shares_of) :]
     pieces, out_ref = refs[: sum(len(group) for group in groups)], refs[-2]
     keeps = kept(rule, band_ref, None)
     rows = out_ref.shape[1]
     lane = lax.broadcasted_iota(jnp.int32, (rows, HEAD), 1)
-    value_at = [(value, n) for value in values for n in range(value.shape[2] // HEAD)]
+    value_at = [(value, n) for value in values for n in range(value[0].shape[2] // HEAD)]
     logs = [table_ref[0]]
     places = []
     at = 0
@@ -273,16 +288,18 @@
         logs.append(log if keep is True else jnp.where(keep, log, NEG))
         places.append(place)
     weights, log = shares(logs)
-    coef = (weights[0] * table_ref[1]).T
-    refs[-1][...] = coef
+    coef = weights[0] * table_ref[1]
     if values:
+        refs[-1][...] = coef.T
         out_ref[0, :, column(heads)] = log
+    else:
+        refs[-1][...] = packed(coef)
     tables = [packed(weight) for weight in weights[1:]]
     for n in range(heads):
         out = 0.0
         if values:
             value, index = value_at[n]
-            summed = weighted(value[0, :, column(index)], weight_ref[n])
+            summed = weighted(sum(ref[0, :, column(index)] for ref in value), weight_ref[n])
             out = (summed * refs[-1][n : n + 1, :]).T
         for table, place in zip(tables, places):
             piece, index = place[n]
@@ -298,22 +315,24 @@
     sizes = tuple(tuple(piece.shape[2] // HEAD - 1 for piece in group) for group in groups)
     pieces = [piece for group in groups for piece in group]
     out_shape = jax.ShapeDtypeStruct((1, rows, width + (HEAD if values else 0)), jnp.float32)
-    coef = jax.ShapeDtypeStruct((HEAD, rows), jnp.float32)
+    coef = jax.ShapeDtypeStruct((rows, HEAD), jnp.bfloat16)
+    shares_of = tuple(len(value) for value in values)
+    flat = [piece for value in values for piece in value]
     if not values:
         weights = table
     out = pl.pallas_call(
-        functools.partial(blend_kernel, len(values), sizes, heads, rule),
-        in_specs=[SMEM] + [VMEM] * (2 + len(values) + len(pieces)),
+        functools.partial(blend_kernel, shares_of, sizes, heads, rule),
+        in_specs=[SMEM] + [VMEM] * (2 + len(flat) + len(pieces)),
         out_specs=[VMEM] if values else [VMEM, VMEM],
         out_shape=[out_shape] if values else [out_shape, coef],
-        scratch_shapes=[pltpu.VMEM(coef.shape, coef.dtype)] if values else [],
+        scratch_shapes=[pltpu.VMEM((HEAD, rows), jnp.float32)] if values else [],
         compiler_params=GRANT,
         cost_estimate=pl.CostEstimate(
             flops=2 * rows * rows * width,
             bytes_accessed=2 * rows * width * (len(pieces) + 4),
             transcendentals=0,
         ),
-    )(band, weights, table, *values, *pieces)
+    )(band, weights, table, *flat, *pieces)
     return out[0] if values else out
 
 
@@ -322,8 +341,12 @@
     copies = []
     for n in range(heads):
         cols = column(first + n)
-        summed = weighted(value_ref[0, :, column(n)], weight_ref[first + n])
-        out = (summed * coef_ref[first + n : first + n + 1, :]).T + base_ref[0, :, cols]
+        summed = jnp.dot(
+            weight_ref[first + n],
+            value_ref[0, :, column(n)],
+            preferred_element_type=jnp.float32,
+        )
+        out = summed * spread(coef_ref[...], first + n) + base_ref[0, :, cols]
         scratch[:, column(n)] = out.astype(scratch.dtype)
         if (n + 1) % BATCH == 0 or n + 1 == heads:
             start = n // BATCH * BATCH
@@ -376,11 +399,24 @@
 
     cuts = [slice(first * HEAD, (first + size) * HEAD) for first, size in spans]
     value_halves = [values[:, :, cut] for cut in cuts]
+    tail = (heads - half) // 5 * 2
+    ends = [0, half, heads - tail, heads]
+    value_thirds = value_halves[:1] + [
+        values[:, :, start * HEAD : stop * HEAD] for start, stop in zip(ends[1:], ends[2:])
+    ]
+    beyond = [(a, b) for a, b in toward if abs(a - b) != 2]
+    within = [(a, b) for a, b in toward if abs(a - b) == 2]
 
     key_one = lax.ppermute(keys, "frame", toward)
-    value_one = [lax.ppermute(value_halves[span], "frame", toward) for span in (0, 1)]
+    value_one = [
+        (lax.ppermute(value_halves[0], "frame", toward),),
+        (
+            lax.ppermute(value_halves[1], "frame", within),
+            lax.ppermute(value_halves[1], "frame", beyond),
+        ),
+    ]
     key_two = lax.ppermute(keys, "frame", away)
-    value_two = [lax.ppermute(value_halves[span], "frame", away) for span in (0, 1)]
+    value_two = [lax.ppermute(piece, "frame", away) for piece in value_thirds]
     query_twin = []
     for cut in cuts:
         query_twin.append(lax.ppermute(queries[:, :, cut], "frame", twin))
@@ -397,7 +433,7 @@
         (band, band),
         [query_even, query_odd, queries],
         [keys],
-        [values],
+        [(values,)],
         beside_rule,
         (narrow, narrow, full),
         0,
@@ -418,7 +454,7 @@
             (band, band_twin),
             [twin_even[span], twin_odd[span], query_twin[span]],
             [keys, key_one],
-            [values, value_one[span]],
+            [(values,), value_one[span]],
             twin_rule,
             (narrow, narrow, full),
             first,
@@ -438,6 +474,7 @@
         queries,
         [key_one],
         lambda own, other, odd_frame, has_odd: [jnp.where(odd_frame, own[0], own[4]) >= 0],
+        False,
     )
     near = blended(
         band,
@@ -451,6 +488,7 @@
         queries,
         [key_two],
         lambda own, other, odd_frame, has_odd: [jnp.where(odd_frame, own[4], own[0]) >= 0],
+        True,
     )
     base, coef = blended(
         band,
@@ -460,8 +498,8 @@
         lambda own, other, odd_frame, has_odd: [True, True],
     )
     out = None
-    for span, (first, size) in enumerate(spans):
-        out = finished(far_score[0], coef, value_two[span], base, out, first)
+    for at, first in enumerate(ends[:-1]):
+        out = finished(far_score[0], coef, value_two[at], base, out, first)
     return out
 
 

time: 101 us -> 99.1 us (0.981)
  the two profiles are of different devices: /device:TPU:0 before, /device:TPU:1 now
where the time goes in v5:
time: 99.1 us; the launch traced here: 98.8 us
  starting transfers between devices  43 us (43%)
  waiting for transfers between devices  27.4 us (28%)
  Pallas kernels  26.5 us (27%)
  local copies, waits for them, and re-layouts  1.43 us (1%)
    ppermute x2, waiting for transfers between devices, per_device(): twin_odd = [lax.ppermute(query_twin[span], 'row', odd) for span in (0, 1)]  12.5 us
    pallas_call x3, Pallas kernels, parts(): pl.pallas_call(functools.partial(parts_kernel, len(queries), len(keys), s...  11.4 us
    ppermute x1, waiting for transfers between devices, per_device(): band_twin = lax.ppermute(band, 'frame', twin)  8.05 us
    ppermute x2, starting transfers between devices, per_device(): from_twin.append(lax.ppermute(whole, 'frame', twin))  6.67 us
    ppermute x1, starting transfers between devices, per_device(): lax.ppermute(value_halves[1], 'frame', beyond)  6.06 us
    pallas_call x2, Pallas kernels, blended(): pl.pallas_call(functools.partial(blend_kernel, shares_of, sizes, heads, r...  5.48 us
    ppermute x2, starting transfers between devices, per_device(): back_odd = lax.ppermute(odd_twin, 'row', odd)  5.37 us
    ppermute x2, starting transfers between devices, per_device(): twin_odd = [lax.ppermute(query_twin[span], 'row', odd) for span in (0, 1)]  5.32 us
  transfers between devices with their start and end apart: 25, of which 6 were waited for; matrix products, arithmetic and copies ran while one was open for 0% of the time, Pallas kernels for 26%

profile of v5, /device:TPU:1, one launch (start us, length us, event | category | flops | bytes accessed | tf_op | source)
XLA Modules:
  0.0 98.8 jit_solution(3178581476203107466)
XLA Ops:
  0.0 1.3 %fusion = (bf16[1,160,1280]{2,1,0:T(8,128)(2,1)S(1)}, bf16[1,160,1280]{2,1,0:T(8,128)(2,1)S(1)}) fusion(bf16[1,160,2560]{2,1,0:T(8,128)(2,1)} %refs_4_.1), kind=kLoop, calls=%fused_computation | loop fusion | bytes 1638400 | tf_op jit(solution)/shard_map/slice | solution.py:422
  1.4 2.1 %collective-permute-start.16 = (bf16[1,160,1280]{2,1,0:T(8,128)(2,1)S(1)}, bf16[1,160,1280]{2,1,0:T(8,128)(2,1)S(1)}, u32[]{:S(2)}, u32[]{:S(2)}) collective-permute-start(bf16[1,160,1280]{2,1,0:T(8,128)(2,1)S(1)} %get-tuple-element.35), channel_id=1, source_target_pairs={{0,4},{4,0},{8,12},{12,8},{16,20},{20,16},{24,28},{28,24},{1,5},{5... | collective-permute-start | bytes 1228808 | tf_op jit(solution)/shard_map/ppermute | solution.py:422
  3.5 1.3 %collective-permute-start.3 = (bf16[1,160,1280]{2,1,0:T(8,128)(2,1)S(1)}, bf16[1,160,1280]{2,1,0:T(8,128)(2,1)S(1)}, u32[]{:S(2)}, u32[]{:S(2)}) collective-permute-start(bf16[1,160,1280]{2,1,0:T(8,128)(2,1)S(1)} %get-tuple-element.37), channel_id=1, source_target_pairs={{4,12},{8,0},{12,20},{16,8},{20,28},{24,16},{5,13},{9,1},{13,21},{... | collective-permute-start | bytes 1228808 | tf_op jit(solution)/shard_map/ppermute | solution.py:414
  4.8 6.1 %collective-permute-start.4 = (bf16[1,160,1280]{2,1,0:T(8,128)(2,1)S(1)}, bf16[1,160,1280]{2,1,0:T(8,128)(2,1)S(1)}, u32[]{:S(2)}, u32[]{:S(2)}) collective-permute-start(bf16[1,160,1280]{2,1,0:T(8,128)(2,1)S(1)} %get-tuple-element.37), channel_id=1, source_target_pairs={{0,24},{28,4},{1,25},{29,5},{2,26},{30,6},{3,27},{31,7}} | collective-permute-start | bytes 1228808 | tf_op jit(solution)/shard_map/ppermute | solution.py:415
  11.0 1.4 %collective-permute-start.9 = (s32[1,5]{1,0:T(1,128)S(1)}, s32[1,5]{1,0:T(1,128)S(1)}, u32[]{:S(2)}, u32[]{:S(2)}) collective-permute-start(s32[1,5]{1,0:T(1,128)S(1)} %copy-done.3), channel_id=1, source_target_pairs={{0,4},{4,0},{8,12},{12,8},{16,20},{20,16},{24,28},{28,24},{1,5},{5... | collective-permute-start | bytes 68 | tf_op jit(solution)/shard_map/ppermute | solution.py:423
  12.4 8.0 %collective-permute-done.9.refs_1_ = s32[1,5]{1,0:T(1,128)S(1)} collective-permute-done((s32[1,5]{1,0:T(1,128)S(1)}, s32[1,5]{1,0:T(1,128)S(1)}, u32[]{:S(2)}, u32[]{:S(2)}) %collective-permute-start.9) | collective-permute-done | bytes 52 | tf_op jit(solution)/shard_map/ppermute | solution.py:423
  20.5 4.2 %collective-permute-start.1 = (bf16[1,160,2560]{2,1,0:T(8,128)(2,1)S(1)}, bf16[1,160,2560]{2,1,0:T(8,128)(2,1)S(1)}, u32[]{:S(2)}, u32[]{:S(2)}) collective-permute-start(bf16[1,160,2560]{2,1,0:T(8,128)(2,1)S(1)} %copy-done.2), channel_id=1, source_target_pairs={{0,24},{4,12},{8,0},{12,20},{16,8},{20,28},{24,16},{28,4},{1,25},{... | collective-permute-start | bytes 2457608 | tf_op jit(solution)/shard_map/ppermute | solution.py:410
  24.7 1.9 %collective-permute-start.17 = (bf16[1,160,1280]{2,1,0:T(8,128)(2,1)S(1)}, bf16[1,160,1280]{2,1,0:T(8,128)(2,1)S(1)}, u32[]{:S(2)}, u32[]{:S(2)}) collective-permute-start(bf16[1,160,1280]{2,1,0:T(8,128)(2,1)S(1)} %collective-permute-done.16.refs_4_), channel_id=1, source_target_pairs={{0,1},{1,0},{2,3},{3,2},{4,5},{5,4},{6,7},{7,6},{8,9},{9,8},{10,11... | collective-permute-start | bytes 1228808 | tf_op jit(solution)/shard_map/ppermute | solution.py:426
  26.7 3.4 %collective-permute-start.6 = (bf16[1,160,2560]{2,1,0:T(8,128)(2,1)S(1)}, bf16[1,160,2560]{2,1,0:T(8,128)(2,1)S(1)}, u32[]{:S(2)}, u32[]{:S(2)}) collective-permute-start(bf16[1,160,2560]{2,1,0:T(8,128)(2,1)S(1)} %copy-done.1), channel_id=1, source_target_pairs={{1,2},{2,1},{5,6},{6,5},{9,10},{10,9},{13,14},{14,13},{17,18},{18,... | collective-permute-start | bytes 2457608 | tf_op jit(solution)/shard_map/ppermute | solution.py:425
  30.1 2.1 %collective-permute-start.18 = (bf16[1,160,1280]{2,1,0:T(8,128)(2,1)S(1)}, bf16[1,160,1280]{2,1,0:T(8,128)(2,1)S(1)}, u32[]{:S(2)}, u32[]{:S(2)}) collective-permute-start(bf16[1,160,1280]{2,1,0:T(8,128)(2,1)S(1)} %collective-permute-done.16.refs_4_), channel_id=1, source_target_pairs={{1,2},{2,1},{5,6},{6,5},{9,10},{10,9},{13,14},{14,13},{17,18},{18,... | collective-permute-start | bytes 1228808 | tf_op jit(solution)/shard_map/ppermute | solution.py:427
  32.5 12.5 %collective-permute-done.18.refs_3_ = bf16[1,160,1280]{2,1,0:T(8,128)(2,1)S(1)} collective-permute-done((bf16[1,160,1280]{2,1,0:T(8,128)(2,1)S(1)}, bf16[1,160,1280]{2,1,0:T(8,128)(2,1)S(1)}, u32[]{:S(2)}, u32[]{:S(2)}) %collective-permute-start.18) | collective-permute-done | bytes 409632 | tf_op jit(solution)/shard_map/ppermute | solution.py:427
  45.0 3.2 %collective-permute-start.12 = (bf16[1,160,1280]{2,1,0:T(8,128)(2,1)S(1)}, bf16[1,160,1280]{2,1,0:T(8,128)(2,1)S(1)}, u32[]{:S(2)}, u32[]{:S(2)}) collective-permute-start(bf16[1,160,1280]{2,1,0:T(8,128)(2,1)S(1)} %collective-permute-done.10.refs_4_), channel_id=1, source_target_pairs={{1,2},{2,1},{5,6},{6,5},{9,10},{10,9},{13,14},{14,13},{17,18},{18,... | collective-permute-start | bytes 1228808 | tf_op jit(solution)/shard_map/ppermute | solution.py:427
  48.2 3.9 %shard_map.52 = (bf16[1,160,1408]{2,1,0:T(8,128)(2,1)S(1)}, bf16[1,160,1408]{2,1,0:T(8,128)(2,1)S(1)}, f32[1,160,1408]{2,1,0:T(8,128)S(1)}) custom-call(s32[1,5]{1,0:T(1,128)S(1)} %copy-done.3, s32[1,5]{1,0:T(1,128)S(1)} %collective-permute-done.9.refs_1_, bf16[1,160,1280]{2,1,0:T(8,128)(2,1)S(1)} %collective-permute-done.17.refs_2_, ...), custom_call_target="tpu_custom_call" | custom-call | flops 786432000 | bytes 4096000 | tf_op jit(solution)/shard_map/pallas_call | solution.py:170
  52.2 2.7 %collective-permute-start.20 = (bf16[1,160,1408]{2,1,0:T(8,128)(2,1)S(1)}, bf16[1,160,1408]{2,1,0:T(8,128)(2,1)S(1)}, u32[]{:S(2)}, u32[]{:S(2)}) collective-permute-start(bf16[1,160,1408]{2,1,0:T(8,128)(2,1)S(1)} %get-tuple-element.32), channel_id=1, source_target_pairs={{1,2},{2,1},{5,6},{6,5},{9,10},{10,9},{13,14},{14,13},{17,18},{18,... | collective-permute-start | bytes 1351688 | tf_op jit(solution)/shard_map/ppermute | solution.py:464
  55.2 3.7 %shard_map.48 = (bf16[1,160,2688]{2,1,0:T(8,128)(2,1)S(1)}, bf16[1,160,2688]{2,1,0:T(8,128)(2,1)S(1)}, f32[1,160,2688]{2,1,0:T(8,128)S(1)}) custom-call(s32[1,5]{1,0:T(1,128)S(1)} %copy-done.3, s32[1,5]{1,0:T(1,128)S(1)} %copy-done.3, bf16[1,160,2560]{2,1,0:T(8,128)(2,1)S(1)} %collective-permute-done.5.refs_2_, ...), custom_call_target="tpu_custom_call" | custom-call | flops 786432000 | bytes 6553600 | tf_op jit(solution)/shard_map/pallas_call | solution.py:170
  58.9 3.1 %collective-permute-start.8 = (bf16[1,160,2688]{2,1,0:T(8,128)(2,1)S(1)}, bf16[1,160,2688]{2,1,0:T(8,128)(2,1)S(1)}, u32[]{:S(2)}, u32[]{:S(2)}) collective-permute-start(bf16[1,160,2688]{2,1,0:T(8,128)(2,1)S(1)} %get-tuple-element.26), channel_id=1, source_target_pairs={{1,2},{2,1},{5,6},{6,5},{9,10},{10,9},{13,14},{14,13},{17,18},{18,... | collective-permute-start | bytes 2580488 | tf_op jit(solution)/shard_map/ppermute | solution.py:443
  62.1 3.8 %shard_map.50 = (bf16[1,160,1408]{2,1,0:T(8,128)(2,1)S(1)}, bf16[1,160,1408]{2,1,0:T(8,128)(2,1)S(1)}, f32[1,160,1408]{2,1,0:T(8,128)S(1)}) custom-call(s32[1,5]{1,0:T(1,128)S(1)} %copy-done.3, s32[1,5]{1,0:T(1,128)S(1)} %collective-permute-done.9.refs_1_, bf16[1,160,1280]{2,1,0:T(8,128)(2,1)S(1)} %collective-permute-done.11.refs_2_, ...), custom_call_target="tpu_custom_call" | custom-call | flops 786432000 | bytes 4096000 | tf_op jit(solution)/shard_map/pallas_call | solution.py:170
  66.0 2.6 %collective-permute-start.14 = (bf16[1,160,1408]{2,1,0:T(8,128)(2,1)S(1)}, bf16[1,160,1408]{2,1,0:T(8,128)(2,1)S(1)}, u32[]{:S(2)}, u32[]{:S(2)}) collective-permute-start(bf16[1,160,1408]{2,1,0:T(8,128)(2,1)S(1)} %get-tuple-element.29), channel_id=1, source_target_pairs={{1,2},{2,1},{5,6},{6,5},{9,10},{10,9},{13,14},{14,13},{17,18},{18,... | collective-permute-start | bytes 1351688 | tf_op jit(solution)/shard_map/ppermute | solution.py:464
  68.6 1.2 %shard_map.53 = bf16[1,160,1408]{2,1,0:T(8,128)(2,1)S(1)} custom-call(s32[1,5]{1,0:T(1,128)S(1)} %copy-done.3, f32[1,160,1408]{2,1,0:T(8,128)S(1)} %get-tuple-element.30.refs_0_, bf16[1,160,1408]{2,1,0:T(8,128)(2,1)S(1)} %collective-permute-done.19.refs_1_, bf16[1,160,1408]{2,1,0:T(8,128)(2,1)S(1)} %collective-permute-done.20.refs_2_), custom_call_target="tpu_custom_call" | custom-call | flops 1351680 | bytes 1802240 | tf_op jit(solution)/shard_map/pallas_call | solution.py:210
  69.8 3.3 %collective-permute-start.21 = (bf16[1,160,1408]{2,1,0:T(8,128)(2,1)S(1)}, bf16[1,160,1408]{2,1,0:T(8,128)(2,1)S(1)}, u32[]{:S(2)}, u32[]{:S(2)}) collective-permute-start(bf16[1,160,1408]{2,1,0:T(8,128)(2,1)S(1)} %shard_map.53), channel_id=1, source_target_pairs={{0,4},{4,0},{8,12},{12,8},{16,20},{20,16},{24,28},{28,24},{1,5},{5... | collective-permute-start | bytes 1351688 | tf_op jit(solution)/shard_map/ppermute | solution.py:470
  73.2 5.0 %collective-permute-done.14.refs_2_ = bf16[1,160,1408]{2,1,0:T(8,128)(2,1)S(1)} collective-permute-done((bf16[1,160,1408]{2,1,0:T(8,128)(2,1)S(1)}, bf16[1,160,1408]{2,1,0:T(8,128)(2,1)S(1)}, u32[]{:S(2)}, u32[]{:S(2)}) %collective-permute-start.14) | collective-permute-done | bytes 450592 | tf_op jit(solution)/shard_map/ppermute | solution.py:464
  78.2 1.2 %shard_map.51 = bf16[1,160,1408]{2,1,0:T(8,128)(2,1)S(1)} custom-call(s32[1,5]{1,0:T(1,128)S(1)} %copy-done.3, f32[1,160,1408]{2,1,0:T(8,128)S(1)} %get-tuple-element.27.refs_0_, bf16[1,160,1408]{2,1,0:T(8,128)(2,1)S(1)} %collective-permute-done.13.refs_1_, bf16[1,160,1408]{2,1,0:T(8,128)(2,1)S(1)} %collective-permute-done.14.refs_2_), custom_call_target="tpu_custom_call" | custom-call | flops 1351680 | bytes 1802240 | tf_op jit(solution)/shard_map/pallas_call | solution.py:210
  79.4 3.3 %collective-permute-start.15 = (bf16[1,160,1408]{2,1,0:T(8,128)(2,1)S(1)}, bf16[1,160,1408]{2,1,0:T(8,128)(2,1)S(1)}, u32[]{:S(2)}, u32[]{:S(2)}) collective-permute-start(bf16[1,160,1408]{2,1,0:T(8,128)(2,1)S(1)} %shard_map.51), channel_id=1, source_target_pairs={{0,4},{4,0},{8,12},{12,8},{16,20},{20,16},{24,28},{28,24},{1,5},{5... | collective-permute-start | bytes 1351688 | tf_op jit(solution)/shard_map/ppermute | solution.py:470
  82.8 1.2 %collective-permute-start.23 = (bf16[1,160,768]{2,1,0:T(8,128)(2,1)S(1)}, bf16[1,160,768]{2,1,0:T(8,128)(2,1)S(1)}, u32[]{:S(2)}, u32[]{:S(2)}) collective-permute-start(bf16[1,160,768]{2,1,0:T(8,128)(2,1)S(1)} %slice.23), channel_id=1, source_target_pairs={{24,0},{12,4},{0,8},{20,12},{8,16},{28,20},{16,24},{4,28},{25,1},{... | collective-permute-start | bytes 737288 | tf_op jit(solution)/shard_map/ppermute | solution.py:419
  84.1 2.0 %shard_map.47 = (bf16[20,160,160]{2,1,0:T(8,128)(2,1)S(1)}, f32[2,160,128]{2,1,0:T(8,128)S(1)}) custom-call(s32[1,5]{1,0:T(1,128)S(1)} %copy-done.3, bf16[1,160,2560]{2,1,0:T(8,128)(2,1)S(1)} %copy-done.1, bf16[1,160,2560]{2,1,0:T(8,128)(2,1)S(1)} %collective-permute-done.1.refs_0_.refs_6_), custom_call_target="tpu_custom_call" | custom-call | flops 131072000 | bytes 2457600 | tf_op jit(solution)/shard_map/pallas_call | solution.py:249
  86.1 2.0 %shard_map.46 = (bf16[20,160,160]{2,1,0:T(8,128)(2,1)S(1)}, f32[2,160,128]{2,1,0:T(8,128)S(1)}) custom-call(s32[1,5]{1,0:T(1,128)S(1)} %copy-done.3, bf16[1,160,2560]{2,1,0:T(8,128)(2,1)S(1)} %copy-done.1, bf16[1,160,2560]{2,1,0:T(8,128)(2,1)S(1)} %collective-permute-done.refs_0_), custom_call_target="tpu_custom_call" | custom-call | flops 131072000 | bytes 2457600 | tf_op jit(solution)/shard_map/pallas_call | solution.py:249
  88.1 4.1 %shard_map.49.refs_0_ = f32[1,160,2688]{2,1,0:T(8,128)S(1)} custom-call(s32[1,5]{1,0:T(1,128)S(1)} %copy-done.3, bf16[20,160,160]{2,1,0:T(8,128)(2,1)S(1)} %get-tuple-element.22.weight_ref, f32[2,160,128]{2,1,0:T(8,128)S(1)} %get-tuple-element.23.table_ref, bf16[1,160,1280]{2,1,0:T(8,128)(2,1)S(1)} %collective-permute-done.2.refs_0_.refs_8_, ...), custom_call_target="tpu_custom_call" | custom-call | flops 131072000 | bytes 5734400 | tf_op jit(solution)/shard_map/pallas_call | solution.py:323
  92.3 1.4 %shard_map.54 = (f32[1,160,2560]{2,1,0:T(8,128)S(1)}, bf16[160,128]{1,0:T(8,128)(2,1)S(1)}) custom-call(s32[1,5]{1,0:T(1,128)S(1)} %copy-done.3, f32[2,160,128]{2,1,0:T(8,128)S(1)} %get-tuple-element.21.weight_ref.table_ref, f32[2,160,128]{2,1,0:T(8,128)S(1)} %get-tuple-element.21.weight_ref.table_ref, f32[1,160,2688]{2,1,0:T(8,128)S(1)} %shard_map.49.refs_0_, ...), custom_call_target="tpu_custom_call" | custom-call | flops 131072000 | bytes 5734400 | tf_op jit(solution)/shard_map/pallas_call | solution.py:323
  93.7 1.2 %shard_map.55.refs_0_ = bf16[1,160,2560]{2,1,0:T(8,128)(2,1)} custom-call(bf16[20,160,160]{2,1,0:T(8,128)(2,1)S(1)} %get-tuple-element.20.weight_ref, bf16[160,128]{1,0:T(8,128)(2,1)S(1)} %get-tuple-element.33.coef_ref, bf16[1,160,1280]{2,1,0:T(8,128)(2,1)S(1)} %collective-permute-done.24.value_ref, f32[1,160,2560]{2,1,0:T(8,128)S(1)} %get-tuple-element.34.base_ref), custom_call_target="tpu_custom_call" | custom-call | flops 65536000 | bytes 1638400 | tf_op jit(solution)/shard_map/pallas_call | solution.py:367
  94.9 1.0 collective-permute-done.23.value_ref
  95.9 1.0 %shard_map.56.refs_0_ = bf16[1,160,2560]{2,1,0:T(8,128)(2,1)} custom-call(bf16[20,160,160]{2,1,0:T(8,128)(2,1)S(1)} %get-tuple-element.20.weight_ref, bf16[160,128]{1,0:T(8,128)(2,1)S(1)} %get-tuple-element.33.coef_ref, bf16[1,160,768]{2,1,0:T(8,128)(2,1)S(1)} %collective-permute-done.23.value_ref, ...), custom_call_target="tpu_custom_call", output_to_operand_aliasing={{}: (4, {})} | custom-call | flops 39321600 | bytes 983040 | tf_op jit(solution)/shard_map/pallas_call | solution.py:367
  97.7 1.0 shard_map.57
  (42 shorter events, 1.8 us)
Async XLA Ops:
  0.0 26.6 %copy-start.1 = (bf16[1,160,2560]{2,1,0:T(8,128)(2,1)S(1)}, bf16[1,160,2560]{2,1,0:T(8,128)(2,1)}, u32[]{:S(2)}) copy-start(bf16[1,160,2560]{2,1,0:T(8,128)(2,1)} %refs_4_.1) | copy-start | bytes 2457604
  0.0 3.5 %copy-start = (bf16[1,160,2560]{2,1,0:T(8,128)(2,1)S(1)}, bf16[1,160,2560]{2,1,0:T(8,128)(2,1)}, u32[]{:S(2)}) copy-start(bf16[1,160,2560]{2,1,0:T(8,128)(2,1)} %refs_7_.3) | copy-start | bytes 2457604
  0.0 11.0 %copy-start.3 = (s32[1,5]{1,0:T(1,128)S(1)}, s32[1,5]{1,0:T(1,128)}, u32[]{:S(2)}) copy-start(s32[1,5]{1,0:T(1,128)} %band_ref.11) | copy-start | bytes 64
  0.0 20.5 %copy-start.2 = (bf16[1,160,2560]{2,1,0:T(8,128)(2,1)S(1)}, bf16[1,160,2560]{2,1,0:T(8,128)(2,1)}, u32[]{:S(2)}) copy-start(bf16[1,160,2560]{2,1,0:T(8,128)(2,1)} %refs_5_.5) | copy-start | bytes 2457604
  1.4 23.4 %collective-permute-start.16 = (bf16[1,160,1280]{2,1,0:T(8,128)(2,1)S(1)}, bf16[1,160,1280]{2,1,0:T(8,128)(2,1)S(1)}, u32[]{:S(2)}, u32[]{:S(2)}) collective-permute-start(bf16[1,160,1280]{2,1,0:T(8,128)(2,1)S(1)} %get-tuple-element.35), channel_id=1, source_target_pairs={{0,4},{4,0},{8,12},{12,8},{16,20},{20,16},{24,28},{28,24},{1,5},{5... | collective-permute-start | bytes 1228808 | tf_op jit(solution)/shard_map/ppermute | solution.py:422
  3.5 23.1 %collective-permute-start.3 = (bf16[1,160,1280]{2,1,0:T(8,128)(2,1)S(1)}, bf16[1,160,1280]{2,1,0:T(8,128)(2,1)S(1)}, u32[]{:S(2)}, u32[]{:S(2)}) collective-permute-start(bf16[1,160,1280]{2,1,0:T(8,128)(2,1)S(1)} %get-tuple-element.37), channel_id=1, source_target_pairs={{4,12},{8,0},{12,20},{16,8},{20,28},{24,16},{5,13},{9,1},{13,21},{... | collective-permute-start | bytes 1228808 | tf_op jit(solution)/shard_map/ppermute | solution.py:414
  4.8 21.9 %collective-permute-start.4 = (bf16[1,160,1280]{2,1,0:T(8,128)(2,1)S(1)}, bf16[1,160,1280]{2,1,0:T(8,128)(2,1)S(1)}, u32[]{:S(2)}, u32[]{:S(2)}) collective-permute-start(bf16[1,160,1280]{2,1,0:T(8,128)(2,1)S(1)} %get-tuple-element.37), channel_id=1, source_target_pairs={{0,24},{28,4},{1,25},{29,5},{2,26},{30,6},{3,27},{31,7}} | collective-permute-start | bytes 1228808 | tf_op jit(solution)/shard_map/ppermute | solution.py:415
  10.9 19.2 %collective-permute-start.10 = (bf16[1,160,1280]{2,1,0:T(8,128)(2,1)S(1)}, bf16[1,160,1280]{2,1,0:T(8,128)(2,1)S(1)}, u32[]{:S(2)}, u32[]{:S(2)}) collective-permute-start(bf16[1,160,1280]{2,1,0:T(8,128)(2,1)S(1)} %get-tuple-element.36), channel_id=1, source_target_pairs={{0,4},{4,0},{8,12},{12,8},{16,20},{20,16},{24,28},{28,24},{1,5},{5... | collective-permute-start | bytes 1228808 | tf_op jit(solution)/shard_map/ppermute | solution.py:422
  11.0 9.5 %collective-permute-start.9 = (s32[1,5]{1,0:T(1,128)S(1)}, s32[1,5]{1,0:T(1,128)S(1)}, u32[]{:S(2)}, u32[]{:S(2)}) collective-permute-start(s32[1,5]{1,0:T(1,128)S(1)} %copy-done.3), channel_id=1, source_target_pairs={{0,4},{4,0},{8,12},{12,8},{16,20},{20,16},{24,28},{28,24},{1,5},{5... | collective-permute-start | bytes 68 | tf_op jit(solution)/shard_map/ppermute | solution.py:423
  20.5 24.5 %collective-permute-start.1 = (bf16[1,160,2560]{2,1,0:T(8,128)(2,1)S(1)}, bf16[1,160,2560]{2,1,0:T(8,128)(2,1)S(1)}, u32[]{:S(2)}, u32[]{:S(2)}) collective-permute-start(bf16[1,160,2560]{2,1,0:T(8,128)(2,1)S(1)} %copy-done.2), channel_id=1, source_target_pairs={{0,24},{4,12},{8,0},{12,20},{16,8},{20,28},{24,16},{28,4},{1,25},{... | collective-permute-start | bytes 2457608 | tf_op jit(solution)/shard_map/ppermute | solution.py:410
  24.7 7.6 %collective-permute-start.17 = (bf16[1,160,1280]{2,1,0:T(8,128)(2,1)S(1)}, bf16[1,160,1280]{2,1,0:T(8,128)(2,1)S(1)}, u32[]{:S(2)}, u32[]{:S(2)}) collective-permute-start(bf16[1,160,1280]{2,1,0:T(8,128)(2,1)S(1)} %collective-permute-done.16.refs_4_), channel_id=1, source_target_pairs={{0,1},{1,0},{2,3},{3,2},{4,5},{5,4},{6,7},{7,6},{8,9},{9,8},{10,11... | collective-permute-start | bytes 1228808 | tf_op jit(solution)/shard_map/ppermute | solution.py:426
  26.6 25.6 %collective-permute-start.5 = (bf16[1,160,2560]{2,1,0:T(8,128)(2,1)S(1)}, bf16[1,160,2560]{2,1,0:T(8,128)(2,1)S(1)}, u32[]{:S(2)}, u32[]{:S(2)}) collective-permute-start(bf16[1,160,2560]{2,1,0:T(8,128)(2,1)S(1)} %copy-done.1), channel_id=1, source_target_pairs={{0,1},{1,0},{2,3},{3,2},{4,5},{5,4},{6,7},{7,6},{8,9},{9,8},{10,11... | collective-permute-start | bytes 2457608 | tf_op jit(solution)/shard_map/ppermute | solution.py:424
  26.7 28.3 %collective-permute-start.6 = (bf16[1,160,2560]{2,1,0:T(8,128)(2,1)S(1)}, bf16[1,160,2560]{2,1,0:T(8,128)(2,1)S(1)}, u32[]{:S(2)}, u32[]{:S(2)}) collective-permute-start(bf16[1,160,2560]{2,1,0:T(8,128)(2,1)S(1)} %copy-done.1), channel_id=1, source_target_pairs={{1,2},{2,1},{5,6},{6,5},{9,10},{10,9},{13,14},{14,13},{17,18},{18,... | collective-permute-start | bytes 2457608 | tf_op jit(solution)/shard_map/ppermute | solution.py:425
  30.1 14.9 %collective-permute-start.18 = (bf16[1,160,1280]{2,1,0:T(8,128)(2,1)S(1)}, bf16[1,160,1280]{2,1,0:T(8,128)(2,1)S(1)}, u32[]{:S(2)}, u32[]{:S(2)}) collective-permute-start(bf16[1,160,1280]{2,1,0:T(8,128)(2,1)S(1)} %collective-permute-done.16.refs_4_), channel_id=1, source_target_pairs={{1,2},{2,1},{5,6},{6,5},{9,10},{10,9},{13,14},{14,13},{17,18},{18,... | collective-permute-start | bytes 1228808 | tf_op jit(solution)/shard_map/ppermute | solution.py:427
  32.3 19.8 %collective-permute-start.2 = (bf16[1,160,1280]{2,1,0:T(8,128)(2,1)S(1)}, bf16[1,160,1280]{2,1,0:T(8,128)(2,1)S(1)}, u32[]{:S(2)}, u32[]{:S(2)}) collective-permute-start(bf16[1,160,1280]{2,1,0:T(8,128)(2,1)S(1)} %get-tuple-element.38), channel_id=1, source_target_pairs={{0,24},{4,12},{8,0},{12,20},{16,8},{20,28},{24,16},{28,4},{1,25},{... | collective-permute-start | bytes 1228808 | tf_op jit(solution)/shard_map/ppermute | solution.py:412
  45.0 13.8 %collective-permute-start.11 = (bf16[1,160,1280]{2,1,0:T(8,128)(2,1)S(1)}, bf16[1,160,1280]{2,1,0:T(8,128)(2,1)S(1)}, u32[]{:S(2)}, u32[]{:S(2)}) collective-permute-start(bf16[1,160,1280]{2,1,0:T(8,128)(2,1)S(1)} %collective-permute-done.10.refs_4_), channel_id=1, source_target_pairs={{0,1},{1,0},{2,3},{3,2},{4,5},{5,4},{6,7},{7,6},{8,9},{9,8},{10,11... | collective-permute-start | bytes 1228808 | tf_op jit(solution)/shard_map/ppermute | solution.py:426
  45.0 13.9 %collective-permute-start.12 = (bf16[1,160,1280]{2,1,0:T(8,128)(2,1)S(1)}, bf16[1,160,1280]{2,1,0:T(8,128)(2,1)S(1)}, u32[]{:S(2)}, u32[]{:S(2)}) collective-permute-start(bf16[1,160,1280]{2,1,0:T(8,128)(2,1)S(1)} %collective-permute-done.10.refs_4_), channel_id=1, source_target_pairs={{1,2},{2,1},{5,6},{6,5},{9,10},{10,9},{13,14},{14,13},{17,18},{18,... | collective-permute-start | bytes 1228808 | tf_op jit(solution)/shard_map/ppermute | solution.py:427
  52.1 13.8 %collective-permute-start.19 = (bf16[1,160,1408]{2,1,0:T(8,128)(2,1)S(1)}, bf16[1,160,1408]{2,1,0:T(8,128)(2,1)S(1)}, u32[]{:S(2)}, u32[]{:S(2)}) collective-permute-start(bf16[1,160,1408]{2,1,0:T(8,128)(2,1)S(1)} %get-tuple-element.31), channel_id=1, source_target_pairs={{0,1},{1,0},{2,3},{3,2},{4,5},{5,4},{6,7},{7,6},{8,9},{9,8},{10,11... | collective-permute-start | bytes 1351688 | tf_op jit(solution)/shard_map/ppermute | solution.py:463
  52.2 13.8 %collective-permute-start.20 = (bf16[1,160,1408]{2,1,0:T(8,128)(2,1)S(1)}, bf16[1,160,1408]{2,1,0:T(8,128)(2,1)S(1)}, u32[]{:S(2)}, u32[]{:S(2)}) collective-permute-start(bf16[1,160,1408]{2,1,0:T(8,128)(2,1)S(1)} %get-tuple-element.32), channel_id=1, source_target_pairs={{1,2},{2,1},{5,6},{6,5},{9,10},{10,9},{13,14},{14,13},{17,18},{18,... | collective-permute-start | bytes 1351688 | tf_op jit(solution)/shard_map/ppermute | solution.py:464
  55.0 27.8 %collective-permute-start = (bf16[1,160,2560]{2,1,0:T(8,128)(2,1)S(1)}, bf16[1,160,2560]{2,1,0:T(8,128)(2,1)S(1)}, u32[]{:S(2)}, u32[]{:S(2)}) collective-permute-start(bf16[1,160,2560]{2,1,0:T(8,128)(2,1)S(1)} %copy-done.2), channel_id=1, source_target_pairs={{24,0},{12,4},{0,8},{20,12},{8,16},{28,20},{16,24},{4,28},{25,1},{... | collective-permute-start | bytes 2457608 | tf_op jit(solution)/shard_map/ppermute | solution.py:418
  58.9 23.9 %collective-permute-start.7 = (bf16[1,160,2688]{2,1,0:T(8,128)(2,1)S(1)}, bf16[1,160,2688]{2,1,0:T(8,128)(2,1)S(1)}, u32[]{:S(2)}, u32[]{:S(2)}) collective-permute-start(bf16[1,160,2688]{2,1,0:T(8,128)(2,1)S(1)} %get-tuple-element.25), channel_id=1, source_target_pairs={{0,1},{1,0},{2,3},{3,2},{4,5},{5,4},{6,7},{7,6},{8,9},{9,8},{10,11... | collective-permute-start | bytes 2580488 | tf_op jit(solution)/shard_map/ppermute | solution.py:442
  58.9 25.1 %collective-permute-start.8 = (bf16[1,160,2688]{2,1,0:T(8,128)(2,1)S(1)}, bf16[1,160,2688]{2,1,0:T(8,128)(2,1)S(1)}, u32[]{:S(2)}, u32[]{:S(2)}) collective-permute-start(bf16[1,160,2688]{2,1,0:T(8,128)(2,1)S(1)} %get-tuple-element.26), channel_id=1, source_target_pairs={{1,2},{2,1},{5,6},{6,5},{9,10},{10,9},{13,14},{14,13},{17,18},{18,... | collective-permute-start | bytes 2580488 | tf_op jit(solution)/shard_map/ppermute | solution.py:443
  65.9 3.9 %collective-permute-start.13 = (bf16[1,160,1408]{2,1,0:T(8,128)(2,1)S(1)}, bf16[1,160,1408]{2,1,0:T(8,128)(2,1)S(1)}, u32[]{:S(2)}, u32[]{:S(2)}) collective-permute-start(bf16[1,160,1408]{2,1,0:T(8,128)(2,1)S(1)} %get-tuple-element.28), channel_id=1, source_target_pairs={{0,1},{1,0},{2,3},{3,2},{4,5},{5,4},{6,7},{7,6},{8,9},{9,8},{10,11... | collective-permute-start | bytes 1351688 | tf_op jit(solution)/shard_map/ppermute | solution.py:463
  66.0 12.2 %collective-permute-start.14 = (bf16[1,160,1408]{2,1,0:T(8,128)(2,1)S(1)}, bf16[1,160,1408]{2,1,0:T(8,128)(2,1)S(1)}, u32[]{:S(2)}, u32[]{:S(2)}) collective-permute-start(bf16[1,160,1408]{2,1,0:T(8,128)(2,1)S(1)} %get-tuple-element.29), channel_id=1, source_target_pairs={{1,2},{2,1},{5,6},{6,5},{9,10},{10,9},{13,14},{14,13},{17,18},{18,... | collective-permute-start | bytes 1351688 | tf_op jit(solution)/shard_map/ppermute | solution.py:464
  69.8 22.4 %collective-permute-start.21 = (bf16[1,160,1408]{2,1,0:T(8,128)(2,1)S(1)}, bf16[1,160,1408]{2,1,0:T(8,128)(2,1)S(1)}, u32[]{:S(2)}, u32[]{:S(2)}) collective-permute-start(bf16[1,160,1408]{2,1,0:T(8,128)(2,1)S(1)} %shard_map.53), channel_id=1, source_target_pairs={{0,4},{4,0},{8,12},{12,8},{16,20},{20,16},{24,28},{28,24},{1,5},{5... | collective-permute-start | bytes 1351688 | tf_op jit(solution)/shard_map/ppermute | solution.py:470
  79.4 13.0 %collective-permute-start.15 = (bf16[1,160,1408]{2,1,0:T(8,128)(2,1)S(1)}, bf16[1,160,1408]{2,1,0:T(8,128)(2,1)S(1)}, u32[]{:S(2)}, u32[]{:S(2)}) collective-permute-start(bf16[1,160,1408]{2,1,0:T(8,128)(2,1)S(1)} %shard_map.51), channel_id=1, source_target_pairs={{0,4},{4,0},{8,12},{12,8},{16,20},{20,16},{24,28},{28,24},{1,5},{5... | collective-permute-start | bytes 1351688 | tf_op jit(solution)/shard_map/ppermute | solution.py:470
  82.7 11.0 %collective-permute-start.24 = (bf16[1,160,1280]{2,1,0:T(8,128)(2,1)S(1)}, bf16[1,160,1280]{2,1,0:T(8,128)(2,1)S(1)}, u32[]{:S(2)}, u32[]{:S(2)}) collective-permute-start(bf16[1,160,1280]{2,1,0:T(8,128)(2,1)S(1)} %get-tuple-element.38), channel_id=1, source_target_pairs={{24,0},{12,4},{0,8},{20,12},{8,16},{28,20},{16,24},{4,28},{25,1},{... | collective-permute-start | bytes 1228808 | tf_op jit(solution)/shard_map/ppermute | solution.py:419
  82.8 13.1 %collective-permute-start.23 = (bf16[1,160,768]{2,1,0:T(8,128)(2,1)S(1)}, bf16[1,160,768]{2,1,0:T(8,128)(2,1)S(1)}, u32[]{:S(2)}, u32[]{:S(2)}) collective-permute-start(bf16[1,160,768]{2,1,0:T(8,128)(2,1)S(1)} %slice.23), channel_id=1, source_target_pairs={{24,0},{12,4},{0,8},{20,12},{8,16},{28,20},{16,24},{4,28},{25,1},{... | collective-permute-start | bytes 737288 | tf_op jit(solution)/shard_map/ppermute | solution.py:419
  84.0 13.6 %collective-permute-start.22 = (bf16[1,160,512]{2,1,0:T(8,128)(2,1)S(1)}, bf16[1,160,512]{2,1,0:T(8,128)(2,1)S(1)}, u32[]{:S(2)}, u32[]{:S(2)}) collective-permute-start(bf16[1,160,512]{2,1,0:T(8,128)(2,1)S(1)} %slice.22), channel_id=1, source_target_pairs={{24,0},{12,4},{0,8},{20,12},{8,16},{28,20},{16,24},{4,28},{25,1},{... | collective-permute-start | bytes 491528 | tf_op jit(solution)/shard_map/ppermute | solution.py:419

commit v6 on v5

--- a/solution.py
+++ b/solution.py
@@ -221,7 +221,7 @@
     )(band, *blocks)
 
 
-def score_kernel(rule, upright, band_ref, query_ref, *refs):
+def score_kernel(rule, band_ref, query_ref, *refs):
     keys, (weight_ref, table_ref, scratch) = refs[:-3], refs[-3:]
     bias = jnp.where(kept(rule, band_ref, None)[0], 0.0, NEG)
     places = [(key, n) for key in keys for n in range(key.shape[2] // HEAD)]
@@ -235,7 +235,7 @@
     for n in range(len(places)):
         later = score(n + 1) if n + 1 < len(places) else None
         (weights,), total, largest = softmax_rows(raw)
-        weight_ref[n] = weights.T if upright else weights
+        weight_ref[n] = weights.T
         scratch[0, n : n + 1, :] = largest * RATE + jnp.log2(total)
         scratch[1, n : n + 1, :] = 1.0 / total
         raw = later
@@ -243,11 +243,11 @@
     table_ref[1] = scratch[1].T
 
 
-def scored(band, query, keys, rule, upright):
+def scored(band, query, keys, rule):
     rows, width = query.shape[1:]
     heads = width // HEAD
     return pl.pallas_call(
-        functools.partial(score_kernel, rule, upright),
+        functools.partial(score_kernel, rule),
         in_specs=[SMEM] + [VMEM] * (1 + len(keys)),
         out_specs=[VMEM] * 2,
         out_shape=[
@@ -266,7 +266,8 @@
 
 def blend_kernel(shares_of, groups, heads, rule, band_ref, weight_ref, table_ref, *refs):
     values, refs = grouped(refs[: sum(shares_of)], shares_of), refs[sum(shares_of) :]
-    pieces, out_ref = refs[: sum(len(group) for group in groups)], refs[-2]
+    count = sum(len(group) for group in groups)
+    pieces, out_ref = refs[:count], refs[count]
     keeps = kept(rule, band_ref, None)
     rows = out_ref.shape[1]
     lane = lax.broadcasted_iota(jnp.int32, (rows, HEAD), 1)
@@ -290,7 +291,7 @@
     weights, log = shares(logs)
     coef = weights[0] * table_ref[1]
     if values:
-        refs[-1][...] = coef.T
+        own_table = packed(coef)
         out_ref[0, :, column(heads)] = log
     else:
         refs[-1][...] = packed(coef)
@@ -299,8 +300,12 @@
         out = 0.0
         if values:
             value, index = value_at[n]
-            summed = weighted(sum(ref[0, :, column(index)] for ref in value), weight_ref[n])
-            out = (summed * refs[-1][n : n + 1, :]).T
+            summed = jnp.dot(
+                weight_ref[n],
+                sum(ref[0, :, column(index)] for ref in value),
+                preferred_element_type=jnp.float32,
+            )
+            out = summed * spread(own_table, n)
         for table, place in zip(tables, places):
             piece, index = place[n]
             block = pieces[piece][0, :, column(index)].astype(jnp.float32)
@@ -325,7 +330,6 @@
         in_specs=[SMEM] + [VMEM] * (2 + len(flat) + len(pieces)),
         out_specs=[VMEM] if values else [VMEM, VMEM],
         out_shape=[out_shape] if values else [out_shape, coef],
-        scratch_shapes=[pltpu.VMEM((HEAD, rows), jnp.float32)] if values else [],
         compiler_params=GRANT,
         cost_estimate=pl.CostEstimate(
             flops=2 * rows * rows * width,
@@ -474,7 +478,6 @@
         queries,
         [key_one],
         lambda own, other, odd_frame, has_odd: [jnp.where(odd_frame, own[0], own[4]) >= 0],
-        False,
     )
     near = blended(
         band,
@@ -488,7 +491,6 @@
         queries,
         [key_two],
         lambda own, other, odd_frame, has_odd: [jnp.where(odd_frame, own[4], own[0]) >= 0],
-        True,
     )
     base, coef = blended(
         band,

time: 99.1 us -> 99.1 us (level)
  Pallas kernels: 26.5 us -> 24.5 us
  waiting for transfers between devices: 27.4 us -> 29.4 us
    ppermute x2, waiting for transfers between devices: 0.1 us -> 2.04 us  [per_device(): from_twin.append(lax.ppermute(whole, 'frame', twin))]
    pallas_call x2, Pallas kernels: 5.48 us -> 3.61 us  [blended(): pl.pallas_call(functools.partial(blend_kernel, shares_of, sizes, heads, r...]
  transfers between devices with their start and end apart: 25 -> 25, of which waited for: 6 -> 6; matrix products, arithmetic and copies ran while one was open for 0% -> 0% of each run, Pallas kernels for 26% -> 24%
where the time goes in v6:
time: 99.1 us; the launch traced here: 98.8 us
  starting transfers between devices  43 us (43%)
  waiting for transfers between devices  29.4 us (30%)
  Pallas kernels  24.5 us (25%)
  local copies, waits for them, and re-layouts  1.43 us (1%)
    ppermute x2, waiting for transfers between devices, per_device(): twin_odd = [lax.ppermute(query_twin[span], 'row', odd) for span in (0, 1)]  12.5 us
    pallas_call x3, Pallas kernels, parts(): pl.pallas_call(functools.partial(parts_kernel, len(queries), len(keys), s...  11.4 us
    ppermute x1, waiting for transfers between devices, per_device(): band_twin = lax.ppermute(band, 'frame', twin)  8.05 us
    ppermute x2, starting transfers between devices, per_device(): from_twin.append(lax.ppermute(whole, 'frame', twin))  6.67 us
    ppermute x1, starting transfers between devices, per_device(): lax.ppermute(value_halves[1], 'frame', beyond)  6.06 us
    ppermute x2, starting transfers between devices, per_device(): back_odd = lax.ppermute(odd_twin, 'row', odd)  5.37 us
    ppermute x2, starting transfers between devices, per_device(): twin_odd = [lax.ppermute(query_twin[span], 'row', odd) for span in (0, 1)]  5.32 us
    ppermute x2, waiting for transfers between devices, per_device(): back_odd = lax.ppermute(odd_twin, 'row', odd)  5 us
  transfers between devices with their start and end apart: 25, of which 6 were waited for; matrix products, arithmetic and copies ran while one was open for 0% of the time, Pallas kernels for 24%

profile of v6, /device:TPU:1, one launch (start us, length us, event | category | flops | bytes accessed | tf_op | source)
XLA Modules:
  0.0 98.8 jit_solution(7464068371651508572)
XLA Ops:
  0.0 1.3 %fusion = (bf16[1,160,1280]{2,1,0:T(8,128)(2,1)S(1)}, bf16[1,160,1280]{2,1,0:T(8,128)(2,1)S(1)}) fusion(bf16[1,160,2560]{2,1,0:T(8,128)(2,1)} %refs_4_.1), kind=kLoop, calls=%fused_computation | loop fusion | bytes 1638400 | tf_op jit(solution)/shard_map/slice | solution.py:426
  1.4 2.1 %collective-permute-start.16 = (bf16[1,160,1280]{2,1,0:T(8,128)(2,1)S(1)}, bf16[1,160,1280]{2,1,0:T(8,128)(2,1)S(1)}, u32[]{:S(2)}, u32[]{:S(2)}) collective-permute-start(bf16[1,160,1280]{2,1,0:T(8,128)(2,1)S(1)} %get-tuple-element.35), channel_id=1, source_target_pairs={{0,4},{4,0},{8,12},{12,8},{16,20},{20,16},{24,28},{28,24},{1,5},{5... | collective-permute-start | bytes 1228808 | tf_op jit(solution)/shard_map/ppermute | solution.py:426
  3.5 1.3 %collective-permute-start.3 = (bf16[1,160,1280]{2,1,0:T(8,128)(2,1)S(1)}, bf16[1,160,1280]{2,1,0:T(8,128)(2,1)S(1)}, u32[]{:S(2)}, u32[]{:S(2)}) collective-permute-start(bf16[1,160,1280]{2,1,0:T(8,128)(2,1)S(1)} %get-tuple-element.37), channel_id=1, source_target_pairs={{4,12},{8,0},{12,20},{16,8},{20,28},{24,16},{5,13},{9,1},{13,21},{... | collective-permute-start | bytes 1228808 | tf_op jit(solution)/shard_map/ppermute | solution.py:418
  4.8 6.1 %collective-permute-start.4 = (bf16[1,160,1280]{2,1,0:T(8,128)(2,1)S(1)}, bf16[1,160,1280]{2,1,0:T(8,128)(2,1)S(1)}, u32[]{:S(2)}, u32[]{:S(2)}) collective-permute-start(bf16[1,160,1280]{2,1,0:T(8,128)(2,1)S(1)} %get-tuple-element.37), channel_id=1, source_target_pairs={{0,24},{28,4},{1,25},{29,5},{2,26},{30,6},{3,27},{31,7}} | collective-permute-start | bytes 1228808 | tf_op jit(solution)/shard_map/ppermute | solution.py:419
  11.0 1.4 %collective-permute-start.9 = (s32[1,5]{1,0:T(1,128)S(1)}, s32[1,5]{1,0:T(1,128)S(1)}, u32[]{:S(2)}, u32[]{:S(2)}) collective-permute-start(s32[1,5]{1,0:T(1,128)S(1)} %copy-done.3), channel_id=1, source_target_pairs={{0,4},{4,0},{8,12},{12,8},{16,20},{20,16},{24,28},{28,24},{1,5},{5... | collective-permute-start | bytes 68 | tf_op jit(solution)/shard_map/ppermute | solution.py:427
  12.4 8.0 %collective-permute-done.9.refs_1_ = s32[1,5]{1,0:T(1,128)S(1)} collective-permute-done((s32[1,5]{1,0:T(1,128)S(1)}, s32[1,5]{1,0:T(1,128)S(1)}, u32[]{:S(2)}, u32[]{:S(2)}) %collective-permute-start.9) | collective-permute-done | bytes 52 | tf_op jit(solution)/shard_map/ppermute | solution.py:427
  20.5 4.2 %collective-permute-start.1 = (bf16[1,160,2560]{2,1,0:T(8,128)(2,1)S(1)}, bf16[1,160,2560]{2,1,0:T(8,128)(2,1)S(1)}, u32[]{:S(2)}, u32[]{:S(2)}) collective-permute-start(bf16[1,160,2560]{2,1,0:T(8,128)(2,1)S(1)} %copy-done.2), channel_id=1, source_target_pairs={{0,24},{4,12},{8,0},{12,20},{16,8},{20,28},{24,16},{28,4},{1,25},{... | collective-permute-start | bytes 2457608 | tf_op jit(solution)/shard_map/ppermute | solution.py:414
  24.7 1.9 %collective-permute-start.17 = (bf16[1,160,1280]{2,1,0:T(8,128)(2,1)S(1)}, bf16[1,160,1280]{2,1,0:T(8,128)(2,1)S(1)}, u32[]{:S(2)}, u32[]{:S(2)}) collective-permute-start(bf16[1,160,1280]{2,1,0:T(8,128)(2,1)S(1)} %collective-permute-done.16.refs_4_), channel_id=1, source_target_pairs={{0,1},{1,0},{2,3},{3,2},{4,5},{5,4},{6,7},{7,6},{8,9},{9,8},{10,11... | collective-permute-start | bytes 1228808 | tf_op jit(solution)/shard_map/ppermute | solution.py:430
  26.7 3.4 %collective-permute-start.6 = (bf16[1,160,2560]{2,1,0:T(8,128)(2,1)S(1)}, bf16[1,160,2560]{2,1,0:T(8,128)(2,1)S(1)}, u32[]{:S(2)}, u32[]{:S(2)}) collective-permute-start(bf16[1,160,2560]{2,1,0:T(8,128)(2,1)S(1)} %copy-done.1), channel_id=1, source_target_pairs={{1,2},{2,1},{5,6},{6,5},{9,10},{10,9},{13,14},{14,13},{17,18},{18,... | collective-permute-start | bytes 2457608 | tf_op jit(solution)/shard_map/ppermute | solution.py:429
  30.1 2.1 %collective-permute-start.18 = (bf16[1,160,1280]{2,1,0:T(8,128)(2,1)S(1)}, bf16[1,160,1280]{2,1,0:T(8,128)(2,1)S(1)}, u32[]{:S(2)}, u32[]{:S(2)}) collective-permute-start(bf16[1,160,1280]{2,1,0:T(8,128)(2,1)S(1)} %collective-permute-done.16.refs_4_), channel_id=1, source_target_pairs={{1,2},{2,1},{5,6},{6,5},{9,10},{10,9},{13,14},{14,13},{17,18},{18,... | collective-permute-start | bytes 1228808 | tf_op jit(solution)/shard_map/ppermute | solution.py:431
  32.5 12.5 %collective-permute-done.18.refs_3_ = bf16[1,160,1280]{2,1,0:T(8,128)(2,1)S(1)} collective-permute-done((bf16[1,160,1280]{2,1,0:T(8,128)(2,1)S(1)}, bf16[1,160,1280]{2,1,0:T(8,128)(2,1)S(1)}, u32[]{:S(2)}, u32[]{:S(2)}) %collective-permute-start.18) | collective-permute-done | bytes 409632 | tf_op jit(solution)/shard_map/ppermute | solution.py:431
  45.0 3.2 %collective-permute-start.12 = (bf16[1,160,1280]{2,1,0:T(8,128)(2,1)S(1)}, bf16[1,160,1280]{2,1,0:T(8,128)(2,1)S(1)}, u32[]{:S(2)}, u32[]{:S(2)}) collective-permute-start(bf16[1,160,1280]{2,1,0:T(8,128)(2,1)S(1)} %collective-permute-done.10.refs_4_), channel_id=1, source_target_pairs={{1,2},{2,1},{5,6},{6,5},{9,10},{10,9},{13,14},{14,13},{17,18},{18,... | collective-permute-start | bytes 1228808 | tf_op jit(solution)/shard_map/ppermute | solution.py:431
  48.2 3.9 %shard_map.52 = (bf16[1,160,1408]{2,1,0:T(8,128)(2,1)S(1)}, bf16[1,160,1408]{2,1,0:T(8,128)(2,1)S(1)}, f32[1,160,1408]{2,1,0:T(8,128)S(1)}) custom-call(s32[1,5]{1,0:T(1,128)S(1)} %copy-done.3, s32[1,5]{1,0:T(1,128)S(1)} %collective-permute-done.9.refs_1_, bf16[1,160,1280]{2,1,0:T(8,128)(2,1)S(1)} %collective-permute-done.17.refs_2_, ...), custom_call_target="tpu_custom_call" | custom-call | flops 786432000 | bytes 4096000 | tf_op jit(solution)/shard_map/pallas_call | solution.py:170
  52.2 2.7 %collective-permute-start.20 = (bf16[1,160,1408]{2,1,0:T(8,128)(2,1)S(1)}, bf16[1,160,1408]{2,1,0:T(8,128)(2,1)S(1)}, u32[]{:S(2)}, u32[]{:S(2)}) collective-permute-start(bf16[1,160,1408]{2,1,0:T(8,128)(2,1)S(1)} %get-tuple-element.32), channel_id=1, source_target_pairs={{1,2},{2,1},{5,6},{6,5},{9,10},{10,9},{13,14},{14,13},{17,18},{18,... | collective-permute-start | bytes 1351688 | tf_op jit(solution)/shard_map/ppermute | solution.py:468
  55.2 3.7 %shard_map.48 = (bf16[1,160,2688]{2,1,0:T(8,128)(2,1)S(1)}, bf16[1,160,2688]{2,1,0:T(8,128)(2,1)S(1)}, f32[1,160,2688]{2,1,0:T(8,128)S(1)}) custom-call(s32[1,5]{1,0:T(1,128)S(1)} %copy-done.3, s32[1,5]{1,0:T(1,128)S(1)} %copy-done.3, bf16[1,160,2560]{2,1,0:T(8,128)(2,1)S(1)} %collective-permute-done.5.refs_2_, ...), custom_call_target="tpu_custom_call" | custom-call | flops 786432000 | bytes 6553600 | tf_op jit(solution)/shard_map/pallas_call | solution.py:170
  58.9 3.1 %collective-permute-start.8 = (bf16[1,160,2688]{2,1,0:T(8,128)(2,1)S(1)}, bf16[1,160,2688]{2,1,0:T(8,128)(2,1)S(1)}, u32[]{:S(2)}, u32[]{:S(2)}) collective-permute-start(bf16[1,160,2688]{2,1,0:T(8,128)(2,1)S(1)} %get-tuple-element.26), channel_id=1, source_target_pairs={{1,2},{2,1},{5,6},{6,5},{9,10},{10,9},{13,14},{14,13},{17,18},{18,... | collective-permute-start | bytes 2580488 | tf_op jit(solution)/shard_map/ppermute | solution.py:447
  62.1 3.8 %shard_map.50 = (bf16[1,160,1408]{2,1,0:T(8,128)(2,1)S(1)}, bf16[1,160,1408]{2,1,0:T(8,128)(2,1)S(1)}, f32[1,160,1408]{2,1,0:T(8,128)S(1)}) custom-call(s32[1,5]{1,0:T(1,128)S(1)} %copy-done.3, s32[1,5]{1,0:T(1,128)S(1)} %collective-permute-done.9.refs_1_, bf16[1,160,1280]{2,1,0:T(8,128)(2,1)S(1)} %collective-permute-done.11.refs_2_, ...), custom_call_target="tpu_custom_call" | custom-call | flops 786432000 | bytes 4096000 | tf_op jit(solution)/shard_map/pallas_call | solution.py:170
  66.0 2.6 %collective-permute-start.14 = (bf16[1,160,1408]{2,1,0:T(8,128)(2,1)S(1)}, bf16[1,160,1408]{2,1,0:T(8,128)(2,1)S(1)}, u32[]{:S(2)}, u32[]{:S(2)}) collective-permute-start(bf16[1,160,1408]{2,1,0:T(8,128)(2,1)S(1)} %get-tuple-element.29), channel_id=1, source_target_pairs={{1,2},{2,1},{5,6},{6,5},{9,10},{10,9},{13,14},{14,13},{17,18},{18,... | collective-permute-start | bytes 1351688 | tf_op jit(solution)/shard_map/ppermute | solution.py:468
  68.6 1.2 %shard_map.53 = bf16[1,160,1408]{2,1,0:T(8,128)(2,1)S(1)} custom-call(s32[1,5]{1,0:T(1,128)S(1)} %copy-done.3, f32[1,160,1408]{2,1,0:T(8,128)S(1)} %get-tuple-element.30.refs_0_, bf16[1,160,1408]{2,1,0:T(8,128)(2,1)S(1)} %collective-permute-done.19.refs_1_, bf16[1,160,1408]{2,1,0:T(8,128)(2,1)S(1)} %collective-permute-done.20.refs_2_), custom_call_target="tpu_custom_call" | custom-call | flops 1351680 | bytes 1802240 | tf_op jit(solution)/shard_map/pallas_call | solution.py:210
  69.8 3.3 %collective-permute-start.21 = (bf16[1,160,1408]{2,1,0:T(8,128)(2,1)S(1)}, bf16[1,160,1408]{2,1,0:T(8,128)(2,1)S(1)}, u32[]{:S(2)}, u32[]{:S(2)}) collective-permute-start(bf16[1,160,1408]{2,1,0:T(8,128)(2,1)S(1)} %shard_map.53), channel_id=1, source_target_pairs={{0,4},{4,0},{8,12},{12,8},{16,20},{20,16},{24,28},{28,24},{1,5},{5... | collective-permute-start | bytes 1351688 | tf_op jit(solution)/shard_map/ppermute | solution.py:474
  73.2 5.0 %collective-permute-done.14.refs_2_ = bf16[1,160,1408]{2,1,0:T(8,128)(2,1)S(1)} collective-permute-done((bf16[1,160,1408]{2,1,0:T(8,128)(2,1)S(1)}, bf16[1,160,1408]{2,1,0:T(8,128)(2,1)S(1)}, u32[]{:S(2)}, u32[]{:S(2)}) %collective-permute-start.14) | collective-permute-done | bytes 450592 | tf_op jit(solution)/shard_map/ppermute | solution.py:468
  78.2 1.2 %shard_map.51 = bf16[1,160,1408]{2,1,0:T(8,128)(2,1)S(1)} custom-call(s32[1,5]{1,0:T(1,128)S(1)} %copy-done.3, f32[1,160,1408]{2,1,0:T(8,128)S(1)} %get-tuple-element.27.refs_0_, bf16[1,160,1408]{2,1,0:T(8,128)(2,1)S(1)} %collective-permute-done.13.refs_1_, bf16[1,160,1408]{2,1,0:T(8,128)(2,1)S(1)} %collective-permute-done.14.refs_2_), custom_call_target="tpu_custom_call" | custom-call | flops 1351680 | bytes 1802240 | tf_op jit(solution)/shard_map/pallas_call | solution.py:210
  79.4 3.3 %collective-permute-start.15 = (bf16[1,160,1408]{2,1,0:T(8,128)(2,1)S(1)}, bf16[1,160,1408]{2,1,0:T(8,128)(2,1)S(1)}, u32[]{:S(2)}, u32[]{:S(2)}) collective-permute-start(bf16[1,160,1408]{2,1,0:T(8,128)(2,1)S(1)} %shard_map.51), channel_id=1, source_target_pairs={{0,4},{4,0},{8,12},{12,8},{16,20},{20,16},{24,28},{28,24},{1,5},{5... | collective-permute-start | bytes 1351688 | tf_op jit(solution)/shard_map/ppermute | solution.py:474
  82.8 1.2 %collective-permute-start.23 = (bf16[1,160,768]{2,1,0:T(8,128)(2,1)S(1)}, bf16[1,160,768]{2,1,0:T(8,128)(2,1)S(1)}, u32[]{:S(2)}, u32[]{:S(2)}) collective-permute-start(bf16[1,160,768]{2,1,0:T(8,128)(2,1)S(1)} %slice.23), channel_id=1, source_target_pairs={{24,0},{12,4},{0,8},{20,12},{8,16},{28,20},{16,24},{4,28},{25,1},{... | collective-permute-start | bytes 737288 | tf_op jit(solution)/shard_map/ppermute | solution.py:423
  84.1 2.0 %shard_map.47 = (bf16[20,160,160]{2,1,0:T(8,128)(2,1)S(1)}, f32[2,160,128]{2,1,0:T(8,128)S(1)}) custom-call(s32[1,5]{1,0:T(1,128)S(1)} %copy-done.3, bf16[1,160,2560]{2,1,0:T(8,128)(2,1)S(1)} %copy-done.1, bf16[1,160,2560]{2,1,0:T(8,128)(2,1)S(1)} %collective-permute-done.1.refs_0_.refs_6_), custom_call_target="tpu_custom_call" | custom-call | flops 131072000 | bytes 2457600 | tf_op jit(solution)/shard_map/pallas_call | solution.py:249
  86.1 2.0 %shard_map.46 = (bf16[20,160,160]{2,1,0:T(8,128)(2,1)S(1)}, f32[2,160,128]{2,1,0:T(8,128)S(1)}) custom-call(s32[1,5]{1,0:T(1,128)S(1)} %copy-done.3, bf16[1,160,2560]{2,1,0:T(8,128)(2,1)S(1)} %copy-done.1, bf16[1,160,2560]{2,1,0:T(8,128)(2,1)S(1)} %collective-permute-done.refs_0_), custom_call_target="tpu_custom_call" | custom-call | flops 131072000 | bytes 2457600 | tf_op jit(solution)/shard_map/pallas_call | solution.py:249
  88.0 2.2 %shard_map.49.refs_0_ = f32[1,160,2688]{2,1,0:T(8,128)S(1)} custom-call(s32[1,5]{1,0:T(1,128)S(1)} %copy-done.3, bf16[20,160,160]{2,1,0:T(8,128)(2,1)S(1)} %get-tuple-element.22.weight_ref, f32[2,160,128]{2,1,0:T(8,128)S(1)} %get-tuple-element.23.table_ref, bf16[1,160,1280]{2,1,0:T(8,128)(2,1)S(1)} %collective-permute-done.2.refs_0_.refs_8_, ...), custom_call_target="tpu_custom_call" | custom-call | flops 131072000 | bytes 5734400 | tf_op jit(solution)/shard_map/pallas_call | solution.py:328
  90.3 2.0 %collective-permute-done.15.refs_1_ = bf16[1,160,1408]{2,1,0:T(8,128)(2,1)S(1)} collective-permute-done((bf16[1,160,1408]{2,1,0:T(8,128)(2,1)S(1)}, bf16[1,160,1408]{2,1,0:T(8,128)(2,1)S(1)}, u32[]{:S(2)}, u32[]{:S(2)}) %collective-permute-start.15) | collective-permute-done | bytes 450592 | tf_op jit(solution)/shard_map/ppermute | solution.py:474
  92.3 1.4 %shard_map.54 = (f32[1,160,2560]{2,1,0:T(8,128)S(1)}, bf16[160,128]{1,0:T(8,128)(2,1)S(1)}) custom-call(s32[1,5]{1,0:T(1,128)S(1)} %copy-done.3, f32[2,160,128]{2,1,0:T(8,128)S(1)} %get-tuple-element.21.weight_ref.table_ref, f32[2,160,128]{2,1,0:T(8,128)S(1)} %get-tuple-element.21.weight_ref.table_ref, f32[1,160,2688]{2,1,0:T(8,128)S(1)} %shard_map.49.refs_0_, ...), custom_call_target="tpu_custom_call" | custom-call | flops 131072000 | bytes 5734400 | tf_op jit(solution)/shard_map/pallas_call | solution.py:328
  93.7 1.2 %shard_map.55.refs_0_ = bf16[1,160,2560]{2,1,0:T(8,128)(2,1)} custom-call(bf16[20,160,160]{2,1,0:T(8,128)(2,1)S(1)} %get-tuple-element.20.weight_ref, bf16[160,128]{1,0:T(8,128)(2,1)S(1)} %get-tuple-element.33.coef_ref, bf16[1,160,1280]{2,1,0:T(8,128)(2,1)S(1)} %collective-permute-done.24.value_ref, f32[1,160,2560]{2,1,0:T(8,128)S(1)} %get-tuple-element.34.base_ref), custom_call_target="tpu_custom_call" | custom-call | flops 65536000 | bytes 1638400 | tf_op jit(solution)/shard_map/pallas_call | solution.py:371
  94.9 1.0 collective-permute-done.23.value_ref
  95.9 1.0 %shard_map.56.refs_0_ = bf16[1,160,2560]{2,1,0:T(8,128)(2,1)} custom-call(bf16[20,160,160]{2,1,0:T(8,128)(2,1)S(1)} %get-tuple-element.20.weight_ref, bf16[160,128]{1,0:T(8,128)(2,1)S(1)} %get-tuple-element.33.coef_ref, bf16[1,160,768]{2,1,0:T(8,128)(2,1)S(1)} %collective-permute-done.23.value_ref, ...), custom_call_target="tpu_custom_call", output_to_operand_aliasing={{}: (4, {})} | custom-call | flops 39321600 | bytes 983040 | tf_op jit(solution)/shard_map/pallas_call | solution.py:371
  (42 shorter events, 2.7 us)
Async XLA Ops:
  0.0 26.6 %copy-start.1 = (bf16[1,160,2560]{2,1,0:T(8,128)(2,1)S(1)}, bf16[1,160,2560]{2,1,0:T(8,128)(2,1)}, u32[]{:S(2)}) copy-start(bf16[1,160,2560]{2,1,0:T(8,128)(2,1)} %refs_4_.1) | copy-start | bytes 2457604
  0.0 3.5 %copy-start = (bf16[1,160,2560]{2,1,0:T(8,128)(2,1)S(1)}, bf16[1,160,2560]{2,1,0:T(8,128)(2,1)}, u32[]{:S(2)}) copy-start(bf16[1,160,2560]{2,1,0:T(8,128)(2,1)} %refs_7_.3) | copy-start | bytes 2457604
  0.0 11.0 %copy-start.3 = (s32[1,5]{1,0:T(1,128)S(1)}, s32[1,5]{1,0:T(1,128)}, u32[]{:S(2)}) copy-start(s32[1,5]{1,0:T(1,128)} %band_ref.11) | copy-start | bytes 64
  0.0 20.5 %copy-start.2 = (bf16[1,160,2560]{2,1,0:T(8,128)(2,1)S(1)}, bf16[1,160,2560]{2,1,0:T(8,128)(2,1)}, u32[]{:S(2)}) copy-start(bf16[1,160,2560]{2,1,0:T(8,128)(2,1)} %refs_5_.5) | copy-start | bytes 2457604
  1.4 23.4 %collective-permute-start.16 = (bf16[1,160,1280]{2,1,0:T(8,128)(2,1)S(1)}, bf16[1,160,1280]{2,1,0:T(8,128)(2,1)S(1)}, u32[]{:S(2)}, u32[]{:S(2)}) collective-permute-start(bf16[1,160,1280]{2,1,0:T(8,128)(2,1)S(1)} %get-tuple-element.35), channel_id=1, source_target_pairs={{0,4},{4,0},{8,12},{12,8},{16,20},{20,16},{24,28},{28,24},{1,5},{5... | collective-permute-start | bytes 1228808 | tf_op jit(solution)/shard_map/ppermute | solution.py:426
  3.5 23.1 %collective-permute-start.3 = (bf16[1,160,1280]{2,1,0:T(8,128)(2,1)S(1)}, bf16[1,160,1280]{2,1,0:T(8,128)(2,1)S(1)}, u32[]{:S(2)}, u32[]{:S(2)}) collective-permute-start(bf16[1,160,1280]{2,1,0:T(8,128)(2,1)S(1)} %get-tuple-element.37), channel_id=1, source_target_pairs={{4,12},{8,0},{12,20},{16,8},{20,28},{24,16},{5,13},{9,1},{13,21},{... | collective-permute-start | bytes 1228808 | tf_op jit(solution)/shard_map/ppermute | solution.py:418
  4.8 21.9 %collective-permute-start.4 = (bf16[1,160,1280]{2,1,0:T(8,128)(2,1)S(1)}, bf16[1,160,1280]{2,1,0:T(8,128)(2,1)S(1)}, u32[]{:S(2)}, u32[]{:S(2)}) collective-permute-start(bf16[1,160,1280]{2,1,0:T(8,128)(2,1)S(1)} %get-tuple-element.37), channel_id=1, source_target_pairs={{0,24},{28,4},{1,25},{29,5},{2,26},{30,6},{3,27},{31,7}} | collective-permute-start | bytes 1228808 | tf_op jit(solution)/shard_map/ppermute | solution.py:419
  10.9 19.2 %collective-permute-start.10 = (bf16[1,160,1280]{2,1,0:T(8,128)(2,1)S(1)}, bf16[1,160,1280]{2,1,0:T(8,128)(2,1)S(1)}, u32[]{:S(2)}, u32[]{:S(2)}) collective-permute-start(bf16[1,160,1280]{2,1,0:T(8,128)(2,1)S(1)} %get-tuple-element.36), channel_id=1, source_target_pairs={{0,4},{4,0},{8,12},{12,8},{16,20},{20,16},{24,28},{28,24},{1,5},{5... | collective-permute-start | bytes 1228808 | tf_op jit(solution)/shard_map/ppermute | solution.py:426
  11.0 9.5 %collective-permute-start.9 = (s32[1,5]{1,0:T(1,128)S(1)}, s32[1,5]{1,0:T(1,128)S(1)}, u32[]{:S(2)}, u32[]{:S(2)}) collective-permute-start(s32[1,5]{1,0:T(1,128)S(1)} %copy-done.3), channel_id=1, source_target_pairs={{0,4},{4,0},{8,12},{12,8},{16,20},{20,16},{24,28},{28,24},{1,5},{5... | collective-permute-start | bytes 68 | tf_op jit(solution)/shard_map/ppermute | solution.py:427
  20.5 24.5 %collective-permute-start.1 = (bf16[1,160,2560]{2,1,0:T(8,128)(2,1)S(1)}, bf16[1,160,2560]{2,1,0:T(8,128)(2,1)S(1)}, u32[]{:S(2)}, u32[]{:S(2)}) collective-permute-start(bf16[1,160,2560]{2,1,0:T(8,128)(2,1)S(1)} %copy-done.2), channel_id=1, source_target_pairs={{0,24},{4,12},{8,0},{12,20},{16,8},{20,28},{24,16},{28,4},{1,25},{... | collective-permute-start | bytes 2457608 | tf_op jit(solution)/shard_map/ppermute | solution.py:414
  24.7 7.6 %collective-permute-start.17 = (bf16[1,160,1280]{2,1,0:T(8,128)(2,1)S(1)}, bf16[1,160,1280]{2,1,0:T(8,128)(2,1)S(1)}, u32[]{:S(2)}, u32[]{:S(2)}) collective-permute-start(bf16[1,160,1280]{2,1,0:T(8,128)(2,1)S(1)} %collective-permute-done.16.refs_4_), channel_id=1, source_target_pairs={{0,1},{1,0},{2,3},{3,2},{4,5},{5,4},{6,7},{7,6},{8,9},{9,8},{10,11... | collective-permute-start | bytes 1228808 | tf_op jit(solution)/shard_map/ppermute | solution.py:430
  26.6 25.6 %collective-permute-start.5 = (bf16[1,160,2560]{2,1,0:T(8,128)(2,1)S(1)}, bf16[1,160,2560]{2,1,0:T(8,128)(2,1)S(1)}, u32[]{:S(2)}, u32[]{:S(2)}) collective-permute-start(bf16[1,160,2560]{2,1,0:T(8,128)(2,1)S(1)} %copy-done.1), channel_id=1, source_target_pairs={{0,1},{1,0},{2,3},{3,2},{4,5},{5,4},{6,7},{7,6},{8,9},{9,8},{10,11... | collective-permute-start | bytes 2457608 | tf_op jit(solution)/shard_map/ppermute | solution.py:428
  26.7 28.3 %collective-permute-start.6 = (bf16[1,160,2560]{2,1,0:T(8,128)(2,1)S(1)}, bf16[1,160,2560]{2,1,0:T(8,128)(2,1)S(1)}, u32[]{:S(2)}, u32[]{:S(2)}) collective-permute-start(bf16[1,160,2560]{2,1,0:T(8,128)(2,1)S(1)} %copy-done.1), channel_id=1, source_target_pairs={{1,2},{2,1},{5,6},{6,5},{9,10},{10,9},{13,14},{14,13},{17,18},{18,... | collective-permute-start | bytes 2457608 | tf_op jit(solution)/shard_map/ppermute | solution.py:429
  30.1 14.9 %collective-permute-start.18 = (bf16[1,160,1280]{2,1,0:T(8,128)(2,1)S(1)}, bf16[1,160,1280]{2,1,0:T(8,128)(2,1)S(1)}, u32[]{:S(2)}, u32[]{:S(2)}) collective-permute-start(bf16[1,160,1280]{2,1,0:T(8,128)(2,1)S(1)} %collective-permute-done.16.refs_4_), channel_id=1, source_target_pairs={{1,2},{2,1},{5,6},{6,5},{9,10},{10,9},{13,14},{14,13},{17,18},{18,... | collective-permute-start | bytes 1228808 | tf_op jit(solution)/shard_map/ppermute | solution.py:431
  32.3 19.8 %collective-permute-start.2 = (bf16[1,160,1280]{2,1,0:T(8,128)(2,1)S(1)}, bf16[1,160,1280]{2,1,0:T(8,128)(2,1)S(1)}, u32[]{:S(2)}, u32[]{:S(2)}) collective-permute-start(bf16[1,160,1280]{2,1,0:T(8,128)(2,1)S(1)} %get-tuple-element.38), channel_id=1, source_target_pairs={{0,24},{4,12},{8,0},{12,20},{16,8},{20,28},{24,16},{28,4},{1,25},{... | collective-permute-start | bytes 1228808 | tf_op jit(solution)/shard_map/ppermute | solution.py:416
  45.0 13.8 %collective-permute-start.11 = (bf16[1,160,1280]{2,1,0:T(8,128)(2,1)S(1)}, bf16[1,160,1280]{2,1,0:T(8,128)(2,1)S(1)}, u32[]{:S(2)}, u32[]{:S(2)}) collective-permute-start(bf16[1,160,1280]{2,1,0:T(8,128)(2,1)S(1)} %collective-permute-done.10.refs_4_), channel_id=1, source_target_pairs={{0,1},{1,0},{2,3},{3,2},{4,5},{5,4},{6,7},{7,6},{8,9},{9,8},{10,11... | collective-permute-start | bytes 1228808 | tf_op jit(solution)/shard_map/ppermute | solution.py:430
  45.0 13.9 %collective-permute-start.12 = (bf16[1,160,1280]{2,1,0:T(8,128)(2,1)S(1)}, bf16[1,160,1280]{2,1,0:T(8,128)(2,1)S(1)}, u32[]{:S(2)}, u32[]{:S(2)}) collective-permute-start(bf16[1,160,1280]{2,1,0:T(8,128)(2,1)S(1)} %collective-permute-done.10.refs_4_), channel_id=1, source_target_pairs={{1,2},{2,1},{5,6},{6,5},{9,10},{10,9},{13,14},{14,13},{17,18},{18,... | collective-permute-start | bytes 1228808 | tf_op jit(solution)/shard_map/ppermute | solution.py:431
  52.1 13.8 %collective-permute-start.19 = (bf16[1,160,1408]{2,1,0:T(8,128)(2,1)S(1)}, bf16[1,160,1408]{2,1,0:T(8,128)(2,1)S(1)}, u32[]{:S(2)}, u32[]{:S(2)}) collective-permute-start(bf16[1,160,1408]{2,1,0:T(8,128)(2,1)S(1)} %get-tuple-element.31), channel_id=1, source_target_pairs={{0,1},{1,0},{2,3},{3,2},{4,5},{5,4},{6,7},{7,6},{8,9},{9,8},{10,11... | collective-permute-start | bytes 1351688 | tf_op jit(solution)/shard_map/ppermute | solution.py:467
  52.2 13.8 %collective-permute-start.20 = (bf16[1,160,1408]{2,1,0:T(8,128)(2,1)S(1)}, bf16[1,160,1408]{2,1,0:T(8,128)(2,1)S(1)}, u32[]{:S(2)}, u32[]{:S(2)}) collective-permute-start(bf16[1,160,1408]{2,1,0:T(8,128)(2,1)S(1)} %get-tuple-element.32), channel_id=1, source_target_pairs={{1,2},{2,1},{5,6},{6,5},{9,10},{10,9},{13,14},{14,13},{17,18},{18,... | collective-permute-start | bytes 1351688 | tf_op jit(solution)/shard_map/ppermute | solution.py:468
  55.0 27.8 %collective-permute-start = (bf16[1,160,2560]{2,1,0:T(8,128)(2,1)S(1)}, bf16[1,160,2560]{2,1,0:T(8,128)(2,1)S(1)}, u32[]{:S(2)}, u32[]{:S(2)}) collective-permute-start(bf16[1,160,2560]{2,1,0:T(8,128)(2,1)S(1)} %copy-done.2), channel_id=1, source_target_pairs={{24,0},{12,4},{0,8},{20,12},{8,16},{28,20},{16,24},{4,28},{25,1},{... | collective-permute-start | bytes 2457608 | tf_op jit(solution)/shard_map/ppermute | solution.py:422
  58.9 23.9 %collective-permute-start.7 = (bf16[1,160,2688]{2,1,0:T(8,128)(2,1)S(1)}, bf16[1,160,2688]{2,1,0:T(8,128)(2,1)S(1)}, u32[]{:S(2)}, u32[]{:S(2)}) collective-permute-start(bf16[1,160,2688]{2,1,0:T(8,128)(2,1)S(1)} %get-tuple-element.25), channel_id=1, source_target_pairs={{0,1},{1,0},{2,3},{3,2},{4,5},{5,4},{6,7},{7,6},{8,9},{9,8},{10,11... | collective-permute-start | bytes 2580488 | tf_op jit(solution)/shard_map/ppermute | solution.py:446
  58.9 25.1 %collective-permute-start.8 = (bf16[1,160,2688]{2,1,0:T(8,128)(2,1)S(1)}, bf16[1,160,2688]{2,1,0:T(8,128)(2,1)S(1)}, u32[]{:S(2)}, u32[]{:S(2)}) collective-permute-start(bf16[1,160,2688]{2,1,0:T(8,128)(2,1)S(1)} %get-tuple-element.26), channel_id=1, source_target_pairs={{1,2},{2,1},{5,6},{6,5},{9,10},{10,9},{13,14},{14,13},{17,18},{18,... | collective-permute-start | bytes 2580488 | tf_op jit(solution)/shard_map/ppermute | solution.py:447
  65.9 3.9 %collective-permute-start.13 = (bf16[1,160,1408]{2,1,0:T(8,128)(2,1)S(1)}, bf16[1,160,1408]{2,1,0:T(8,128)(2,1)S(1)}, u32[]{:S(2)}, u32[]{:S(2)}) collective-permute-start(bf16[1,160,1408]{2,1,0:T(8,128)(2,1)S(1)} %get-tuple-element.28), channel_id=1, source_target_pairs={{0,1},{1,0},{2,3},{3,2},{4,5},{5,4},{6,7},{7,6},{8,9},{9,8},{10,11... | collective-permute-start | bytes 1351688 | tf_op jit(solution)/shard_map/ppermute | solution.py:467
  66.0 12.2 %collective-permute-start.14 = (bf16[1,160,1408]{2,1,0:T(8,128)(2,1)S(1)}, bf16[1,160,1408]{2,1,0:T(8,128)(2,1)S(1)}, u32[]{:S(2)}, u32[]{:S(2)}) collective-permute-start(bf16[1,160,1408]{2,1,0:T(8,128)(2,1)S(1)} %get-tuple-element.29), channel_id=1, source_target_pairs={{1,2},{2,1},{5,6},{6,5},{9,10},{10,9},{13,14},{14,13},{17,18},{18,... | collective-permute-start | bytes 1351688 | tf_op jit(solution)/shard_map/ppermute | solution.py:468
  69.8 20.5 %collective-permute-start.21 = (bf16[1,160,1408]{2,1,0:T(8,128)(2,1)S(1)}, bf16[1,160,1408]{2,1,0:T(8,128)(2,1)S(1)}, u32[]{:S(2)}, u32[]{:S(2)}) collective-permute-start(bf16[1,160,1408]{2,1,0:T(8,128)(2,1)S(1)} %shard_map.53), channel_id=1, source_target_pairs={{0,4},{4,0},{8,12},{12,8},{16,20},{20,16},{24,28},{28,24},{1,5},{5... | collective-permute-start | bytes 1351688 | tf_op jit(solution)/shard_map/ppermute | solution.py:474
  79.4 13.0 %collective-permute-start.15 = (bf16[1,160,1408]{2,1,0:T(8,128)(2,1)S(1)}, bf16[1,160,1408]{2,1,0:T(8,128)(2,1)S(1)}, u32[]{:S(2)}, u32[]{:S(2)}) collective-permute-start(bf16[1,160,1408]{2,1,0:T(8,128)(2,1)S(1)} %shard_map.51), channel_id=1, source_target_pairs={{0,4},{4,0},{8,12},{12,8},{16,20},{20,16},{24,28},{28,24},{1,5},{5... | collective-permute-start | bytes 1351688 | tf_op jit(solution)/shard_map/ppermute | solution.py:474
  82.7 11.0 %collective-permute-start.24 = (bf16[1,160,1280]{2,1,0:T(8,128)(2,1)S(1)}, bf16[1,160,1280]{2,1,0:T(8,128)(2,1)S(1)}, u32[]{:S(2)}, u32[]{:S(2)}) collective-permute-start(bf16[1,160,1280]{2,1,0:T(8,128)(2,1)S(1)} %get-tuple-element.38), channel_id=1, source_target_pairs={{24,0},{12,4},{0,8},{20,12},{8,16},{28,20},{16,24},{4,28},{25,1},{... | collective-permute-start | bytes 1228808 | tf_op jit(solution)/shard_map/ppermute | solution.py:423
  82.8 13.1 %collective-permute-start.23 = (bf16[1,160,768]{2,1,0:T(8,128)(2,1)S(1)}, bf16[1,160,768]{2,1,0:T(8,128)(2,1)S(1)}, u32[]{:S(2)}, u32[]{:S(2)}) collective-permute-start(bf16[1,160,768]{2,1,0:T(8,128)(2,1)S(1)} %slice.23), channel_id=1, source_target_pairs={{24,0},{12,4},{0,8},{20,12},{8,16},{28,20},{16,24},{4,28},{25,1},{... | collective-permute-start | bytes 737288 | tf_op jit(solution)/shard_map/ppermute | solution.py:423
  84.0 13.6 %collective-permute-start.22 = (bf16[1,160,512]{2,1,0:T(8,128)(2,1)S(1)}, bf16[1,160,512]{2,1,0:T(8,128)(2,1)S(1)}, u32[]{:S(2)}, u32[]{:S(2)}) collective-permute-start(bf16[1,160,512]{2,1,0:T(8,128)(2,1)S(1)} %slice.22), channel_id=1, source_target_pairs={{24,0},{12,4},{0,8},{20,12},{8,16},{28,20},{16,24},{4,28},{25,1},{... | collective-permute-start | bytes 491528 | tf_op jit(solution)/shard_map/ppermute | solution.py:423

commit v7 on v6

--- a/solution.py
+++ b/solution.py
@@ -221,21 +221,25 @@
     )(band, *blocks)
 
 
-def score_kernel(rule, band_ref, query_ref, *refs):
+def score_kernel(heads, rule, band_ref, query_ref, *refs):
     keys, (weight_ref, table_ref, scratch) = refs[:-3], refs[-3:]
-    bias = jnp.where(kept(rule, band_ref, None)[0], 0.0, NEG)
-    places = [(key, n) for key in keys for n in range(key.shape[2] // HEAD)]
+    biases = [
+        None if keep is True else jnp.where(keep, 0.0, NEG)
+        for keep in kept(rule, band_ref, None)
+    ]
     scratch[...] = jnp.zeros(scratch.shape, jnp.float32)
 
-    def score(at):
-        key, n = places[at]
-        return [raw_scores(key[0, :, column(n)], query_ref[0, :, column(at)]) + bias]
+    def score(n):
+        cols = column(n)
+        parts = [raw_scores(key[0, :, cols], query_ref[0, :, cols]) for key in keys]
+        return [part if bias is None else part + bias for part, bias in zip(parts, biases)]
 
     raw = score(0)
-    for n in range(len(places)):
-        later = score(n + 1) if n + 1 < len(places) else None
-        (weights,), total, largest = softmax_rows(raw)
-        weight_ref[n] = weights.T
+    for n in range(heads):
+        later = score(n + 1) if n + 1 < heads else None
+        weights, total, largest = softmax_rows(raw)
+        for at, weight in enumerate(weights):
+            weight_ref[at, n] = weight.T
         scratch[0, n : n + 1, :] = largest * RATE + jnp.log2(total)
         scratch[1, n : n + 1, :] = 1.0 / total
         raw = later
@@ -247,97 +251,108 @@
     rows, width = query.shape[1:]
     heads = width // HEAD
     return pl.pallas_call(
-        functools.partial(score_kernel, rule),
+        functools.partial(score_kernel, heads, rule),
         in_specs=[SMEM] + [VMEM] * (1 + len(keys)),
         out_specs=[VMEM] * 2,
         out_shape=[
-            jax.ShapeDtypeStruct((heads, rows, rows), jnp.bfloat16),
+            jax.ShapeDtypeStruct((len(keys), heads, rows, rows), jnp.bfloat16),
             jax.ShapeDtypeStruct((2, rows, HEAD), jnp.float32),
         ],
         scratch_shapes=[pltpu.VMEM((2, HEAD, rows), jnp.float32)],
         compiler_params=GRANT,
         cost_estimate=pl.CostEstimate(
-            flops=2 * rows * rows * width,
+            flops=2 * rows * rows * width * len(keys),
             bytes_accessed=6 * rows * width,
-            transcendentals=rows * rows * heads,
+            transcendentals=rows * rows * heads * len(keys),
         ),
     )(band, query, *keys)
 
 
-def blend_kernel(shares_of, groups, heads, rule, band_ref, weight_ref, table_ref, *refs):
-    values, refs = grouped(refs[: sum(shares_of)], shares_of), refs[sum(shares_of) :]
-    count = sum(len(group) for group in groups)
-    pieces, out_ref = refs[:count], refs[count]
-    keeps = kept(rule, band_ref, None)
-    rows = out_ref.shape[1]
-    lane = lax.broadcasted_iota(jnp.int32, (rows, HEAD), 1)
-    value_at = [(value, n) for value in values for n in range(value[0].shape[2] // HEAD)]
-    logs = [table_ref[0]]
-    places = []
-    at = 0
-    for keep, group in zip(keeps, groups):
-        log = None
-        place = []
-        for size in group:
-            part = read_log(pieces[at], size)
-            if log is None:
-                log = part
-            else:
-                log = jnp.where(lane >= len(place), pltpu.roll(part, len(place), 1), log)
-            place += [(at, n) for n in range(size)]
-            at += 1
-        logs.append(log if keep is True else jnp.where(keep, log, NEG))
-        places.append(place)
-    weights, log = shares(logs)
-    coef = weights[0] * table_ref[1]
-    if values:
-        own_table = packed(coef)
-        out_ref[0, :, column(heads)] = log
-    else:
-        refs[-1][...] = packed(coef)
-    tables = [packed(weight) for weight in weights[1:]]
+def near_kernel(shares_of, sources, heads, weight_ref, table_ref, *refs):
+    pieces, out_ref = grouped(refs[:-1], shares_of), refs[-1]
+    table = packed(table_ref[1])
     for n in range(heads):
-        out = 0.0
-        if values:
-            value, index = value_at[n]
-            summed = jnp.dot(
-                weight_ref[n],
-                sum(ref[0, :, column(index)] for ref in value),
-                preferred_element_type=jnp.float32,
+        summed = 0.0
+        for at, source in enumerate(sources):
+            piece, index = source[n]
+            value = sum(ref[0, :, column(index)] for ref in pieces[piece])
+            summed = summed + jnp.dot(
+                weight_ref[at, n], value, preferred_element_type=jnp.float32
             )
-            out = summed * spread(own_table, n)
-        for table, place in zip(tables, places):
-            piece, index = place[n]
-            block = pieces[piece][0, :, column(index)].astype(jnp.float32)
-            out = out + spread(table, n) * block
-        out_ref[0, :, column(n)] = out
-
-
-def blended(band, score, values, groups, rule):
+        out_ref[0, :, column(n)] = summed * spread(table, n)
+    out_ref[0, :, column(heads)] = table_ref[0]
+
+
+def neared(score, values):
     weights, table = score
-    heads, rows = weights.shape[:2]
+    heads, rows = weights.shape[1:3]
+    sources, pieces = [], []
+    for value in values:
+        source = []
+        for piece in value:
+            size = piece[0].shape[2] // HEAD
+            source += [(len(pieces), n) for n in range(size)]
+            pieces.append(piece)
+        sources.append(tuple(source))
+    flat = [ref for piece in pieces for ref in piece]
     width = heads * HEAD
-    sizes = tuple(tuple(piece.shape[2] // HEAD - 1 for piece in group) for group in groups)
-    pieces = [piece for group in groups for piece in group]
-    out_shape = jax.ShapeDtypeStruct((1, rows, width + (HEAD if values else 0)), jnp.float32)
-    coef = jax.ShapeDtypeStruct((rows, HEAD), jnp.bfloat16)
-    shares_of = tuple(len(value) for value in values)
-    flat = [piece for value in values for piece in value]
-    if not values:
-        weights = table
-    out = pl.pallas_call(
-        functools.partial(blend_kernel, shares_of, sizes, heads, rule),
-        in_specs=[SMEM] + [VMEM] * (2 + len(flat) + len(pieces)),
-        out_specs=[VMEM] if values else [VMEM, VMEM],
-        out_shape=[out_shape] if values else [out_shape, coef],
+    return pl.pallas_call(
+        functools.partial(
+            near_kernel, tuple(len(piece) for piece in pieces), tuple(sources), heads
+        ),
+        in_specs=[VMEM] * (2 + len(flat)),
+        out_specs=VMEM,
+        out_shape=jax.ShapeDtypeStruct((1, rows, width + HEAD), jnp.float32),
         compiler_params=GRANT,
         cost_estimate=pl.CostEstimate(
-            flops=2 * rows * rows * width,
-            bytes_accessed=2 * rows * width * (len(pieces) + 4),
+            flops=2 * rows * rows * width * len(values),
+            bytes_accessed=2 * rows * width * (len(values) + 4),
             transcendentals=0,
         ),
-    )(band, weights, table, *flat, *pieces)
-    return out[0] if values else out
+    )(weights, table, *flat)
+
+
+def base_kernel(sizes, heads, table_ref, near_ref, *refs):
+    pieces, (out_ref, coef_ref) = refs[: len(sizes)], refs[len(sizes) :]
+    lane = lax.broadcasted_iota(jnp.int32, (out_ref.shape[1], HEAD), 1)
+    log, place = None, []
+    for at, (piece, size) in enumerate(zip(pieces, sizes)):
+        part = read_log(piece, size)
+        if at:
+            part = jnp.where(lane >= len(place), pltpu.roll(part, len(place), 1), log)
+        log = part
+        place += [(at, n) for n in range(size)]
+    weights, _ = shares([table_ref[0], read_log(near_ref, heads), log])
+    coef_ref[...] = packed(weights[0] * table_ref[1])
+    near_table, twin_table = packed(weights[1]), packed(weights[2])
+    for n in range(heads):
+        piece, index = place[n]
+        block = pieces[piece][0, :, column(index)].astype(jnp.float32)
+        out_ref[0, :, column(n)] = (
+            spread(near_table, n) * near_ref[0, :, column(n)] + spread(twin_table, n) * block
+        )
+
+
+def based(score, near, pieces):
+    table = score[1]
+    rows = near.shape[1]
+    heads = near.shape[2] // HEAD - 1
+    sizes = tuple(piece.shape[2] // HEAD - 1 for piece in pieces)
+    return pl.pallas_call(
+        functools.partial(base_kernel, sizes, heads),
+        in_specs=[VMEM] * (2 + len(pieces)),
+        out_specs=[VMEM, VMEM],
+        out_shape=[
+            jax.ShapeDtypeStruct((1, rows, heads * HEAD), jnp.float32),
+            jax.ShapeDtypeStruct((rows, HEAD), jnp.bfloat16),
+        ],
+        compiler_params=GRANT,
+        cost_estimate=pl.CostEstimate(
+            flops=4 * rows * heads * HEAD,
+            bytes_accessed=12 * rows * heads * HEAD,
+            transcendentals=0,
+        ),
+    )(table, near, *pieces)
 
 
 def final_kernel(first, heads, weight_ref, coef_ref, value_ref, base_ref, *refs):
@@ -346,7 +361,7 @@
     for n in range(heads):
         cols = column(first + n)
         summed = jnp.dot(
-            weight_ref[first + n],
+            weight_ref[0, first + n],
             value_ref[0, :, column(n)],
             preferred_element_type=jnp.float32,
         )
@@ -425,26 +440,12 @@
     for cut in cuts:
         query_twin.append(lax.ppermute(queries[:, :, cut], "frame", twin))
     band_twin = lax.ppermute(band, "frame", twin)
-    query_even = lax.ppermute(queries, "row", even)
-    query_odd = lax.ppermute(queries, "row", odd)
+    key_even = lax.ppermute(keys, "row", even)
+    key_odd = lax.ppermute(keys, "row", odd)
+    value_even = lax.ppermute(values, "row", even)
+    value_odd = lax.ppermute(values, "row", odd)
     twin_even = [lax.ppermute(query_twin[span], "row", even) for span in (0, 1)]
     twin_odd = [lax.ppermute(query_twin[span], "row", odd) for span in (0, 1)]
-
-    def beside_rule(own, other, odd_frame, has_odd):
-        return [[own[2] >= 1], [own[2] >= 1], [True]]
-
-    even_part, odd_part, own_part = parts(
-        (band, band),
-        [query_even, query_odd, queries],
-        [keys],
-        [(values,)],
-        beside_rule,
-        (narrow, narrow, full),
-        0,
-        heads,
-    )
-    from_even = lax.ppermute(even_part, "row", even)
-    from_odd = lax.ppermute(odd_part, "row", odd)
 
     def twin_rule(own, other, odd_frame, has_odd):
         here = jnp.where(odd_frame, other[3], other[1])
@@ -473,32 +474,19 @@
         )
         from_twin.append(lax.ppermute(whole, "frame", twin))
 
-    near_score = scored(
-        band,
-        queries,
-        [key_one],
-        lambda own, other, odd_frame, has_odd: [jnp.where(odd_frame, own[0], own[4]) >= 0],
-    )
-    near = blended(
-        band,
-        near_score,
-        value_one,
-        [[own_part], [from_even], [from_odd]],
-        lambda own, other, odd_frame, has_odd: [True, True, has_odd],
-    )
+    def near_rule(own, other, odd_frame, has_odd):
+        beside = own[2] >= 1
+        return [True, jnp.where(odd_frame, own[0], own[4]) >= 0, beside, beside & has_odd]
+
+    near_score = scored(band, queries, [keys, key_one, key_even, key_odd], near_rule)
+    near = neared(near_score, [[(values,)], value_one, [(value_even,)], [(value_odd,)]])
     far_score = scored(
         band,
         queries,
         [key_two],
         lambda own, other, odd_frame, has_odd: [jnp.where(odd_frame, own[4], own[0]) >= 0],
     )
-    base, coef = blended(
-        band,
-        far_score,
-        [],
-        [[near], from_twin],
-        lambda own, other, odd_frame, has_odd: [True, True],
-    )
+    base, coef = based(far_score, near, from_twin)
     out = None
     for at, first in enumerate(ends[:-1]):
         out = finished(far_score[0], coef, value_two[at], base, out, first)

time: 99.1 us -> 102 us (1.029)
  waiting for transfers between devices: 29.4 us -> 36.1 us
  starting transfers between devices: 43 us -> 39.7 us
    ppermute x4, waiting for transfers between devices: 0.01 us -> 14 us  [the longest x1 8.74 us: per_device(): value_odd = lax.ppermute(values, 'row', odd)]
    ppermute x2, waiting for transfers between devices: 12.5 us -> 0.01 us  [per_device(): twin_odd = [lax.ppermute(query_twin[span], 'row', odd) for span in (0, 1)]]
    ppermute x1, waiting for transfers between devices: 0.01 us -> 12.4 us  [per_device(): lax.ppermute(value_halves[1], 'frame', beyond)]
    ppermute x1, waiting for transfers between devices: 8.05 us -> 2.7 us  [per_device(): band_twin = lax.ppermute(band, 'frame', twin)]
    ppermute x2, starting transfers between devices: 6.67 us -> 1.37 us  [per_device(): from_twin.append(lax.ppermute(whole, 'frame', twin))]
    ppermute x1, waiting for transfers between devices: 0.01 us -> 4.19 us  [per_device(): key_two = lax.ppermute(keys, 'frame', away)]
    ppermute x2, waiting for transfers between devices: 5 us -> 0.9 us  [per_device(): back_odd = lax.ppermute(odd_twin, 'row', odd)]
    ppermute x1, starting transfers between devices: 6.06 us -> 2.07 us  [per_device(): lax.ppermute(value_halves[1], 'frame', beyond)]
  transfers between devices with their start and end apart: 25 -> 25, of which waited for: 6 -> 8; matrix products, arithmetic and copies ran while one was open for 0% -> 0% of each run, Pallas kernels for 24% -> 23%
where the time goes in v7:
time: 102 us
  starting transfers between devices  39.7 us (39%)
  waiting for transfers between devices  36.1 us (35%)
  Pallas kernels  24 us (24%)
  local copies, waits for them, and re-layouts  1.4 us (1%)
    ppermute x1, waiting for transfers between devices, per_device(): lax.ppermute(value_halves[1], 'frame', beyond)  12.4 us
    ppermute x1, waiting for transfers between devices, per_device(): value_odd = lax.ppermute(values, 'row', odd)  8.74 us
    ppermute x2, starting transfers between devices, per_device(): twin_odd = [lax.ppermute(query_twin[span], 'row', odd) for span in (0, 1)]  8.17 us
    pallas_call x2, Pallas kernels, scored(): pl.pallas_call(functools.partial(score_kernel, heads, rule), in_specs=[SM...  7.94 us
    pallas_call x2, Pallas kernels, parts(): pl.pallas_call(functools.partial(parts_kernel, len(queries), len(keys), s...  7.53 us
    ppermute x2, starting transfers between devices, per_device(): back_odd = lax.ppermute(odd_twin, 'row', odd)  5.56 us
    ppermute x1, waiting for transfers between devices, per_device(): key_odd = lax.ppermute(keys, 'row', odd)  5.24 us
    ppermute x2, starting transfers between devices, per_device(): twin_even = [lax.ppermute(query_twin[span], 'row', even) for span in (0, 1)]  5.03 us
  transfers between devices with their start and end apart: 25, of which 8 were waited for; matrix products, arithmetic and copies ran while one was open for 0% of the time, Pallas kernels for 23%

profile of v7, /device:TPU:1, one launch (start us, length us, event | category | flops | bytes accessed | tf_op | source)
XLA Modules:
  0.0 101.7 jit_solution(9685033687127266725)
XLA Ops:
  0.0 1.3 %fusion = (bf16[1,160,1280]{2,1,0:T(8,128)(2,1)S(1)}, bf16[1,160,1280]{2,1,0:T(8,128)(2,1)S(1)}) fusion(bf16[1,160,2560]{2,1,0:T(8,128)(2,1)} %query_ref.3), kind=kLoop, calls=%fused_computation | loop fusion | bytes 1638400 | tf_op jit(solution)/shard_map/slice | solution.py:441
  1.3 2.1 %collective-permute-start.16 = (bf16[1,160,1280]{2,1,0:T(8,128)(2,1)S(1)}, bf16[1,160,1280]{2,1,0:T(8,128)(2,1)S(1)}, u32[]{:S(2)}, u32[]{:S(2)}) collective-permute-start(bf16[1,160,1280]{2,1,0:T(8,128)(2,1)S(1)} %get-tuple-element.29), channel_id=1, source_target_pairs={{0,4},{4,0},{8,12},{12,8},{16,20},{20,16},{24,28},{28,24},{1,5},{5... | collective-permute-start | bytes 1228808 | tf_op jit(solution)/shard_map/ppermute | solution.py:441
  3.5 1.3 %collective-permute-start.5 = (bf16[1,160,1280]{2,1,0:T(8,128)(2,1)S(1)}, bf16[1,160,1280]{2,1,0:T(8,128)(2,1)S(1)}, u32[]{:S(2)}, u32[]{:S(2)}) collective-permute-start(bf16[1,160,1280]{2,1,0:T(8,128)(2,1)S(1)} %get-tuple-element.31), channel_id=1, source_target_pairs={{4,12},{8,0},{12,20},{16,8},{20,28},{24,16},{5,13},{9,1},{13,21},{... | collective-permute-start | bytes 1228808 | tf_op jit(solution)/shard_map/ppermute | solution.py:433
  4.8 4.2 %collective-permute-start.1 = (bf16[1,160,2560]{2,1,0:T(8,128)(2,1)S(1)}, bf16[1,160,2560]{2,1,0:T(8,128)(2,1)S(1)}, u32[]{:S(2)}, u32[]{:S(2)}) collective-permute-start(bf16[1,160,2560]{2,1,0:T(8,128)(2,1)S(1)} %copy-done.2), channel_id=1, source_target_pairs={{0,24},{4,12},{8,0},{12,20},{16,8},{20,28},{24,16},{28,4},{1,25},{... | collective-permute-start | bytes 2457608 | tf_op jit(solution)/shard_map/ppermute | solution.py:429
  9.0 2.1 %collective-permute-start.6 = (bf16[1,160,1280]{2,1,0:T(8,128)(2,1)S(1)}, bf16[1,160,1280]{2,1,0:T(8,128)(2,1)S(1)}, u32[]{:S(2)}, u32[]{:S(2)}) collective-permute-start(bf16[1,160,1280]{2,1,0:T(8,128)(2,1)S(1)} %get-tuple-element.31), channel_id=1, source_target_pairs={{0,24},{28,4},{1,25},{29,5},{2,26},{30,6},{3,27},{31,7}} | collective-permute-start | bytes 1228808 | tf_op jit(solution)/shard_map/ppermute | solution.py:434
  11.2 2.7 %collective-permute-done.9.refs_1_ = s32[1,5]{1,0:T(1,128)S(1)} collective-permute-done((s32[1,5]{1,0:T(1,128)S(1)}, s32[1,5]{1,0:T(1,128)S(1)}, u32[]{:S(2)}, u32[]{:S(2)}) %collective-permute-start.9) | collective-permute-done | bytes 52 | tf_op jit(solution)/shard_map/ppermute | solution.py:442
  13.9 2.6 %collective-permute-start.17 = (bf16[1,160,1280]{2,1,0:T(8,128)(2,1)S(1)}, bf16[1,160,1280]{2,1,0:T(8,128)(2,1)S(1)}, u32[]{:S(2)}, u32[]{:S(2)}) collective-permute-start(bf16[1,160,1280]{2,1,0:T(8,128)(2,1)S(1)} %collective-permute-done.16.refs_4_), channel_id=1, source_target_pairs={{0,1},{1,0},{2,3},{3,2},{4,5},{5,4},{6,7},{7,6},{8,9},{9,8},{10,11... | collective-permute-start | bytes 1228808 | tf_op jit(solution)/shard_map/ppermute | solution.py:447
  16.5 5.2 %collective-permute-start.18 = (bf16[1,160,1280]{2,1,0:T(8,128)(2,1)S(1)}, bf16[1,160,1280]{2,1,0:T(8,128)(2,1)S(1)}, u32[]{:S(2)}, u32[]{:S(2)}) collective-permute-start(bf16[1,160,1280]{2,1,0:T(8,128)(2,1)S(1)} %collective-permute-done.16.refs_4_), channel_id=1, source_target_pairs={{1,2},{2,1},{5,6},{6,5},{9,10},{10,9},{13,14},{14,13},{17,18},{18,... | collective-permute-start | bytes 1228808 | tf_op jit(solution)/shard_map/ppermute | solution.py:448
  21.7 12.4 %collective-permute-done.6.refs_3_.refs_9_ = bf16[1,160,1280]{2,1,0:T(8,128)(2,1)S(1)} collective-permute-done((bf16[1,160,1280]{2,1,0:T(8,128)(2,1)S(1)}, bf16[1,160,1280]{2,1,0:T(8,128)(2,1)S(1)}, u32[]{:S(2)}, u32[]{:S(2)}) %collective-permute-start.6) | collective-permute-done | bytes 409632 | tf_op jit(solution)/shard_map/ppermute | solution.py:434
  34.1 4.0 %collective-permute-start.4 = (bf16[1,160,1280]{2,1,0:T(8,128)(2,1)S(1)}, bf16[1,160,1280]{2,1,0:T(8,128)(2,1)S(1)}, u32[]{:S(2)}, u32[]{:S(2)}) collective-permute-start(bf16[1,160,1280]{2,1,0:T(8,128)(2,1)S(1)} %get-tuple-element.32), channel_id=1, source_target_pairs={{0,24},{4,12},{8,0},{12,20},{16,8},{20,28},{24,16},{28,4},{1,25},{... | collective-permute-start | bytes 1228808 | tf_op jit(solution)/shard_map/ppermute | solution.py:431
  38.1 2.4 %collective-permute-start.11 = (bf16[1,160,1280]{2,1,0:T(8,128)(2,1)S(1)}, bf16[1,160,1280]{2,1,0:T(8,128)(2,1)S(1)}, u32[]{:S(2)}, u32[]{:S(2)}) collective-permute-start(bf16[1,160,1280]{2,1,0:T(8,128)(2,1)S(1)} %collective-permute-done.10.refs_4_), channel_id=1, source_target_pairs={{0,1},{1,0},{2,3},{3,2},{4,5},{5,4},{6,7},{7,6},{8,9},{9,8},{10,11... | collective-permute-start | bytes 1228808 | tf_op jit(solution)/shard_map/ppermute | solution.py:447
  40.5 3.0 %collective-permute-start.12 = (bf16[1,160,1280]{2,1,0:T(8,128)(2,1)S(1)}, bf16[1,160,1280]{2,1,0:T(8,128)(2,1)S(1)}, u32[]{:S(2)}, u32[]{:S(2)}) collective-permute-start(bf16[1,160,1280]{2,1,0:T(8,128)(2,1)S(1)} %collective-permute-done.10.refs_4_), channel_id=1, source_target_pairs={{1,2},{2,1},{5,6},{6,5},{9,10},{10,9},{13,14},{14,13},{17,18},{18,... | collective-permute-start | bytes 1228808 | tf_op jit(solution)/shard_map/ppermute | solution.py:448
  43.6 3.8 %shard_map.51 = (bf16[1,160,1408]{2,1,0:T(8,128)(2,1)S(1)}, bf16[1,160,1408]{2,1,0:T(8,128)(2,1)S(1)}, f32[1,160,1408]{2,1,0:T(8,128)S(1)}) custom-call(s32[1,5]{1,0:T(1,128)S(1)} %copy-done.3, s32[1,5]{1,0:T(1,128)S(1)} %collective-permute-done.9.refs_1_, bf16[1,160,1280]{2,1,0:T(8,128)(2,1)S(1)} %collective-permute-done.17.refs_2_, ...), custom_call_target="tpu_custom_call" | custom-call | flops 786432000 | bytes 4096000 | tf_op jit(solution)/shard_map/pallas_call | solution.py:170
  47.4 2.5 %collective-permute-start.20 = (bf16[1,160,1408]{2,1,0:T(8,128)(2,1)S(1)}, bf16[1,160,1408]{2,1,0:T(8,128)(2,1)S(1)}, u32[]{:S(2)}, u32[]{:S(2)}) collective-permute-start(bf16[1,160,1408]{2,1,0:T(8,128)(2,1)S(1)} %get-tuple-element.26), channel_id=1, source_target_pairs={{1,2},{2,1},{5,6},{6,5},{9,10},{10,9},{13,14},{14,13},{17,18},{18,... | collective-permute-start | bytes 1351688 | tf_op jit(solution)/shard_map/ppermute | solution.py:469
  49.9 3.8 %shard_map.49 = (bf16[1,160,1408]{2,1,0:T(8,128)(2,1)S(1)}, bf16[1,160,1408]{2,1,0:T(8,128)(2,1)S(1)}, f32[1,160,1408]{2,1,0:T(8,128)S(1)}) custom-call(s32[1,5]{1,0:T(1,128)S(1)} %copy-done.3, s32[1,5]{1,0:T(1,128)S(1)} %collective-permute-done.9.refs_1_, bf16[1,160,1280]{2,1,0:T(8,128)(2,1)S(1)} %collective-permute-done.11.refs_2_, ...), custom_call_target="tpu_custom_call" | custom-call | flops 786432000 | bytes 4096000 | tf_op jit(solution)/shard_map/pallas_call | solution.py:170
  53.8 3.0 %collective-permute-start.14 = (bf16[1,160,1408]{2,1,0:T(8,128)(2,1)S(1)}, bf16[1,160,1408]{2,1,0:T(8,128)(2,1)S(1)}, u32[]{:S(2)}, u32[]{:S(2)}) collective-permute-start(bf16[1,160,1408]{2,1,0:T(8,128)(2,1)S(1)} %get-tuple-element.23), channel_id=1, source_target_pairs={{1,2},{2,1},{5,6},{6,5},{9,10},{10,9},{13,14},{14,13},{17,18},{18,... | collective-permute-start | bytes 1351688 | tf_op jit(solution)/shard_map/ppermute | solution.py:469
  56.9 2.5 %collective-permute-start.3 = (bf16[1,160,2560]{2,1,0:T(8,128)(2,1)S(1)}, bf16[1,160,2560]{2,1,0:T(8,128)(2,1)S(1)}, u32[]{:S(2)}, u32[]{:S(2)}) collective-permute-start(bf16[1,160,2560]{2,1,0:T(8,128)(2,1)S(1)} %copy-done.2), channel_id=1, source_target_pairs={{1,2},{2,1},{5,6},{6,5},{9,10},{10,9},{13,14},{14,13},{17,18},{18,... | collective-permute-start | bytes 2457608 | tf_op jit(solution)/shard_map/ppermute | solution.py:444
  59.5 3.0 %collective-permute-start.8 = (bf16[1,160,2560]{2,1,0:T(8,128)(2,1)S(1)}, bf16[1,160,2560]{2,1,0:T(8,128)(2,1)S(1)}, u32[]{:S(2)}, u32[]{:S(2)}) collective-permute-start(bf16[1,160,2560]{2,1,0:T(8,128)(2,1)S(1)} %copy-done), channel_id=1, source_target_pairs={{1,2},{2,1},{5,6},{6,5},{9,10},{10,9},{13,14},{14,13},{17,18},{18,... | collective-permute-start | bytes 2457608 | tf_op jit(solution)/shard_map/ppermute | solution.py:446
  62.6 0.9 collective-permute-done.14.refs_2_
  63.5 1.2 %shard_map.52 = bf16[1,160,1408]{2,1,0:T(8,128)(2,1)S(1)} custom-call(s32[1,5]{1,0:T(1,128)S(1)} %copy-done.3, f32[1,160,1408]{2,1,0:T(8,128)S(1)} %get-tuple-element.24.refs_0_, bf16[1,160,1408]{2,1,0:T(8,128)(2,1)S(1)} %collective-permute-done.19.refs_1_, bf16[1,160,1408]{2,1,0:T(8,128)(2,1)S(1)} %collective-permute-done.20.refs_2_), custom_call_target="tpu_custom_call" | custom-call | flops 1351680 | bytes 1802240 | tf_op jit(solution)/shard_map/pallas_call | solution.py:210
  64.7 1.2 %shard_map.50 = bf16[1,160,1408]{2,1,0:T(8,128)(2,1)S(1)} custom-call(s32[1,5]{1,0:T(1,128)S(1)} %copy-done.3, f32[1,160,1408]{2,1,0:T(8,128)S(1)} %get-tuple-element.21.refs_0_, bf16[1,160,1408]{2,1,0:T(8,128)(2,1)S(1)} %collective-permute-done.13.refs_1_, bf16[1,160,1408]{2,1,0:T(8,128)(2,1)S(1)} %collective-permute-done.14.refs_2_), custom_call_target="tpu_custom_call" | custom-call | flops 1351680 | bytes 1802240 | tf_op jit(solution)/shard_map/pallas_call | solution.py:210
  66.0 1.4 %collective-permute-start.21 = (bf16[1,160,1408]{2,1,0:T(8,128)(2,1)S(1)}, bf16[1,160,1408]{2,1,0:T(8,128)(2,1)S(1)}, u32[]{:S(2)}, u32[]{:S(2)}) collective-permute-start(bf16[1,160,1408]{2,1,0:T(8,128)(2,1)S(1)} %shard_map.52), channel_id=1, source_target_pairs={{0,4},{4,0},{8,12},{12,8},{16,20},{20,16},{24,28},{28,24},{1,5},{5... | collective-permute-start | bytes 1351688 | tf_op jit(solution)/shard_map/ppermute | solution.py:475
  67.3 5.2 %collective-permute-done.3.refs_3_ = bf16[1,160,2560]{2,1,0:T(8,128)(2,1)S(1)} collective-permute-done((bf16[1,160,2560]{2,1,0:T(8,128)(2,1)S(1)}, bf16[1,160,2560]{2,1,0:T(8,128)(2,1)S(1)}, u32[]{:S(2)}, u32[]{:S(2)}) %collective-permute-start.3) | collective-permute-done | bytes 819232 | tf_op jit(solution)/shard_map/ppermute | solution.py:444
  72.6 8.7 %collective-permute-done.8.refs_5_ = bf16[1,160,2560]{2,1,0:T(8,128)(2,1)S(1)} collective-permute-done((bf16[1,160,2560]{2,1,0:T(8,128)(2,1)S(1)}, bf16[1,160,2560]{2,1,0:T(8,128)(2,1)S(1)}, u32[]{:S(2)}, u32[]{:S(2)}) %collective-permute-start.8) | collective-permute-done | bytes 819232 | tf_op jit(solution)/shard_map/ppermute | solution.py:446
  81.4 4.2 %collective-permute-done.refs_0_ = bf16[1,160,2560]{2,1,0:T(8,128)(2,1)S(1)} collective-permute-done((bf16[1,160,2560]{2,1,0:T(8,128)(2,1)S(1)}, bf16[1,160,2560]{2,1,0:T(8,128)(2,1)S(1)}, u32[]{:S(2)}, u32[]{:S(2)}) %collective-permute-start) | collective-permute-done | bytes 819232 | tf_op jit(solution)/shard_map/ppermute | solution.py:437
  85.5 2.0 %shard_map.46 = (bf16[1,20,160,160]{3,2,1,0:T(8,128)(2,1)S(1)}, f32[2,160,128]{2,1,0:T(8,128)S(1)}) custom-call(s32[1,5]{1,0:T(1,128)S(1)} %copy-done.3, bf16[1,160,2560]{2,1,0:T(8,128)(2,1)S(1)} %copy-done.1, bf16[1,160,2560]{2,1,0:T(8,128)(2,1)S(1)} %collective-permute-done.refs_0_), custom_call_target="tpu_custom_call" | custom-call | flops 131072000 | bytes 2457600 | tf_op jit(solution)/shard_map/pallas_call | solution.py:253
  87.5 6.0 %shard_map.47 = (bf16[4,20,160,160]{3,2,1,0:T(8,128)(2,1)S(1)}, f32[2,160,128]{2,1,0:T(8,128)S(1)}) custom-call(s32[1,5]{1,0:T(1,128)S(1)} %copy-done.3, bf16[1,160,2560]{2,1,0:T(8,128)(2,1)S(1)} %copy-done.1, bf16[1,160,2560]{2,1,0:T(8,128)(2,1)S(1)} %copy-done.2, bf16[1,160,2560]{2,1,0:T(8,128)(2,1)S(1)} %collective-permute-done.1.refs_1_.refs_6_, ...), custom_call_target="tpu_custom_call" | custom-call | flops 524288000 | bytes 2457600 | tf_op jit(solution)/shard_map/pallas_call | solution.py:253
  93.5 2.1 %shard_map.48.near_ref = f32[1,160,2688]{2,1,0:T(8,128)S(1)} custom-call(bf16[4,20,160,160]{3,2,1,0:T(8,128)(2,1)S(1)} %get-tuple-element.19.weight_ref, f32[2,160,128]{2,1,0:T(8,128)S(1)} %get-tuple-element.20.table_ref, bf16[1,160,2560]{2,1,0:T(8,128)(2,1)S(1)} %copy-done, bf16[1,160,1280]{2,1,0:T(8,128)(2,1)S(1)} %collective-permute-done.4.refs_1_.refs_8_, ...), custom_call_target="tpu_custom_call" | custom-call | flops 524288000 | bytes 6553600 | tf_op jit(solution)/shard_map/pallas_call | solution.py:299
  96.5 1.2 %shard_map.54.refs_0_ = bf16[1,160,2560]{2,1,0:T(8,128)(2,1)} custom-call(bf16[1,20,160,160]{3,2,1,0:T(8,128)(2,1)S(1)} %get-tuple-element.17.weight_ref, bf16[160,128]{1,0:T(8,128)(2,1)S(1)} %get-tuple-element.27.coef_ref, bf16[1,160,1280]{2,1,0:T(8,128)(2,1)S(1)} %collective-permute-done.24.value_ref, f32[1,160,2560]{2,1,0:T(8,128)S(1)} %get-tuple-element.28.base_ref), custom_call_target="tpu_custom_call" | custom-call | flops 65536000 | bytes 1638400 | tf_op jit(solution)/shard_map/pallas_call | solution.py:386
  97.7 1.2 %collective-permute-done.23.value_ref = bf16[1,160,768]{2,1,0:T(8,128)(2,1)S(1)} collective-permute-done((bf16[1,160,768]{2,1,0:T(8,128)(2,1)S(1)}, bf16[1,160,768]{2,1,0:T(8,128)(2,1)S(1)}, u32[]{:S(2)}, u32[]{:S(2)}) %collective-permute-start.23) | collective-permute-done | bytes 245792 | tf_op jit(solution)/shard_map/ppermute | solution.py:438
  98.8 1.0 %shard_map.55.refs_0_ = bf16[1,160,2560]{2,1,0:T(8,128)(2,1)} custom-call(bf16[1,20,160,160]{3,2,1,0:T(8,128)(2,1)S(1)} %get-tuple-element.17.weight_ref, bf16[160,128]{1,0:T(8,128)(2,1)S(1)} %get-tuple-element.27.coef_ref, bf16[1,160,768]{2,1,0:T(8,128)(2,1)S(1)} %collective-permute-done.23.value_ref, ...), custom_call_target="tpu_custom_call", output_to_operand_aliasing={{}: (4, {})} | custom-call | flops 39321600 | bytes 983040 | tf_op jit(solution)/shard_map/pallas_call | solution.py:386
  100.6 1.0 shard_map.56
  (41 shorter events, 2.0 us)
Async XLA Ops:
  0.0 3.4 %copy-start = (bf16[1,160,2560]{2,1,0:T(8,128)(2,1)S(1)}, bf16[1,160,2560]{2,1,0:T(8,128)(2,1)}, u32[]{:S(2)}) copy-start(bf16[1,160,2560]{2,1,0:T(8,128)(2,1)} %refs_7_.3) | copy-start | bytes 2457604
  0.0 4.8 %copy-start.2 = (bf16[1,160,2560]{2,1,0:T(8,128)(2,1)S(1)}, bf16[1,160,2560]{2,1,0:T(8,128)(2,1)}, u32[]{:S(2)}) copy-start(bf16[1,160,2560]{2,1,0:T(8,128)(2,1)} %refs_5_.3) | copy-start | bytes 2457604
  0.0 11.1 %copy-start.3 = (s32[1,5]{1,0:T(1,128)S(1)}, s32[1,5]{1,0:T(1,128)}, u32[]{:S(2)}) copy-start(s32[1,5]{1,0:T(1,128)} %band_ref.7) | copy-start | bytes 64
  1.3 12.5 %collective-permute-start.16 = (bf16[1,160,1280]{2,1,0:T(8,128)(2,1)S(1)}, bf16[1,160,1280]{2,1,0:T(8,128)(2,1)S(1)}, u32[]{:S(2)}, u32[]{:S(2)}) collective-permute-start(bf16[1,160,1280]{2,1,0:T(8,128)(2,1)S(1)} %get-tuple-element.29), channel_id=1, source_target_pairs={{0,4},{4,0},{8,12},{12,8},{16,20},{20,16},{24,28},{28,24},{1,5},{5... | collective-permute-start | bytes 1228808 | tf_op jit(solution)/shard_map/ppermute | solution.py:441
  3.5 13.0 %collective-permute-start.5 = (bf16[1,160,1280]{2,1,0:T(8,128)(2,1)S(1)}, bf16[1,160,1280]{2,1,0:T(8,128)(2,1)S(1)}, u32[]{:S(2)}, u32[]{:S(2)}) collective-permute-start(bf16[1,160,1280]{2,1,0:T(8,128)(2,1)S(1)} %get-tuple-element.31), channel_id=1, source_target_pairs={{4,12},{8,0},{12,20},{16,8},{20,28},{24,16},{5,13},{9,1},{13,21},{... | collective-permute-start | bytes 1228808 | tf_op jit(solution)/shard_map/ppermute | solution.py:433
  4.8 38.7 %collective-permute-start.1 = (bf16[1,160,2560]{2,1,0:T(8,128)(2,1)S(1)}, bf16[1,160,2560]{2,1,0:T(8,128)(2,1)S(1)}, u32[]{:S(2)}, u32[]{:S(2)}) collective-permute-start(bf16[1,160,2560]{2,1,0:T(8,128)(2,1)S(1)} %copy-done.2), channel_id=1, source_target_pairs={{0,24},{4,12},{8,0},{12,20},{16,8},{20,28},{24,16},{28,4},{1,25},{... | collective-permute-start | bytes 2457608 | tf_op jit(solution)/shard_map/ppermute | solution.py:429
  9.0 25.1 %collective-permute-start.6 = (bf16[1,160,1280]{2,1,0:T(8,128)(2,1)S(1)}, bf16[1,160,1280]{2,1,0:T(8,128)(2,1)S(1)}, u32[]{:S(2)}, u32[]{:S(2)}) collective-permute-start(bf16[1,160,1280]{2,1,0:T(8,128)(2,1)S(1)} %get-tuple-element.31), channel_id=1, source_target_pairs={{0,24},{28,4},{1,25},{29,5},{2,26},{30,6},{3,27},{31,7}} | collective-permute-start | bytes 1228808 | tf_op jit(solution)/shard_map/ppermute | solution.py:434
  11.1 2.8 %collective-permute-start.9 = (s32[1,5]{1,0:T(1,128)S(1)}, s32[1,5]{1,0:T(1,128)S(1)}, u32[]{:S(2)}, u32[]{:S(2)}) collective-permute-start(s32[1,5]{1,0:T(1,128)S(1)} %copy-done.3), channel_id=1, source_target_pairs={{0,4},{4,0},{8,12},{12,8},{16,20},{20,16},{24,28},{28,24},{1,5},{5... | collective-permute-start | bytes 68 | tf_op jit(solution)/shard_map/ppermute | solution.py:442
  13.9 24.3 %collective-permute-start.10 = (bf16[1,160,1280]{2,1,0:T(8,128)(2,1)S(1)}, bf16[1,160,1280]{2,1,0:T(8,128)(2,1)S(1)}, u32[]{:S(2)}, u32[]{:S(2)}) collective-permute-start(bf16[1,160,1280]{2,1,0:T(8,128)(2,1)S(1)} %get-tuple-element.30), channel_id=1, source_target_pairs={{0,4},{4,0},{8,12},{12,8},{16,20},{20,16},{24,28},{28,24},{1,5},{5... | collective-permute-start | bytes 1228808 | tf_op jit(solution)/shard_map/ppermute | solution.py:441
  13.9 26.6 %collective-permute-start.17 = (bf16[1,160,1280]{2,1,0:T(8,128)(2,1)S(1)}, bf16[1,160,1280]{2,1,0:T(8,128)(2,1)S(1)}, u32[]{:S(2)}, u32[]{:S(2)}) collective-permute-start(bf16[1,160,1280]{2,1,0:T(8,128)(2,1)S(1)} %collective-permute-done.16.refs_4_), channel_id=1, source_target_pairs={{0,1},{1,0},{2,3},{3,2},{4,5},{5,4},{6,7},{7,6},{8,9},{9,8},{10,11... | collective-permute-start | bytes 1228808 | tf_op jit(solution)/shard_map/ppermute | solution.py:447
  16.5 27.0 %collective-permute-start.18 = (bf16[1,160,1280]{2,1,0:T(8,128)(2,1)S(1)}, bf16[1,160,1280]{2,1,0:T(8,128)(2,1)S(1)}, u32[]{:S(2)}, u32[]{:S(2)}) collective-permute-start(bf16[1,160,1280]{2,1,0:T(8,128)(2,1)S(1)} %collective-permute-done.16.refs_4_), channel_id=1, source_target_pairs={{1,2},{2,1},{5,6},{6,5},{9,10},{10,9},{13,14},{14,13},{17,18},{18,... | collective-permute-start | bytes 1228808 | tf_op jit(solution)/shard_map/ppermute | solution.py:448
  34.1 15.8 %collective-permute-start.4 = (bf16[1,160,1280]{2,1,0:T(8,128)(2,1)S(1)}, bf16[1,160,1280]{2,1,0:T(8,128)(2,1)S(1)}, u32[]{:S(2)}, u32[]{:S(2)}) collective-permute-start(bf16[1,160,1280]{2,1,0:T(8,128)(2,1)S(1)} %get-tuple-element.32), channel_id=1, source_target_pairs={{0,24},{4,12},{8,0},{12,20},{16,8},{20,28},{24,16},{28,4},{1,25},{... | collective-permute-start | bytes 1228808 | tf_op jit(solution)/shard_map/ppermute | solution.py:431
  38.1 11.8 %collective-permute-start.11 = (bf16[1,160,1280]{2,1,0:T(8,128)(2,1)S(1)}, bf16[1,160,1280]{2,1,0:T(8,128)(2,1)S(1)}, u32[]{:S(2)}, u32[]{:S(2)}) collective-permute-start(bf16[1,160,1280]{2,1,0:T(8,128)(2,1)S(1)} %collective-permute-done.10.refs_4_), channel_id=1, source_target_pairs={{0,1},{1,0},{2,3},{3,2},{4,5},{5,4},{6,7},{7,6},{8,9},{9,8},{10,11... | collective-permute-start | bytes 1228808 | tf_op jit(solution)/shard_map/ppermute | solution.py:447
  40.5 9.4 %collective-permute-start.12 = (bf16[1,160,1280]{2,1,0:T(8,128)(2,1)S(1)}, bf16[1,160,1280]{2,1,0:T(8,128)(2,1)S(1)}, u32[]{:S(2)}, u32[]{:S(2)}) collective-permute-start(bf16[1,160,1280]{2,1,0:T(8,128)(2,1)S(1)} %collective-permute-done.10.refs_4_), channel_id=1, source_target_pairs={{1,2},{2,1},{5,6},{6,5},{9,10},{10,9},{13,14},{14,13},{17,18},{18,... | collective-permute-start | bytes 1228808 | tf_op jit(solution)/shard_map/ppermute | solution.py:448
  47.3 9.6 %collective-permute-start.19 = (bf16[1,160,1408]{2,1,0:T(8,128)(2,1)S(1)}, bf16[1,160,1408]{2,1,0:T(8,128)(2,1)S(1)}, u32[]{:S(2)}, u32[]{:S(2)}) collective-permute-start(bf16[1,160,1408]{2,1,0:T(8,128)(2,1)S(1)} %get-tuple-element.25), channel_id=1, source_target_pairs={{0,1},{1,0},{2,3},{3,2},{4,5},{5,4},{6,7},{7,6},{8,9},{9,8},{10,11... | collective-permute-start | bytes 1351688 | tf_op jit(solution)/shard_map/ppermute | solution.py:468
  47.4 12.1 %collective-permute-start.20 = (bf16[1,160,1408]{2,1,0:T(8,128)(2,1)S(1)}, bf16[1,160,1408]{2,1,0:T(8,128)(2,1)S(1)}, u32[]{:S(2)}, u32[]{:S(2)}) collective-permute-start(bf16[1,160,1408]{2,1,0:T(8,128)(2,1)S(1)} %get-tuple-element.26), channel_id=1, source_target_pairs={{1,2},{2,1},{5,6},{6,5},{9,10},{10,9},{13,14},{14,13},{17,18},{18,... | collective-permute-start | bytes 1351688 | tf_op jit(solution)/shard_map/ppermute | solution.py:469
  53.7 5.8 %collective-permute-start.13 = (bf16[1,160,1408]{2,1,0:T(8,128)(2,1)S(1)}, bf16[1,160,1408]{2,1,0:T(8,128)(2,1)S(1)}, u32[]{:S(2)}, u32[]{:S(2)}) collective-permute-start(bf16[1,160,1408]{2,1,0:T(8,128)(2,1)S(1)} %get-tuple-element.22), channel_id=1, source_target_pairs={{0,1},{1,0},{2,3},{3,2},{4,5},{5,4},{6,7},{7,6},{8,9},{9,8},{10,11... | collective-permute-start | bytes 1351688 | tf_op jit(solution)/shard_map/ppermute | solution.py:468
  53.8 9.7 %collective-permute-start.14 = (bf16[1,160,1408]{2,1,0:T(8,128)(2,1)S(1)}, bf16[1,160,1408]{2,1,0:T(8,128)(2,1)S(1)}, u32[]{:S(2)}, u32[]{:S(2)}) collective-permute-start(bf16[1,160,1408]{2,1,0:T(8,128)(2,1)S(1)} %get-tuple-element.23), channel_id=1, source_target_pairs={{1,2},{2,1},{5,6},{6,5},{9,10},{10,9},{13,14},{14,13},{17,18},{18,... | collective-permute-start | bytes 1351688 | tf_op jit(solution)/shard_map/ppermute | solution.py:469
  56.8 9.1 %collective-permute-start.2 = (bf16[1,160,2560]{2,1,0:T(8,128)(2,1)S(1)}, bf16[1,160,2560]{2,1,0:T(8,128)(2,1)S(1)}, u32[]{:S(2)}, u32[]{:S(2)}) collective-permute-start(bf16[1,160,2560]{2,1,0:T(8,128)(2,1)S(1)} %copy-done.2), channel_id=1, source_target_pairs={{0,1},{1,0},{2,3},{3,2},{4,5},{5,4},{6,7},{7,6},{8,9},{9,8},{10,11... | collective-permute-start | bytes 2457608 | tf_op jit(solution)/shard_map/ppermute | solution.py:443
  56.9 15.6 %collective-permute-start.3 = (bf16[1,160,2560]{2,1,0:T(8,128)(2,1)S(1)}, bf16[1,160,2560]{2,1,0:T(8,128)(2,1)S(1)}, u32[]{:S(2)}, u32[]{:S(2)}) collective-permute-start(bf16[1,160,2560]{2,1,0:T(8,128)(2,1)S(1)} %copy-done.2), channel_id=1, source_target_pairs={{1,2},{2,1},{5,6},{6,5},{9,10},{10,9},{13,14},{14,13},{17,18},{18,... | collective-permute-start | bytes 2457608 | tf_op jit(solution)/shard_map/ppermute | solution.py:444
  59.5 13.1 %collective-permute-start.7 = (bf16[1,160,2560]{2,1,0:T(8,128)(2,1)S(1)}, bf16[1,160,2560]{2,1,0:T(8,128)(2,1)S(1)}, u32[]{:S(2)}, u32[]{:S(2)}) collective-permute-start(bf16[1,160,2560]{2,1,0:T(8,128)(2,1)S(1)} %copy-done), channel_id=1, source_target_pairs={{0,1},{1,0},{2,3},{3,2},{4,5},{5,4},{6,7},{7,6},{8,9},{9,8},{10,11... | collective-permute-start | bytes 2457608 | tf_op jit(solution)/shard_map/ppermute | solution.py:445
  59.5 21.8 %collective-permute-start.8 = (bf16[1,160,2560]{2,1,0:T(8,128)(2,1)S(1)}, bf16[1,160,2560]{2,1,0:T(8,128)(2,1)S(1)}, u32[]{:S(2)}, u32[]{:S(2)}) collective-permute-start(bf16[1,160,2560]{2,1,0:T(8,128)(2,1)S(1)} %copy-done), channel_id=1, source_target_pairs={{1,2},{2,1},{5,6},{6,5},{9,10},{10,9},{13,14},{14,13},{17,18},{18,... | collective-permute-start | bytes 2457608 | tf_op jit(solution)/shard_map/ppermute | solution.py:446
  63.5 22.1 %collective-permute-start = (bf16[1,160,2560]{2,1,0:T(8,128)(2,1)S(1)}, bf16[1,160,2560]{2,1,0:T(8,128)(2,1)S(1)}, u32[]{:S(2)}, u32[]{:S(2)}) collective-permute-start(bf16[1,160,2560]{2,1,0:T(8,128)(2,1)S(1)} %copy-done.2), channel_id=1, source_target_pairs={{24,0},{12,4},{0,8},{20,12},{8,16},{28,20},{16,24},{4,28},{25,1},{... | collective-permute-start | bytes 2457608 | tf_op jit(solution)/shard_map/ppermute | solution.py:437
  64.7 20.8 %copy-start.1 = (bf16[1,160,2560]{2,1,0:T(8,128)(2,1)S(1)}, bf16[1,160,2560]{2,1,0:T(8,128)(2,1)}, u32[]{:S(2)}) copy-start(bf16[1,160,2560]{2,1,0:T(8,128)(2,1)} %query_ref.3) | copy-start | bytes 2457604
  66.0 29.7 %collective-permute-start.21 = (bf16[1,160,1408]{2,1,0:T(8,128)(2,1)S(1)}, bf16[1,160,1408]{2,1,0:T(8,128)(2,1)S(1)}, u32[]{:S(2)}, u32[]{:S(2)}) collective-permute-start(bf16[1,160,1408]{2,1,0:T(8,128)(2,1)S(1)} %shard_map.52), channel_id=1, source_target_pairs={{0,4},{4,0},{8,12},{12,8},{16,20},{20,16},{24,28},{28,24},{1,5},{5... | collective-permute-start | bytes 1351688 | tf_op jit(solution)/shard_map/ppermute | solution.py:475
  72.6 23.1 %collective-permute-start.15 = (bf16[1,160,1408]{2,1,0:T(8,128)(2,1)S(1)}, bf16[1,160,1408]{2,1,0:T(8,128)(2,1)S(1)}, u32[]{:S(2)}, u32[]{:S(2)}) collective-permute-start(bf16[1,160,1408]{2,1,0:T(8,128)(2,1)S(1)} %shard_map.50), channel_id=1, source_target_pairs={{0,4},{4,0},{8,12},{12,8},{16,20},{20,16},{24,28},{28,24},{1,5},{5... | collective-permute-start | bytes 1351688 | tf_op jit(solution)/shard_map/ppermute | solution.py:475
  72.6 23.9 %collective-permute-start.24 = (bf16[1,160,1280]{2,1,0:T(8,128)(2,1)S(1)}, bf16[1,160,1280]{2,1,0:T(8,128)(2,1)S(1)}, u32[]{:S(2)}, u32[]{:S(2)}) collective-permute-start(bf16[1,160,1280]{2,1,0:T(8,128)(2,1)S(1)} %get-tuple-element.32), channel_id=1, source_target_pairs={{24,0},{12,4},{0,8},{20,12},{8,16},{28,20},{16,24},{4,28},{25,1},{... | collective-permute-start | bytes 1228808 | tf_op jit(solution)/shard_map/ppermute | solution.py:438
  81.3 17.5 %collective-permute-start.23 = (bf16[1,160,768]{2,1,0:T(8,128)(2,1)S(1)}, bf16[1,160,768]{2,1,0:T(8,128)(2,1)S(1)}, u32[]{:S(2)}, u32[]{:S(2)}) collective-permute-start(bf16[1,160,768]{2,1,0:T(8,128)(2,1)S(1)} %slice.23), channel_id=1, source_target_pairs={{24,0},{12,4},{0,8},{20,12},{8,16},{28,20},{16,24},{4,28},{25,1},{... | collective-permute-start | bytes 737288 | tf_op jit(solution)/shard_map/ppermute | solution.py:438
  85.5 15.0 %collective-permute-start.22 = (bf16[1,160,512]{2,1,0:T(8,128)(2,1)S(1)}, bf16[1,160,512]{2,1,0:T(8,128)(2,1)S(1)}, u32[]{:S(2)}, u32[]{:S(2)}) collective-permute-start(bf16[1,160,512]{2,1,0:T(8,128)(2,1)S(1)} %slice.22), channel_id=1, source_target_pairs={{24,0},{12,4},{0,8},{20,12},{8,16},{28,20},{16,24},{4,28},{25,1},{... | collective-permute-start | bytes 491528 | tf_op jit(solution)/shard_map/ppermute | solution.py:438

commit v8 on v7

--- a/solution.py
+++ b/solution.py
@@ -268,24 +268,34 @@
     )(band, query, *keys)
 
 
-def near_kernel(shares_of, sources, heads, weight_ref, table_ref, *refs):
-    pieces, out_ref = grouped(refs[:-1], shares_of), refs[-1]
-    table = packed(table_ref[1])
+def near_kernel(counts, shares_of, sources, heads, *refs):
+    size = len(counts)
+    weight_refs, table_refs = refs[:size], refs[size : 2 * size]
+    pieces, out_ref = grouped(refs[2 * size : -1], shares_of), refs[-1]
+    portions, log = shares([table_ref[0] for table_ref in table_refs])
+    tables = [
+        packed(portion * table_ref[1]) for portion, table_ref in zip(portions, table_refs)
+    ]
     for n in range(heads):
-        summed = 0.0
-        for at, source in enumerate(sources):
-            piece, index = source[n]
-            value = sum(ref[0, :, column(index)] for ref in pieces[piece])
-            summed = summed + jnp.dot(
-                weight_ref[at, n], value, preferred_element_type=jnp.float32
-            )
-        out_ref[0, :, column(n)] = summed * spread(table, n)
-    out_ref[0, :, column(heads)] = table_ref[0]
-
-
-def neared(score, values):
-    weights, table = score
-    heads, rows = weights.shape[1:3]
+        out = 0.0
+        at = 0
+        for count, weight_ref, table in zip(counts, weight_refs, tables):
+            summed = 0.0
+            for i in range(count):
+                piece, index = sources[at][n]
+                value = sum(ref[0, :, column(index)] for ref in pieces[piece])
+                summed = summed + jnp.dot(
+                    weight_ref[i, n], value, preferred_element_type=jnp.float32
+                )
+                at += 1
+            out = out + summed * spread(table, n)
+        out_ref[0, :, column(n)] = out
+    out_ref[0, :, column(heads)] = log
+
+
+def neared(scores, values):
+    heads, rows = scores[0][0].shape[1:3]
+    counts = tuple(weights.shape[0] for weights, _ in scores)
     sources, pieces = [], []
     for value in values:
         source = []
@@ -298,9 +308,13 @@
     width = heads * HEAD
     return pl.pallas_call(
         functools.partial(
-            near_kernel, tuple(len(piece) for piece in pieces), tuple(sources), heads
-        ),
-        in_specs=[VMEM] * (2 + len(flat)),
+            near_kernel,
+            counts,
+            tuple(len(piece) for piece in pieces),
+            tuple(sources),
+            heads,
+        ),
+        in_specs=[VMEM] * (2 * len(scores) + len(flat)),
         out_specs=VMEM,
         out_shape=jax.ShapeDtypeStruct((1, rows, width + HEAD), jnp.float32),
         compiler_params=GRANT,
@@ -309,7 +323,7 @@
             bytes_accessed=2 * rows * width * (len(values) + 4),
             transcendentals=0,
         ),
-    )(weights, table, *flat)
+    )(*[score[0] for score in scores], *[score[1] for score in scores], *flat)
 
 
 def base_kernel(sizes, heads, table_ref, near_ref, *refs):
@@ -474,12 +488,21 @@
         )
         from_twin.append(lax.ppermute(whole, "frame", twin))
 
-    def near_rule(own, other, odd_frame, has_odd):
-        beside = own[2] >= 1
-        return [True, jnp.where(odd_frame, own[0], own[4]) >= 0, beside, beside & has_odd]
-
-    near_score = scored(band, queries, [keys, key_one, key_even, key_odd], near_rule)
-    near = neared(near_score, [[(values,)], value_one, [(value_even,)], [(value_odd,)]])
+    early_score = scored(
+        band, queries, [keys, key_even], lambda own, other, odd_frame, has_odd: [True, own[2] >= 1]
+    )
+    late_score = scored(
+        band,
+        queries,
+        [key_one, key_odd],
+        lambda own, other, odd_frame, has_odd: [
+            jnp.where(odd_frame, own[0], own[4]) >= 0,
+            (own[2] >= 1) & has_odd,
+        ],
+    )
+    near = neared(
+        [early_score, late_score], [[(values,)], [(value_even,)], value_one, [(value_odd,)]]
+    )
     far_score = scored(
         band,
         queries,

time: 102 us -> 102 us (level)
  waiting for transfers between devices: 36.1 us -> 34.4 us
  Pallas kernels: 24 us -> 25.4 us
    ppermute x1, waiting for transfers between devices: 8.74 us -> 7.28 us  [per_device(): value_odd = lax.ppermute(values, 'row', odd)]
    ppermute x1, waiting for transfers between devices: 5.24 us -> 6.63 us  [per_device(): key_odd = lax.ppermute(keys, 'row', odd)]
    ppermute x3, waiting for transfers between devices: 1.88 us -> 0.6 us  [per_device(): value_two = [lax.ppermute(piece, 'frame', away) for piece in value_thirds]]
    pallas_call x2 -> x3, Pallas kernels: 7.94 us -> 8.89 us  [scored(): pl.pallas_call(functools.partial(score_kernel, heads, rule), in_specs=[SM...]
  transfers between devices with their start and end apart: 25 -> 25, of which waited for: 8 -> 7; matrix products, arithmetic and copies ran while one was open for 0% -> 0% of each run, Pallas kernels for 23% -> 24%
where the time goes in v8:
time: 102 us
  starting transfers between devices  40.2 us (39%)
  waiting for transfers between devices  34.4 us (34%)
  Pallas kernels  25.4 us (25%)
  local copies, waits for them, and re-layouts  1.4 us (1%)
    ppermute x1, waiting for transfers between devices, per_device(): lax.ppermute(value_halves[1], 'frame', beyond)  12.4 us
    pallas_call x3, Pallas kernels, scored(): pl.pallas_call(functools.partial(score_kernel, heads, rule), in_specs=[SM...  8.89 us
    ppermute x2, starting transfers between devices, per_device(): twin_odd = [lax.ppermute(query_twin[span], 'row', odd) for span in (0, 1)]  8.17 us
    pallas_call x2, Pallas kernels, parts(): pl.pallas_call(functools.partial(parts_kernel, len(queries), len(keys), s...  7.64 us
    ppermute x1, waiting for transfers between devices, per_device(): value_odd = lax.ppermute(values, 'row', odd)  7.28 us
    ppermute x1, waiting for transfers between devices, per_device(): key_odd = lax.ppermute(keys, 'row', odd)  6.63 us
    ppermute x2, starting transfers between devices, per_device(): back_odd = lax.ppermute(odd_twin, 'row', odd)  5.55 us
    ppermute x2, starting transfers between devices, per_device(): twin_even = [lax.ppermute(query_twin[span], 'row', even) for span in (0, 1)]  5.03 us
  transfers between devices with their start and end apart: 25, of which 7 were waited for; matrix products, arithmetic and copies ran while one was open for 0% of the time, Pallas kernels for 24%

profile of v8, /device:TPU:1, one launch (start us, length us, event | category | flops | bytes accessed | tf_op | source)
XLA Modules:
  0.0 101.9 jit_solution(12750008453733729468)
XLA Ops:
  0.0 1.3 %fusion = (bf16[1,160,1280]{2,1,0:T(8,128)(2,1)S(1)}, bf16[1,160,1280]{2,1,0:T(8,128)(2,1)S(1)}) fusion(bf16[1,160,2560]{2,1,0:T(8,128)(2,1)} %query_ref.5), kind=kLoop, calls=%fused_computation | loop fusion | bytes 1638400 | tf_op jit(solution)/shard_map/slice | solution.py:455
  1.3 2.1 %collective-permute-start.16 = (bf16[1,160,1280]{2,1,0:T(8,128)(2,1)S(1)}, bf16[1,160,1280]{2,1,0:T(8,128)(2,1)S(1)}, u32[]{:S(2)}, u32[]{:S(2)}) collective-permute-start(bf16[1,160,1280]{2,1,0:T(8,128)(2,1)S(1)} %get-tuple-element.33), channel_id=1, source_target_pairs={{0,4},{4,0},{8,12},{12,8},{16,20},{20,16},{24,28},{28,24},{1,5},{5... | collective-permute-start | bytes 1228808 | tf_op jit(solution)/shard_map/ppermute | solution.py:455
  3.5 1.3 %collective-permute-start.6 = (bf16[1,160,1280]{2,1,0:T(8,128)(2,1)S(1)}, bf16[1,160,1280]{2,1,0:T(8,128)(2,1)S(1)}, u32[]{:S(2)}, u32[]{:S(2)}) collective-permute-start(bf16[1,160,1280]{2,1,0:T(8,128)(2,1)S(1)} %get-tuple-element.35), channel_id=1, source_target_pairs={{4,12},{8,0},{12,20},{16,8},{20,28},{24,16},{5,13},{9,1},{13,21},{... | collective-permute-start | bytes 1228808 | tf_op jit(solution)/shard_map/ppermute | solution.py:447
  4.8 4.2 %collective-permute-start.2 = (bf16[1,160,2560]{2,1,0:T(8,128)(2,1)S(1)}, bf16[1,160,2560]{2,1,0:T(8,128)(2,1)S(1)}, u32[]{:S(2)}, u32[]{:S(2)}) collective-permute-start(bf16[1,160,2560]{2,1,0:T(8,128)(2,1)S(1)} %copy-done.2), channel_id=1, source_target_pairs={{0,24},{4,12},{8,0},{12,20},{16,8},{20,28},{24,16},{28,4},{1,25},{... | collective-permute-start | bytes 2457608 | tf_op jit(solution)/shard_map/ppermute | solution.py:443
  9.0 2.1 %collective-permute-start.7 = (bf16[1,160,1280]{2,1,0:T(8,128)(2,1)S(1)}, bf16[1,160,1280]{2,1,0:T(8,128)(2,1)S(1)}, u32[]{:S(2)}, u32[]{:S(2)}) collective-permute-start(bf16[1,160,1280]{2,1,0:T(8,128)(2,1)S(1)} %get-tuple-element.35), channel_id=1, source_target_pairs={{0,24},{28,4},{1,25},{29,5},{2,26},{30,6},{3,27},{31,7}} | collective-permute-start | bytes 1228808 | tf_op jit(solution)/shard_map/ppermute | solution.py:448
  11.2 2.7 %collective-permute-done.9.refs_1_ = s32[1,5]{1,0:T(1,128)S(1)} collective-permute-done((s32[1,5]{1,0:T(1,128)S(1)}, s32[1,5]{1,0:T(1,128)S(1)}, u32[]{:S(2)}, u32[]{:S(2)}) %collective-permute-start.9) | collective-permute-done | bytes 52 | tf_op jit(solution)/shard_map/ppermute | solution.py:456
  13.9 2.6 %collective-permute-start.17 = (bf16[1,160,1280]{2,1,0:T(8,128)(2,1)S(1)}, bf16[1,160,1280]{2,1,0:T(8,128)(2,1)S(1)}, u32[]{:S(2)}, u32[]{:S(2)}) collective-permute-start(bf16[1,160,1280]{2,1,0:T(8,128)(2,1)S(1)} %collective-permute-done.16.refs_4_), channel_id=1, source_target_pairs={{0,1},{1,0},{2,3},{3,2},{4,5},{5,4},{6,7},{7,6},{8,9},{9,8},{10,11... | collective-permute-start | bytes 1228808 | tf_op jit(solution)/shard_map/ppermute | solution.py:461
  16.5 5.2 %collective-permute-start.18 = (bf16[1,160,1280]{2,1,0:T(8,128)(2,1)S(1)}, bf16[1,160,1280]{2,1,0:T(8,128)(2,1)S(1)}, u32[]{:S(2)}, u32[]{:S(2)}) collective-permute-start(bf16[1,160,1280]{2,1,0:T(8,128)(2,1)S(1)} %collective-permute-done.16.refs_4_), channel_id=1, source_target_pairs={{1,2},{2,1},{5,6},{6,5},{9,10},{10,9},{13,14},{14,13},{17,18},{18,... | collective-permute-start | bytes 1228808 | tf_op jit(solution)/shard_map/ppermute | solution.py:462
  21.7 12.4 %collective-permute-done.7.refs_8_.refs_9_ = bf16[1,160,1280]{2,1,0:T(8,128)(2,1)S(1)} collective-permute-done((bf16[1,160,1280]{2,1,0:T(8,128)(2,1)S(1)}, bf16[1,160,1280]{2,1,0:T(8,128)(2,1)S(1)}, u32[]{:S(2)}, u32[]{:S(2)}) %collective-permute-start.7) | collective-permute-done | bytes 409632 | tf_op jit(solution)/shard_map/ppermute | solution.py:448
  34.1 4.0 %collective-permute-start.5 = (bf16[1,160,1280]{2,1,0:T(8,128)(2,1)S(1)}, bf16[1,160,1280]{2,1,0:T(8,128)(2,1)S(1)}, u32[]{:S(2)}, u32[]{:S(2)}) collective-permute-start(bf16[1,160,1280]{2,1,0:T(8,128)(2,1)S(1)} %get-tuple-element.36), channel_id=1, source_target_pairs={{0,24},{4,12},{8,0},{12,20},{16,8},{20,28},{24,16},{28,4},{1,25},{... | collective-permute-start | bytes 1228808 | tf_op jit(solution)/shard_map/ppermute | solution.py:445
  38.1 2.4 %collective-permute-start.11 = (bf16[1,160,1280]{2,1,0:T(8,128)(2,1)S(1)}, bf16[1,160,1280]{2,1,0:T(8,128)(2,1)S(1)}, u32[]{:S(2)}, u32[]{:S(2)}) collective-permute-start(bf16[1,160,1280]{2,1,0:T(8,128)(2,1)S(1)} %collective-permute-done.10.refs_4_), channel_id=1, source_target_pairs={{0,1},{1,0},{2,3},{3,2},{4,5},{5,4},{6,7},{7,6},{8,9},{9,8},{10,11... | collective-permute-start | bytes 1228808 | tf_op jit(solution)/shard_map/ppermute | solution.py:461
  40.5 3.0 %collective-permute-start.12 = (bf16[1,160,1280]{2,1,0:T(8,128)(2,1)S(1)}, bf16[1,160,1280]{2,1,0:T(8,128)(2,1)S(1)}, u32[]{:S(2)}, u32[]{:S(2)}) collective-permute-start(bf16[1,160,1280]{2,1,0:T(8,128)(2,1)S(1)} %collective-permute-done.10.refs_4_), channel_id=1, source_target_pairs={{1,2},{2,1},{5,6},{6,5},{9,10},{10,9},{13,14},{14,13},{17,18},{18,... | collective-permute-start | bytes 1228808 | tf_op jit(solution)/shard_map/ppermute | solution.py:462
  43.6 3.8 %shard_map.52 = (bf16[1,160,1408]{2,1,0:T(8,128)(2,1)S(1)}, bf16[1,160,1408]{2,1,0:T(8,128)(2,1)S(1)}, f32[1,160,1408]{2,1,0:T(8,128)S(1)}) custom-call(s32[1,5]{1,0:T(1,128)S(1)} %copy-done.3, s32[1,5]{1,0:T(1,128)S(1)} %collective-permute-done.9.refs_1_, bf16[1,160,1280]{2,1,0:T(8,128)(2,1)S(1)} %collective-permute-done.17.refs_2_, ...), custom_call_target="tpu_custom_call" | custom-call | flops 786432000 | bytes 4096000 | tf_op jit(solution)/shard_map/pallas_call | solution.py:170
  47.4 2.6 %collective-permute-start.20 = (bf16[1,160,1408]{2,1,0:T(8,128)(2,1)S(1)}, bf16[1,160,1408]{2,1,0:T(8,128)(2,1)S(1)}, u32[]{:S(2)}, u32[]{:S(2)}) collective-permute-start(bf16[1,160,1408]{2,1,0:T(8,128)(2,1)S(1)} %get-tuple-element.30), channel_id=1, source_target_pairs={{1,2},{2,1},{5,6},{6,5},{9,10},{10,9},{13,14},{14,13},{17,18},{18,... | collective-permute-start | bytes 1351688 | tf_op jit(solution)/shard_map/ppermute | solution.py:483
  50.0 3.8 %shard_map.50 = (bf16[1,160,1408]{2,1,0:T(8,128)(2,1)S(1)}, bf16[1,160,1408]{2,1,0:T(8,128)(2,1)S(1)}, f32[1,160,1408]{2,1,0:T(8,128)S(1)}) custom-call(s32[1,5]{1,0:T(1,128)S(1)} %copy-done.3, s32[1,5]{1,0:T(1,128)S(1)} %collective-permute-done.9.refs_1_, bf16[1,160,1280]{2,1,0:T(8,128)(2,1)S(1)} %collective-permute-done.11.refs_2_, ...), custom_call_target="tpu_custom_call" | custom-call | flops 786432000 | bytes 4096000 | tf_op jit(solution)/shard_map/pallas_call | solution.py:170
  53.9 3.0 %collective-permute-start.14 = (bf16[1,160,1408]{2,1,0:T(8,128)(2,1)S(1)}, bf16[1,160,1408]{2,1,0:T(8,128)(2,1)S(1)}, u32[]{:S(2)}, u32[]{:S(2)}) collective-permute-start(bf16[1,160,1408]{2,1,0:T(8,128)(2,1)S(1)} %get-tuple-element.27), channel_id=1, source_target_pairs={{1,2},{2,1},{5,6},{6,5},{9,10},{10,9},{13,14},{14,13},{17,18},{18,... | collective-permute-start | bytes 1351688 | tf_op jit(solution)/shard_map/ppermute | solution.py:483
  56.9 2.6 %collective-permute-start.3 = (bf16[1,160,2560]{2,1,0:T(8,128)(2,1)S(1)}, bf16[1,160,2560]{2,1,0:T(8,128)(2,1)S(1)}, u32[]{:S(2)}, u32[]{:S(2)}) collective-permute-start(bf16[1,160,2560]{2,1,0:T(8,128)(2,1)S(1)} %copy-done.2), channel_id=1, source_target_pairs={{1,2},{2,1},{5,6},{6,5},{9,10},{10,9},{13,14},{14,13},{17,18},{18,... | collective-permute-start | bytes 2457608 | tf_op jit(solution)/shard_map/ppermute | solution.py:458
  60.1 3.0 %collective-permute-start.8 = (bf16[1,160,2560]{2,1,0:T(8,128)(2,1)S(1)}, bf16[1,160,2560]{2,1,0:T(8,128)(2,1)S(1)}, u32[]{:S(2)}, u32[]{:S(2)}) collective-permute-start(bf16[1,160,2560]{2,1,0:T(8,128)(2,1)S(1)} %copy-done), channel_id=1, source_target_pairs={{1,2},{2,1},{5,6},{6,5},{9,10},{10,9},{13,14},{14,13},{17,18},{18,... | collective-permute-start | bytes 2457608 | tf_op jit(solution)/shard_map/ppermute | solution.py:460
  63.6 1.2 %shard_map.53 = bf16[1,160,1408]{2,1,0:T(8,128)(2,1)S(1)} custom-call(s32[1,5]{1,0:T(1,128)S(1)} %copy-done.3, f32[1,160,1408]{2,1,0:T(8,128)S(1)} %get-tuple-element.28.refs_0_, bf16[1,160,1408]{2,1,0:T(8,128)(2,1)S(1)} %collective-permute-done.19.refs_1_, bf16[1,160,1408]{2,1,0:T(8,128)(2,1)S(1)} %collective-permute-done.20.refs_2_), custom_call_target="tpu_custom_call" | custom-call | flops 1351680 | bytes 1802240 | tf_op jit(solution)/shard_map/pallas_call | solution.py:210
  64.9 1.2 %shard_map.51 = bf16[1,160,1408]{2,1,0:T(8,128)(2,1)S(1)} custom-call(s32[1,5]{1,0:T(1,128)S(1)} %copy-done.3, f32[1,160,1408]{2,1,0:T(8,128)S(1)} %get-tuple-element.25.refs_0_, bf16[1,160,1408]{2,1,0:T(8,128)(2,1)S(1)} %collective-permute-done.13.refs_1_, bf16[1,160,1408]{2,1,0:T(8,128)(2,1)S(1)} %collective-permute-done.14.refs_2_), custom_call_target="tpu_custom_call" | custom-call | flops 1351680 | bytes 1802240 | tf_op jit(solution)/shard_map/pallas_call | solution.py:210
  66.1 6.6 %collective-permute-done.3.refs_1_ = bf16[1,160,2560]{2,1,0:T(8,128)(2,1)S(1)} collective-permute-done((bf16[1,160,2560]{2,1,0:T(8,128)(2,1)S(1)}, bf16[1,160,2560]{2,1,0:T(8,128)(2,1)S(1)}, u32[]{:S(2)}, u32[]{:S(2)}) %collective-permute-start.3) | collective-permute-done | bytes 819232 | tf_op jit(solution)/shard_map/ppermute | solution.py:458
  72.7 1.5 %collective-permute-start.15 = (bf16[1,160,1408]{2,1,0:T(8,128)(2,1)S(1)}, bf16[1,160,1408]{2,1,0:T(8,128)(2,1)S(1)}, u32[]{:S(2)}, u32[]{:S(2)}) collective-permute-start(bf16[1,160,1408]{2,1,0:T(8,128)(2,1)S(1)} %shard_map.51), channel_id=1, source_target_pairs={{0,4},{4,0},{8,12},{12,8},{16,20},{20,16},{24,28},{28,24},{1,5},{5... | collective-permute-start | bytes 1351688 | tf_op jit(solution)/shard_map/ppermute | solution.py:489
  74.2 7.3 %collective-permute-done.8.refs_9_ = bf16[1,160,2560]{2,1,0:T(8,128)(2,1)S(1)} collective-permute-done((bf16[1,160,2560]{2,1,0:T(8,128)(2,1)S(1)}, bf16[1,160,2560]{2,1,0:T(8,128)(2,1)S(1)}, u32[]{:S(2)}, u32[]{:S(2)}) %collective-permute-start.8) | collective-permute-done | bytes 819232 | tf_op jit(solution)/shard_map/ppermute | solution.py:460
  81.5 4.2 %collective-permute-done.refs_0_ = bf16[1,160,2560]{2,1,0:T(8,128)(2,1)S(1)} collective-permute-done((bf16[1,160,2560]{2,1,0:T(8,128)(2,1)S(1)}, bf16[1,160,2560]{2,1,0:T(8,128)(2,1)S(1)}, u32[]{:S(2)}, u32[]{:S(2)}) %collective-permute-start) | collective-permute-done | bytes 819232 | tf_op jit(solution)/shard_map/ppermute | solution.py:451
  85.7 2.0 %shard_map.46 = (bf16[1,20,160,160]{3,2,1,0:T(8,128)(2,1)S(1)}, f32[2,160,128]{2,1,0:T(8,128)S(1)}) custom-call(s32[1,5]{1,0:T(1,128)S(1)} %copy-done.3, bf16[1,160,2560]{2,1,0:T(8,128)(2,1)S(1)} %copy-done.1, bf16[1,160,2560]{2,1,0:T(8,128)(2,1)S(1)} %collective-permute-done.refs_0_), custom_call_target="tpu_custom_call" | custom-call | flops 131072000 | bytes 2457600 | tf_op jit(solution)/shard_map/pallas_call | solution.py:253
  87.7 3.5 %shard_map.48 = (bf16[2,20,160,160]{3,2,1,0:T(8,128)(2,1)S(1)}, f32[2,160,128]{2,1,0:T(8,128)S(1)}) custom-call(s32[1,5]{1,0:T(1,128)S(1)} %copy-done.3, bf16[1,160,2560]{2,1,0:T(8,128)(2,1)S(1)} %copy-done.1, bf16[1,160,2560]{2,1,0:T(8,128)(2,1)S(1)} %collective-permute-done.2.refs_0_.refs_6_, bf16[1,160,2560]{2,1,0:T(8,128)(2,1)S(1)} %collective-permute-done.3.refs_1_), custom_call_target="tpu_custom_call" | custom-call | flops 262144000 | bytes 2457600 | tf_op jit(solution)/shard_map/pallas_call | solution.py:253
  91.2 3.4 %shard_map.47 = (bf16[2,20,160,160]{3,2,1,0:T(8,128)(2,1)S(1)}, f32[2,160,128]{2,1,0:T(8,128)S(1)}) custom-call(s32[1,5]{1,0:T(1,128)S(1)} %copy-done.3, bf16[1,160,2560]{2,1,0:T(8,128)(2,1)S(1)} %copy-done.1, bf16[1,160,2560]{2,1,0:T(8,128)(2,1)S(1)} %copy-done.2, bf16[1,160,2560]{2,1,0:T(8,128)(2,1)S(1)} %collective-permute-done.1.refs_1_), custom_call_target="tpu_custom_call" | custom-call | flops 262144000 | bytes 2457600 | tf_op jit(solution)/shard_map/pallas_call | solution.py:253
  94.6 2.4 %shard_map.49.near_ref = f32[1,160,2688]{2,1,0:T(8,128)S(1)} custom-call(bf16[2,20,160,160]{3,2,1,0:T(8,128)(2,1)S(1)} %get-tuple-element.21.refs_0_, bf16[2,20,160,160]{3,2,1,0:T(8,128)(2,1)S(1)} %get-tuple-element.22.refs_1_, f32[2,160,128]{2,1,0:T(8,128)S(1)} %get-tuple-element.23.refs_2_, f32[2,160,128]{2,1,0:T(8,128)S(1)} %get-tuple-element.24.refs_3_, ...), custom_call_target="tpu_custom_call" | custom-call | flops 524288000 | bytes 6553600 | tf_op jit(solution)/shard_map/pallas_call | solution.py:309
  97.0 0.8 shard_map.54
  97.9 1.2 %shard_map.55.refs_0_ = bf16[1,160,2560]{2,1,0:T(8,128)(2,1)} custom-call(bf16[1,20,160,160]{3,2,1,0:T(8,128)(2,1)S(1)} %get-tuple-element.19.weight_ref, bf16[160,128]{1,0:T(8,128)(2,1)S(1)} %get-tuple-element.31.coef_ref, bf16[1,160,1280]{2,1,0:T(8,128)(2,1)S(1)} %collective-permute-done.24.value_ref, f32[1,160,2560]{2,1,0:T(8,128)S(1)} %get-tuple-element.32.base_ref), custom_call_target="tpu_custom_call" | custom-call | flops 65536000 | bytes 1638400 | tf_op jit(solution)/shard_map/pallas_call | solution.py:400
  99.1 1.0 %shard_map.56.refs_0_ = bf16[1,160,2560]{2,1,0:T(8,128)(2,1)} custom-call(bf16[1,20,160,160]{3,2,1,0:T(8,128)(2,1)S(1)} %get-tuple-element.19.weight_ref, bf16[160,128]{1,0:T(8,128)(2,1)S(1)} %get-tuple-element.31.coef_ref, bf16[1,160,768]{2,1,0:T(8,128)(2,1)S(1)} %collective-permute-done.23.value_ref, ...), custom_call_target="tpu_custom_call", output_to_operand_aliasing={{}: (4, {})} | custom-call | flops 39321600 | bytes 983040 | tf_op jit(solution)/shard_map/pallas_call | solution.py:400
  100.7 1.0 shard_map.57
  (42 shorter events, 2.1 us)
Async XLA Ops:
  0.0 3.4 %copy-start = (bf16[1,160,2560]{2,1,0:T(8,128)(2,1)S(1)}, bf16[1,160,2560]{2,1,0:T(8,128)(2,1)}, u32[]{:S(2)}) copy-start(bf16[1,160,2560]{2,1,0:T(8,128)(2,1)} %refs_7_.3) | copy-start | bytes 2457604
  0.0 4.8 %copy-start.2 = (bf16[1,160,2560]{2,1,0:T(8,128)(2,1)S(1)}, bf16[1,160,2560]{2,1,0:T(8,128)(2,1)}, u32[]{:S(2)}) copy-start(bf16[1,160,2560]{2,1,0:T(8,128)(2,1)} %refs_5_.3) | copy-start | bytes 2457604
  0.0 11.1 %copy-start.3 = (s32[1,5]{1,0:T(1,128)S(1)}, s32[1,5]{1,0:T(1,128)}, u32[]{:S(2)}) copy-start(s32[1,5]{1,0:T(1,128)} %band_ref.9) | copy-start | bytes 64
  1.3 12.5 %collective-permute-start.16 = (bf16[1,160,1280]{2,1,0:T(8,128)(2,1)S(1)}, bf16[1,160,1280]{2,1,0:T(8,128)(2,1)S(1)}, u32[]{:S(2)}, u32[]{:S(2)}) collective-permute-start(bf16[1,160,1280]{2,1,0:T(8,128)(2,1)S(1)} %get-tuple-element.33), channel_id=1, source_target_pairs={{0,4},{4,0},{8,12},{12,8},{16,20},{20,16},{24,28},{28,24},{1,5},{5... | collective-permute-start | bytes 1228808 | tf_op jit(solution)/shard_map/ppermute | solution.py:455
  3.5 13.0 %collective-permute-start.6 = (bf16[1,160,1280]{2,1,0:T(8,128)(2,1)S(1)}, bf16[1,160,1280]{2,1,0:T(8,128)(2,1)S(1)}, u32[]{:S(2)}, u32[]{:S(2)}) collective-permute-start(bf16[1,160,1280]{2,1,0:T(8,128)(2,1)S(1)} %get-tuple-element.35), channel_id=1, source_target_pairs={{4,12},{8,0},{12,20},{16,8},{20,28},{24,16},{5,13},{9,1},{13,21},{... | collective-permute-start | bytes 1228808 | tf_op jit(solution)/shard_map/ppermute | solution.py:447
  4.8 38.7 %collective-permute-start.2 = (bf16[1,160,2560]{2,1,0:T(8,128)(2,1)S(1)}, bf16[1,160,2560]{2,1,0:T(8,128)(2,1)S(1)}, u32[]{:S(2)}, u32[]{:S(2)}) collective-permute-start(bf16[1,160,2560]{2,1,0:T(8,128)(2,1)S(1)} %copy-done.2), channel_id=1, source_target_pairs={{0,24},{4,12},{8,0},{12,20},{16,8},{20,28},{24,16},{28,4},{1,25},{... | collective-permute-start | bytes 2457608 | tf_op jit(solution)/shard_map/ppermute | solution.py:443
  9.0 25.1 %collective-permute-start.7 = (bf16[1,160,1280]{2,1,0:T(8,128)(2,1)S(1)}, bf16[1,160,1280]{2,1,0:T(8,128)(2,1)S(1)}, u32[]{:S(2)}, u32[]{:S(2)}) collective-permute-start(bf16[1,160,1280]{2,1,0:T(8,128)(2,1)S(1)} %get-tuple-element.35), channel_id=1, source_target_pairs={{0,24},{28,4},{1,25},{29,5},{2,26},{30,6},{3,27},{31,7}} | collective-permute-start | bytes 1228808 | tf_op jit(solution)/shard_map/ppermute | solution.py:448
  11.1 2.8 %collective-permute-start.9 = (s32[1,5]{1,0:T(1,128)S(1)}, s32[1,5]{1,0:T(1,128)S(1)}, u32[]{:S(2)}, u32[]{:S(2)}) collective-permute-start(s32[1,5]{1,0:T(1,128)S(1)} %copy-done.3), channel_id=1, source_target_pairs={{0,4},{4,0},{8,12},{12,8},{16,20},{20,16},{24,28},{28,24},{1,5},{5... | collective-permute-start | bytes 68 | tf_op jit(solution)/shard_map/ppermute | solution.py:456
  13.9 24.3 %collective-permute-start.10 = (bf16[1,160,1280]{2,1,0:T(8,128)(2,1)S(1)}, bf16[1,160,1280]{2,1,0:T(8,128)(2,1)S(1)}, u32[]{:S(2)}, u32[]{:S(2)}) collective-permute-start(bf16[1,160,1280]{2,1,0:T(8,128)(2,1)S(1)} %get-tuple-element.34), channel_id=1, source_target_pairs={{0,4},{4,0},{8,12},{12,8},{16,20},{20,16},{24,28},{28,24},{1,5},{5... | collective-permute-start | bytes 1228808 | tf_op jit(solution)/shard_map/ppermute | solution.py:455
  13.9 26.6 %collective-permute-start.17 = (bf16[1,160,1280]{2,1,0:T(8,128)(2,1)S(1)}, bf16[1,160,1280]{2,1,0:T(8,128)(2,1)S(1)}, u32[]{:S(2)}, u32[]{:S(2)}) collective-permute-start(bf16[1,160,1280]{2,1,0:T(8,128)(2,1)S(1)} %collective-permute-done.16.refs_4_), channel_id=1, source_target_pairs={{0,1},{1,0},{2,3},{3,2},{4,5},{5,4},{6,7},{7,6},{8,9},{9,8},{10,11... | collective-permute-start | bytes 1228808 | tf_op jit(solution)/shard_map/ppermute | solution.py:461
  16.5 27.0 %collective-permute-start.18 = (bf16[1,160,1280]{2,1,0:T(8,128)(2,1)S(1)}, bf16[1,160,1280]{2,1,0:T(8,128)(2,1)S(1)}, u32[]{:S(2)}, u32[]{:S(2)}) collective-permute-start(bf16[1,160,1280]{2,1,0:T(8,128)(2,1)S(1)} %collective-permute-done.16.refs_4_), channel_id=1, source_target_pairs={{1,2},{2,1},{5,6},{6,5},{9,10},{10,9},{13,14},{14,13},{17,18},{18,... | collective-permute-start | bytes 1228808 | tf_op jit(solution)/shard_map/ppermute | solution.py:462
  34.1 15.9 %collective-permute-start.5 = (bf16[1,160,1280]{2,1,0:T(8,128)(2,1)S(1)}, bf16[1,160,1280]{2,1,0:T(8,128)(2,1)S(1)}, u32[]{:S(2)}, u32[]{:S(2)}) collective-permute-start(bf16[1,160,1280]{2,1,0:T(8,128)(2,1)S(1)} %get-tuple-element.36), channel_id=1, source_target_pairs={{0,24},{4,12},{8,0},{12,20},{16,8},{20,28},{24,16},{28,4},{1,25},{... | collective-permute-start | bytes 1228808 | tf_op jit(solution)/shard_map/ppermute | solution.py:445
  38.1 11.9 %collective-permute-start.11 = (bf16[1,160,1280]{2,1,0:T(8,128)(2,1)S(1)}, bf16[1,160,1280]{2,1,0:T(8,128)(2,1)S(1)}, u32[]{:S(2)}, u32[]{:S(2)}) collective-permute-start(bf16[1,160,1280]{2,1,0:T(8,128)(2,1)S(1)} %collective-permute-done.10.refs_4_), channel_id=1, source_target_pairs={{0,1},{1,0},{2,3},{3,2},{4,5},{5,4},{6,7},{7,6},{8,9},{9,8},{10,11... | collective-permute-start | bytes 1228808 | tf_op jit(solution)/shard_map/ppermute | solution.py:461
  40.5 9.5 %collective-permute-start.12 = (bf16[1,160,1280]{2,1,0:T(8,128)(2,1)S(1)}, bf16[1,160,1280]{2,1,0:T(8,128)(2,1)S(1)}, u32[]{:S(2)}, u32[]{:S(2)}) collective-permute-start(bf16[1,160,1280]{2,1,0:T(8,128)(2,1)S(1)} %collective-permute-done.10.refs_4_), channel_id=1, source_target_pairs={{1,2},{2,1},{5,6},{6,5},{9,10},{10,9},{13,14},{14,13},{17,18},{18,... | collective-permute-start | bytes 1228808 | tf_op jit(solution)/shard_map/ppermute | solution.py:462
  47.4 12.1 %collective-permute-start.19 = (bf16[1,160,1408]{2,1,0:T(8,128)(2,1)S(1)}, bf16[1,160,1408]{2,1,0:T(8,128)(2,1)S(1)}, u32[]{:S(2)}, u32[]{:S(2)}) collective-permute-start(bf16[1,160,1408]{2,1,0:T(8,128)(2,1)S(1)} %get-tuple-element.29), channel_id=1, source_target_pairs={{0,1},{1,0},{2,3},{3,2},{4,5},{5,4},{6,7},{7,6},{8,9},{9,8},{10,11... | collective-permute-start | bytes 1351688 | tf_op jit(solution)/shard_map/ppermute | solution.py:482
  47.4 12.1 %collective-permute-start.20 = (bf16[1,160,1408]{2,1,0:T(8,128)(2,1)S(1)}, bf16[1,160,1408]{2,1,0:T(8,128)(2,1)S(1)}, u32[]{:S(2)}, u32[]{:S(2)}) collective-permute-start(bf16[1,160,1408]{2,1,0:T(8,128)(2,1)S(1)} %get-tuple-element.30), channel_id=1, source_target_pairs={{1,2},{2,1},{5,6},{6,5},{9,10},{10,9},{13,14},{14,13},{17,18},{18,... | collective-permute-start | bytes 1351688 | tf_op jit(solution)/shard_map/ppermute | solution.py:483
  53.9 6.2 %collective-permute-start.13 = (bf16[1,160,1408]{2,1,0:T(8,128)(2,1)S(1)}, bf16[1,160,1408]{2,1,0:T(8,128)(2,1)S(1)}, u32[]{:S(2)}, u32[]{:S(2)}) collective-permute-start(bf16[1,160,1408]{2,1,0:T(8,128)(2,1)S(1)} %get-tuple-element.26), channel_id=1, source_target_pairs={{0,1},{1,0},{2,3},{3,2},{4,5},{5,4},{6,7},{7,6},{8,9},{9,8},{10,11... | collective-permute-start | bytes 1351688 | tf_op jit(solution)/shard_map/ppermute | solution.py:482
  53.9 9.7 %collective-permute-start.14 = (bf16[1,160,1408]{2,1,0:T(8,128)(2,1)S(1)}, bf16[1,160,1408]{2,1,0:T(8,128)(2,1)S(1)}, u32[]{:S(2)}, u32[]{:S(2)}) collective-permute-start(bf16[1,160,1408]{2,1,0:T(8,128)(2,1)S(1)} %get-tuple-element.27), channel_id=1, source_target_pairs={{1,2},{2,1},{5,6},{6,5},{9,10},{10,9},{13,14},{14,13},{17,18},{18,... | collective-permute-start | bytes 1351688 | tf_op jit(solution)/shard_map/ppermute | solution.py:483
  56.9 15.8 %collective-permute-start.3 = (bf16[1,160,2560]{2,1,0:T(8,128)(2,1)S(1)}, bf16[1,160,2560]{2,1,0:T(8,128)(2,1)S(1)}, u32[]{:S(2)}, u32[]{:S(2)}) collective-permute-start(bf16[1,160,2560]{2,1,0:T(8,128)(2,1)S(1)} %copy-done.2), channel_id=1, source_target_pairs={{1,2},{2,1},{5,6},{6,5},{9,10},{10,9},{13,14},{14,13},{17,18},{18,... | collective-permute-start | bytes 2457608 | tf_op jit(solution)/shard_map/ppermute | solution.py:458
  59.5 13.2 %collective-permute-start.1 = (bf16[1,160,2560]{2,1,0:T(8,128)(2,1)S(1)}, bf16[1,160,2560]{2,1,0:T(8,128)(2,1)S(1)}, u32[]{:S(2)}, u32[]{:S(2)}) collective-permute-start(bf16[1,160,2560]{2,1,0:T(8,128)(2,1)S(1)} %copy-done.2), channel_id=1, source_target_pairs={{0,1},{1,0},{2,3},{3,2},{4,5},{5,4},{6,7},{7,6},{8,9},{9,8},{10,11... | collective-permute-start | bytes 2457608 | tf_op jit(solution)/shard_map/ppermute | solution.py:457
  59.6 14.6 %collective-permute-start.4 = (bf16[1,160,2560]{2,1,0:T(8,128)(2,1)S(1)}, bf16[1,160,2560]{2,1,0:T(8,128)(2,1)S(1)}, u32[]{:S(2)}, u32[]{:S(2)}) collective-permute-start(bf16[1,160,2560]{2,1,0:T(8,128)(2,1)S(1)} %copy-done), channel_id=1, source_target_pairs={{0,1},{1,0},{2,3},{3,2},{4,5},{5,4},{6,7},{7,6},{8,9},{9,8},{10,11... | collective-permute-start | bytes 2457608 | tf_op jit(solution)/shard_map/ppermute | solution.py:459
  60.1 21.4 %collective-permute-start.8 = (bf16[1,160,2560]{2,1,0:T(8,128)(2,1)S(1)}, bf16[1,160,2560]{2,1,0:T(8,128)(2,1)S(1)}, u32[]{:S(2)}, u32[]{:S(2)}) collective-permute-start(bf16[1,160,2560]{2,1,0:T(8,128)(2,1)S(1)} %copy-done), channel_id=1, source_target_pairs={{1,2},{2,1},{5,6},{6,5},{9,10},{10,9},{13,14},{14,13},{17,18},{18,... | collective-permute-start | bytes 2457608 | tf_op jit(solution)/shard_map/ppermute | solution.py:460
  63.6 22.1 %collective-permute-start = (bf16[1,160,2560]{2,1,0:T(8,128)(2,1)S(1)}, bf16[1,160,2560]{2,1,0:T(8,128)(2,1)S(1)}, u32[]{:S(2)}, u32[]{:S(2)}) collective-permute-start(bf16[1,160,2560]{2,1,0:T(8,128)(2,1)S(1)} %copy-done.2), channel_id=1, source_target_pairs={{24,0},{12,4},{0,8},{20,12},{8,16},{28,20},{16,24},{4,28},{25,1},{... | collective-permute-start | bytes 2457608 | tf_op jit(solution)/shard_map/ppermute | solution.py:451
  64.8 20.8 %copy-start.1 = (bf16[1,160,2560]{2,1,0:T(8,128)(2,1)S(1)}, bf16[1,160,2560]{2,1,0:T(8,128)(2,1)}, u32[]{:S(2)}) copy-start(bf16[1,160,2560]{2,1,0:T(8,128)(2,1)} %query_ref.5) | copy-start | bytes 2457604
  72.7 24.3 %collective-permute-start.21 = (bf16[1,160,1408]{2,1,0:T(8,128)(2,1)S(1)}, bf16[1,160,1408]{2,1,0:T(8,128)(2,1)S(1)}, u32[]{:S(2)}, u32[]{:S(2)}) collective-permute-start(bf16[1,160,1408]{2,1,0:T(8,128)(2,1)S(1)} %shard_map.53), channel_id=1, source_target_pairs={{0,4},{4,0},{8,12},{12,8},{16,20},{20,16},{24,28},{28,24},{1,5},{5... | collective-permute-start | bytes 1351688 | tf_op jit(solution)/shard_map/ppermute | solution.py:489
  72.7 24.3 %collective-permute-start.15 = (bf16[1,160,1408]{2,1,0:T(8,128)(2,1)S(1)}, bf16[1,160,1408]{2,1,0:T(8,128)(2,1)S(1)}, u32[]{:S(2)}, u32[]{:S(2)}) collective-permute-start(bf16[1,160,1408]{2,1,0:T(8,128)(2,1)S(1)} %shard_map.51), channel_id=1, source_target_pairs={{0,4},{4,0},{8,12},{12,8},{16,20},{20,16},{24,28},{28,24},{1,5},{5... | collective-permute-start | bytes 1351688 | tf_op jit(solution)/shard_map/ppermute | solution.py:489
  74.2 23.7 %collective-permute-start.24 = (bf16[1,160,1280]{2,1,0:T(8,128)(2,1)S(1)}, bf16[1,160,1280]{2,1,0:T(8,128)(2,1)S(1)}, u32[]{:S(2)}, u32[]{:S(2)}) collective-permute-start(bf16[1,160,1280]{2,1,0:T(8,128)(2,1)S(1)} %get-tuple-element.36), channel_id=1, source_target_pairs={{24,0},{12,4},{0,8},{20,12},{8,16},{28,20},{16,24},{4,28},{25,1},{... | collective-permute-start | bytes 1228808 | tf_op jit(solution)/shard_map/ppermute | solution.py:452
  81.5 17.6 %collective-permute-start.23 = (bf16[1,160,768]{2,1,0:T(8,128)(2,1)S(1)}, bf16[1,160,768]{2,1,0:T(8,128)(2,1)S(1)}, u32[]{:S(2)}, u32[]{:S(2)}) collective-permute-start(bf16[1,160,768]{2,1,0:T(8,128)(2,1)S(1)} %slice.23), channel_id=1, source_target_pairs={{24,0},{12,4},{0,8},{20,12},{8,16},{28,20},{16,24},{4,28},{25,1},{... | collective-permute-start | bytes 737288 | tf_op jit(solution)/shard_map/ppermute | solution.py:452
  85.7 15.0 %collective-permute-start.22 = (bf16[1,160,512]{2,1,0:T(8,128)(2,1)S(1)}, bf16[1,160,512]{2,1,0:T(8,128)(2,1)S(1)}, u32[]{:S(2)}, u32[]{:S(2)}) collective-permute-start(bf16[1,160,512]{2,1,0:T(8,128)(2,1)S(1)} %slice.22), channel_id=1, source_target_pairs={{24,0},{12,4},{0,8},{20,12},{8,16},{28,20},{16,24},{4,28},{25,1},{... | collective-permute-start | bytes 491528 | tf_op jit(solution)/shard_map/ppermute | solution.py:452

commit v9 on v8

--- a/solution.py
+++ b/solution.py
@@ -432,10 +432,9 @@
 
     cuts = [slice(first * HEAD, (first + size) * HEAD) for first, size in spans]
     value_halves = [values[:, :, cut] for cut in cuts]
-    tail = (heads - half) // 5 * 2
-    ends = [0, half, heads - tail, heads]
-    value_thirds = value_halves[:1] + [
-        values[:, :, start * HEAD : stop * HEAD] for start, stop in zip(ends[1:], ends[2:])
+    ends = [0, heads - heads // 5, heads]
+    value_parts = [
+        values[:, :, start * HEAD : stop * HEAD] for start, stop in zip(ends, ends[1:])
     ]
     beyond = [(a, b) for a, b in toward if abs(a - b) != 2]
     within = [(a, b) for a, b in toward if abs(a - b) == 2]
@@ -449,7 +448,7 @@
         ),
     ]
     key_two = lax.ppermute(keys, "frame", away)
-    value_two = [lax.ppermute(piece, "frame", away) for piece in value_thirds]
+    value_two = [lax.ppermute(piece, "frame", away) for piece in value_parts]
     query_twin = []
     for cut in cuts:
         query_twin.append(lax.ppermute(queries[:, :, cut], "frame", twin))
@@ -475,7 +474,7 @@
             [keys, key_one],
             [(values,), value_one[span]],
             twin_rule,
-            (narrow, narrow, full),
+            (full, narrow, full),
             first,
             size,
         )
@@ -489,7 +488,10 @@
         from_twin.append(lax.ppermute(whole, "frame", twin))
 
     early_score = scored(
-        band, queries, [keys, key_even], lambda own, other, odd_frame, has_odd: [True, own[2] >= 1]
+        band,
+        queries,
+        [keys, key_even],
+        lambda own, other, odd_frame, has_odd: [True, own[2] >= 1],
     )
     late_score = scored(
         band,
@@ -501,7 +503,8 @@
         ],
     )
     near = neared(
-        [early_score, late_score], [[(values,)], [(value_even,)], value_one, [(value_odd,)]]
+        [early_score, late_score],
+        [[(values,)], [(value_even,)], value_one, [(value_odd,)]],
     )
     far_score = scored(
         band,

time: 102 us -> 109 us (1.069)
  the two profiles are of different devices: /device:TPU:1 before, /device:TPU:6 now
where the time goes in v9:
time: 109 us; the launch traced here: 108 us
  waiting for transfers between devices  44.7 us (41%)
  starting transfers between devices  37.7 us (35%)
  Pallas kernels  24.1 us (22%)
  local copies, waits for them, and re-layouts  1.45 us (1%)
    ppermute x1, waiting for transfers between devices, per_device(): lax.ppermute(value_halves[1], 'frame', beyond)  17.4 us
    ppermute x1, waiting for transfers between devices, per_device(): key_two = lax.ppermute(keys, 'frame', away)  11.7 us
    pallas_call x3, Pallas kernels, scored(): pl.pallas_call(functools.partial(score_kernel, heads, rule), in_specs=[SM...  8.84 us
    pallas_call x2, Pallas kernels, parts(): pl.pallas_call(functools.partial(parts_kernel, len(queries), len(keys), s...  7.27 us
    ppermute x2, waiting for transfers between devices, per_device(): back_odd = lax.ppermute(odd_twin, 'row', odd)  7.19 us
    ppermute x2, starting transfers between devices, per_device(): twin_odd = [lax.ppermute(query_twin[span], 'row', odd) for span in (0, 1)]  6.18 us
    ppermute x2, starting transfers between devices, per_device(): value_two = [lax.ppermute(piece, 'frame', away) for piece in value_parts]  4.62 us
    ppermute x2, waiting for transfers between devices, per_device(): twin_odd = [lax.ppermute(query_twin[span], 'row', odd) for span in (0, 1)]  4.54 us
  transfers between devices with their start and end apart: 24, of which 6 were waited for; matrix products, arithmetic and copies ran while one was open for 0% of the time, Pallas kernels for 21%

profile of v9, /device:TPU:6, one launch (start us, length us, event | category | flops | bytes accessed | tf_op | source)
XLA Modules:
  0.0 108.4 jit_solution(363710749575266134)
XLA Ops:
  0.0 1.3 %fusion = (bf16[1,160,1280]{2,1,0:T(8,128)(2,1)S(1)}, bf16[1,160,1280]{2,1,0:T(8,128)(2,1)S(1)}) fusion(bf16[1,160,2560]{2,1,0:T(8,128)(2,1)} %query_ref.5), kind=kLoop, calls=%fused_computation | loop fusion | bytes 1638400 | tf_op jit(solution)/shard_map/slice | solution.py:454
  1.9 3.5 %collective-permute-start.6 = (bf16[1,160,1280]{2,1,0:T(8,128)(2,1)S(1)}, bf16[1,160,1280]{2,1,0:T(8,128)(2,1)S(1)}, u32[]{:S(2)}, u32[]{:S(2)}) collective-permute-start(bf16[1,160,1280]{2,1,0:T(8,128)(2,1)S(1)} %get-tuple-element.35), channel_id=1, source_target_pairs={{4,12},{8,0},{12,20},{16,8},{20,28},{24,16},{5,13},{9,1},{13,21},{... | collective-permute-start | bytes 1228808 | tf_op jit(solution)/shard_map/ppermute | solution.py:446
  5.5 1.6 %collective-permute-start.2 = (bf16[1,160,2560]{2,1,0:T(8,128)(2,1)S(1)}, bf16[1,160,2560]{2,1,0:T(8,128)(2,1)S(1)}, u32[]{:S(2)}, u32[]{:S(2)}) collective-permute-start(bf16[1,160,2560]{2,1,0:T(8,128)(2,1)S(1)} %copy-done.2), channel_id=1, source_target_pairs={{0,24},{4,12},{8,0},{12,20},{16,8},{20,28},{24,16},{28,4},{1,25},{... | collective-permute-start | bytes 2457608 | tf_op jit(solution)/shard_map/ppermute | solution.py:442
  7.1 1.3 %collective-permute-start.7 = (bf16[1,160,1280]{2,1,0:T(8,128)(2,1)S(1)}, bf16[1,160,1280]{2,1,0:T(8,128)(2,1)S(1)}, u32[]{:S(2)}, u32[]{:S(2)}) collective-permute-start(bf16[1,160,1280]{2,1,0:T(8,128)(2,1)S(1)} %get-tuple-element.35), channel_id=1, source_target_pairs={{0,24},{28,4},{1,25},{29,5},{2,26},{30,6},{3,27},{31,7}} | collective-permute-start | bytes 1228808 | tf_op jit(solution)/shard_map/ppermute | solution.py:447
  8.4 3.6 %collective-permute-start.9 = (s32[1,5]{1,0:T(1,128)S(1)}, s32[1,5]{1,0:T(1,128)S(1)}, u32[]{:S(2)}, u32[]{:S(2)}) collective-permute-start(s32[1,5]{1,0:T(1,128)S(1)} %copy-done.3), channel_id=1, source_target_pairs={{0,4},{4,0},{8,12},{12,8},{16,20},{20,16},{24,28},{28,24},{1,5},{5... | collective-permute-start | bytes 68 | tf_op jit(solution)/shard_map/ppermute | solution.py:455
  11.9 1.5 %collective-permute-done.9.refs_1_ = s32[1,5]{1,0:T(1,128)S(1)} collective-permute-done((s32[1,5]{1,0:T(1,128)S(1)}, s32[1,5]{1,0:T(1,128)S(1)}, u32[]{:S(2)}, u32[]{:S(2)}) %collective-permute-start.9) | collective-permute-done | bytes 52 | tf_op jit(solution)/shard_map/ppermute | solution.py:455
  13.5 2.0 %collective-permute-start.10 = (bf16[1,160,1280]{2,1,0:T(8,128)(2,1)S(1)}, bf16[1,160,1280]{2,1,0:T(8,128)(2,1)S(1)}, u32[]{:S(2)}, u32[]{:S(2)}) collective-permute-start(bf16[1,160,1280]{2,1,0:T(8,128)(2,1)S(1)} %get-tuple-element.34), channel_id=1, source_target_pairs={{0,4},{4,0},{8,12},{12,8},{16,20},{20,16},{24,28},{28,24},{1,5},{5... | collective-permute-start | bytes 1228808 | tf_op jit(solution)/shard_map/ppermute | solution.py:454
  15.5 2.5 %collective-permute-start.18 = (bf16[1,160,1280]{2,1,0:T(8,128)(2,1)S(1)}, bf16[1,160,1280]{2,1,0:T(8,128)(2,1)S(1)}, u32[]{:S(2)}, u32[]{:S(2)}) collective-permute-start(bf16[1,160,1280]{2,1,0:T(8,128)(2,1)S(1)} %collective-permute-done.16.refs_4_), channel_id=1, source_target_pairs={{1,2},{2,1},{5,6},{6,5},{9,10},{10,9},{13,14},{14,13},{17,18},{18,... | collective-permute-start | bytes 1228808 | tf_op jit(solution)/shard_map/ppermute | solution.py:461
  18.1 17.4 %collective-permute-done.7.refs_8_.refs_9_ = bf16[1,160,1280]{2,1,0:T(8,128)(2,1)S(1)} collective-permute-done((bf16[1,160,1280]{2,1,0:T(8,128)(2,1)S(1)}, bf16[1,160,1280]{2,1,0:T(8,128)(2,1)S(1)}, u32[]{:S(2)}, u32[]{:S(2)}) %collective-permute-start.7) | collective-permute-done | bytes 409632 | tf_op jit(solution)/shard_map/ppermute | solution.py:447
  35.5 1.9 %collective-permute-start.3 = (bf16[1,160,2560]{2,1,0:T(8,128)(2,1)S(1)}, bf16[1,160,2560]{2,1,0:T(8,128)(2,1)S(1)}, u32[]{:S(2)}, u32[]{:S(2)}) collective-permute-start(bf16[1,160,2560]{2,1,0:T(8,128)(2,1)S(1)} %copy-done.2), channel_id=1, source_target_pairs={{1,2},{2,1},{5,6},{6,5},{9,10},{10,9},{13,14},{14,13},{17,18},{18,... | collective-permute-start | bytes 2457608 | tf_op jit(solution)/shard_map/ppermute | solution.py:457
  37.5 3.6 %collective-permute-start.12 = (bf16[1,160,1280]{2,1,0:T(8,128)(2,1)S(1)}, bf16[1,160,1280]{2,1,0:T(8,128)(2,1)S(1)}, u32[]{:S(2)}, u32[]{:S(2)}) collective-permute-start(bf16[1,160,1280]{2,1,0:T(8,128)(2,1)S(1)} %collective-permute-done.10.refs_4_), channel_id=1, source_target_pairs={{1,2},{2,1},{5,6},{6,5},{9,10},{10,9},{13,14},{14,13},{17,18},{18,... | collective-permute-start | bytes 1228808 | tf_op jit(solution)/shard_map/ppermute | solution.py:461
  41.2 3.7 %shard_map.52 = (f32[1,160,1408]{2,1,0:T(8,128)S(1)}, bf16[1,160,1408]{2,1,0:T(8,128)(2,1)S(1)}, f32[1,160,1408]{2,1,0:T(8,128)S(1)}) custom-call(s32[1,5]{1,0:T(1,128)S(1)} %copy-done.3, s32[1,5]{1,0:T(1,128)S(1)} %collective-permute-done.9.refs_1_, bf16[1,160,1280]{2,1,0:T(8,128)(2,1)S(1)} %collective-permute-done.17.refs_2_, ...), custom_call_target="tpu_custom_call" | custom-call | flops 786432000 | bytes 4096000 | tf_op jit(solution)/shard_map/pallas_call | solution.py:170
  44.9 2.2 %collective-permute-done.5.refs_6_.refs_8_ = bf16[1,160,1280]{2,1,0:T(8,128)(2,1)S(1)} collective-permute-done((bf16[1,160,1280]{2,1,0:T(8,128)(2,1)S(1)}, bf16[1,160,1280]{2,1,0:T(8,128)(2,1)S(1)}, u32[]{:S(2)}, u32[]{:S(2)}) %collective-permute-start.5) | collective-permute-done | bytes 409632 | tf_op jit(solution)/shard_map/ppermute | solution.py:444
  47.1 1.9 %collective-permute-start.20 = (bf16[1,160,1408]{2,1,0:T(8,128)(2,1)S(1)}, bf16[1,160,1408]{2,1,0:T(8,128)(2,1)S(1)}, u32[]{:S(2)}, u32[]{:S(2)}) collective-permute-start(bf16[1,160,1408]{2,1,0:T(8,128)(2,1)S(1)} %get-tuple-element.30), channel_id=1, source_target_pairs={{1,2},{2,1},{5,6},{6,5},{9,10},{10,9},{13,14},{14,13},{17,18},{18,... | collective-permute-start | bytes 1351688 | tf_op jit(solution)/shard_map/ppermute | solution.py:482
  49.0 4.5 %collective-permute-done.12.refs_3_ = bf16[1,160,1280]{2,1,0:T(8,128)(2,1)S(1)} collective-permute-done((bf16[1,160,1280]{2,1,0:T(8,128)(2,1)S(1)}, bf16[1,160,1280]{2,1,0:T(8,128)(2,1)S(1)}, u32[]{:S(2)}, u32[]{:S(2)}) %collective-permute-start.12) | collective-permute-done | bytes 409632 | tf_op jit(solution)/shard_map/ppermute | solution.py:461
  53.6 3.6 %shard_map.50 = (f32[1,160,1408]{2,1,0:T(8,128)S(1)}, bf16[1,160,1408]{2,1,0:T(8,128)(2,1)S(1)}, f32[1,160,1408]{2,1,0:T(8,128)S(1)}) custom-call(s32[1,5]{1,0:T(1,128)S(1)} %copy-done.3, s32[1,5]{1,0:T(1,128)S(1)} %collective-permute-done.9.refs_1_, bf16[1,160,1280]{2,1,0:T(8,128)(2,1)S(1)} %collective-permute-done.11.refs_2_, ...), custom_call_target="tpu_custom_call" | custom-call | flops 786432000 | bytes 4096000 | tf_op jit(solution)/shard_map/pallas_call | solution.py:170
  57.2 1.9 %collective-permute-start.14 = (bf16[1,160,1408]{2,1,0:T(8,128)(2,1)S(1)}, bf16[1,160,1408]{2,1,0:T(8,128)(2,1)S(1)}, u32[]{:S(2)}, u32[]{:S(2)}) collective-permute-start(bf16[1,160,1408]{2,1,0:T(8,128)(2,1)S(1)} %get-tuple-element.27), channel_id=1, source_target_pairs={{1,2},{2,1},{5,6},{6,5},{9,10},{10,9},{13,14},{14,13},{17,18},{18,... | collective-permute-start | bytes 1351688 | tf_op jit(solution)/shard_map/ppermute | solution.py:482
  59.7 7.2 %collective-permute-done.14.refs_2_ = bf16[1,160,1408]{2,1,0:T(8,128)(2,1)S(1)} collective-permute-done((bf16[1,160,1408]{2,1,0:T(8,128)(2,1)S(1)}, bf16[1,160,1408]{2,1,0:T(8,128)(2,1)S(1)}, u32[]{:S(2)}, u32[]{:S(2)}) %collective-permute-start.14) | collective-permute-done | bytes 450592 | tf_op jit(solution)/shard_map/ppermute | solution.py:482
  66.9 3.8 %collective-permute-start = (bf16[1,160,2560]{2,1,0:T(8,128)(2,1)S(1)}, bf16[1,160,2560]{2,1,0:T(8,128)(2,1)S(1)}, u32[]{:S(2)}, u32[]{:S(2)}) collective-permute-start(bf16[1,160,2560]{2,1,0:T(8,128)(2,1)S(1)} %copy-done.2), channel_id=1, source_target_pairs={{24,0},{12,4},{0,8},{20,12},{8,16},{28,20},{16,24},{4,28},{25,1},{... | collective-permute-start | bytes 2457608 | tf_op jit(solution)/shard_map/ppermute | solution.py:450
  70.8 1.9 %collective-permute-start.8 = (bf16[1,160,2560]{2,1,0:T(8,128)(2,1)S(1)}, bf16[1,160,2560]{2,1,0:T(8,128)(2,1)S(1)}, u32[]{:S(2)}, u32[]{:S(2)}) collective-permute-start(bf16[1,160,2560]{2,1,0:T(8,128)(2,1)S(1)} %copy-done), channel_id=1, source_target_pairs={{1,2},{2,1},{5,6},{6,5},{9,10},{10,9},{13,14},{14,13},{17,18},{18,... | collective-permute-start | bytes 2457608 | tf_op jit(solution)/shard_map/ppermute | solution.py:459
  73.1 1.2 %shard_map.53 = bf16[1,160,1408]{2,1,0:T(8,128)(2,1)S(1)} custom-call(s32[1,5]{1,0:T(1,128)S(1)} %copy-done.3, f32[1,160,1408]{2,1,0:T(8,128)S(1)} %get-tuple-element.28.refs_0_, f32[1,160,1408]{2,1,0:T(8,128)S(1)} %collective-permute-done.19.refs_1_, bf16[1,160,1408]{2,1,0:T(8,128)(2,1)S(1)} %collective-permute-done.20.refs_2_), custom_call_target="tpu_custom_call" | custom-call | flops 1351680 | bytes 1802240 | tf_op jit(solution)/shard_map/pallas_call | solution.py:210
  74.3 1.2 %shard_map.51 = bf16[1,160,1408]{2,1,0:T(8,128)(2,1)S(1)} custom-call(s32[1,5]{1,0:T(1,128)S(1)} %copy-done.3, f32[1,160,1408]{2,1,0:T(8,128)S(1)} %get-tuple-element.25.refs_0_, f32[1,160,1408]{2,1,0:T(8,128)S(1)} %collective-permute-done.13.refs_1_, bf16[1,160,1408]{2,1,0:T(8,128)(2,1)S(1)} %collective-permute-done.14.refs_2_), custom_call_target="tpu_custom_call" | custom-call | flops 1351680 | bytes 1802240 | tf_op jit(solution)/shard_map/pallas_call | solution.py:210
  75.8 1.8 %collective-permute-start.15 = (bf16[1,160,1408]{2,1,0:T(8,128)(2,1)S(1)}, bf16[1,160,1408]{2,1,0:T(8,128)(2,1)S(1)}, u32[]{:S(2)}, u32[]{:S(2)}) collective-permute-start(bf16[1,160,1408]{2,1,0:T(8,128)(2,1)S(1)} %shard_map.51), channel_id=1, source_target_pairs={{0,4},{4,0},{8,12},{12,8},{16,20},{20,16},{24,28},{28,24},{1,5},{5... | collective-permute-start | bytes 1351688 | tf_op jit(solution)/shard_map/ppermute | solution.py:488
  77.7 11.7 %collective-permute-done.refs_0_ = bf16[1,160,2560]{2,1,0:T(8,128)(2,1)S(1)} collective-permute-done((bf16[1,160,2560]{2,1,0:T(8,128)(2,1)S(1)}, bf16[1,160,2560]{2,1,0:T(8,128)(2,1)S(1)}, u32[]{:S(2)}, u32[]{:S(2)}) %collective-permute-start) | collective-permute-done | bytes 819232 | tf_op jit(solution)/shard_map/ppermute | solution.py:450
  89.4 4.3 %collective-permute-start.22 = (bf16[1,160,512]{2,1,0:T(8,128)(2,1)S(1)}, bf16[1,160,512]{2,1,0:T(8,128)(2,1)S(1)}, u32[]{:S(2)}, u32[]{:S(2)}) collective-permute-start(bf16[1,160,512]{2,1,0:T(8,128)(2,1)S(1)} %slice.22), channel_id=1, source_target_pairs={{24,0},{12,4},{0,8},{20,12},{8,16},{28,20},{16,24},{4,28},{25,1},{... | collective-permute-start | bytes 491528 | tf_op jit(solution)/shard_map/ppermute | solution.py:451
  93.7 2.0 %shard_map.46 = (bf16[1,20,160,160]{3,2,1,0:T(8,128)(2,1)S(1)}, f32[2,160,128]{2,1,0:T(8,128)S(1)}) custom-call(s32[1,5]{1,0:T(1,128)S(1)} %copy-done.3, bf16[1,160,2560]{2,1,0:T(8,128)(2,1)S(1)} %copy-done.1, bf16[1,160,2560]{2,1,0:T(8,128)(2,1)S(1)} %collective-permute-done.refs_0_), custom_call_target="tpu_custom_call" | custom-call | flops 131072000 | bytes 2457600 | tf_op jit(solution)/shard_map/pallas_call | solution.py:253
  95.7 3.5 %shard_map.48 = (bf16[2,20,160,160]{3,2,1,0:T(8,128)(2,1)S(1)}, f32[2,160,128]{2,1,0:T(8,128)S(1)}) custom-call(s32[1,5]{1,0:T(1,128)S(1)} %copy-done.3, bf16[1,160,2560]{2,1,0:T(8,128)(2,1)S(1)} %copy-done.1, bf16[1,160,2560]{2,1,0:T(8,128)(2,1)S(1)} %collective-permute-done.2.refs_0_.refs_6_, bf16[1,160,2560]{2,1,0:T(8,128)(2,1)S(1)} %collective-permute-done.3.refs_1_), custom_call_target="tpu_custom_call" | custom-call | flops 262144000 | bytes 2457600 | tf_op jit(solution)/shard_map/pallas_call | solution.py:253
  99.2 3.4 %shard_map.47 = (bf16[2,20,160,160]{3,2,1,0:T(8,128)(2,1)S(1)}, f32[2,160,128]{2,1,0:T(8,128)S(1)}) custom-call(s32[1,5]{1,0:T(1,128)S(1)} %copy-done.3, bf16[1,160,2560]{2,1,0:T(8,128)(2,1)S(1)} %copy-done.1, bf16[1,160,2560]{2,1,0:T(8,128)(2,1)S(1)} %copy-done.2, bf16[1,160,2560]{2,1,0:T(8,128)(2,1)S(1)} %collective-permute-done.1.refs_1_), custom_call_target="tpu_custom_call" | custom-call | flops 262144000 | bytes 2457600 | tf_op jit(solution)/shard_map/pallas_call | solution.py:253
  102.5 2.4 %shard_map.49.near_ref = f32[1,160,2688]{2,1,0:T(8,128)S(1)} custom-call(bf16[2,20,160,160]{3,2,1,0:T(8,128)(2,1)S(1)} %get-tuple-element.21.refs_0_, bf16[2,20,160,160]{3,2,1,0:T(8,128)(2,1)S(1)} %get-tuple-element.22.refs_1_, f32[2,160,128]{2,1,0:T(8,128)S(1)} %get-tuple-element.23.refs_2_, f32[2,160,128]{2,1,0:T(8,128)S(1)} %get-tuple-element.24.refs_3_, ...), custom_call_target="tpu_custom_call" | custom-call | flops 524288000 | bytes 6553600 | tf_op jit(solution)/shard_map/pallas_call | solution.py:309
  105.0 0.8 shard_map.54
  105.8 1.4 %shard_map.55.refs_0_ = bf16[1,160,2560]{2,1,0:T(8,128)(2,1)} custom-call(bf16[1,20,160,160]{3,2,1,0:T(8,128)(2,1)S(1)} %get-tuple-element.19.weight_ref, bf16[160,128]{1,0:T(8,128)(2,1)S(1)} %get-tuple-element.31.coef_ref, bf16[1,160,2048]{2,1,0:T(8,128)(2,1)S(1)} %collective-permute-done.23.value_ref, f32[1,160,2560]{2,1,0:T(8,128)S(1)} %get-tuple-element.32.base_ref), custom_call_target="tpu_custom_call" | custom-call | flops 104857600 | bytes 2621440 | tf_op jit(solution)/shard_map/pallas_call | solution.py:400
  107.2 1.0 shard_map.56
  (39 shorter events, 2.1 us)
Async XLA Ops:
  0.0 1.9 %copy-start = (bf16[1,160,2560]{2,1,0:T(8,128)(2,1)S(1)}, bf16[1,160,2560]{2,1,0:T(8,128)(2,1)}, u32[]{:S(2)}) copy-start(bf16[1,160,2560]{2,1,0:T(8,128)(2,1)} %refs_7_.3) | copy-start | bytes 2457604
  0.0 5.5 %copy-start.2 = (bf16[1,160,2560]{2,1,0:T(8,128)(2,1)S(1)}, bf16[1,160,2560]{2,1,0:T(8,128)(2,1)}, u32[]{:S(2)}) copy-start(bf16[1,160,2560]{2,1,0:T(8,128)(2,1)} %refs_5_.3) | copy-start | bytes 2457604
  0.0 8.4 %copy-start.3 = (s32[1,5]{1,0:T(1,128)S(1)}, s32[1,5]{1,0:T(1,128)}, u32[]{:S(2)}) copy-start(s32[1,5]{1,0:T(1,128)} %band_ref.9) | copy-start | bytes 64
  1.3 14.2 %collective-permute-start.16 = (bf16[1,160,1280]{2,1,0:T(8,128)(2,1)S(1)}, bf16[1,160,1280]{2,1,0:T(8,128)(2,1)S(1)}, u32[]{:S(2)}, u32[]{:S(2)}) collective-permute-start(bf16[1,160,1280]{2,1,0:T(8,128)(2,1)S(1)} %get-tuple-element.33), channel_id=1, source_target_pairs={{0,4},{4,0},{8,12},{12,8},{16,20},{20,16},{24,28},{28,24},{1,5},{5... | collective-permute-start | bytes 1228808 | tf_op jit(solution)/shard_map/ppermute | solution.py:454
  1.9 13.6 %collective-permute-start.6 = (bf16[1,160,1280]{2,1,0:T(8,128)(2,1)S(1)}, bf16[1,160,1280]{2,1,0:T(8,128)(2,1)S(1)}, u32[]{:S(2)}, u32[]{:S(2)}) collective-permute-start(bf16[1,160,1280]{2,1,0:T(8,128)(2,1)S(1)} %get-tuple-element.35), channel_id=1, source_target_pairs={{4,12},{8,0},{12,20},{16,8},{20,28},{24,16},{5,13},{9,1},{13,21},{... | collective-permute-start | bytes 1228808 | tf_op jit(solution)/shard_map/ppermute | solution.py:446
  5.5 35.7 %collective-permute-start.2 = (bf16[1,160,2560]{2,1,0:T(8,128)(2,1)S(1)}, bf16[1,160,2560]{2,1,0:T(8,128)(2,1)S(1)}, u32[]{:S(2)}, u32[]{:S(2)}) collective-permute-start(bf16[1,160,2560]{2,1,0:T(8,128)(2,1)S(1)} %copy-done.2), channel_id=1, source_target_pairs={{0,24},{4,12},{8,0},{12,20},{16,8},{20,28},{24,16},{28,4},{1,25},{... | collective-permute-start | bytes 2457608 | tf_op jit(solution)/shard_map/ppermute | solution.py:442
  7.1 28.4 %collective-permute-start.7 = (bf16[1,160,1280]{2,1,0:T(8,128)(2,1)S(1)}, bf16[1,160,1280]{2,1,0:T(8,128)(2,1)S(1)}, u32[]{:S(2)}, u32[]{:S(2)}) collective-permute-start(bf16[1,160,1280]{2,1,0:T(8,128)(2,1)S(1)} %get-tuple-element.35), channel_id=1, source_target_pairs={{0,24},{28,4},{1,25},{29,5},{2,26},{30,6},{3,27},{31,7}} | collective-permute-start | bytes 1228808 | tf_op jit(solution)/shard_map/ppermute | solution.py:447
  8.4 5.1 %collective-permute-start.9 = (s32[1,5]{1,0:T(1,128)S(1)}, s32[1,5]{1,0:T(1,128)S(1)}, u32[]{:S(2)}, u32[]{:S(2)}) collective-permute-start(s32[1,5]{1,0:T(1,128)S(1)} %copy-done.3), channel_id=1, source_target_pairs={{0,4},{4,0},{8,12},{12,8},{16,20},{20,16},{24,28},{28,24},{1,5},{5... | collective-permute-start | bytes 68 | tf_op jit(solution)/shard_map/ppermute | solution.py:455
  13.5 22.0 %collective-permute-start.10 = (bf16[1,160,1280]{2,1,0:T(8,128)(2,1)S(1)}, bf16[1,160,1280]{2,1,0:T(8,128)(2,1)S(1)}, u32[]{:S(2)}, u32[]{:S(2)}) collective-permute-start(bf16[1,160,1280]{2,1,0:T(8,128)(2,1)S(1)} %get-tuple-element.34), channel_id=1, source_target_pairs={{0,4},{4,0},{8,12},{12,8},{16,20},{20,16},{24,28},{28,24},{1,5},{5... | collective-permute-start | bytes 1228808 | tf_op jit(solution)/shard_map/ppermute | solution.py:454
  15.5 21.9 %collective-permute-start.17 = (bf16[1,160,1280]{2,1,0:T(8,128)(2,1)S(1)}, bf16[1,160,1280]{2,1,0:T(8,128)(2,1)S(1)}, u32[]{:S(2)}, u32[]{:S(2)}) collective-permute-start(bf16[1,160,1280]{2,1,0:T(8,128)(2,1)S(1)} %collective-permute-done.16.refs_4_), channel_id=1, source_target_pairs={{0,1},{1,0},{2,3},{3,2},{4,5},{5,4},{6,7},{7,6},{8,9},{9,8},{10,11... | collective-permute-start | bytes 1228808 | tf_op jit(solution)/shard_map/ppermute | solution.py:460
  15.5 22.0 %collective-permute-start.18 = (bf16[1,160,1280]{2,1,0:T(8,128)(2,1)S(1)}, bf16[1,160,1280]{2,1,0:T(8,128)(2,1)S(1)}, u32[]{:S(2)}, u32[]{:S(2)}) collective-permute-start(bf16[1,160,1280]{2,1,0:T(8,128)(2,1)S(1)} %collective-permute-done.16.refs_4_), channel_id=1, source_target_pairs={{1,2},{2,1},{5,6},{6,5},{9,10},{10,9},{13,14},{14,13},{17,18},{18,... | collective-permute-start | bytes 1228808 | tf_op jit(solution)/shard_map/ppermute | solution.py:461
  35.5 11.6 %collective-permute-start.5 = (bf16[1,160,1280]{2,1,0:T(8,128)(2,1)S(1)}, bf16[1,160,1280]{2,1,0:T(8,128)(2,1)S(1)}, u32[]{:S(2)}, u32[]{:S(2)}) collective-permute-start(bf16[1,160,1280]{2,1,0:T(8,128)(2,1)S(1)} %get-tuple-element.36), channel_id=1, source_target_pairs={{0,24},{4,12},{8,0},{12,20},{16,8},{20,28},{24,16},{28,4},{1,25},{... | collective-permute-start | bytes 1228808 | tf_op jit(solution)/shard_map/ppermute | solution.py:444
  35.5 23.6 %collective-permute-start.3 = (bf16[1,160,2560]{2,1,0:T(8,128)(2,1)S(1)}, bf16[1,160,2560]{2,1,0:T(8,128)(2,1)S(1)}, u32[]{:S(2)}, u32[]{:S(2)}) collective-permute-start(bf16[1,160,2560]{2,1,0:T(8,128)(2,1)S(1)} %copy-done.2), channel_id=1, source_target_pairs={{1,2},{2,1},{5,6},{6,5},{9,10},{10,9},{13,14},{14,13},{17,18},{18,... | collective-permute-start | bytes 2457608 | tf_op jit(solution)/shard_map/ppermute | solution.py:457
  37.5 11.6 %collective-permute-start.11 = (bf16[1,160,1280]{2,1,0:T(8,128)(2,1)S(1)}, bf16[1,160,1280]{2,1,0:T(8,128)(2,1)S(1)}, u32[]{:S(2)}, u32[]{:S(2)}) collective-permute-start(bf16[1,160,1280]{2,1,0:T(8,128)(2,1)S(1)} %collective-permute-done.10.refs_4_), channel_id=1, source_target_pairs={{0,1},{1,0},{2,3},{3,2},{4,5},{5,4},{6,7},{7,6},{8,9},{9,8},{10,11... | collective-permute-start | bytes 1228808 | tf_op jit(solution)/shard_map/ppermute | solution.py:460
  37.5 16.0 %collective-permute-start.12 = (bf16[1,160,1280]{2,1,0:T(8,128)(2,1)S(1)}, bf16[1,160,1280]{2,1,0:T(8,128)(2,1)S(1)}, u32[]{:S(2)}, u32[]{:S(2)}) collective-permute-start(bf16[1,160,1280]{2,1,0:T(8,128)(2,1)S(1)} %collective-permute-done.10.refs_4_), channel_id=1, source_target_pairs={{1,2},{2,1},{5,6},{6,5},{9,10},{10,9},{13,14},{14,13},{17,18},{18,... | collective-permute-start | bytes 1228808 | tf_op jit(solution)/shard_map/ppermute | solution.py:461
  44.9 25.9 %collective-permute-start.19 = (f32[1,160,1408]{2,1,0:T(8,128)S(1)}, f32[1,160,1408]{2,1,0:T(8,128)S(1)}, u32[]{:S(2)}, u32[]{:S(2)}) collective-permute-start(f32[1,160,1408]{2,1,0:T(8,128)S(1)} %get-tuple-element.29), channel_id=1, source_target_pairs={{0,1},{1,0},{2,3},{3,2},{4,5},{5,4},{6,7},{7,6},{8,9},{9,8},{10,11... | collective-permute-start | bytes 2703368 | tf_op jit(solution)/shard_map/ppermute | solution.py:481
  47.1 12.1 %collective-permute-start.20 = (bf16[1,160,1408]{2,1,0:T(8,128)(2,1)S(1)}, bf16[1,160,1408]{2,1,0:T(8,128)(2,1)S(1)}, u32[]{:S(2)}, u32[]{:S(2)}) collective-permute-start(bf16[1,160,1408]{2,1,0:T(8,128)(2,1)S(1)} %get-tuple-element.30), channel_id=1, source_target_pairs={{1,2},{2,1},{5,6},{6,5},{9,10},{10,9},{13,14},{14,13},{17,18},{18,... | collective-permute-start | bytes 1351688 | tf_op jit(solution)/shard_map/ppermute | solution.py:482
  57.2 15.6 %collective-permute-start.13 = (f32[1,160,1408]{2,1,0:T(8,128)S(1)}, f32[1,160,1408]{2,1,0:T(8,128)S(1)}, u32[]{:S(2)}, u32[]{:S(2)}) collective-permute-start(f32[1,160,1408]{2,1,0:T(8,128)S(1)} %get-tuple-element.26), channel_id=1, source_target_pairs={{0,1},{1,0},{2,3},{3,2},{4,5},{5,4},{6,7},{7,6},{8,9},{9,8},{10,11... | collective-permute-start | bytes 2703368 | tf_op jit(solution)/shard_map/ppermute | solution.py:481
  57.2 9.7 %collective-permute-start.14 = (bf16[1,160,1408]{2,1,0:T(8,128)(2,1)S(1)}, bf16[1,160,1408]{2,1,0:T(8,128)(2,1)S(1)}, u32[]{:S(2)}, u32[]{:S(2)}) collective-permute-start(bf16[1,160,1408]{2,1,0:T(8,128)(2,1)S(1)} %get-tuple-element.27), channel_id=1, source_target_pairs={{1,2},{2,1},{5,6},{6,5},{9,10},{10,9},{13,14},{14,13},{17,18},{18,... | collective-permute-start | bytes 1351688 | tf_op jit(solution)/shard_map/ppermute | solution.py:482
  59.2 16.4 %collective-permute-start.1 = (bf16[1,160,2560]{2,1,0:T(8,128)(2,1)S(1)}, bf16[1,160,2560]{2,1,0:T(8,128)(2,1)S(1)}, u32[]{:S(2)}, u32[]{:S(2)}) collective-permute-start(bf16[1,160,2560]{2,1,0:T(8,128)(2,1)S(1)} %copy-done.2), channel_id=1, source_target_pairs={{0,1},{1,0},{2,3},{3,2},{4,5},{5,4},{6,7},{7,6},{8,9},{9,8},{10,11... | collective-permute-start | bytes 2457608 | tf_op jit(solution)/shard_map/ppermute | solution.py:456
  59.3 16.6 %collective-permute-start.4 = (bf16[1,160,2560]{2,1,0:T(8,128)(2,1)S(1)}, bf16[1,160,2560]{2,1,0:T(8,128)(2,1)S(1)}, u32[]{:S(2)}, u32[]{:S(2)}) collective-permute-start(bf16[1,160,2560]{2,1,0:T(8,128)(2,1)S(1)} %copy-done), channel_id=1, source_target_pairs={{0,1},{1,0},{2,3},{3,2},{4,5},{5,4},{6,7},{7,6},{8,9},{9,8},{10,11... | collective-permute-start | bytes 2457608 | tf_op jit(solution)/shard_map/ppermute | solution.py:458
  66.9 22.5 %collective-permute-start = (bf16[1,160,2560]{2,1,0:T(8,128)(2,1)S(1)}, bf16[1,160,2560]{2,1,0:T(8,128)(2,1)S(1)}, u32[]{:S(2)}, u32[]{:S(2)}) collective-permute-start(bf16[1,160,2560]{2,1,0:T(8,128)(2,1)S(1)} %copy-done.2), channel_id=1, source_target_pairs={{24,0},{12,4},{0,8},{20,12},{8,16},{28,20},{16,24},{4,28},{25,1},{... | collective-permute-start | bytes 2457608 | tf_op jit(solution)/shard_map/ppermute | solution.py:450
  70.8 31.8 %collective-permute-start.8 = (bf16[1,160,2560]{2,1,0:T(8,128)(2,1)S(1)}, bf16[1,160,2560]{2,1,0:T(8,128)(2,1)S(1)}, u32[]{:S(2)}, u32[]{:S(2)}) collective-permute-start(bf16[1,160,2560]{2,1,0:T(8,128)(2,1)S(1)} %copy-done), channel_id=1, source_target_pairs={{1,2},{2,1},{5,6},{6,5},{9,10},{10,9},{13,14},{14,13},{17,18},{18,... | collective-permute-start | bytes 2457608 | tf_op jit(solution)/shard_map/ppermute | solution.py:459
  72.8 33.0 %collective-permute-start.23 = (bf16[1,160,2048]{2,1,0:T(8,128)(2,1)S(1)}, bf16[1,160,2048]{2,1,0:T(8,128)(2,1)S(1)}, u32[]{:S(2)}, u32[]{:S(2)}) collective-permute-start(bf16[1,160,2048]{2,1,0:T(8,128)(2,1)S(1)} %slice.23), channel_id=1, source_target_pairs={{24,0},{12,4},{0,8},{20,12},{8,16},{28,20},{16,24},{4,28},{25,1},{... | collective-permute-start | bytes 1966088 | tf_op jit(solution)/shard_map/ppermute | solution.py:451
  74.3 19.3 %copy-start.1 = (bf16[1,160,2560]{2,1,0:T(8,128)(2,1)S(1)}, bf16[1,160,2560]{2,1,0:T(8,128)(2,1)}, u32[]{:S(2)}) copy-start(bf16[1,160,2560]{2,1,0:T(8,128)(2,1)} %query_ref.5) | copy-start | bytes 2457604
  75.6 29.4 %collective-permute-start.21 = (bf16[1,160,1408]{2,1,0:T(8,128)(2,1)S(1)}, bf16[1,160,1408]{2,1,0:T(8,128)(2,1)S(1)}, u32[]{:S(2)}, u32[]{:S(2)}) collective-permute-start(bf16[1,160,1408]{2,1,0:T(8,128)(2,1)S(1)} %shard_map.53), channel_id=1, source_target_pairs={{0,4},{4,0},{8,12},{12,8},{16,20},{20,16},{24,28},{28,24},{1,5},{5... | collective-permute-start | bytes 1351688 | tf_op jit(solution)/shard_map/ppermute | solution.py:488
  75.8 29.2 %collective-permute-start.15 = (bf16[1,160,1408]{2,1,0:T(8,128)(2,1)S(1)}, bf16[1,160,1408]{2,1,0:T(8,128)(2,1)S(1)}, u32[]{:S(2)}, u32[]{:S(2)}) collective-permute-start(bf16[1,160,1408]{2,1,0:T(8,128)(2,1)S(1)} %shard_map.51), channel_id=1, source_target_pairs={{0,4},{4,0},{8,12},{12,8},{16,20},{20,16},{24,28},{28,24},{1,5},{5... | collective-permute-start | bytes 1351688 | tf_op jit(solution)/shard_map/ppermute | solution.py:488
  89.4 17.8 %collective-permute-start.22 = (bf16[1,160,512]{2,1,0:T(8,128)(2,1)S(1)}, bf16[1,160,512]{2,1,0:T(8,128)(2,1)S(1)}, u32[]{:S(2)}, u32[]{:S(2)}) collective-permute-start(bf16[1,160,512]{2,1,0:T(8,128)(2,1)S(1)} %slice.22), channel_id=1, source_target_pairs={{24,0},{12,4},{0,8},{20,12},{8,16},{28,20},{16,24},{4,28},{25,1},{... | collective-permute-start | bytes 491528 | tf_op jit(solution)/shard_map/ppermute | solution.py:451

commit v10 on v9

--- a/solution.py
+++ b/solution.py
@@ -186,8 +186,11 @@
     )(*bands, *queries, *keys, *flat)
 
 
-def merge_kernel(heads, rule, band_ref, *refs):
-    blocks, out_ref = refs[:-1], refs[-1]
+def merge_kernel(heads, rule, first, band_ref, *refs):
+    if first:
+        earlier_ref, blocks, out_ref = refs[0], refs[1:-1], refs[-1]
+    else:
+        blocks, (out_ref, log_ref) = refs[:-2], refs[-2:]
     keeps = kept(rule, band_ref, None)
     logs = []
     for keep, block in zip(keeps, blocks):
@@ -201,24 +204,35 @@
             spread(table, n) * block[0, :, cols].astype(jnp.float32)
             for table, block in zip(tables, blocks)
         ).astype(out_ref.dtype)
-    out_ref[0, :, column(heads)] = packed(log)
-
-
-def merged(band, blocks, rule):
+    if first:
+        lane = lax.broadcasted_iota(jnp.int32, log.shape, 1)
+        log = jnp.where(lane < first, earlier_ref[...], pltpu.roll(log, first, 1))
+        out_ref[0, :, column(heads)] = packed(log)
+    else:
+        log_ref[...] = log
+
+
+def merged(band, blocks, rule, earlier, first):
     rows, width = blocks[0].shape[1:]
     heads = width // HEAD - 1
+    extra = [] if earlier is None else [earlier]
+    out_shape = [
+        jax.ShapeDtypeStruct((1, rows, width - (0 if extra else HEAD)), jnp.bfloat16)
+    ]
+    if not extra:
+        out_shape.append(jax.ShapeDtypeStruct((rows, HEAD), jnp.float32))
     return pl.pallas_call(
-        functools.partial(merge_kernel, heads, rule),
-        in_specs=[SMEM] + [VMEM] * len(blocks),
-        out_specs=VMEM,
-        out_shape=jax.ShapeDtypeStruct((1, rows, width), jnp.bfloat16),
+        functools.partial(merge_kernel, heads, rule, first),
+        in_specs=[SMEM] + [VMEM] * (len(extra) + len(blocks)),
+        out_specs=[VMEM] * len(out_shape),
+        out_shape=out_shape,
         compiler_params=GRANT,
         cost_estimate=pl.CostEstimate(
             flops=2 * rows * width * len(blocks),
             bytes_accessed=2 * rows * width * (len(blocks) + 1),
             transcendentals=0,
         ),
-    )(band, *blocks)
+    )(band, *extra, *blocks)
 
 
 def score_kernel(heads, rule, band_ref, query_ref, *refs):
@@ -328,14 +342,8 @@
 
 def base_kernel(sizes, heads, table_ref, near_ref, *refs):
     pieces, (out_ref, coef_ref) = refs[: len(sizes)], refs[len(sizes) :]
-    lane = lax.broadcasted_iota(jnp.int32, (out_ref.shape[1], HEAD), 1)
-    log, place = None, []
-    for at, (piece, size) in enumerate(zip(pieces, sizes)):
-        part = read_log(piece, size)
-        if at:
-            part = jnp.where(lane >= len(place), pltpu.roll(part, len(place), 1), log)
-        log = part
-        place += [(at, n) for n in range(size)]
+    place = [(at, n) for at, size in enumerate(sizes) for n in range(size)]
+    log = read_log(pieces[-1], sizes[-1])
     weights, _ = shares([table_ref[0], read_log(near_ref, heads), log])
     coef_ref[...] = packed(weights[0] * table_ref[1])
     near_table, twin_table = packed(weights[1]), packed(weights[2])
@@ -351,7 +359,8 @@
     table = score[1]
     rows = near.shape[1]
     heads = near.shape[2] // HEAD - 1
-    sizes = tuple(piece.shape[2] // HEAD - 1 for piece in pieces)
+    sizes = tuple(piece.shape[2] // HEAD for piece in pieces[:-1])
+    sizes += (heads - sum(sizes),)
     return pl.pallas_call(
         functools.partial(base_kernel, sizes, heads),
         in_specs=[VMEM] * (2 + len(pieces)),
@@ -467,6 +476,7 @@
         return [beside, beside, [here >= 0, there >= 0]]
 
     from_twin = []
+    merge_log = None
     for span, (first, size) in enumerate(spans):
         even_twin, odd_twin, own_twin = parts(
             (band, band_twin),
@@ -484,8 +494,11 @@
             band,
             [own_twin, back_even, back_odd],
             lambda own, other, odd_frame, has_odd: [True, True, has_odd],
+            merge_log,
+            first,
         )
-        from_twin.append(lax.ppermute(whole, "frame", twin))
+        merge_log = whole[-1]
+        from_twin.append(lax.ppermute(whole[0], "frame", twin))
 
     early_score = scored(
         band,

time: 109 us -> 110 us (level)
  the two profiles are of different devices: /device:TPU:6 before, /device:TPU:1 now
where the time goes in v10:
time: 110 us
  waiting for transfers between devices  42.3 us (38%)
  starting transfers between devices  41.3 us (38%)
  Pallas kernels  24.1 us (22%)
  local copies, waits for them, and re-layouts  1.45 us (1%)
    ppermute x1, waiting for transfers between devices, per_device(): key_two = lax.ppermute(keys, 'frame', away)  14.6 us
    pallas_call x3, Pallas kernels, scored(): pl.pallas_call(functools.partial(score_kernel, heads, rule), in_specs=[SM...  8.84 us
    pallas_call x2, Pallas kernels, parts(): pl.pallas_call(functools.partial(parts_kernel, len(queries), len(keys), s...  7.3 us
    ppermute x2, starting transfers between devices, per_device(): back_odd = lax.ppermute(odd_twin, 'row', odd)  7.29 us
    ppermute x2, starting transfers between devices, per_device(): twin_odd = [lax.ppermute(query_twin[span], 'row', odd) for span in (0, 1)]  6.47 us
    ppermute x1, waiting for transfers between devices, per_device(): lax.ppermute(value_halves[0], 'frame', toward)  6.44 us
    ppermute x1, starting transfers between devices, per_device(): lax.ppermute(value_halves[1], 'frame', beyond)  5.95 us
    ppermute x2, waiting for transfers between devices, per_device(): back_odd = lax.ppermute(odd_twin, 'row', odd)  5.77 us
  transfers between devices with their start and end apart: 24, of which 6 were waited for; matrix products, arithmetic and copies ran while one was open for 0% of the time, Pallas kernels for 21%

profile of v10, /device:TPU:1, one launch (start us, length us, event | category | flops | bytes accessed | tf_op | source)
XLA Modules:
  0.0 109.6 jit_solution(8265166186363308596)
XLA Ops:
  0.0 1.3 %fusion = (bf16[1,160,1280]{2,1,0:T(8,128)(2,1)S(1)}, bf16[1,160,1280]{2,1,0:T(8,128)(2,1)S(1)}) fusion(bf16[1,160,2560]{2,1,0:T(8,128)(2,1)} %query_ref.5), kind=kLoop, calls=%fused_computation | loop fusion | bytes 1638400 | tf_op jit(solution)/shard_map/slice | solution.py:463
  1.3 2.1 %collective-permute-start.10 = (bf16[1,160,1280]{2,1,0:T(8,128)(2,1)S(1)}, bf16[1,160,1280]{2,1,0:T(8,128)(2,1)S(1)}, u32[]{:S(2)}, u32[]{:S(2)}) collective-permute-start(bf16[1,160,1280]{2,1,0:T(8,128)(2,1)S(1)} %get-tuple-element.38), channel_id=1, source_target_pairs={{0,4},{4,0},{8,12},{12,8},{16,20},{20,16},{24,28},{28,24},{1,5},{5... | collective-permute-start | bytes 1228808 | tf_op jit(solution)/shard_map/ppermute | solution.py:463
  3.4 3.3 %collective-permute-start.2 = (bf16[1,160,2560]{2,1,0:T(8,128)(2,1)}, bf16[1,160,2560]{2,1,0:T(8,128)(2,1)S(1)}, u32[]{:S(2)}, u32[]{:S(2)}) collective-permute-start(bf16[1,160,2560]{2,1,0:T(8,128)(2,1)} %refs_5_.3), channel_id=1, source_target_pairs={{0,24},{4,12},{8,0},{12,20},{16,8},{20,28},{24,16},{28,4},{1,25},{... | collective-permute-start | bytes 2457608 | tf_op jit(solution)/shard_map/ppermute | solution.py:451
  7.0 5.6 %collective-permute-done.10.refs_4_ = bf16[1,160,1280]{2,1,0:T(8,128)(2,1)S(1)} collective-permute-done((bf16[1,160,1280]{2,1,0:T(8,128)(2,1)S(1)}, bf16[1,160,1280]{2,1,0:T(8,128)(2,1)S(1)}, u32[]{:S(2)}, u32[]{:S(2)}) %collective-permute-start.10) | collective-permute-done | bytes 409632 | tf_op jit(solution)/shard_map/ppermute | solution.py:463
  12.6 2.1 %collective-permute-start.11 = (bf16[1,160,1280]{2,1,0:T(8,128)(2,1)S(1)}, bf16[1,160,1280]{2,1,0:T(8,128)(2,1)S(1)}, u32[]{:S(2)}, u32[]{:S(2)}) collective-permute-start(bf16[1,160,1280]{2,1,0:T(8,128)(2,1)S(1)} %collective-permute-done.10.refs_4_), channel_id=1, source_target_pairs={{0,1},{1,0},{2,3},{3,2},{4,5},{5,4},{6,7},{7,6},{8,9},{9,8},{10,11... | collective-permute-start | bytes 1228808 | tf_op jit(solution)/shard_map/ppermute | solution.py:469
  14.7 1.7 %collective-permute-start.9 = (s32[1,5]{1,0:T(1,128)S(1)}, s32[1,5]{1,0:T(1,128)S(1)}, u32[]{:S(2)}, u32[]{:S(2)}) collective-permute-start(s32[1,5]{1,0:T(1,128)S(1)} %copy-done.3), channel_id=1, source_target_pairs={{0,4},{4,0},{8,12},{12,8},{16,20},{20,16},{24,28},{28,24},{1,5},{5... | collective-permute-start | bytes 68 | tf_op jit(solution)/shard_map/ppermute | solution.py:464
  16.5 4.9 %collective-permute-done.9.refs_1_ = s32[1,5]{1,0:T(1,128)S(1)} collective-permute-done((s32[1,5]{1,0:T(1,128)S(1)}, s32[1,5]{1,0:T(1,128)S(1)}, u32[]{:S(2)}, u32[]{:S(2)}) %collective-permute-start.9) | collective-permute-done | bytes 52 | tf_op jit(solution)/shard_map/ppermute | solution.py:464
  21.4 4.5 %collective-permute-start.12 = (bf16[1,160,1280]{2,1,0:T(8,128)(2,1)S(1)}, bf16[1,160,1280]{2,1,0:T(8,128)(2,1)S(1)}, u32[]{:S(2)}, u32[]{:S(2)}) collective-permute-start(bf16[1,160,1280]{2,1,0:T(8,128)(2,1)S(1)} %collective-permute-done.10.refs_4_), channel_id=1, source_target_pairs={{1,2},{2,1},{5,6},{6,5},{9,10},{10,9},{13,14},{14,13},{17,18},{18,... | collective-permute-start | bytes 1228808 | tf_op jit(solution)/shard_map/ppermute | solution.py:470
  26.0 6.4 %collective-permute-done.5.refs_6_.refs_8_ = bf16[1,160,1280]{2,1,0:T(8,128)(2,1)S(1)} collective-permute-done((bf16[1,160,1280]{2,1,0:T(8,128)(2,1)S(1)}, bf16[1,160,1280]{2,1,0:T(8,128)(2,1)S(1)}, u32[]{:S(2)}, u32[]{:S(2)}) %collective-permute-start.5) | collective-permute-done | bytes 409632 | tf_op jit(solution)/shard_map/ppermute | solution.py:453
  32.4 1.3 %collective-permute-start.6 = (bf16[1,160,1280]{2,1,0:T(8,128)(2,1)S(1)}, bf16[1,160,1280]{2,1,0:T(8,128)(2,1)S(1)}, u32[]{:S(2)}, u32[]{:S(2)}) collective-permute-start(bf16[1,160,1280]{2,1,0:T(8,128)(2,1)S(1)} %get-tuple-element.39), channel_id=1, source_target_pairs={{4,12},{8,0},{12,20},{16,8},{20,28},{24,16},{5,13},{9,1},{13,21},{... | collective-permute-start | bytes 1228808 | tf_op jit(solution)/shard_map/ppermute | solution.py:455
  33.7 6.0 %collective-permute-start.7 = (bf16[1,160,1280]{2,1,0:T(8,128)(2,1)S(1)}, bf16[1,160,1280]{2,1,0:T(8,128)(2,1)S(1)}, u32[]{:S(2)}, u32[]{:S(2)}) collective-permute-start(bf16[1,160,1280]{2,1,0:T(8,128)(2,1)S(1)} %get-tuple-element.39), channel_id=1, source_target_pairs={{0,24},{28,4},{1,25},{29,5},{2,26},{30,6},{3,27},{31,7}} | collective-permute-start | bytes 1228808 | tf_op jit(solution)/shard_map/ppermute | solution.py:456
  39.7 5.1 %collective-permute-start.3 = (bf16[1,160,2560]{2,1,0:T(8,128)(2,1)S(1)}, bf16[1,160,2560]{2,1,0:T(8,128)(2,1)S(1)}, u32[]{:S(2)}, u32[]{:S(2)}) collective-permute-start(bf16[1,160,2560]{2,1,0:T(8,128)(2,1)S(1)} %copy-done.2), channel_id=1, source_target_pairs={{1,2},{2,1},{5,6},{6,5},{9,10},{10,9},{13,14},{14,13},{17,18},{18,... | collective-permute-start | bytes 2457608 | tf_op jit(solution)/shard_map/ppermute | solution.py:466
  44.9 1.9 %collective-permute-start.18 = (bf16[1,160,1280]{2,1,0:T(8,128)(2,1)S(1)}, bf16[1,160,1280]{2,1,0:T(8,128)(2,1)S(1)}, u32[]{:S(2)}, u32[]{:S(2)}) collective-permute-start(bf16[1,160,1280]{2,1,0:T(8,128)(2,1)S(1)} %collective-permute-done.16.refs_4_), channel_id=1, source_target_pairs={{1,2},{2,1},{5,6},{6,5},{9,10},{10,9},{13,14},{14,13},{17,18},{18,... | collective-permute-start | bytes 1228808 | tf_op jit(solution)/shard_map/ppermute | solution.py:470
  46.8 3.6 %shard_map.50 = (f32[1,160,1408]{2,1,0:T(8,128)S(1)}, bf16[1,160,1408]{2,1,0:T(8,128)(2,1)S(1)}, f32[1,160,1408]{2,1,0:T(8,128)S(1)}) custom-call(s32[1,5]{1,0:T(1,128)S(1)} %copy-done.3, s32[1,5]{1,0:T(1,128)S(1)} %collective-permute-done.9.refs_1_, bf16[1,160,1280]{2,1,0:T(8,128)(2,1)S(1)} %collective-permute-done.11.refs_2_, ...), custom_call_target="tpu_custom_call" | custom-call | flops 786432000 | bytes 4096000 | tf_op jit(solution)/shard_map/pallas_call | solution.py:170
  50.5 3.6 %collective-permute-start.14 = (bf16[1,160,1408]{2,1,0:T(8,128)(2,1)S(1)}, bf16[1,160,1408]{2,1,0:T(8,128)(2,1)S(1)}, u32[]{:S(2)}, u32[]{:S(2)}) collective-permute-start(bf16[1,160,1408]{2,1,0:T(8,128)(2,1)S(1)} %get-tuple-element.29), channel_id=1, source_target_pairs={{1,2},{2,1},{5,6},{6,5},{9,10},{10,9},{13,14},{14,13},{17,18},{18,... | collective-permute-start | bytes 1351688 | tf_op jit(solution)/shard_map/ppermute | solution.py:492
  54.2 5.0 %collective-permute-done.18.refs_3_ = bf16[1,160,1280]{2,1,0:T(8,128)(2,1)S(1)} collective-permute-done((bf16[1,160,1280]{2,1,0:T(8,128)(2,1)S(1)}, bf16[1,160,1280]{2,1,0:T(8,128)(2,1)S(1)}, u32[]{:S(2)}, u32[]{:S(2)}) %collective-permute-start.18) | collective-permute-done | bytes 409632 | tf_op jit(solution)/shard_map/ppermute | solution.py:470
  59.2 3.7 %shard_map.52 = (f32[1,160,1408]{2,1,0:T(8,128)S(1)}, bf16[1,160,1408]{2,1,0:T(8,128)(2,1)S(1)}, f32[1,160,1408]{2,1,0:T(8,128)S(1)}) custom-call(s32[1,5]{1,0:T(1,128)S(1)} %copy-done.3, s32[1,5]{1,0:T(1,128)S(1)} %collective-permute-done.9.refs_1_, bf16[1,160,1280]{2,1,0:T(8,128)(2,1)S(1)} %collective-permute-done.17.refs_2_, ...), custom_call_target="tpu_custom_call" | custom-call | flops 786432000 | bytes 4096000 | tf_op jit(solution)/shard_map/pallas_call | solution.py:170
  62.9 3.6 %collective-permute-start.20 = (bf16[1,160,1408]{2,1,0:T(8,128)(2,1)S(1)}, bf16[1,160,1408]{2,1,0:T(8,128)(2,1)S(1)}, u32[]{:S(2)}, u32[]{:S(2)}) collective-permute-start(bf16[1,160,1408]{2,1,0:T(8,128)(2,1)S(1)} %get-tuple-element.34), channel_id=1, source_target_pairs={{1,2},{2,1},{5,6},{6,5},{9,10},{10,9},{13,14},{14,13},{17,18},{18,... | collective-permute-start | bytes 1351688 | tf_op jit(solution)/shard_map/ppermute | solution.py:492
  67.1 5.8 %collective-permute-done.20.refs_3_ = bf16[1,160,1408]{2,1,0:T(8,128)(2,1)S(1)} collective-permute-done((bf16[1,160,1408]{2,1,0:T(8,128)(2,1)S(1)}, bf16[1,160,1408]{2,1,0:T(8,128)(2,1)S(1)}, u32[]{:S(2)}, u32[]{:S(2)}) %collective-permute-start.20) | collective-permute-done | bytes 450592 | tf_op jit(solution)/shard_map/ppermute | solution.py:492
  72.9 3.3 %collective-permute-start.8 = (bf16[1,160,2560]{2,1,0:T(8,128)(2,1)S(1)}, bf16[1,160,2560]{2,1,0:T(8,128)(2,1)S(1)}, u32[]{:S(2)}, u32[]{:S(2)}) collective-permute-start(bf16[1,160,2560]{2,1,0:T(8,128)(2,1)S(1)} %copy-done), channel_id=1, source_target_pairs={{1,2},{2,1},{5,6},{6,5},{9,10},{10,9},{13,14},{14,13},{17,18},{18,... | collective-permute-start | bytes 2457608 | tf_op jit(solution)/shard_map/ppermute | solution.py:468
  76.4 1.2 %shard_map.51 = (bf16[1,160,1280]{2,1,0:T(8,128)(2,1)S(1)}, f32[160,128]{1,0:T(8,128)S(1)}) custom-call(s32[1,5]{1,0:T(1,128)S(1)} %copy-done.3, f32[1,160,1408]{2,1,0:T(8,128)S(1)} %get-tuple-element.27.refs_0_, f32[1,160,1408]{2,1,0:T(8,128)S(1)} %collective-permute-done.13.refs_1_, bf16[1,160,1408]{2,1,0:T(8,128)(2,1)S(1)} %collective-permute-done.14.refs_2_), custom_call_target="tpu_custom_call" | custom-call | flops 1351680 | bytes 1802240 | tf_op jit(solution)/shard_map/pallas_call | solution.py:224
  77.6 1.2 %shard_map.53 = bf16[1,160,1408]{2,1,0:T(8,128)(2,1)S(1)} custom-call(s32[1,5]{1,0:T(1,128)S(1)} %copy-done.3, f32[160,128]{1,0:T(8,128)S(1)} %get-tuple-element.31.refs_0_, f32[1,160,1408]{2,1,0:T(8,128)S(1)} %get-tuple-element.32.refs_1_, f32[1,160,1408]{2,1,0:T(8,128)S(1)} %collective-permute-done.19.refs_2_, ...), custom_call_target="tpu_custom_call" | custom-call | flops 1351680 | bytes 1802240 | tf_op jit(solution)/shard_map/pallas_call | solution.py:224
  78.9 0.9 collective-permute-start.21
  79.8 0.6 collective-permute-start.15
  80.4 14.6 %collective-permute-done.refs_0_ = bf16[1,160,2560]{2,1,0:T(8,128)(2,1)S(1)} collective-permute-done((bf16[1,160,2560]{2,1,0:T(8,128)(2,1)S(1)}, bf16[1,160,2560]{2,1,0:T(8,128)(2,1)S(1)}, u32[]{:S(2)}, u32[]{:S(2)}) %collective-permute-start) | collective-permute-done | bytes 819232 | tf_op jit(solution)/shard_map/ppermute | solution.py:459
  95.0 2.0 %shard_map.46 = (bf16[1,20,160,160]{3,2,1,0:T(8,128)(2,1)S(1)}, f32[2,160,128]{2,1,0:T(8,128)S(1)}) custom-call(s32[1,5]{1,0:T(1,128)S(1)} %copy-done.3, bf16[1,160,2560]{2,1,0:T(8,128)(2,1)S(1)} %copy-done.1, bf16[1,160,2560]{2,1,0:T(8,128)(2,1)S(1)} %collective-permute-done.refs_0_), custom_call_target="tpu_custom_call" | custom-call | flops 131072000 | bytes 2457600 | tf_op jit(solution)/shard_map/pallas_call | solution.py:267
  96.9 3.5 %shard_map.48 = (bf16[2,20,160,160]{3,2,1,0:T(8,128)(2,1)S(1)}, f32[2,160,128]{2,1,0:T(8,128)S(1)}) custom-call(s32[1,5]{1,0:T(1,128)S(1)} %copy-done.3, bf16[1,160,2560]{2,1,0:T(8,128)(2,1)S(1)} %copy-done.1, bf16[1,160,2560]{2,1,0:T(8,128)(2,1)S(1)} %collective-permute-done.2.refs_0_.refs_6_, bf16[1,160,2560]{2,1,0:T(8,128)(2,1)S(1)} %collective-permute-done.3.refs_1_), custom_call_target="tpu_custom_call" | custom-call | flops 262144000 | bytes 2457600 | tf_op jit(solution)/shard_map/pallas_call | solution.py:267
  100.5 3.4 %shard_map.47 = (bf16[2,20,160,160]{3,2,1,0:T(8,128)(2,1)S(1)}, f32[2,160,128]{2,1,0:T(8,128)S(1)}) custom-call(s32[1,5]{1,0:T(1,128)S(1)} %copy-done.3, bf16[1,160,2560]{2,1,0:T(8,128)(2,1)S(1)} %copy-done.1, bf16[1,160,2560]{2,1,0:T(8,128)(2,1)S(1)} %copy-done.2, bf16[1,160,2560]{2,1,0:T(8,128)(2,1)S(1)} %collective-permute-done.1.refs_1_), custom_call_target="tpu_custom_call" | custom-call | flops 262144000 | bytes 2457600 | tf_op jit(solution)/shard_map/pallas_call | solution.py:267
  103.8 2.4 %shard_map.49.near_ref = f32[1,160,2688]{2,1,0:T(8,128)S(1)} custom-call(bf16[2,20,160,160]{3,2,1,0:T(8,128)(2,1)S(1)} %get-tuple-element.23.refs_0_, bf16[2,20,160,160]{3,2,1,0:T(8,128)(2,1)S(1)} %get-tuple-element.24.refs_1_, f32[2,160,128]{2,1,0:T(8,128)S(1)} %get-tuple-element.25.refs_2_, f32[2,160,128]{2,1,0:T(8,128)S(1)} %get-tuple-element.26.refs_3_, ...), custom_call_target="tpu_custom_call" | custom-call | flops 524288000 | bytes 6553600 | tf_op jit(solution)/shard_map/pallas_call | solution.py:323
  106.3 0.8 shard_map.54
  107.0 1.4 %shard_map.55.refs_0_ = bf16[1,160,2560]{2,1,0:T(8,128)(2,1)} custom-call(bf16[1,20,160,160]{3,2,1,0:T(8,128)(2,1)S(1)} %get-tuple-element.21.weight_ref, bf16[160,128]{1,0:T(8,128)(2,1)S(1)} %get-tuple-element.35.coef_ref, bf16[1,160,2048]{2,1,0:T(8,128)(2,1)S(1)} %collective-permute-done.23.value_ref, f32[1,160,2560]{2,1,0:T(8,128)S(1)} %get-tuple-element.36.base_ref), custom_call_target="tpu_custom_call" | custom-call | flops 104857600 | bytes 2621440 | tf_op jit(solution)/shard_map/pallas_call | solution.py:409
  108.4 1.0 shard_map.56
  (39 shorter events, 1.2 us)
Async XLA Ops:
  0.0 39.7 %copy-start.2 = (bf16[1,160,2560]{2,1,0:T(8,128)(2,1)S(1)}, bf16[1,160,2560]{2,1,0:T(8,128)(2,1)}, u32[]{:S(2)}) copy-start(bf16[1,160,2560]{2,1,0:T(8,128)(2,1)} %refs_5_.3) | copy-start | bytes 2457604
  0.0 6.8 %copy-start = (bf16[1,160,2560]{2,1,0:T(8,128)(2,1)S(1)}, bf16[1,160,2560]{2,1,0:T(8,128)(2,1)}, u32[]{:S(2)}) copy-start(bf16[1,160,2560]{2,1,0:T(8,128)(2,1)} %refs_7_.3) | copy-start | bytes 2457604
  0.0 14.7 %copy-start.3 = (s32[1,5]{1,0:T(1,128)S(1)}, s32[1,5]{1,0:T(1,128)}, u32[]{:S(2)}) copy-start(s32[1,5]{1,0:T(1,128)} %band_ref.9) | copy-start | bytes 64
  1.3 11.3 %collective-permute-start.10 = (bf16[1,160,1280]{2,1,0:T(8,128)(2,1)S(1)}, bf16[1,160,1280]{2,1,0:T(8,128)(2,1)S(1)}, u32[]{:S(2)}, u32[]{:S(2)}) collective-permute-start(bf16[1,160,1280]{2,1,0:T(8,128)(2,1)S(1)} %get-tuple-element.38), channel_id=1, source_target_pairs={{0,4},{4,0},{8,12},{12,8},{16,20},{20,16},{24,28},{28,24},{1,5},{5... | collective-permute-start | bytes 1228808 | tf_op jit(solution)/shard_map/ppermute | solution.py:463
  3.4 41.4 %collective-permute-start.2 = (bf16[1,160,2560]{2,1,0:T(8,128)(2,1)}, bf16[1,160,2560]{2,1,0:T(8,128)(2,1)S(1)}, u32[]{:S(2)}, u32[]{:S(2)}) collective-permute-start(bf16[1,160,2560]{2,1,0:T(8,128)(2,1)} %refs_5_.3), channel_id=1, source_target_pairs={{0,24},{4,12},{8,0},{12,20},{16,8},{20,28},{24,16},{28,4},{1,25},{... | collective-permute-start | bytes 2457608 | tf_op jit(solution)/shard_map/ppermute | solution.py:451
  6.8 25.6 %collective-permute-start.5 = (bf16[1,160,1280]{2,1,0:T(8,128)(2,1)S(1)}, bf16[1,160,1280]{2,1,0:T(8,128)(2,1)S(1)}, u32[]{:S(2)}, u32[]{:S(2)}) collective-permute-start(bf16[1,160,1280]{2,1,0:T(8,128)(2,1)S(1)} %get-tuple-element.40), channel_id=1, source_target_pairs={{0,24},{4,12},{8,0},{12,20},{16,8},{20,28},{24,16},{28,4},{1,25},{... | collective-permute-start | bytes 1228808 | tf_op jit(solution)/shard_map/ppermute | solution.py:453
  7.0 26.6 %collective-permute-start.16 = (bf16[1,160,1280]{2,1,0:T(8,128)(2,1)S(1)}, bf16[1,160,1280]{2,1,0:T(8,128)(2,1)S(1)}, u32[]{:S(2)}, u32[]{:S(2)}) collective-permute-start(bf16[1,160,1280]{2,1,0:T(8,128)(2,1)S(1)} %get-tuple-element.37), channel_id=1, source_target_pairs={{0,4},{4,0},{8,12},{12,8},{16,20},{20,16},{24,28},{28,24},{1,5},{5... | collective-permute-start | bytes 1228808 | tf_op jit(solution)/shard_map/ppermute | solution.py:463
  12.6 27.0 %collective-permute-start.11 = (bf16[1,160,1280]{2,1,0:T(8,128)(2,1)S(1)}, bf16[1,160,1280]{2,1,0:T(8,128)(2,1)S(1)}, u32[]{:S(2)}, u32[]{:S(2)}) collective-permute-start(bf16[1,160,1280]{2,1,0:T(8,128)(2,1)S(1)} %collective-permute-done.10.refs_4_), channel_id=1, source_target_pairs={{0,1},{1,0},{2,3},{3,2},{4,5},{5,4},{6,7},{7,6},{8,9},{9,8},{10,11... | collective-permute-start | bytes 1228808 | tf_op jit(solution)/shard_map/ppermute | solution.py:469
  14.7 6.7 %collective-permute-start.9 = (s32[1,5]{1,0:T(1,128)S(1)}, s32[1,5]{1,0:T(1,128)S(1)}, u32[]{:S(2)}, u32[]{:S(2)}) collective-permute-start(s32[1,5]{1,0:T(1,128)S(1)} %copy-done.3), channel_id=1, source_target_pairs={{0,4},{4,0},{8,12},{12,8},{16,20},{20,16},{24,28},{28,24},{1,5},{5... | collective-permute-start | bytes 68 | tf_op jit(solution)/shard_map/ppermute | solution.py:464
  21.4 23.4 %collective-permute-start.12 = (bf16[1,160,1280]{2,1,0:T(8,128)(2,1)S(1)}, bf16[1,160,1280]{2,1,0:T(8,128)(2,1)S(1)}, u32[]{:S(2)}, u32[]{:S(2)}) collective-permute-start(bf16[1,160,1280]{2,1,0:T(8,128)(2,1)S(1)} %collective-permute-done.10.refs_4_), channel_id=1, source_target_pairs={{1,2},{2,1},{5,6},{6,5},{9,10},{10,9},{13,14},{14,13},{17,18},{18,... | collective-permute-start | bytes 1228808 | tf_op jit(solution)/shard_map/ppermute | solution.py:470
  32.4 18.0 %collective-permute-start.6 = (bf16[1,160,1280]{2,1,0:T(8,128)(2,1)S(1)}, bf16[1,160,1280]{2,1,0:T(8,128)(2,1)S(1)}, u32[]{:S(2)}, u32[]{:S(2)}) collective-permute-start(bf16[1,160,1280]{2,1,0:T(8,128)(2,1)S(1)} %get-tuple-element.39), channel_id=1, source_target_pairs={{4,12},{8,0},{12,20},{16,8},{20,28},{24,16},{5,13},{9,1},{13,21},{... | collective-permute-start | bytes 1228808 | tf_op jit(solution)/shard_map/ppermute | solution.py:455
  33.7 16.8 %collective-permute-start.7 = (bf16[1,160,1280]{2,1,0:T(8,128)(2,1)S(1)}, bf16[1,160,1280]{2,1,0:T(8,128)(2,1)S(1)}, u32[]{:S(2)}, u32[]{:S(2)}) collective-permute-start(bf16[1,160,1280]{2,1,0:T(8,128)(2,1)S(1)} %get-tuple-element.39), channel_id=1, source_target_pairs={{0,24},{28,4},{1,25},{29,5},{2,26},{30,6},{3,27},{31,7}} | collective-permute-start | bytes 1228808 | tf_op jit(solution)/shard_map/ppermute | solution.py:456
  39.7 26.9 %collective-permute-start.3 = (bf16[1,160,2560]{2,1,0:T(8,128)(2,1)S(1)}, bf16[1,160,2560]{2,1,0:T(8,128)(2,1)S(1)}, u32[]{:S(2)}, u32[]{:S(2)}) collective-permute-start(bf16[1,160,2560]{2,1,0:T(8,128)(2,1)S(1)} %copy-done.2), channel_id=1, source_target_pairs={{1,2},{2,1},{5,6},{6,5},{9,10},{10,9},{13,14},{14,13},{17,18},{18,... | collective-permute-start | bytes 2457608 | tf_op jit(solution)/shard_map/ppermute | solution.py:466
  44.8 9.4 %collective-permute-start.17 = (bf16[1,160,1280]{2,1,0:T(8,128)(2,1)S(1)}, bf16[1,160,1280]{2,1,0:T(8,128)(2,1)S(1)}, u32[]{:S(2)}, u32[]{:S(2)}) collective-permute-start(bf16[1,160,1280]{2,1,0:T(8,128)(2,1)S(1)} %collective-permute-done.16.refs_4_), channel_id=1, source_target_pairs={{0,1},{1,0},{2,3},{3,2},{4,5},{5,4},{6,7},{7,6},{8,9},{9,8},{10,11... | collective-permute-start | bytes 1228808 | tf_op jit(solution)/shard_map/ppermute | solution.py:469
  44.9 14.3 %collective-permute-start.18 = (bf16[1,160,1280]{2,1,0:T(8,128)(2,1)S(1)}, bf16[1,160,1280]{2,1,0:T(8,128)(2,1)S(1)}, u32[]{:S(2)}, u32[]{:S(2)}) collective-permute-start(bf16[1,160,1280]{2,1,0:T(8,128)(2,1)S(1)} %collective-permute-done.16.refs_4_), channel_id=1, source_target_pairs={{1,2},{2,1},{5,6},{6,5},{9,10},{10,9},{13,14},{14,13},{17,18},{18,... | collective-permute-start | bytes 1228808 | tf_op jit(solution)/shard_map/ppermute | solution.py:470
  50.4 22.5 %collective-permute-start.13 = (f32[1,160,1408]{2,1,0:T(8,128)S(1)}, f32[1,160,1408]{2,1,0:T(8,128)S(1)}, u32[]{:S(2)}, u32[]{:S(2)}) collective-permute-start(f32[1,160,1408]{2,1,0:T(8,128)S(1)} %get-tuple-element.28), channel_id=1, source_target_pairs={{0,1},{1,0},{2,3},{3,2},{4,5},{5,4},{6,7},{7,6},{8,9},{9,8},{10,11... | collective-permute-start | bytes 2703368 | tf_op jit(solution)/shard_map/ppermute | solution.py:491
  50.5 16.1 %collective-permute-start.14 = (bf16[1,160,1408]{2,1,0:T(8,128)(2,1)S(1)}, bf16[1,160,1408]{2,1,0:T(8,128)(2,1)S(1)}, u32[]{:S(2)}, u32[]{:S(2)}) collective-permute-start(bf16[1,160,1408]{2,1,0:T(8,128)(2,1)S(1)} %get-tuple-element.29), channel_id=1, source_target_pairs={{1,2},{2,1},{5,6},{6,5},{9,10},{10,9},{13,14},{14,13},{17,18},{18,... | collective-permute-start | bytes 1351688 | tf_op jit(solution)/shard_map/ppermute | solution.py:492
  62.8 13.5 %collective-permute-start.19 = (f32[1,160,1408]{2,1,0:T(8,128)S(1)}, f32[1,160,1408]{2,1,0:T(8,128)S(1)}, u32[]{:S(2)}, u32[]{:S(2)}) collective-permute-start(f32[1,160,1408]{2,1,0:T(8,128)S(1)} %get-tuple-element.33), channel_id=1, source_target_pairs={{0,1},{1,0},{2,3},{3,2},{4,5},{5,4},{6,7},{7,6},{8,9},{9,8},{10,11... | collective-permute-start | bytes 2703368 | tf_op jit(solution)/shard_map/ppermute | solution.py:491
  62.9 10.0 %collective-permute-start.20 = (bf16[1,160,1408]{2,1,0:T(8,128)(2,1)S(1)}, bf16[1,160,1408]{2,1,0:T(8,128)(2,1)S(1)}, u32[]{:S(2)}, u32[]{:S(2)}) collective-permute-start(bf16[1,160,1408]{2,1,0:T(8,128)(2,1)S(1)} %get-tuple-element.34), channel_id=1, source_target_pairs={{1,2},{2,1},{5,6},{6,5},{9,10},{10,9},{13,14},{14,13},{17,18},{18,... | collective-permute-start | bytes 1351688 | tf_op jit(solution)/shard_map/ppermute | solution.py:492
  66.6 12.3 %collective-permute-start.1 = (bf16[1,160,2560]{2,1,0:T(8,128)(2,1)S(1)}, bf16[1,160,2560]{2,1,0:T(8,128)(2,1)S(1)}, u32[]{:S(2)}, u32[]{:S(2)}) collective-permute-start(bf16[1,160,2560]{2,1,0:T(8,128)(2,1)S(1)} %copy-done.2), channel_id=1, source_target_pairs={{0,1},{1,0},{2,3},{3,2},{4,5},{5,4},{6,7},{7,6},{8,9},{9,8},{10,11... | collective-permute-start | bytes 2457608 | tf_op jit(solution)/shard_map/ppermute | solution.py:465
  66.7 13.1 %collective-permute-start.4 = (bf16[1,160,2560]{2,1,0:T(8,128)(2,1)S(1)}, bf16[1,160,2560]{2,1,0:T(8,128)(2,1)S(1)}, u32[]{:S(2)}, u32[]{:S(2)}) collective-permute-start(bf16[1,160,2560]{2,1,0:T(8,128)(2,1)S(1)} %copy-done), channel_id=1, source_target_pairs={{0,1},{1,0},{2,3},{3,2},{4,5},{5,4},{6,7},{7,6},{8,9},{9,8},{10,11... | collective-permute-start | bytes 2457608 | tf_op jit(solution)/shard_map/ppermute | solution.py:467
  72.9 22.1 %collective-permute-start = (bf16[1,160,2560]{2,1,0:T(8,128)(2,1)S(1)}, bf16[1,160,2560]{2,1,0:T(8,128)(2,1)S(1)}, u32[]{:S(2)}, u32[]{:S(2)}) collective-permute-start(bf16[1,160,2560]{2,1,0:T(8,128)(2,1)S(1)} %copy-done.2), channel_id=1, source_target_pairs={{24,0},{12,4},{0,8},{20,12},{8,16},{28,20},{16,24},{4,28},{25,1},{... | collective-permute-start | bytes 2457608 | tf_op jit(solution)/shard_map/ppermute | solution.py:459
  72.9 30.9 %collective-permute-start.8 = (bf16[1,160,2560]{2,1,0:T(8,128)(2,1)S(1)}, bf16[1,160,2560]{2,1,0:T(8,128)(2,1)S(1)}, u32[]{:S(2)}, u32[]{:S(2)}) collective-permute-start(bf16[1,160,2560]{2,1,0:T(8,128)(2,1)S(1)} %copy-done), channel_id=1, source_target_pairs={{1,2},{2,1},{5,6},{6,5},{9,10},{10,9},{13,14},{14,13},{17,18},{18,... | collective-permute-start | bytes 2457608 | tf_op jit(solution)/shard_map/ppermute | solution.py:468
  76.3 30.7 %collective-permute-start.23 = (bf16[1,160,2048]{2,1,0:T(8,128)(2,1)S(1)}, bf16[1,160,2048]{2,1,0:T(8,128)(2,1)S(1)}, u32[]{:S(2)}, u32[]{:S(2)}) collective-permute-start(bf16[1,160,2048]{2,1,0:T(8,128)(2,1)S(1)} %slice.23), channel_id=1, source_target_pairs={{24,0},{12,4},{0,8},{20,12},{8,16},{28,20},{16,24},{4,28},{25,1},{... | collective-permute-start | bytes 1966088 | tf_op jit(solution)/shard_map/ppermute | solution.py:460
  77.6 17.3 %copy-start.1 = (bf16[1,160,2560]{2,1,0:T(8,128)(2,1)S(1)}, bf16[1,160,2560]{2,1,0:T(8,128)(2,1)}, u32[]{:S(2)}) copy-start(bf16[1,160,2560]{2,1,0:T(8,128)(2,1)} %query_ref.5) | copy-start | bytes 2457604
  78.9 27.4 %collective-permute-start.21 = (bf16[1,160,1408]{2,1,0:T(8,128)(2,1)S(1)}, bf16[1,160,1408]{2,1,0:T(8,128)(2,1)S(1)}, u32[]{:S(2)}, u32[]{:S(2)}) collective-permute-start(bf16[1,160,1408]{2,1,0:T(8,128)(2,1)S(1)} %shard_map.53), channel_id=1, source_target_pairs={{0,4},{4,0},{8,12},{12,8},{16,20},{20,16},{24,28},{28,24},{1,5},{5... | collective-permute-start | bytes 1351688 | tf_op jit(solution)/shard_map/ppermute | solution.py:501
  79.8 26.5 %collective-permute-start.15 = (bf16[1,160,1280]{2,1,0:T(8,128)(2,1)S(1)}, bf16[1,160,1280]{2,1,0:T(8,128)(2,1)S(1)}, u32[]{:S(2)}, u32[]{:S(2)}) collective-permute-start(bf16[1,160,1280]{2,1,0:T(8,128)(2,1)S(1)} %get-tuple-element.30), channel_id=1, source_target_pairs={{0,4},{4,0},{8,12},{12,8},{16,20},{20,16},{24,28},{28,24},{1,5},{5... | collective-permute-start | bytes 1228808 | tf_op jit(solution)/shard_map/ppermute | solution.py:501
  95.0 13.5 %collective-permute-start.22 = (bf16[1,160,512]{2,1,0:T(8,128)(2,1)S(1)}, bf16[1,160,512]{2,1,0:T(8,128)(2,1)S(1)}, u32[]{:S(2)}, u32[]{:S(2)}) collective-permute-start(bf16[1,160,512]{2,1,0:T(8,128)(2,1)S(1)} %slice.22), channel_id=1, source_target_pairs={{24,0},{12,4},{0,8},{20,12},{8,16},{28,20},{16,24},{4,28},{25,1},{... | collective-permute-start | bytes 491528 | tf_op jit(solution)/shard_map/ppermute | solution.py:460
